TPU v7x, 32 devices: a whole 2x2x4 slice. The times are simulated.
32 devices in a mesh: dp: 2 (over x), row: 4 (over y, core), col: 4 (over z).
Axes of the slice: x: 2, y: 2, z: 4, core: 2. Of those that a mesh axis runs over, the one named last changes fastest.
Arguments:
- tokens: bfloat16 [16384, 2048], P(('dp', 'col'), 'row'), may hold values from -6 to 6
- cotangent: bfloat16 [16384, 2048], P(('dp', 'col'), 'row'), may hold values from -6 to 6
- qkv_weight: bfloat16 [3, 2048, 2048], P(None, 'row', 'col')
- attn_weight: bfloat16 [2048, 2048], P('col', 'row')
- expand_weight: bfloat16 [2, 2048, 8192], P(None, 'row', 'col'), may hold values from -0.125 to 0.125
- reduce_weight: bfloat16 [8192, 2048], P('col', 'row')
- headnorm_gain: float32 [2, 2048], P(None, 'col'), may hold values from 0.6 to 1.8
- post_gain: float32 [2, 2048], P(None, 'row'), may hold values from 0.5 to 1.5
- qkv_lowrank: bfloat16 [3, 8, 2048, 16], P(None, None, 'row'), may hold values from -0.125 to 0.125
- qkv_uprank: bfloat16 [3, 8, 16, 2048], P(None, None, None, 'col'), may hold values from -1.5 to 1.5
- attn_lowrank: bfloat16 [8, 2048, 16], P(None, 'col'), may hold values from -0.125 to 0.125
- attn_uprank: bfloat16 [8, 16, 2048], P(None, None, 'row'), may hold values from -1.5 to 1.5
- expand_lowrank: bfloat16 [2, 8, 2048, 16], P(None, None, 'row'), may hold values from -0.125 to 0.125
- expand_uprank: bfloat16 [2, 8, 16, 8192], P(None, None, None, 'col'), may hold values from -1.5 to 1.5
- reduce_lowrank: bfloat16 [8, 8192, 16], P(None, 'col'), may hold values from -0.0625 to 0.0625
- reduce_uprank: bfloat16 [8, 16, 2048], P(None, None, 'row'), may hold values from -1.5 to 1.5
- prefix_length: int32 [8], replicated, may hold values from 204 to 1024, as said below
- adapter_set: int32 [8], replicated, may hold values from 0 to 7
Outputs:
- layer_out: bfloat16 [16384, 2048], P(('dp', 'col'), 'row')
- input_grad: float32 [16384, 2048], P(('dp', 'col'), 'row')
- qkv_lowgrad: float32 [3, 8, 2048, 16], P(None, None, 'row')
- qkv_upgrad: float32 [3, 8, 16, 2048], P(None, None, None, 'col')
- attn_lowgrad: float32 [8, 2048, 16], P(None, 'col')
- attn_upgrad: float32 [8, 16, 2048], P(None, None, 'row')
- expand_lowgrad: float32 [2, 8, 2048, 16], P(None, None, 'row')
- expand_upgrad: float32 [2, 8, 16, 8192], P(None, None, None, 'col')
- reduce_lowgrad: float32 [8, 8192, 16], P(None, 'col')
- reduce_upgrad: float32 [8, 16, 2048], P(None, None, 'row')
Inputs may be any that keep to these rules, and one draw needn't show every extreme that they name: The first prefix_length tokens of a sequence see one another; later tokens see the prefix and every earlier token.
All inputs are finite; a program needn't handle non-finite values.
Results may differ from a plain program's by a relative error of at most 0.02.
Values may be sent and summed in bfloat16 or wider, within the bound.
A program may use at most 384 MiB of HBM per device.

v0:
```python
import jax
import jax.numpy as jnp
from jax import lax
from jax.sharding import PartitionSpec as P

D = 2048
HEAD = 128
ADAPTER_RANK = 16
SETS = 8
SEQUENCE_LENGTH = 2048


EPS = 1e-06
THETA = 500000.0
ADAPTER_FACTOR = 0.5
NEG = -1e30


def via_col_row(input_rows, weight_matrix, adapt_mat, compute, seq_pick):
    gathered = lax.all_gather(input_rows, "col", axis=0, tiled=True)
    main, inner_value = compute(gathered, weight_matrix, adapt_mat, seq_pick, False)
    return (
        lax.psum_scatter(main, "row", scatter_dimension=0, tiled=True),
        lax.psum_scatter(inner_value, "row", scatter_dimension=0, tiled=True),
    )


def via_row_col(input_rows, weight_matrix, adapt_mat, compute, seq_pick):
    gathered = lax.all_gather(input_rows, "row", axis=0, tiled=True)
    main, inner_value = compute(gathered, weight_matrix, adapt_mat, seq_pick, False)
    return (
        lax.psum_scatter(main, "col", scatter_dimension=0, tiled=True),
        lax.psum_scatter(inner_value, "col", scatter_dimension=0, tiled=True),
    )


def row_total(values):
    return lax.psum(jnp.sum(values, axis=-1), "row")


def head_totals(first, second):
    return lax.psum((jnp.sum(first, axis=-1), jnp.sum(second, axis=-1)), "col")


def sum_col_tokens(values):
    return lax.psum(values.astype(jnp.bfloat16), ("dp", "col")).astype(jnp.float32)


def sum_row_tokens(values):
    return lax.psum(values.astype(jnp.bfloat16), ("dp", "row")).astype(jnp.float32)


def set_rows(group_sets, first_row, item_count):
    sequence = (first_row + jnp.arange(item_count, dtype=jnp.int32)) // SEQUENCE_LENGTH
    member = sequence[:, None] == jnp.arange(group_sets.shape[0], dtype=jnp.int32)[None, :]
    chosen = jnp.sum(jnp.where(member, group_sets[None, :], 0), axis=1)
    return (chosen[:, None] == jnp.arange(SETS, dtype=jnp.int32)[None, :]).astype(jnp.bfloat16)


def widen(inner_value, onehot, part_list):
    rows = inner_value.shape[0]
    spread = onehot[:, None, :, None] * inner_value.reshape(rows, part_list, 1, ADAPTER_RANK)
    return spread.reshape(rows, part_list, SETS * ADAPTER_RANK)


def adapter_in(gathered, pick, lowrank):
    part_list = lowrank.shape[0]
    width_in = lowrank.shape[2]
    item_count = pick.shape[0]
    chosen = jnp.einsum("sk,pkdr->sdpr", pick, lowrank, preferred_element_type=jnp.float32).astype(
        jnp.bfloat16
    )
    chosen = chosen.reshape(item_count, width_in, part_list * ADAPTER_RANK)
    product_value = jnp.einsum(
        "ehm,emx->ehx",
        gathered.reshape(item_count, SEQUENCE_LENGTH, width_in),
        chosen,
        preferred_element_type=jnp.float32,
    )
    return product_value.reshape(item_count * SEQUENCE_LENGTH, part_list * ADAPTER_RANK)


def adapter_back(gathered, pick, upward_rank):
    part_list = upward_rank.shape[0]
    width_out = upward_rank.shape[-1]
    item_count = pick.shape[0]
    chosen = jnp.einsum(
        "sk,pkre->sper", pick, upward_rank, preferred_element_type=jnp.float32
    ).astype(jnp.bfloat16)
    product_value = jnp.einsum(
        "slpe,sper->slpr",
        gathered.reshape(item_count, SEQUENCE_LENGTH, part_list, width_out),
        chosen,
        preferred_element_type=jnp.float32,
    )
    return ADAPTER_FACTOR * product_value.reshape(
        item_count * SEQUENCE_LENGTH, part_list * ADAPTER_RANK
    )


def adapter_out(wide_output, upward_rank):
    part_list = upward_rank.shape[0]
    flat_up = upward_rank.reshape(part_list, SETS * ADAPTER_RANK, upward_rank.shape[-1])
    return ADAPTER_FACTOR * jnp.einsum(
        "tpk,pke->tpe", wide_output, flat_up, preferred_element_type=jnp.float32
    )


def adapter_grad_in(wide_output, lowrank):
    part_list = lowrank.shape[0]
    width_in = lowrank.shape[2]
    flat_low = lowrank.transpose(0, 1, 3, 2).reshape(part_list, SETS * ADAPTER_RANK, width_in)
    return jnp.einsum("tpk,pkd->td", wide_output, flat_low, preferred_element_type=jnp.float32)


def up_grad(wide_output, gradient_list):
    part_list = gradient_list.shape[1]
    total_sum = ADAPTER_FACTOR * jnp.einsum(
        "jox,joq->oxq", wide_output, gradient_list, preferred_element_type=jnp.float32
    )
    return total_sum.reshape(part_list, SETS, ADAPTER_RANK, gradient_list.shape[2])


def low_grad(input_rows, wide_output):
    part_list = wide_output.shape[1]
    total_sum = jnp.einsum(
        "td,tpk->pkd", input_rows, wide_output, preferred_element_type=jnp.float32
    )
    return total_sum.reshape(part_list, SETS, ADAPTER_RANK, input_rows.shape[1]).transpose(
        0, 1, 3, 2
    )


def swiglu(gate, upper):
    return jax.nn.silu(gate) * upper


def norm_back(grad, values, scale, gain):
    weighted = gain * grad
    inner_sum = row_total(weighted * values)
    return scale[:, None] * weighted - values * (scale**3 * inner_sum / D)[:, None]


def qkv_forward(gathered, weight_matrix, low_flat, pick, per_row):
    input_rows = gathered[:, 0]
    main = jnp.einsum("td,pde->tpe", input_rows, weight_matrix, preferred_element_type=jnp.float32)
    lowrank = low_flat.reshape(3, SETS, low_flat.shape[1], ADAPTER_RANK)
    return (main, adapter_in(input_rows, pick, lowrank))


def expand_forward(gathered, weight_matrix, low_flat, pick, per_row):
    input_rows = gathered[:, 0]
    main = jnp.einsum("td,pdf->tpf", input_rows, weight_matrix, preferred_element_type=jnp.float32)
    lowrank = low_flat.reshape(2, SETS, low_flat.shape[1], ADAPTER_RANK)
    return (main, adapter_in(input_rows, pick, lowrank))


def single_forward(gathered, weight_matrix, low_four, pick, per_row):
    input_rows = gathered[:, 0]
    main = jnp.dot(input_rows, weight_matrix[0, 0], preferred_element_type=jnp.float32)
    return (main, adapter_in(input_rows, pick, low_four))


def single_backward(gathered, weight_matrix, up_flat, pick, per_row):
    main = jnp.einsum(
        "te,fe->tf", gathered[:, 0], weight_matrix, preferred_element_type=jnp.float32
    )
    upward_rank = up_flat.reshape(1, SETS, ADAPTER_RANK, up_flat.shape[1])
    return (main, adapter_back(gathered, pick, upward_rank))


def multi_backward(gathered, weight_matrix, up_flat, pick, per_row):
    part_list = weight_matrix.shape[0]
    main = jnp.einsum("tpf,pdf->td", gathered, weight_matrix, preferred_element_type=jnp.float32)
    upward_rank = up_flat.reshape(part_list, SETS, ADAPTER_RANK, up_flat.shape[2])
    return (main, adapter_back(gathered, pick, upward_rank))


def shards(
    tokens,
    cotangent,
    qkv_weight,
    attn_weight,
    expand_weight,
    reduce_weight,
    headnorm_gain,
    post_gain,
    qkv_lowrank,
    qkv_uprank,
    attn_lowrank,
    attn_uprank,
    expand_lowrank,
    expand_uprank,
    reduce_lowrank,
    reduce_uprank,
    prefix_length,
    adapter_set,
):
    rows_a = tokens.shape[0]
    group_rows = rows_a * lax.axis_size("col")
    rows_b = group_rows // lax.axis_size("row")
    group_seqs = group_rows // SEQUENCE_LENGTH
    group_first = lax.axis_index("dp") * group_seqs
    group_sets = lax.dynamic_slice_in_dim(adapter_set, group_first, group_seqs)
    group_prefix = lax.dynamic_slice_in_dim(prefix_length, group_first, group_seqs)
    seq_pick = (group_sets[:, None] == jnp.arange(SETS, dtype=jnp.int32)[None, :]).astype(
        jnp.bfloat16
    )
    pick_a = set_rows(group_sets, lax.axis_index("col") * rows_a, rows_a)
    pick_b = set_rows(group_sets, lax.axis_index("row") * rows_b, rows_b)
    width_row = qkv_weight.shape[1]
    width_col = qkv_weight.shape[2]
    ff_col = expand_weight.shape[2]
    qkv_low_flat = qkv_lowrank.reshape(3 * SETS, width_row, ADAPTER_RANK)
    projected, inner_value = via_col_row(
        tokens[:, None], qkv_weight, qkv_low_flat, qkv_forward, seq_pick
    )
    qkv_wide = widen(inner_value.astype(jnp.bfloat16), pick_b, 3)
    projected = projected + adapter_out(qkv_wide, qkv_uprank)
    queries = projected[:, 0]
    keys = projected[:, 1]
    values = projected[:, 2]
    query_sq, key_sq = head_totals(queries * queries, keys * keys)
    query_scale = lax.rsqrt(query_sq / D + EPS)
    key_scale = lax.rsqrt(key_sq / D + EPS)
    query_norm = queries * query_scale[:, None] * headnorm_gain[0]
    key_norm = keys * key_scale[:, None] * headnorm_gain[1]
    local_heads = queries.shape[1] // HEAD
    half = HEAD // 2
    freq = THETA ** (-2.0 * jnp.arange(half, dtype=jnp.float32) / HEAD)
    position = (jnp.arange(rows_b, dtype=jnp.int32) % SEQUENCE_LENGTH).astype(jnp.float32)
    angle = position[:, None] * freq[None, :]
    cosine = jnp.cos(angle)[:, None, :]
    sine = jnp.sin(angle)[:, None, :]

    def rotate(source):
        heads = source.reshape(rows_b, local_heads, HEAD)
        first = heads[..., :half]
        second = heads[..., half:]
        return jnp.concatenate(
            [first * cosine - second * sine, second * cosine + first * sine], axis=-1
        )

    def unrotate(gradient_list):
        first = gradient_list[..., :half]
        second = gradient_list[..., half:]
        return jnp.concatenate(
            [first * cosine + second * sine, second * cosine - first * sine], axis=-1
        ).reshape(rows_b, local_heads * HEAD)

    query_b = rotate(query_norm).astype(jnp.bfloat16)
    key_b = rotate(key_norm).astype(jnp.bfloat16)
    value_b = values.astype(jnp.bfloat16).reshape(rows_b, local_heads, HEAD)
    block = min(512, SEQUENCE_LENGTH)
    blocks = rows_b // block
    key_pos = jnp.arange(SEQUENCE_LENGTH, dtype=jnp.int32)
    local_first = lax.axis_index("row") * (rows_b // SEQUENCE_LENGTH)
    scale = HEAD ** (-0.5)

    def scores_of(index):
        start = index * block
        seq_start = start // SEQUENCE_LENGTH * SEQUENCE_LENGTH
        which = local_first + start // SEQUENCE_LENGTH
        prefix = jnp.sum(
            jnp.where(jnp.arange(group_seqs, dtype=jnp.int32) == which, group_prefix, 0)
        )
        rows = start - seq_start + jnp.arange(block, dtype=jnp.int32)
        allowed = (key_pos[None, :] <= rows[:, None]) | (key_pos[None, :] < prefix)
        query_blk = lax.dynamic_slice_in_dim(query_b, start, block, 0)
        raw = (
            jnp.einsum("qhd,khd->hqk", query_blk, key_b, preferred_element_type=jnp.float32) * scale
        )
        return (jnp.where(allowed[None], raw, NEG), start, seq_start)

    def attend_block(index):
        scores, start, seq_start = scores_of(index)
        top = jnp.max(scores, axis=-1, keepdims=True)
        powers = jnp.exp(scores - top)
        total_sum = jnp.sum(powers, axis=-1, keepdims=True)
        weights = (powers / total_sum).astype(jnp.bfloat16)
        output = jnp.einsum("hqk,khd->qhd", weights, value_b, preferred_element_type=jnp.float32)
        return (output, (top + jnp.log(total_sum))[..., 0])

    attended, logsum = lax.map(attend_block, jnp.arange(blocks, dtype=jnp.int32))
    mixed_b = attended.reshape(rows_b, local_heads * HEAD).astype(jnp.bfloat16)
    attn_weight_four = attn_weight.reshape(1, 1, width_col, width_row)
    attn_low_four = attn_lowrank.reshape(1, SETS, width_col, ADAPTER_RANK)
    branch, inner_value = via_row_col(
        mixed_b[:, None], attn_weight_four, attn_low_four, single_forward, seq_pick
    )
    attn_wide = widen(inner_value.astype(jnp.bfloat16), pick_a, 1)
    branch = branch + adapter_out(attn_wide, attn_uprank[None])[:, 0]
    branch_scale = lax.rsqrt(row_total(branch * branch) / D + EPS)
    hidden = tokens.astype(jnp.float32) + post_gain[0] * branch * branch_scale[:, None]
    hidden_b = hidden.astype(jnp.bfloat16)
    expand_low_flat = expand_lowrank.reshape(2 * SETS, width_row, ADAPTER_RANK)
    gate_up, inner_value = via_col_row(
        hidden_b[:, None], expand_weight, expand_low_flat, expand_forward, seq_pick
    )
    expand_wide = widen(inner_value.astype(jnp.bfloat16), pick_b, 2)
    gate_up = gate_up + adapter_out(expand_wide, expand_uprank)
    gate = gate_up[:, 0]
    upper = gate_up[:, 1]
    act_b = swiglu(gate, upper).astype(jnp.bfloat16)
    reduce_weight_four = reduce_weight.reshape(1, 1, ff_col, width_row)
    reduce_low_four = reduce_lowrank.reshape(1, SETS, ff_col, ADAPTER_RANK)
    result, inner_value = via_row_col(
        act_b[:, None], reduce_weight_four, reduce_low_four, single_forward, seq_pick
    )
    reduce_wide = widen(inner_value.astype(jnp.bfloat16), pick_a, 1)
    result = result + adapter_out(reduce_wide, reduce_uprank[None])[:, 0]
    result_scale = lax.rsqrt(row_total(result * result) / D + EPS)
    layer_out = (hidden + post_gain[1] * result * result_scale[:, None]).astype(jnp.bfloat16)
    incoming = cotangent.astype(jnp.float32)
    d_result = norm_back(incoming, result, result_scale, post_gain[1]).astype(jnp.bfloat16)
    grad_reduce_up = up_grad(reduce_wide, d_result[:, None])[0]
    grad_reduce_up = sum_col_tokens(grad_reduce_up)
    reduce_up_flat = reduce_uprank.reshape(SETS * ADAPTER_RANK, width_row)
    d_act, inner_value = via_col_row(
        d_result[:, None], reduce_weight, reduce_up_flat, single_backward, seq_pick
    )
    act_wide = widen(inner_value.astype(jnp.bfloat16), pick_b, 1)
    d_act = d_act + adapter_grad_in(act_wide, reduce_lowrank[None])
    grad_reduce_low = low_grad(act_b, act_wide)[0]
    grad_reduce_low = sum_row_tokens(grad_reduce_low)
    unused, pullback = jax.vjp(swiglu, gate, upper)
    d_gate, d_upper = pullback(d_act)
    d_gate_up = jnp.stack([d_gate, d_upper], axis=1).astype(jnp.bfloat16)
    grad_expand_up = up_grad(expand_wide, d_gate_up)
    grad_expand_up = sum_row_tokens(grad_expand_up)
    expand_up_flat = expand_uprank.reshape(2 * SETS, ADAPTER_RANK, ff_col)
    d_hidden_in, inner_value = via_row_col(
        d_gate_up, expand_weight, expand_up_flat, multi_backward, seq_pick
    )
    hidden_wide = widen(inner_value.astype(jnp.bfloat16), pick_a, 2)
    d_hidden = incoming + d_hidden_in + adapter_grad_in(hidden_wide, expand_lowrank)
    grad_expand_low = low_grad(hidden_b, hidden_wide)
    grad_expand_low = sum_col_tokens(grad_expand_low)
    d_branch = norm_back(d_hidden, branch, branch_scale, post_gain[0]).astype(jnp.bfloat16)
    grad_attn_up = up_grad(attn_wide, d_branch[:, None])[0]
    grad_attn_up = sum_col_tokens(grad_attn_up)
    attn_up_flat = attn_uprank.reshape(SETS * ADAPTER_RANK, width_row)
    d_mixed, inner_value = via_col_row(
        d_branch[:, None], attn_weight, attn_up_flat, single_backward, seq_pick
    )
    mixed_wide = widen(inner_value.astype(jnp.bfloat16), pick_b, 1)
    d_mixed = (d_mixed + adapter_grad_in(mixed_wide, attn_lowrank[None])).astype(jnp.bfloat16)
    grad_attn_low = low_grad(mixed_b, mixed_wide)[0]
    grad_attn_low = sum_row_tokens(grad_attn_low)
    d_mixed_heads = d_mixed.reshape(rows_b, local_heads, HEAD)

    def back_block(index, carry):
        d_query, d_key, d_value = carry
        scores, start, seq_start = scores_of(index)
        probs = jnp.exp(
            scores - lax.dynamic_index_in_dim(logsum, index, 0, keepdims=False)[..., None]
        )
        grad_blk = lax.dynamic_slice_in_dim(d_mixed_heads, start, block, 0)
        query_blk = lax.dynamic_slice_in_dim(query_b, start, block, 0)
        d_probs = jnp.einsum("qhd,khd->hqk", grad_blk, value_b, preferred_element_type=jnp.float32)
        delta = jnp.sum(probs * d_probs, axis=-1, keepdims=True)
        d_scores = (probs * (d_probs - delta)).astype(jnp.bfloat16)
        query_part = scale * jnp.einsum(
            "hqk,khd->qhd", d_scores, key_b, preferred_element_type=jnp.float32
        )
        key_part = scale * jnp.einsum(
            "hqk,qhd->khd", d_scores, query_blk, preferred_element_type=jnp.float32
        )
        value_part = jnp.einsum(
            "hqk,qhd->khd", probs.astype(jnp.bfloat16), grad_blk, preferred_element_type=jnp.float32
        )
        d_query = lax.dynamic_update_slice_in_dim(d_query, query_part, start, 0)
        d_key = d_key + key_part
        d_value = d_value + value_part
        return (d_query, d_key, d_value)

    zeros = jnp.zeros((rows_b, local_heads, HEAD), jnp.float32)
    d_query, d_key, d_value = lax.fori_loop(0, blocks, back_block, (zeros, zeros, zeros))
    query_weighted = headnorm_gain[0] * unrotate(d_query)
    key_weighted = headnorm_gain[1] * unrotate(d_key)
    query_sum, key_sum = head_totals(query_weighted * queries, key_weighted * keys)
    d_queries = (
        query_scale[:, None] * query_weighted - queries * (query_scale**3 * query_sum / D)[:, None]
    )
    d_keys = key_scale[:, None] * key_weighted - keys * (key_scale**3 * key_sum / D)[:, None]
    d_qkv = jnp.stack(
        [d_queries, d_keys, d_value.reshape(rows_b, local_heads * HEAD)], axis=1
    ).astype(jnp.bfloat16)
    grad_qkv_up = up_grad(qkv_wide, d_qkv)
    grad_qkv_up = sum_row_tokens(grad_qkv_up)
    qkv_up_flat = qkv_uprank.reshape(3 * SETS, ADAPTER_RANK, width_col)
    d_tokens_in, inner_value = via_row_col(d_qkv, qkv_weight, qkv_up_flat, multi_backward, seq_pick)
    tokens_wide = widen(inner_value.astype(jnp.bfloat16), pick_a, 3)
    input_grad = d_hidden + d_tokens_in + adapter_grad_in(tokens_wide, qkv_lowrank)
    grad_qkv_low = low_grad(tokens, tokens_wide)
    grad_qkv_low = sum_col_tokens(grad_qkv_low)
    return (
        layer_out,
        input_grad,
        grad_qkv_low,
        grad_qkv_up,
        grad_attn_low,
        grad_attn_up,
        grad_expand_low,
        grad_expand_up,
        grad_reduce_low,
        grad_reduce_up,
    )


def solution(mesh):
    placed = (
        P(("dp", "col"), "row"),
        P(("dp", "col"), "row"),
        P(None, "row", "col"),
        P("col", "row"),
        P(None, "row", "col"),
        P("col", "row"),
        P(None, "col"),
        P(None, "row"),
        P(None, None, "row", None),
        P(None, None, None, "col"),
        P(None, "col", None),
        P(None, None, "row"),
        P(None, None, "row", None),
        P(None, None, None, "col"),
        P(None, "col", None),
        P(None, None, "row"),
        P(),
        P(),
    )
    return jax.shard_map(
        shards,
        mesh=mesh,
        in_specs=placed,
        out_specs=(
            P(("dp", "col"), "row"),
            P(("dp", "col"), "row"),
            P(None, None, "row", None),
            P(None, None, None, "col"),
            P(None, "col", None),
            P(None, None, "row"),
            P(None, None, "row", None),
            P(None, None, None, "col"),
            P(None, "col", None),
            P(None, None, "row"),
        ),
        check_vma=False,
    )
```

profile of v0, /device:TPU:0, one launch (start us, length us, event | category | flops | bytes accessed | tf_op | source)
XLA Modules:
  0.0 5515.9 jit_solution(823969466538266186)
XLA Ops:
  10.1 151.9 %all-gather.21.cloned.1.call-done = bf16[8192,512]{1,0:T(8,128)(2,1)} async-done(((bf16[2048,512]{1,0:T(8,128)(2,1)}), bf16[8192,512]{1,0:T(8,128)(2,1)}) %all-gather.21.cloned.1.call-update) | async-done | bytes 8388624 | tf_op jit(solution)/shard_map/all_gather | solution.py:20
  169.2 25.7 fusion.55
  203.2 338.6 %reduce-scatter.19.cloned.1.call-done = f32[2048,3,512]{2,0,1:T(8,128)} async-done(((f32[8192,3,512]{2,0,1:T(8,128)}), f32[2048,3,512]{2,0,1:T(8,128)}) %reduce-scatter.19.cloned.1.call-update) | async-done | bytes 12582928 | tf_op jit(solution)/shard_map/reduce_scatter | solution.py:23
  557.3 19.1 all-reduce.2
  613.2 77.9 %while.37 = (s32[]{:T(128)}, bf16[4,512,4,128]{3,1,2,0:T(8,128)(2,1)}, f32[4,4,512]{2,1,0:T(4,128)}, s32[4]{0:T(128)S(1)}, s32[]{:T(128)}, /*index=5*/s32[4]{0:T...) while((s32[]{:T(128)}, ...), condition=%wide.region_11.12_spmd.clone.clone, body=%wide.region_7.0_spmd.clone.clone.sunk | while | flops 2199912960 | bytes 68756928 | solution.py:284
  700.5 55.0 all-gather.13.cloned.1.call-done
  784.8 279.9 %reduce-scatter.23.cloned.1.call-done = f32[2048,512]{1,0:T(8,128)} async-done(((f32[8192,512]{1,0:T(8,128)}), f32[2048,512]{1,0:T(8,128)}) %reduce-scatter.23.cloned.1.call-update) | async-done | bytes 4194320 | tf_op jit(solution)/shard_map/reduce_scatter | solution.py:32
  1082.0 149.7 %all-gather.23.cloned.1.call-done = bf16[8192,512]{1,0:T(8,128)(2,1)} async-done(((bf16[2048,512]{1,0:T(8,128)(2,1)}), bf16[8192,512]{1,0:T(8,128)(2,1)}) %all-gather.23.cloned.1.call-update) | async-done | bytes 8388624 | tf_op jit(solution)/shard_map/all_gather | solution.py:20
  1239.0 53.1 fusion.51
  1294.3 885.1 %reduce-scatter.27.cloned.1.call-done = f32[2048,2,2048]{2,0,1:T(8,128)} async-done(((f32[8192,2,2048]{2,0,1:T(8,128)}), f32[2048,2,2048]{2,0,1:T(8,128)}) %reduce-scatter.27.cloned.1.call-update) | async-done | bytes 33554448 | tf_op jit(solution)/shard_map/reduce_scatter | solution.py:23
  2179.4 21.8 bitcast_add_fusion.2
  2201.3 14.8 multiply_convert_fusion.1
  2217.6 200.2 %all-gather.15.cloned.1.call-done = bf16[8192,1,2048]{2,0,1:T(8,128)(2,1)} async-done(((bf16[2048,1,2048]{2,0,1:T(8,128)(2,1)}), bf16[8192,1,2048]{2,0,1:T(8,128)(2,1)}) %all-gather.15.cloned.1.call-update) | async-done | bytes 33554448 | tf_op jit(solution)/shard_map/all_gather | solution.py:29
  2432.9 24.8 fusion.37
  2458.7 279.5 %reduce-scatter.31.cloned.1.call-done = f32[2048,512]{1,0:T(8,128)} async-done(((f32[8192,512]{1,0:T(8,128)}), f32[2048,512]{1,0:T(8,128)}) %reduce-scatter.31.cloned.1.call-update) | async-done | bytes 4194320 | tf_op jit(solution)/shard_map/reduce_scatter | solution.py:32
  2759.6 149.8 %all-gather.25.cloned.1.call-done = bf16[8192,512]{1,0:T(8,128)(2,1)} async-done(((bf16[2048,512]{1,0:T(8,128)(2,1)}), bf16[8192,512]{1,0:T(8,128)(2,1)}) %all-gather.25.cloned.1.call-update) | async-done | bytes 8388624 | tf_op jit(solution)/shard_map/all_gather | solution.py:20
  2917.0 29.2 fusion.170
  2947.3 449.9 %reduce-scatter.49.cloned.1.call-done = f32[2048,2048]{1,0:T(8,128)} async-done(((f32[8192,2048]{1,0:T(8,128)}), f32[2048,2048]{1,0:T(8,128)}) %reduce-scatter.49.cloned.1.call-update) | async-done | bytes 16777232
  3397.2 21.3 fusion.58
  3434.4 390.8 %all-gather.17.cloned.1.call-done = bf16[8192,2,2048]{2,0,1:T(8,128)(2,1)} async-done(((bf16[2048,2,2048]{2,0,1:T(8,128)(2,1)}), bf16[8192,2,2048]{2,0,1:T(8,128)(2,1)}) %all-gather.17.cloned.1.call-update) | async-done | bytes 67108880 | tf_op jit(solution)/shard_map/all_gather | solution.py:29
  3825.2 25.8 fusion.81
  3853.6 43.2 convolution_bitcast_fusion.1
  3898.0 279.2 %reduce-scatter.37.cloned.1.call-done = f32[2048,512]{1,0:T(8,128)} async-done(((f32[8192,512]{1,0:T(8,128)}), f32[2048,512]{1,0:T(8,128)}) %reduce-scatter.37.cloned.1.call-update) | async-done | bytes 4194320 | tf_op jit(solution)/shard_map/reduce_scatter | solution.py:32
  4198.6 149.8 %all-gather.27.cloned.1.call-done = bf16[8192,512]{1,0:T(8,128)(2,1)} async-done(((bf16[2048,512]{1,0:T(8,128)(2,1)}), bf16[8192,512]{1,0:T(8,128)(2,1)}) %all-gather.27.cloned.1.call-update) | async-done | bytes 8388624 | tf_op jit(solution)/shard_map/all_gather | solution.py:20
  4376.6 128.0 %reduce-scatter.41.cloned.1.call-done = f32[2048,512]{1,0:T(8,128)} async-done(((f32[8192,512]{1,0:T(8,128)}), f32[2048,512]{1,0:T(8,128)}) %reduce-scatter.41.cloned.1.call-update) | async-done | bytes 4194320 | tf_op jit(solution)/shard_map/reduce_scatter | solution.py:23
  4515.4 279.8 %while.38 = (s32[]{:T(128)}, f32[2048,4,128]{0,2,1:T(8,128)}, f32[2048,4,128]{0,2,1:T(8,128)}, f32[2048,4,128]{0,2,1:T(8,128)}, s32[]{:T(128)}, /*index=5*/s32[4...) while((s32[]{:T(128)}, f32[2048,4,128]{0,2,1:T(8,128)}, ...), condition=%wide.region_36.37_spmd.clone.clone, body=%wide.region_33.36_spmd.clone.clone.sunk | while | flops 5439226368 | bytes 207684128 | solution.py:378
  4825.8 18.7 all-reduce.1
  4872.9 150.9 %all-gather.19.cloned.1.call-done = bf16[8192,3,512]{2,0,1:T(8,128)(2,1)} async-done(((bf16[2048,3,512]{2,0,1:T(8,128)(2,1)}), bf16[8192,3,512]{2,0,1:T(8,128)(2,1)}) %all-gather.19.cloned.1.call-update) | async-done | bytes 25165840 | tf_op jit(solution)/shard_map/all_gather | solution.py:29
  5077.1 22.1 convolution_bitcast_fusion
  5099.2 39.7 all-reduce.11.cloned.1.call-done
  5145.6 74.2 %all-reduce.9.cloned.1.call-done = (bf16[3,8,512,16]{2,3,1,0:T(8,128)(2,1)}, bf16[8,16,512]{2,1,0:T(8,128)(2,1)}, bf16[2,8,512,16]{2,3,1,0:T(8,128)(2,1)}, bf16[8,16,512]{2,1,0:T(8,128)(2,1)}) async-done(((bf16[3,8,512,16]{2,3,1,0:T(8,128)(2,1)}, bf16[8,16,512]{2,1,0:T(8,128)(2,1)}, bf16[2,8,512,16]{2,3,1,0:T(8,128)(2,1)}, bf16[8,16,512]{2,1,0:T(8,128)(2,1)}), (bf16[3,8,512,16]{2,3,1,0:T(8,128)(2,1)}, ...) | async-done | bytes 917520 | tf_op jit(solution)/shard_map/psum | solution.py:46
  5226.7 275.0 %reduce-scatter.45.cloned.1.call-done = f32[2048,512]{1,0:T(8,128)} async-done(((f32[8192,512]{1,0:T(8,128)}), f32[2048,512]{1,0:T(8,128)}) %reduce-scatter.45.cloned.1.call-update) | async-done | bytes 4194320 | tf_op jit(solution)/shard_map/reduce_scatter | solution.py:32
  (508 shorter events, 750.2 us)
Async XLA Ops:
  7.2 2425.7 %copy-start = (bf16[2048,512]{1,0:T(8,128)(2,1)S(1)}, bf16[2048,512]{1,0:T(8,128)(2,1)}, u32[]{:S(2)}) copy-start(bf16[2048,512]{1,0:T(8,128)(2,1)} %param.27) | copy-start | bytes 6291460
  7.2 154.8 %all-gather.21.cloned.1.call-start = ((), (), s32[]{:S(2)}) async-start(), calls=%async_computation.35 | async-start | bytes 10485760 | tf_op jit(solution)/shard_map/all_gather | solution.py:20
  7.9 191.0 %reduce-scatter.21.cloned.1.call-start = ((), (), s32[]{:S(2)}) async-start(), calls=%async_computation.17 | async-start | bytes 1966080 | tf_op jit(solution)/shard_map/reduce_scatter | solution.py:24
  169.2 372.6 %reduce-scatter.19.cloned.1.call-start = ((), (), s32[]{:S(2)}) async-start(), calls=%async_computation.16 | async-start | bytes 62914560 | tf_op jit(solution)/shard_map/reduce_scatter | solution.py:23
  194.9 560.5 %all-gather.13.cloned.1.call-start = ((), (), s32[]{:S(2)}) async-start(), calls=%async_computation.18 | async-start | bytes 10485760 | tf_op jit(solution)/shard_map/all_gather | solution.py:29
  196.4 393.7 %copy-start.85 = (f32[1,512]{1,0:T(1,128)}, f32[1,512]{1,0:T(1,128)S(1)}, u32[]{:S(2)}) copy-start(f32[1,512]{1,0:T(1,128)S(1)} %get-tuple-element.723) | copy-start | bytes 6148
  198.9 392.3 %copy-start.30 = (f32[2048,64]{0,1:T(8,128)}, f32[2048,64]{0,1:T(8,128)S(1)}, u32[]{:S(2)}) copy-start(f32[2048,64]{0,1:T(8,128)S(1)} %get-tuple-element.717) | copy-start | bytes 1572868
  198.9 392.3 %copy-start.31 = (f32[2048,64]{0,1:T(8,128)}, f32[2048,64]{0,1:T(8,128)S(1)}, u32[]{:S(2)}) copy-start(f32[2048,64]{0,1:T(8,128)S(1)} %get-tuple-element.718) | copy-start | bytes 1572868
  699.8 84.1 %reduce-scatter.25.cloned.1.call-start = ((), (), s32[]{:S(2)}) async-start(), calls=%async_computation.20 | async-start | bytes 655360 | tf_op jit(solution)/shard_map/reduce_scatter | solution.py:33
  762.0 302.6 %reduce-scatter.23.cloned.1.call-start = ((), (), s32[]{:S(2)}) async-start(), calls=%async_computation.19 | async-start | bytes 20971520 | tf_op jit(solution)/shard_map/reduce_scatter | solution.py:32
  773.8 458.0 %all-gather.23.cloned.1.call-start = ((), (), s32[]{:S(2)}) async-start(), calls=%async_computation.36 | async-start | bytes 10485760 | tf_op jit(solution)/shard_map/all_gather | solution.py:20
  1081.7 210.5 %reduce-scatter.29.cloned.1.call-start = ((), (), s32[]{:S(2)}) async-start(), calls=%async_computation.22 | async-start | bytes 1310720 | tf_op jit(solution)/shard_map/reduce_scatter | solution.py:24
  1238.7 940.7 %reduce-scatter.27.cloned.1.call-start = ((), (), s32[]{:S(2)}) async-start(), calls=%async_computation.21 | async-start | bytes 167772160 | tf_op jit(solution)/shard_map/reduce_scatter | solution.py:23
  1292.1 1125.7 %all-gather.15.cloned.1.call-start = ((), (), s32[]{:S(2)}) async-start(), calls=%async_computation.23 | async-start | bytes 41943040 | tf_op jit(solution)/shard_map/all_gather | solution.py:29
  1294.3 906.9 %copy-start.24 = (bf16[2048,2,128]{0,2,1:T(8,128)(2,1)}, bf16[2048,2,128]{0,2,1:T(8,128)(2,1)S(1)}, u32[]{:S(2)}) copy-start(bf16[2048,2,128]{0,2,1:T(8,128)(2,1)S(1)} %bitcast_multiply_fusion.12) | copy-start | bytes 3145732
  2216.1 241.7 %reduce-scatter.33.cloned.1.call-start = ((), (), s32[]{:S(2)}) async-start(), calls=%async_computation.25 | async-start | bytes 655360 | tf_op jit(solution)/shard_map/reduce_scatter | solution.py:33
  2432.6 305.6 %reduce-scatter.31.cloned.1.call-start = ((), (), s32[]{:S(2)}) async-start(), calls=%async_computation.24 | async-start | bytes 20971520 | tf_op jit(solution)/shard_map/reduce_scatter | solution.py:32
  2457.7 451.7 %all-gather.25.cloned.1.call-start = ((), (), s32[]{:S(2)}) async-start(), calls=%async_computation.37 | async-start | bytes 10485760 | tf_op jit(solution)/shard_map/all_gather | solution.py:20
  2759.3 186.9 %reduce-scatter.35.cloned.1.call-start = ((), (), s32[]{:S(2)}) async-start(), calls=%async_computation.26 | async-start | bytes 655360 | tf_op jit(solution)/shard_map/reduce_scatter | solution.py:24
  2916.5 480.7 %reduce-scatter.49.cloned.1.call-start = ((), (), s32[]{:S(2)}) async-start(), calls=%async_computation.39 | async-start | bytes 83886080
  2946.2 879.0 %all-gather.17.cloned.1.call-start = ((), (), s32[]{:S(2)}) async-start(), calls=%async_computation.27 | async-start | bytes 83886080 | tf_op jit(solution)/shard_map/all_gather | solution.py:29
  2947.2 471.3 %copy-start.47 = (bf16[2048,16]{0,1:T(8,128)(2,1)}, bf16[2048,16]{0,1:T(8,128)(2,1)S(1)}, u32[]{:S(2)}) copy-start(bf16[2048,16]{0,1:T(8,128)(2,1)S(1)} %convert_element_type.317) | copy-start | bytes 196612
  3432.4 464.5 %reduce-scatter.39.cloned.1.call-start = ((), (), s32[]{:S(2)}) async-start(), calls=%async_computation.29 | async-start | bytes 1310720 | tf_op jit(solution)/shard_map/reduce_scatter | solution.py:33
  3853.4 323.9 %reduce-scatter.37.cloned.1.call-start = ((), (), s32[]{:S(2)}) async-start(), calls=%async_computation.28 | async-start | bytes 20971520 | tf_op jit(solution)/shard_map/reduce_scatter | solution.py:32
  3896.8 451.5 %all-gather.27.cloned.1.call-start = ((), (), s32[]{:S(2)}) async-start(), calls=%async_computation.38 | async-start | bytes 10485760 | tf_op jit(solution)/shard_map/all_gather | solution.py:20
  4198.3 177.3 %reduce-scatter.43.cloned.1.call-start = ((), (), s32[]{:S(2)}) async-start(), calls=%async_computation.31 | async-start | bytes 655360 | tf_op jit(solution)/shard_map/reduce_scatter | solution.py:24
  4355.6 149.0 %reduce-scatter.41.cloned.1.call-start = ((), (), s32[]{:S(2)}) async-start(), calls=%async_computation.30 | async-start | bytes 20971520 | tf_op jit(solution)/shard_map/reduce_scatter | solution.py:23
  4367.3 656.5 %all-gather.19.cloned.1.call-start = ((), (), s32[]{:S(2)}) async-start(), calls=%async_computation.32 | async-start | bytes 31457280 | tf_op jit(solution)/shard_map/all_gather | solution.py:29
  4871.6 202.5 %reduce-scatter.47.cloned.1.call-start = ((), (), s32[]{:S(2)}) async-start(), calls=%async_computation.34 | async-start | bytes 1966080 | tf_op jit(solution)/shard_map/reduce_scatter | solution.py:33
  5038.6 100.2 %all-reduce.11.cloned.1.call-start = ((), (), s32[]{:S(2)}) async-start(), calls=%async_computation.41 | async-start | bytes 4194304 | tf_op jit(solution)/shard_map/psum | solution.py:50
  5059.6 160.1 %all-reduce.9.cloned.1.call-start = ((), (), s32[]{:S(2)}) async-start(), calls=%async_computation.40 | async-start | bytes 1835008 | tf_op jit(solution)/shard_map/psum | solution.py:46
  5077.0 424.7 %reduce-scatter.45.cloned.1.call-start = ((), (), s32[]{:S(2)}) async-start(), calls=%async_computation.33 | async-start | bytes 20971520 | tf_op jit(solution)/shard_map/reduce_scatter | solution.py:32
  (107 other events, 5571.6 us)
Sparse Core Ops, SparseCore 0:
  9.6 152.3 all-gather.20
  169.3 26.4 reduce-scatter.20
  198.5 343.1 reduce-scatter.18
  699.9 55.5 all-gather.12
  762.2 21.6 reduce-scatter.24
  786.0 278.5 reduce-scatter.22
  1081.8 149.9 all-gather.22
  1238.9 23.1 reduce-scatter.28
  1292.2 887.1 reduce-scatter.26
  2216.2 201.5 all-gather.14
  2432.7 21.6 reduce-scatter.32
  2457.8 280.2 reduce-scatter.30
  2759.5 149.8 all-gather.24
  2916.6 19.8 reduce-scatter.34
  2946.3 450.8 reduce-scatter.48
  3432.5 392.7 all-gather.16
  3853.5 27.1 reduce-scatter.38
  3896.9 280.3 reduce-scatter.36
  4198.4 149.9 all-gather.26
  4355.7 19.8 reduce-scatter.42
  4378.4 126.1 reduce-scatter.40
  4871.7 152.0 all-gather.18
  5038.7 35.2 reduce-scatter.46
  5078.0 60.8 all-reduce.10
  5143.8 75.8 all-reduce.8
  5221.9 279.7 reduce-scatter.44
where the time goes:
time: 5530 us; the launch traced here: 5520 us
  waiting for transfers between devices  4450 us (80%)
  matrix products  637 us (12%)
  other arithmetic  198 us (4%)
  local copies, waits for them, and re-layouts  144 us (3%)
  blocking collectives  61.5 us (1%)
    reduce_scatter x3, waiting for transfers between devices, via_col_row(): lax.psum_scatter(main, 'row', scatter_dimension=0, tiled=True)  1350 us
    reduce_scatter x4, waiting for transfers between devices, via_row_col(): lax.psum_scatter(main, 'col', scatter_dimension=0, tiled=True)  1110 us
    all_gather x4, waiting for transfers between devices, via_row_col(): gathered = lax.all_gather(input_rows, 'row', axis=0, tiled=True)  797 us
    all_gather x4, waiting for transfers between devices, via_col_row(): gathered = lax.all_gather(input_rows, 'col', axis=0, tiled=True)  601 us
    unnamed x27, waiting for transfers between devices  451 us
  transfers between devices with their start and end apart: 26, of which 21 were waited for; matrix products, arithmetic and copies ran while one was open for 5% of the time, Pallas kernels for 0%

commit v1 on v0

--- a/solution.py
+++ b/solution.py
@@ -1,6 +1,10 @@
+import functools
+
 import jax
 import jax.numpy as jnp
 from jax import lax
+from jax.experimental import pallas as pl
+from jax.experimental.pallas import tpu as pltpu
 from jax.sharding import PartitionSpec as P
 
 D = 2048
@@ -176,7 +180,7 @@
     return (main, adapter_back(gathered, pick, upward_rank))
 
 
-def shards(
+def general_shards(
     tokens,
     cotangent,
     qkv_weight,
@@ -408,6 +412,622 @@
     )
 
 
+LOG2E = 1.4426950408889634
+CHUNKS = 2
+Q_BLOCK = 512
+K_BLOCK = 512
+BF = jnp.bfloat16
+F32 = jnp.float32
+
+
+def dot_of(left, right, left_dim, right_dim, out=F32):
+    return lax.dot_general(
+        left, right, (((left_dim,), (right_dim,)), ((), ())), preferred_element_type=out
+    )
+
+
+def attend_kernel(prefix_ref, q_ref, k_ref, v_ref, out_ref, log_ref, *, first):
+    rows = q_ref.shape[0]
+    start = first + pl.program_id(1) * rows
+    prefix = prefix_ref[0]
+    blocks = lax.div(jnp.maximum(start + rows, prefix) + K_BLOCK - 1, K_BLOCK)
+    query = q_ref[...]
+    limit = jnp.maximum(lax.broadcasted_iota(jnp.int32, (1, rows), 1) + start, prefix - 1)
+    key_pos = lax.broadcasted_iota(jnp.int32, (K_BLOCK, rows), 0)
+
+    def body(index, carry):
+        top, total, mixed = carry
+        at = pl.multiple_of(index * K_BLOCK, K_BLOCK)
+        scores = dot_of(k_ref[pl.ds(at, K_BLOCK), :], query, 1, 1) * (HEAD**-0.5 * LOG2E)
+        scores = jnp.where(key_pos <= limit - at, scores, NEG)
+        top_now = jnp.maximum(top, jnp.max(scores, axis=0, keepdims=True))
+        fade = jnp.exp2(top - top_now)
+        powers = jnp.exp2(scores - top_now)
+        total = fade * total + jnp.sum(powers, axis=0, keepdims=True)
+        mixed = mixed * fade + dot_of(v_ref[pl.ds(at, K_BLOCK), :], powers.astype(BF), 0, 0)
+        return top_now, total, mixed
+
+    top, total, mixed = lax.fori_loop(
+        0,
+        blocks,
+        body,
+        (
+            jnp.full((1, rows), NEG, F32),
+            jnp.zeros((1, rows), F32),
+            jnp.zeros((HEAD, rows), F32),
+        ),
+    )
+    out_ref[...] = (mixed / total).T.astype(BF)
+    log_ref[0] = top + jnp.log2(total)
+
+
+def attend(prefix, query, key, value, first):
+    rows, length, heads = query.shape[0], key.shape[0], query.shape[1] // HEAD
+    q_spec = pl.BlockSpec((Q_BLOCK, HEAD), lambda h, i, p: (i, h))
+    k_spec = pl.BlockSpec((length, HEAD), lambda h, i, p: (0, h))
+    return pl.pallas_call(
+        functools.partial(attend_kernel, first=first),
+        out_shape=(
+            jax.ShapeDtypeStruct(query.shape, BF),
+            jax.ShapeDtypeStruct((heads, 1, rows), F32),
+        ),
+        grid_spec=pltpu.PrefetchScalarGridSpec(
+            num_scalar_prefetch=1,
+            grid=(heads, rows // Q_BLOCK),
+            in_specs=[q_spec, k_spec, k_spec],
+            out_specs=[q_spec, pl.BlockSpec((1, 1, Q_BLOCK), lambda h, i, p: (h, 0, i))],
+        ),
+        cost_estimate=pl.CostEstimate(
+            flops=3 * rows * length * heads * HEAD,
+            bytes_accessed=8 * rows * heads * HEAD,
+            transcendentals=rows * length * heads,
+        ),
+        name="attend",
+    )(prefix, query, key, value)
+
+
+def attend_back_kernel(
+    prefix_ref, q_ref, grad_ref, out_ref, log_ref, k_ref, v_ref, dq_ref, dk_ref, dv_ref
+):
+    rows = q_ref.shape[0]
+    start = pl.program_id(1) * rows
+    prefix = prefix_ref[0]
+    blocks = lax.div(jnp.maximum(start + rows, prefix) + K_BLOCK - 1, K_BLOCK)
+
+    @pl.when(pl.program_id(1) == 0)
+    def _():
+        dk_ref[...] = jnp.zeros_like(dk_ref)
+        dv_ref[...] = jnp.zeros_like(dv_ref)
+
+    query = q_ref[...]
+    grad = grad_ref[...]
+    limit = jnp.maximum(lax.broadcasted_iota(jnp.int32, (1, rows), 1) + start, prefix - 1)
+    key_pos = lax.broadcasted_iota(jnp.int32, (K_BLOCK, rows), 0)
+    log_total = log_ref[0]
+    delta = lax.dot_general(
+        jnp.ones((8, HEAD), F32),
+        grad.astype(F32) * out_ref[...].astype(F32),
+        (((1,), (1,)), ((), ())),
+        precision=lax.Precision.HIGHEST,
+        preferred_element_type=F32,
+    )[0:1]
+
+    def body(index, d_query):
+        at = pl.multiple_of(index * K_BLOCK, K_BLOCK)
+        span = pl.ds(at, K_BLOCK)
+        key = k_ref[span, :]
+        scores = dot_of(key, query, 1, 1) * (HEAD**-0.5 * LOG2E)
+        probs = jnp.where(key_pos <= limit - at, jnp.exp2(scores - log_total), 0.0)
+        d_probs = dot_of(v_ref[span, :], grad, 1, 1)
+        d_scores = (probs * (d_probs - delta)).astype(BF)
+        dv_ref[span, :] += dot_of(probs.astype(BF), grad, 1, 0)
+        dk_ref[span, :] += dot_of(d_scores, query, 1, 0)
+        return d_query + dot_of(d_scores, key, 0, 0)
+
+    dq_ref[...] = lax.fori_loop(0, blocks, body, jnp.zeros((rows, HEAD), F32)) * HEAD**-0.5
+
+    @pl.when(pl.program_id(1) == pl.num_programs(1) - 1)
+    def _():
+        dk_ref[...] = dk_ref[...] * HEAD**-0.5
+
+
+def attend_back(prefix, query, grad, mixed, log_total, key, value):
+    rows, length, heads = query.shape[0], key.shape[0], query.shape[1] // HEAD
+    q_spec = pl.BlockSpec((Q_BLOCK, HEAD), lambda h, i, p: (i, h))
+    k_spec = pl.BlockSpec((length, HEAD), lambda h, i, p: (0, h))
+    return pl.pallas_call(
+        attend_back_kernel,
+        out_shape=(
+            jax.ShapeDtypeStruct(query.shape, F32),
+            jax.ShapeDtypeStruct(key.shape, F32),
+            jax.ShapeDtypeStruct(key.shape, F32),
+        ),
+        grid_spec=pltpu.PrefetchScalarGridSpec(
+            num_scalar_prefetch=1,
+            grid=(heads, rows // Q_BLOCK),
+            in_specs=[
+                q_spec,
+                q_spec,
+                q_spec,
+                pl.BlockSpec((1, 1, Q_BLOCK), lambda h, i, p: (h, 0, i)),
+                k_spec,
+                k_spec,
+            ],
+            out_specs=[q_spec, k_spec, k_spec],
+        ),
+        cost_estimate=pl.CostEstimate(
+            flops=7 * rows * length * heads * HEAD,
+            bytes_accessed=24 * rows * heads * HEAD,
+            transcendentals=rows * length * heads,
+        ),
+        name="attend_back",
+    )(prefix, query, grad, mixed, log_total, key, value)
+
+
+def rotate_kernel(raw_ref, scale_ref, gain_ref, cos_ref, sin_ref, q_ref, k_ref, v_ref):
+    width = q_ref.shape[1]
+    cosine = cos_ref[...]
+    sine = sin_ref[...]
+    for part, out in ((0, q_ref), (1, k_ref)):
+        scale = scale_ref[:, part : part + 1]
+        for at in range(0, width, HEAD):
+            normed = raw_ref[:, part * width + at : part * width + at + HEAD] * scale
+            normed = normed * gain_ref[part : part + 1, at : at + HEAD]
+            turned = normed * cosine + pltpu.roll(normed, HEAD // 2, 1) * sine
+            out[:, at : at + HEAD] = turned.astype(BF)
+    v_ref[...] = raw_ref[:, 2 * width :].astype(BF)
+
+
+def rotate_rows(raw, scales, gains, cosine, sine):
+    rows, width = raw.shape[0], raw.shape[1] // 3
+    step = min(512, rows)
+    out_spec = pl.BlockSpec((step, width), lambda i: (i, 0))
+    table = pl.BlockSpec((step, HEAD), lambda i: (i, 0))
+    return pl.pallas_call(
+        rotate_kernel,
+        out_shape=(jax.ShapeDtypeStruct((rows, width), BF),) * 3,
+        grid=(rows // step,),
+        in_specs=[
+            pl.BlockSpec((step, 3 * width), lambda i: (i, 0)),
+            pl.BlockSpec((step, 2), lambda i: (i, 0)),
+            pl.BlockSpec((2, width), lambda i: (0, 0)),
+            table,
+            table,
+        ],
+        out_specs=[out_spec] * 3,
+        name="rotate_rows",
+    )(raw, scales, gains, cosine, sine)
+
+
+def unrotate_kernel(
+    raw_ref, dq_ref, dk_ref, dv_ref, scale_ref, back_ref, gain_ref, cos_ref, sin_ref, out_ref
+):
+    width = dq_ref.shape[1]
+    cosine = cos_ref[...]
+    sine = sin_ref[...]
+    for part, grad in ((0, dq_ref), (1, dk_ref)):
+        scale = scale_ref[:, part : part + 1]
+        back = back_ref[:, part : part + 1]
+        for at in range(0, width, HEAD):
+            turned = grad[:, at : at + HEAD]
+            turned = turned * cosine - pltpu.roll(turned, HEAD // 2, 1) * sine
+            turned = turned * gain_ref[part : part + 1, at : at + HEAD] * scale
+            lane = part * width + at
+            out_ref[:, lane : lane + HEAD] = (
+                turned - raw_ref[:, lane : lane + HEAD] * back
+            ).astype(BF)
+    out_ref[:, 2 * width :] = dv_ref[...].astype(BF)
+
+
+def unrotate_rows(raw, d_query, d_key, d_value, scales, backs, gains, cosine, sine):
+    rows, width = d_query.shape
+    step = min(512, rows)
+    part = pl.BlockSpec((step, width), lambda i: (i, 0))
+    table = pl.BlockSpec((step, HEAD), lambda i: (i, 0))
+    pair = pl.BlockSpec((step, 2), lambda i: (i, 0))
+    wide = pl.BlockSpec((step, 3 * width), lambda i: (i, 0))
+    return pl.pallas_call(
+        unrotate_kernel,
+        out_shape=jax.ShapeDtypeStruct((rows, 3 * width), BF),
+        grid=(rows // step,),
+        in_specs=[
+            wide,
+            part,
+            part,
+            part,
+            pair,
+            pair,
+            pl.BlockSpec((2, width), lambda i: (0, 0)),
+            table,
+            table,
+        ],
+        out_specs=wide,
+        name="unrotate_rows",
+    )(raw, d_query, d_key, d_value, scales, backs, gains, cosine, sine)
+
+
+def across(values, step):
+    return lax.ppermute(values, "row", [(i, i ^ step) for i in range(4)])
+
+
+def gather_row(own):
+    core = across(own, 1)
+    side = across(own, 2)
+    return [own, core, side, across(side, 1)]
+
+
+def sum_row(values):
+    values = values + across(values, 1)
+    return values + across(values, 2)
+
+
+def scatter_row(parts):
+    near = parts[0].astype(F32) + across(parts[1], 1).astype(F32)
+    far = parts[2].astype(F32) + across(parts[3], 1).astype(F32)
+    return near + across(far.astype(BF), 2).astype(F32)
+
+
+def deal_row(pieces, me):
+    out = []
+    for step in range(4):
+        piece = lax.dynamic_index_in_dim(pieces, me ^ step, 0, keepdims=False)
+        out.append(piece if step == 0 else across(piece, step))
+    return out
+
+
+def gather_col(values):
+    return lax.all_gather(values, "col", axis=0, tiled=False)
+
+
+def swap_pair(values):
+    return lax.ppermute(values, "dp", [(0, 1), (1, 0)])
+
+
+def group_shards(
+    tokens,
+    cotangent,
+    qkv_weight,
+    attn_weight,
+    expand_weight,
+    reduce_weight,
+    headnorm_gain,
+    post_gain,
+    qkv_lowrank,
+    qkv_uprank,
+    attn_lowrank,
+    attn_uprank,
+    expand_lowrank,
+    expand_uprank,
+    reduce_lowrank,
+    reduce_uprank,
+    prefix_length,
+    adapter_set,
+):
+    cols = lax.axis_size("col")
+    pair = lax.axis_index("dp")
+    me = lax.axis_index("row")
+    col = lax.axis_index("col")
+    rows, width = tokens.shape
+    sub = qkv_weight.shape[2] // 4
+    ff = expand_weight.shape[2]
+    ff_sub = ff // 4
+    ff_half = ff_sub // 2
+    local = cols * sub
+    ff_local = cols * ff_sub
+    out_half = width // 2
+    sequence = pair * cols + col
+    mine = lax.dynamic_index_in_dim(adapter_set, sequence, 0, keepdims=False)
+    prefix = lax.dynamic_slice_in_dim(prefix_length, sequence, 1)
+    cols_sets = lax.dynamic_slice_in_dim(adapter_set, pair * cols, cols)
+
+    def own_set(array, axis):
+        return lax.dynamic_index_in_dim(array, mine, axis, keepdims=False)
+
+    row_pack = jnp.concatenate(
+        [
+            own_set(qkv_lowrank, 1).transpose(0, 2, 1).reshape(3 * ADAPTER_RANK, width),
+            own_set(attn_uprank, 0),
+            own_set(expand_lowrank, 1).transpose(0, 2, 1).reshape(2 * ADAPTER_RANK, width),
+            own_set(reduce_uprank, 0),
+        ],
+        axis=0,
+    )
+    row_all = jnp.concatenate(gather_row(row_pack), axis=1)
+    qkv_low = row_all[:48]
+    attn_up = row_all[48:64]
+    expand_low = row_all[64:96]
+    reduce_up = row_all[96:112]
+
+    def col_pack_of(which):
+        one = lambda array, axis: lax.dynamic_index_in_dim(array, which, axis, keepdims=False)
+        cut = lambda array, axis, size: lax.dynamic_slice_in_dim(array, me * size, size, axis)
+        up_qkv = cut(one(qkv_uprank, 1), 2, sub)
+        up_exp = cut(one(expand_uprank, 1), 2, ff_sub)
+        return jnp.concatenate(
+            [
+                up_qkv[0],
+                up_qkv[1],
+                up_qkv[2],
+                cut(one(attn_lowrank, 0), 0, sub).T,
+                up_exp[0],
+                up_exp[1],
+                cut(one(reduce_lowrank, 0), 0, ff_sub).T,
+            ],
+            axis=1,
+        )
+
+    col_pack = jnp.stack([col_pack_of(cols_sets[i]) for i in range(cols)])
+    col_all = lax.all_to_all(col_pack, "col", split_axis=0, concat_axis=0, tiled=True)
+    heads_of = lambda at: col_all[:, :, at : at + sub].transpose(1, 0, 2).reshape(16, local)
+
+    def swap_halves(array):
+        return jnp.where(pair == 0, array, array[:, ::-1])
+
+    def ff_of(at):
+        part = col_all[:, :, at : at + ff_sub].reshape(cols, 16, 2, ff_half)
+        part = part.transpose(1, 2, 0, 3)
+        return swap_halves(part).reshape(16, ff_local)
+
+    qkv_up = [heads_of(i * sub) for i in range(3)]
+    attn_low = heads_of(3 * sub)
+    expand_up = [ff_of(4 * sub), ff_of(4 * sub + ff_sub)]
+    reduce_low = ff_of(4 * sub + 2 * ff_sub)
+    gains = lax.dynamic_slice_in_dim(headnorm_gain, me * sub, sub, 1)
+    gains = gather_col(gains).transpose(1, 0, 2).reshape(2, local)
+
+    def merged(base, low, up):
+        return (base.astype(F32) + ADAPTER_FACTOR * dot_of(low, up, 0, 0)).astype(BF)
+
+    pieces = qkv_weight.reshape(3, width, 4, sub).transpose(2, 0, 1, 3)
+    qkv_all = gather_col(jnp.stack(deal_row(pieces, me)))
+    qkv_all = qkv_all.transpose(2, 1, 3, 0, 4).reshape(3, 4 * width, local)
+    qkv_w = jnp.concatenate(
+        [merged(qkv_all[i], qkv_low[16 * i : 16 * i + 16], qkv_up[i]) for i in range(3)], axis=1
+    )
+
+    pieces = attn_weight.reshape(4, sub, 2, out_half)
+    pieces = lax.dynamic_index_in_dim(pieces, pair, 2, keepdims=False)
+    own = gather_col(jnp.stack(deal_row(pieces, me)))
+    other = swap_pair(own)
+    both = jnp.where(pair == 0, jnp.stack([own, other]), jnp.stack([other, own]))
+    attn_all = both.transpose(1, 3, 2, 0, 4).reshape(local, 4 * width)
+    attn_w = merged(attn_all, attn_low, attn_up)
+
+    expand_w = []
+    for part in range(2):
+        pieces = expand_weight[part].reshape(width, 4, 2, ff_half)
+        pieces = lax.dynamic_index_in_dim(pieces, pair, 2, keepdims=False).transpose(1, 0, 2)
+        own = gather_col(jnp.stack(deal_row(pieces, me)))
+        both = jnp.stack([own, swap_pair(own)])
+        whole = both.transpose(2, 3, 0, 1, 4).reshape(4 * width, ff_local)
+        expand_w.append(merged(whole, expand_low[16 * part : 16 * part + 16], expand_up[part]))
+
+    pieces = reduce_weight.reshape(4, 2, ff_half, width)
+    pieces = lax.dynamic_index_in_dim(pieces, pair, 1, keepdims=False)
+    own = gather_col(jnp.stack(deal_row(pieces, me)))
+    both = jnp.stack([own, swap_pair(own)])
+    whole = both.transpose(0, 1, 3, 2, 4).reshape(ff_local, 4 * width)
+    reduce_w = merged(whole, reduce_low, reduce_up)
+
+    def in_parts(left, matrix):
+        return [
+            dot_of(left, matrix[:, i * width : (i + 1) * width], 1, 0, BF if i in (1, 3) else F32)
+            for i in range(4)
+        ]
+
+    half = HEAD // 2
+    freq = THETA ** (-2.0 * jnp.arange(half, dtype=F32) / HEAD)
+    angle = jnp.arange(rows, dtype=jnp.int32).astype(F32)[:, None] * freq[None, :]
+    cosine = jnp.concatenate([jnp.cos(angle)] * 2, axis=1)
+    sine = jnp.sin(angle)
+    sine = jnp.concatenate([-sine, sine], axis=1)
+    step = rows // CHUNKS
+    spans = [slice(i * step, (i + 1) * step) for i in range(CHUNKS)]
+    raws, scales, turned, qkv_inner = [], [], [], []
+    for span in spans:
+        full = jnp.concatenate(gather_row(tokens[span]), axis=1)
+        qkv_inner.append(dot_of(qkv_low, full, 1, 1).astype(BF))
+        raw = dot_of(full, qkv_w, 1, 0)
+        squares = jnp.stack(
+            [jnp.sum(raw[:, i * local : (i + 1) * local] ** 2, axis=1) for i in range(2)]
+        )
+        scale = lax.rsqrt(sum_row(squares) / D + EPS).T
+        raws.append(raw)
+        scales.append(scale)
+        turned.append(rotate_rows(raw, scale, gains, cosine[span], sine[span]))
+    key = jnp.concatenate([part[1] for part in turned])
+    value = jnp.concatenate([part[2] for part in turned])
+
+    layer_parts, d_hiddens, mixeds, logs, d_mixeds = [], [], [], [], []
+    grads = []
+    for index, span in enumerate(spans):
+        query = turned[index][0]
+        mixed, log_total = attend(prefix, query, key, value, index * step)
+        mixeds.append(mixed)
+        logs.append(log_total)
+        attn_inner = sum_row(dot_of(attn_low, mixed, 0 + 1, 1)).astype(BF)
+        branch = scatter_row(in_parts(mixed, attn_w))
+        branch_scale = lax.rsqrt(sum_row(jnp.sum(branch * branch, axis=1)) / D + EPS)[:, None]
+        hidden = tokens[span].astype(F32) + post_gain[0] * branch * branch_scale
+        hidden_b = hidden.astype(BF)
+        full = jnp.concatenate(gather_row(hidden_b), axis=1)
+        expand_inner = dot_of(expand_low, full, 1, 1).astype(BF)
+        gate = dot_of(full, expand_w[0], 1, 0)
+        upper = dot_of(full, expand_w[1], 1, 0)
+        act = (jax.nn.silu(gate) * upper).astype(BF)
+        gate_b = gate.astype(BF)
+        upper_b = upper.astype(BF)
+        reduce_inner = sum_row(dot_of(reduce_low, act, 1, 1)).astype(BF)
+        result = scatter_row(in_parts(act, reduce_w))
+        incoming = cotangent[span].astype(F32)
+        weighted = post_gain[1] * incoming
+        sums = sum_row(
+            jnp.stack([jnp.sum(result * result, axis=1), jnp.sum(weighted * result, axis=1)])
+        )
+        result_scale = lax.rsqrt(sums[0] / D + EPS)[:, None]
+        layer_parts.append((hidden + post_gain[1] * result * result_scale).astype(BF))
+        d_result = (
+            result_scale * weighted - result * (result_scale**3 * sums[1][:, None] / D)
+        ).astype(BF)
+        full = jnp.concatenate(gather_row(d_result), axis=1)
+        g_reduce_up = ADAPTER_FACTOR * dot_of(reduce_inner, d_result, 1, 0)
+        d_inner = (ADAPTER_FACTOR * dot_of(reduce_up, full, 1, 1)).astype(BF)
+        g_reduce_low = dot_of(d_inner, act, 1, 0)
+        d_act = dot_of(full, reduce_w, 1, 1)
+        gate = gate_b.astype(F32)
+        upper = upper_b.astype(F32)
+        sigma = jax.nn.sigmoid(gate)
+        d_gate = (d_act * upper * sigma * (1 + gate * (1 - sigma))).astype(BF)
+        d_upper = (d_act * gate * sigma).astype(BF)
+        g_expand_up = [
+            ADAPTER_FACTOR * dot_of(expand_inner[:16], d_gate, 1, 0),
+            ADAPTER_FACTOR * dot_of(expand_inner[16:], d_upper, 1, 0),
+        ]
+        d_inner = sum_row(
+            ADAPTER_FACTOR
+            * jnp.concatenate(
+                [dot_of(expand_up[0], d_gate, 1, 1), dot_of(expand_up[1], d_upper, 1, 1)]
+            )
+        ).astype(BF)
+        g_expand_low = dot_of(d_inner, hidden_b, 1, 0)
+        parts = []
+        for i in range(4):
+            cut = slice(i * width, (i + 1) * width)
+            part = dot_of(d_gate, expand_w[0][cut], 1, 1) + dot_of(d_upper, expand_w[1][cut], 1, 1)
+            parts.append(part.astype(BF) if i in (1, 3) else part)
+        d_hidden = incoming + scatter_row(parts)
+        weighted = post_gain[0] * d_hidden
+        inner_sum = sum_row(jnp.sum(weighted * branch, axis=1))[:, None]
+        d_branch = (
+            branch_scale * weighted - branch * (branch_scale**3 * inner_sum / D)
+        ).astype(BF)
+        d_hiddens.append(d_hidden)
+        full = jnp.concatenate(gather_row(d_branch), axis=1)
+        g_attn_up = ADAPTER_FACTOR * dot_of(attn_inner, d_branch, 1, 0)
+        d_inner = (ADAPTER_FACTOR * dot_of(attn_up, full, 1, 1)).astype(BF)
+        g_attn_low = dot_of(d_inner, mixed, 1, 0)
+        d_mixeds.append(dot_of(full, attn_w, 1, 1, BF))
+        grads.append(
+            (g_attn_up, g_expand_low, g_reduce_up, g_attn_low, *g_expand_up, g_reduce_low)
+        )
+
+    d_query, d_key, d_value = attend_back(
+        prefix,
+        jnp.concatenate([part[0] for part in turned]),
+        jnp.concatenate(d_mixeds),
+        jnp.concatenate(mixeds),
+        jnp.concatenate(logs, axis=2),
+        key,
+        value,
+    )
+    grads = [functools.reduce(jnp.add, parts) for parts in zip(*grads)]
+    input_parts, g_low, g_up = [], [], []
+    for index, span in enumerate(spans):
+        scale = scales[index]
+        inner = sum_row(
+            jnp.stack(
+                [
+                    jnp.sum(d_query[span] * turned[index][0].astype(F32), axis=1),
+                    jnp.sum(d_key[span] * turned[index][1].astype(F32), axis=1),
+                ]
+            )
+        ).T
+        d_qkv = unrotate_rows(
+            raws[index],
+            d_query[span],
+            d_key[span],
+            d_value[span],
+            scale,
+            scale * scale * inner / D,
+            gains,
+            cosine[span],
+            sine[span],
+        )
+        part = [d_qkv[:, i * local : (i + 1) * local] for i in range(3)]
+        g_up.append(
+            [
+                ADAPTER_FACTOR * dot_of(qkv_inner[index][16 * i : 16 * i + 16], part[i], 1, 0)
+                for i in range(3)
+            ]
+        )
+        d_inner = sum_row(
+            ADAPTER_FACTOR
+            * jnp.concatenate([dot_of(qkv_up[i], part[i], 1, 1) for i in range(3)])
+        ).astype(BF)
+        g_low.append(dot_of(d_inner, tokens[span], 1, 0))
+        parts = [
+            dot_of(d_qkv, qkv_w[i * width : (i + 1) * width], 1, 1, BF if i in (1, 3) else F32)
+            for i in range(4)
+        ]
+        input_parts.append(d_hiddens[index] + scatter_row(parts))
+    g_qkv_low = functools.reduce(jnp.add, g_low)
+    g_qkv_up = [functools.reduce(jnp.add, parts) for parts in zip(*g_up)]
+    g_attn_up, g_expand_low, g_reduce_up, g_attn_low, g_gate_up, g_upper_up, g_reduce_low = grads
+
+    member = (adapter_set[None, :] == jnp.arange(SETS, dtype=jnp.int32)[:, None]).astype(F32)
+
+    def to_sets(by_sequence):
+        return jnp.einsum(
+            "ks,sab->kab", member, by_sequence.astype(F32), precision=lax.Precision.HIGHEST
+        )
+
+    def sum_groups(pack):
+        return to_sets(lax.all_gather(pack.astype(BF), ("dp", "col"), axis=0, tiled=False))
+
+    early = sum_groups(jnp.concatenate([g_attn_up, g_expand_low, g_reduce_up], axis=0))
+    late = sum_groups(g_qkv_low)
+
+    def heads_back(grad):
+        return grad.reshape(16, cols, sub).transpose(1, 0, 2)
+
+    def ff_back(grad):
+        part = swap_halves(grad.reshape(16, 2, cols, ff_half))
+        return part.transpose(2, 0, 1, 3).reshape(cols, 16, ff_sub)
+
+    def sum_tokens(pack):
+        dealt = lax.all_to_all(pack.astype(BF), "col", split_axis=0, concat_axis=0, tiled=True)
+        every = lax.all_gather(dealt, "row", axis=0, tiled=False)
+        every = lax.all_gather(every, "dp", axis=0, tiled=False)
+        every = every.transpose(0, 2, 3, 1, 4)
+        return to_sets(every.reshape(2 * cols, 16, -1)).reshape(SETS, 16, 4, -1)
+
+    early_col = sum_tokens(
+        jnp.concatenate(
+            [heads_back(g_attn_low), ff_back(g_gate_up), ff_back(g_upper_up), ff_back(g_reduce_low)],
+            axis=2,
+        )
+    )
+    late_col = sum_tokens(jnp.concatenate([heads_back(grad) for grad in g_qkv_up], axis=2))
+
+    def low_of(array):
+        return array.transpose(0, 2, 1)
+
+    def piece_of(array, at, size):
+        return array[:, :, :, at : at + size].reshape(SETS, 16, 4 * size)
+
+    return (
+        jnp.concatenate(layer_parts),
+        jnp.concatenate(input_parts),
+        jnp.stack([low_of(late[:, 16 * i : 16 * i + 16]) for i in range(3)]),
+        jnp.stack([piece_of(late_col, i * sub, sub) for i in range(3)]),
+        low_of(piece_of(early_col, 0, sub)),
+        early[:, :16],
+        jnp.stack([low_of(early[:, 16 + 16 * i : 32 + 16 * i]) for i in range(2)]),
+        jnp.stack([piece_of(early_col, sub + i * ff_sub, ff_sub) for i in range(2)]),
+        low_of(piece_of(early_col, sub + 2 * ff_sub, ff_sub)),
+        early[:, 48:64],
+    )
+
+
+def shards(*arrays):
+    whole = (
+        lax.axis_size("dp") == 2
+        and lax.axis_size("row") == 4
+        and arrays[0].shape[0] == SEQUENCE_LENGTH
+    )
+    return group_shards(*arrays) if whole else general_shards(*arrays)
+
+
 def solution(mesh):
     placed = (
         P(("dp", "col"), "row"),

time: 5530 us -> 1520 us (0.27)
  waiting for transfers between devices: 4450 us -> 363 us
  matrix products: 637 us -> 393 us
  local copies, waits for them, and re-layouts: 144 us -> 282 us
  Pallas kernels: 0 us -> 125 us
  starting transfers between devices: 2.63 us -> 73.7 us
    reduce_scatter x15 -> x0, waiting for transfers between devices: 2490 us -> none  [the longest x3 1350 us: via_col_row(): lax.psum_scatter(main, 'row', scatter_dimension=0, tiled=True)]
    all_gather x8 -> x6, waiting for transfers between devices: 1400 us -> 99.9 us  [the longest x5 99.9 us: gather_col(): return lax.all_gather(values, 'col', axis=0, tiled=False)]
    unnamed x27 -> x6, waiting for transfers between devices: 451 us -> 0.1 us
    ppermute x0 -> x106, waiting for transfers between devices: none -> 259 us  [the longest x102 248 us: across(): return lax.ppermute(values, 'row', [(i, i ^ step) for i in range(4)])]
    dot_general x68 -> x101, matrix products: 637 us -> 393 us  [the longest x97 392 us: dot_of(): lax.dot_general(left, right, (((left_dim,), (right_dim,)), ((), ())), pre...]
    pallas_call x0 -> x7, Pallas kernels: none -> 125 us  [the longest x1 57.6 us: attend_back(): pl.pallas_call(attend_back_kernel, out_shape=(jax.ShapeDtypeStruct(query....]
    convert_element_type x4 -> x10, local copies, waits for them, and re-layouts: 14.8 us -> 131 us  [merged(): base.astype(F32) + ADAPTER_FACTOR * dot_of(low, up, 0, 0)]
    psum x2 -> x0, waiting for transfers between devices: 114 us -> none  [the longest x1 74.2 us: sum_col_tokens(): lax.psum(values.astype(jnp.bfloat16), ('dp', 'col')).astype(jnp.float32)]
  transfers between devices with their start and end apart: 26 -> 115, of which waited for: 21 -> 28; matrix products, arithmetic and copies ran while one was open for 5% -> 49% of each run, Pallas kernels for 0% -> 4%
where the time goes in v1:
time: 1520 us; the launch traced here: 1510 us
  matrix products  393 us (26%)
  waiting for transfers between devices  363 us (24%)
  local copies, waits for them, and re-layouts  282 us (19%)
  other arithmetic  144 us (9%)
  Pallas kernels  125 us (8%)
  blocking collectives  103 us (7%)
  starting transfers between devices  73.7 us (5%)
  between operations  26.6 us (2%)
    dot_general x97, matrix products, dot_of(): lax.dot_general(left, right, (((left_dim,), (right_dim,)), ((), ())), pre...  392 us
    ppermute x102, waiting for transfers between devices, across(): return lax.ppermute(values, 'row', [(i, i ^ step) for i in range(4)])  248 us
    convert_element_type x10, local copies, waits for them, and re-layouts, merged(): base.astype(F32) + ADAPTER_FACTOR * dot_of(low, up, 0, 0)  131 us
    all_gather x5, waiting for transfers between devices, gather_col(): return lax.all_gather(values, 'col', axis=0, tiled=False)  99.9 us
    unnamed x344, local copies, waits for them, and re-layouts  81.6 us
    all_gather x2, blocking collectives, sum_groups(): lax.all_gather(pack.astype(BF), ('dp', 'col'), axis=0, tiled=False)  64.7 us
    pallas_call x1, Pallas kernels, attend_back(): pl.pallas_call(attend_back_kernel, out_shape=(jax.ShapeDtypeStruct(query....  57.6 us
    ppermute x102, starting transfers between devices, across(): return lax.ppermute(values, 'row', [(i, i ^ step) for i in range(4)])  57 us
  transfers between devices with their start and end apart: 115, of which 28 were waited for; matrix products, arithmetic and copies ran while one was open for 49% of the time, Pallas kernels for 4%

profile of v1, /device:TPU:0, one launch (start us, length us, event | category | flops | bytes accessed | tf_op | source)
XLA Modules:
  0.0 1509.7 jit_solution(3735069139480697536)
XLA Ops:
  148.9 12.7 all-gather.11
  162.8 13.9 collective-permute-done.33
  231.9 99.9 %all-gather.19.cloned.1.call-done = bf16[16,3,512,128]{3,2,1,0:T(8,128)(2,1)} async-done(((bf16[4,3,512,128]{3,2,1,0:T(8,128)(2,1)}), bf16[16,3,512,128]{3,2,1,0:T(8,128)(2,1)}) %all-gather.19.cloned.1.call-update) | async-done | bytes 6291472 | tf_op jit(solution)/shard_map/all_gather | solution.py:679
  379.6 11.5 pad_maximum_fusion
  402.1 15.1 fusion.168.raw_ref
  422.8 12.2 collective-permute-done.15
  458.7 23.9 %attend.3 = (bf16[1024,512]{1,0:T(8,128)(2,1)}, f32[4,1,1024]{2,1,0:T(1,128)}) custom-call(s32[1]{0:T(128)} %dynamic_slice.169.prefix_ref, bf16[1024,512]{1,0:T(8,128)(2,1)} %get-tuple-element.29.q_ref, bf16[2048,512]{1,0:T(8,128)(2,1)} %copy-done.89, bf16[2048,512]{1,0:T(8,128)(2,1)} %copy-done.88), custom_call_target="tpu_custom_call" | custom-call | flops 3221225472 | bytes 4194304 | tf_op jit(solution)/shard_map/attend/pallas_call | solution.py:468
  485.7 15.8 %attend.2 = (bf16[1024,512]{1,0:T(8,128)(2,1)}, f32[4,1,1024]{2,1,0:T(1,128)}) custom-call(s32[1]{0:T(128)} %dynamic_slice.169.prefix_ref, bf16[1024,512]{1,0:T(8,128)(2,1)} %get-tuple-element.23.q_ref, bf16[2048,512]{1,0:T(8,128)(2,1)} %copy-done.89, bf16[2048,512]{1,0:T(8,128)(2,1)} %copy-done.88), custom_call_target="tpu_custom_call" | custom-call | flops 3221225472 | bytes 4194304 | tf_op jit(solution)/shard_map/attend/pallas_call | solution.py:468
  537.0 19.0 %copy.393 = f32[2,4,256,4,512]{4,3,2,1,0:T(4,128)S(1)} copy(f32[2,4,256,4,512]{4,2,3,1,0:T(8,128)} %convert_bitcast_fusion) | data formatting | bytes 33554432 | tf_op jit(solution)/shard_map/convert_element_type | solution.py:779
  556.0 11.4 copy.513
  574.1 11.5 add_convert_fusion
  601.7 20.9 %copy.384 = f32[4,512,2,4,256]{4,3,2,1,0:T(4,128)} copy(f32[4,512,2,4,256]{4,1,0,3,2:T(8,128)} %convert_bitcast_fusion.2) | data formatting | bytes 33554432 | tf_op jit(solution)/shard_map/convert_element_type | solution.py:779
  622.7 20.9 %reshape.410 = f32[2048,2048]{1,0:T(8,128)} reshape(f32[4,512,2,4,256]{4,3,2,1,0:T(4,128)} %copy.384) | data formatting | bytes 33554432 | tf_op jit(solution)/shard_map/convert_element_type | solution.py:779
  643.6 11.6 add_convert_fusion.2
  666.0 20.9 %copy.391 = f32[4,512,2,4,256]{4,3,2,1,0:T(4,128)} copy(f32[4,512,2,4,256]{4,1,0,3,2:T(8,128)} %convert_bitcast_fusion.1) | data formatting | bytes 33554432 | tf_op jit(solution)/shard_map/convert_element_type | solution.py:779
  687.0 20.7 %reshape.411 = f32[2048,2048]{1,0:T(8,128)} reshape(f32[4,512,2,4,256]{4,3,2,1,0:T(4,128)} %copy.391) | data formatting | bytes 33554432 | tf_op jit(solution)/shard_map/convert_element_type | solution.py:779
  716.4 16.4 %fusion.342 = f32[1024,2048]{1,0:T(8,128)} fusion(bf16[2048,2048]{1,0:T(8,128)(2,1)} %add_convert_fusion.2, bf16[1024,512]{0,1:T(8,128)(2,1)} %collective-permute-done.52, bf16[1024,512]{0,1:T(8,128)(2,1)S(1)} %collective-permute-done.51, bf16[1024,512]{0,1:T(8,128)(2,1)} %collective-permute-done.50, bf16[1024,512]{0,1:T(8,128)(2,1)S(1)} %get-tuple-element.214), kind=kOutput, calls=%fused_computation.564 | convolution fusion | flops 8606711808 | bytes 20971520 | tf_op jit(solution)/shard_map/dot_general | solution.py:424
  732.8 15.0 multiply_convert_fusion
  759.9 12.7 fusion.344
  772.6 15.9 %multiply_convert_fusion.1 = (bf16[1024,2048]{1,0:T(8,128)(2,1)}, bf16[1024,2048]{1,0:T(8,128)(2,1)}) fusion(f32[1024,2048]{1,0:T(8,128)} %fusion.344, bf16[2048,2048]{1,0:T(8,128)(2,1)S(1)} %add_convert_fusion.1, bf16[1024,512]{0,1:T(8,128)(2,1)} %collective-permute-done.27, bf16[1024,512]{0,1:T(8,128)(2,1)} %collective-permute-done.26, ...), kind=kOutput, calls=%fused_computation.29 | convolution fusion | flops 8621391872 | bytes 29360128 | tf_op jit(solution)/shard_map/dot_general | solution.py:424
  804.2 19.8 %collective-permute-done.55 = bf16[1024,512]{0,1:T(8,128)(2,1)S(1)} collective-permute-done((bf16[1024,512]{0,1:T(8,128)(2,1)S(1)}, bf16[1024,512]{0,1:T(8,128)(2,1)S(1)}, u32[]{:S(2)}, u32[]{:S(2)}) %collective-permute-start.55) | collective-permute-done | bytes 1048608 | tf_op jit(solution)/shard_map/ppermute | solution.py:650
  833.4 21.2 %collective-permute-done.57 = f32[2,1024]{1,0:T(2,128)S(1)} collective-permute-done((f32[2,1024]{1,0:T(2,128)S(1)}, f32[2,1024]{1,0:T(2,128)S(1)}, u32[]{:S(2)}, u32[]{:S(2)}) %collective-permute-start.57) | collective-permute-done | bytes 8224 | tf_op jit(solution)/shard_map/ppermute | solution.py:650
  861.9 21.4 %collective-permute-done.44 = f32[2,1024]{1,0:T(2,128)S(1)} collective-permute-done((f32[2,1024]{1,0:T(2,128)S(1)}, f32[2,1024]{1,0:T(2,128)S(1)}, u32[]{:S(2)}, u32[]{:S(2)}) %collective-permute-start.44) | collective-permute-done | bytes 8224 | tf_op jit(solution)/shard_map/ppermute | solution.py:650
  894.7 15.6 %collective-permute-done.105 = f32[16,1024]{1,0:T(8,128)S(1)} collective-permute-done((f32[16,1024]{1,0:T(8,128)S(1)}, f32[16,1024]{1,0:T(8,128)S(1)}, u32[]{:S(2)}, u32[]{:S(2)}) %collective-permute-start.105) | collective-permute-done | bytes 65568 | tf_op jit(solution)/shard_map/ppermute | solution.py:650
  917.9 20.0 %fusion.13 = (bf16[1024,2048]{1,0:T(8,128)(2,1)}, bf16[1024,2048]{1,0:T(8,128)(2,1)}) fusion(bf16[1024,2048]{1,0:T(8,128)(2,1)} %get-tuple-element.222, f32[1024,2048]{1,0:T(8,128)} %fusion.342, bf16[2048,2048]{1,0:T(8,128)(2,1)} %add_convert_fusion, bf16[1024,512]{0,1:T(8,128)(2,1)} %copy-done.135, bf16[1024,512]{0,1:T(8,128)(2,1)} %copy-done.133, ...), kind=kOutput, calls=%fused_computation.25 | convolution fusion | flops 8640266240 | bytes 33554432 | tf_op jit(solution)/shard_map/dot_general | solution.py:424
  968.5 19.8 %fusion.5 = (bf16[1024,2048]{1,0:T(8,128)(2,1)}, bf16[1024,2048]{1,0:T(8,128)(2,1)}) fusion(bf16[1024,2048]{1,0:T(8,128)(2,1)} %get-tuple-element.220, f32[1024,2048]{1,0:T(8,128)} %fusion.344, bf16[2048,2048]{1,0:T(8,128)(2,1)} %add_convert_fusion, bf16[1024,512]{0,1:T(8,128)(2,1)} %collective-permute-done.60, ...), kind=kOutput, calls=%fused_computation.17 | convolution fusion | flops 8640266240 | bytes 33554432 | tf_op jit(solution)/shard_map/dot_general | solution.py:424
  1069.2 22.1 %collective-permute-done.63 = bf16[1024,512]{0,1:T(8,128)(2,1)} collective-permute-done((bf16[1024,512]{0,1:T(8,128)(2,1)}, bf16[1024,512]{0,1:T(8,128)(2,1)}, u32[]{:S(2)}, u32[]{:S(2)}) %collective-permute-start.63) | collective-permute-done | bytes 1048608 | tf_op jit(solution)/shard_map/ppermute | solution.py:650
  1124.5 24.7 %collective-permute-done.99 = f32[32,1024]{1,0:T(8,128)S(1)} collective-permute-done((f32[32,1024]{1,0:T(8,128)S(1)}, f32[32,1024]{1,0:T(8,128)S(1)}, u32[]{:S(2)}, u32[]{:S(2)}) %collective-permute-start.99) | collective-permute-done | bytes 131104 | tf_op jit(solution)/shard_map/ppermute | solution.py:650
  1158.0 32.7 %all_gather.92 = bf16[8,64,512]{2,1,0:T(8,128)(2,1)S(1)} all-gather(bf16[1,64,512]{2,1,0:T(8,128)(2,1)S(1)} %pad_maximum_fusion.45), channel_id=1, replica_groups=mesh['dp'=2,'row'=4,'col'=4] {'dp','col'}, dimensions={0}, use_global_device_ids=true | all-gather | bytes 589824 | tf_op jit(solution)/shard_map/all_gather | solution.py:975
  1210.1 57.6 %attend_back.1 = (f32[2048,512]{1,0:T(8,128)}, f32[2048,512]{1,0:T(8,128)}, f32[2048,512]{1,0:T(8,128)}) custom-call(s32[1]{0:T(128)} %dynamic_slice.169.prefix_ref, bf16[2048,512]{1,0:T(8,128)(2,1)} %pad_maximum_fusion.11.q_ref, bf16[2048,512]{1,0:T(8,128)(2,1)} %pad_maximum_fusion.12.grad_ref, bf16[2048,512]{1,0:T(8,128)(2,1)} %pad_maximum_fusion.13.out_ref, ...), custom_call_target="tpu_custom_call" | custom-call | flops 15032385536 | bytes 25165824 | tf_op jit(solution)/shard_map/attend_back/pallas_call | solution.py:538
  1392.2 11.7 all-gather.9
  1412.7 32.0 %all-gather.6 = bf16[384,512]{1,0:T(8,128)(2,1)S(1)} all-gather(bf16[48,512]{1,0:T(8,128)(2,1)S(1)} %fusion.118), channel_id=8, replica_groups=mesh['dp'=2,'row'=4,'col'=4] {'dp','col'}, dimensions={0}, use_global_device_ids=true | all-gather | bytes 442368 | tf_op jit(solution)/shard_map/all_gather | solution.py:975
  (860 shorter events, 782.8 us)
Async XLA Ops:
  7.2 178.9 %all-gather.21.cloned.1.call-start = ((), (), s32[]{:S(2)}) async-start(), calls=%async_computation.4 | async-start | bytes 1310720 | tf_op jit(solution)/shard_map/all_gather | solution.py:679
  17.1 212.7 %all-gather.23.cloned.1.call-start = ((), (), s32[]{:S(2)}) async-start(), calls=%async_computation.5 | async-start | bytes 5242880 | tf_op jit(solution)/shard_map/all_gather | solution.py:679
  47.6 183.7 %all-gather.27.cloned.1.call-start = ((), (), s32[]{:S(2)}) async-start(), calls=%async_computation.7 | async-start | bytes 5242880 | tf_op jit(solution)/shard_map/all_gather | solution.py:679
  64.3 267.4 %all-gather.19.cloned.1.call-start = ((), (), s32[]{:S(2)}) async-start(), calls=%async_computation.3 | async-start | bytes 7864320 | tf_op jit(solution)/shard_map/all_gather | solution.py:679
  115.0 67.3 %all-to-all-start = ((bf16[4,16,2048]{2,1,0:T(8,128)(2,1)}), bf16[4,16,2048]{2,1,0:T(8,128)(2,1)}, u32[]{:S(2)}, u32[]{:S(2)}) async-start(bf16[4,16,2048]{2,1,0:T(8,128)(2,1)} %pad_maximum_fusion.41), calls=%async_computation | async-start | bytes 524288 | tf_op jit(solution)/shard_map/all_to_all | solution.py:760
  119.8 406.9 %all-gather.25.cloned.1.call-start = ((), (), s32[]{:S(2)}) async-start(), calls=%async_computation.6 | async-start | bytes 5242880 | tf_op jit(solution)/shard_map/all_gather | solution.py:679
  122.5 54.2 %collective-permute-start.12 = (bf16[1024,512]{0,1:T(8,128)(2,1)S(1)}, bf16[1024,512]{0,1:T(8,128)(2,1)}, u32[]{:S(2)}, u32[]{:S(2)}) collective-permute-start(bf16[1024,512]{0,1:T(8,128)(2,1)S(1)} %copy.497), channel_id=1, source_target_pairs={{0,8},{4,12},{8,0},{12,4},{1,9},{5,13},{9,1},{13,5},{2,10},{6,14},... | collective-permute-start | bytes 3145736 | tf_op jit(solution)/shard_map/ppermute | solution.py:650
  123.8 59.8 %collective-permute-start.1 = (bf16[1024,512]{0,1:T(8,128)(2,1)S(1)}, bf16[1024,512]{0,1:T(8,128)(2,1)}, u32[]{:S(2)}, u32[]{:S(2)}) collective-permute-start(bf16[1024,512]{0,1:T(8,128)(2,1)S(1)} %copy.496), channel_id=1, source_target_pairs={{0,8},{4,12},{8,0},{12,4},{1,9},{5,13},{9,1},{13,5},{2,10},{6,14},... | collective-permute-start | bytes 3145736 | tf_op jit(solution)/shard_map/ppermute | solution.py:650
  229.9 361.6 %collective-permute-start.31 = (bf16[4,4,512,256]{3,2,1,0:T(8,128)(2,1)}, bf16[4,4,512,256]{3,2,1,0:T(8,128)(2,1)}, u32[]{:S(2)}, u32[]{:S(2)}) collective-permute-start(bf16[4,4,512,256]{3,2,1,0:T(8,128)(2,1)} %bitcast.514), channel_id=1, source_target_pairs={{0,16},{16,0},{1,17},{17,1},{2,18},{18,2},{3,19},{19,3},{4,20},{20... | collective-permute-start | bytes 12582920 | tf_op jit(solution)/shard_map/ppermute | solution.py:683
  231.3 293.0 %collective-permute-start.39 = (bf16[4,4,256,512]{3,2,1,0:T(8,128)(2,1)}, bf16[4,4,256,512]{3,2,1,0:T(8,128)(2,1)}, u32[]{:S(2)}, u32[]{:S(2)}) collective-permute-start(bf16[4,4,256,512]{3,2,1,0:T(8,128)(2,1)} %bitcast.516), channel_id=1, source_target_pairs={{0,16},{16,0},{1,17},{17,1},{2,18},{18,2},{3,19},{19,3},{4,20},{20... | collective-permute-start | bytes 12582920 | tf_op jit(solution)/shard_map/ppermute | solution.py:683
  519.6 47.9 %collective-permute-start.22 = (bf16[1024,512]{0,1:T(8,128)(2,1)}, bf16[1024,512]{0,1:T(8,128)(2,1)}, u32[]{:S(2)}, u32[]{:S(2)}) collective-permute-start(bf16[1024,512]{0,1:T(8,128)(2,1)} %add_convert_fusion.20), channel_id=1, source_target_pairs={{0,8},{4,12},{8,0},{12,4},{1,9},{5,13},{9,1},{13,5},{2,10},{6,14},... | collective-permute-start | bytes 3145736 | tf_op jit(solution)/shard_map/ppermute | solution.py:650
  526.7 130.2 %collective-permute-start.35 = (bf16[4,4,512,256]{3,2,1,0:T(8,128)(2,1)}, bf16[4,4,512,256]{3,2,1,0:T(8,128)(2,1)}, u32[]{:S(2)}, u32[]{:S(2)}) collective-permute-start(bf16[4,4,512,256]{3,2,1,0:T(8,128)(2,1)} %bitcast.518), channel_id=1, source_target_pairs={{0,16},{16,0},{1,17},{17,1},{2,18},{18,2},{3,19},{19,3},{4,20},{20... | collective-permute-start | bytes 12582920 | tf_op jit(solution)/shard_map/ppermute | solution.py:683
  590.9 65.7 %collective-permute-start.51 = (bf16[1024,512]{0,1:T(8,128)(2,1)S(1)}, bf16[1024,512]{0,1:T(8,128)(2,1)S(1)}, u32[]{:S(2)}, u32[]{:S(2)}) collective-permute-start(bf16[1024,512]{0,1:T(8,128)(2,1)S(1)} %get-tuple-element.214), channel_id=1, source_target_pairs={{0,8},{4,12},{8,0},{12,4},{1,9},{5,13},{9,1},{13,5},{2,10},{6,14},... | collective-permute-start | bytes 3145736 | tf_op jit(solution)/shard_map/ppermute | solution.py:650
  655.1 61.3 %collective-permute-start.50 = (bf16[1024,512]{0,1:T(8,128)(2,1)S(1)}, bf16[1024,512]{0,1:T(8,128)(2,1)}, u32[]{:S(2)}, u32[]{:S(2)}) collective-permute-start(bf16[1024,512]{0,1:T(8,128)(2,1)S(1)} %get-tuple-element.214), channel_id=1, source_target_pairs={{0,4},{4,0},{8,12},{12,8},{1,5},{5,1},{9,13},{13,9},{2,6},{6,2},{1... | collective-permute-start | bytes 3145736 | tf_op jit(solution)/shard_map/ppermute | solution.py:650
  655.1 61.0 %collective-permute-start.26 = (bf16[1024,512]{0,1:T(8,128)(2,1)}, bf16[1024,512]{0,1:T(8,128)(2,1)}, u32[]{:S(2)}, u32[]{:S(2)}) collective-permute-start(bf16[1024,512]{0,1:T(8,128)(2,1)} %get-tuple-element.213), channel_id=1, source_target_pairs={{0,8},{4,12},{8,0},{12,4},{1,9},{5,13},{9,1},{13,5},{2,10},{6,14},... | collective-permute-start | bytes 3145736 | tf_op jit(solution)/shard_map/ppermute | solution.py:650
  656.6 59.8 %collective-permute-start.52 = (bf16[1024,512]{0,1:T(8,128)(2,1)S(1)}, bf16[1024,512]{0,1:T(8,128)(2,1)}, u32[]{:S(2)}, u32[]{:S(2)}) collective-permute-start(bf16[1024,512]{0,1:T(8,128)(2,1)S(1)} %collective-permute-done.51), channel_id=1, source_target_pairs={{0,4},{4,0},{8,12},{12,8},{1,5},{5,1},{9,13},{13,9},{2,6},{6,2},{1... | collective-permute-start | bytes 3145736 | tf_op jit(solution)/shard_map/ppermute | solution.py:650
  754.3 49.9 %collective-permute-start.53 = (bf16[1024,512]{0,1:T(8,128)(2,1)}, bf16[1024,512]{0,1:T(8,128)(2,1)}, u32[]{:S(2)}, u32[]{:S(2)}) collective-permute-start(bf16[1024,512]{0,1:T(8,128)(2,1)} %fusion.72), channel_id=1, source_target_pairs={{0,4},{4,0},{8,12},{12,8},{1,5},{5,1},{9,13},{13,9},{2,6},{6,2},{1... | collective-permute-start | bytes 3145736 | tf_op jit(solution)/shard_map/ppermute | solution.py:650
  793.9 60.7 %collective-permute-start.40 = (bf16[1024,512]{0,1:T(8,128)(2,1)S(1)}, bf16[1024,512]{0,1:T(8,128)(2,1)S(1)}, u32[]{:S(2)}, u32[]{:S(2)}) collective-permute-start(bf16[1024,512]{0,1:T(8,128)(2,1)S(1)} %fusion.74), channel_id=1, source_target_pairs={{0,4},{4,0},{8,12},{12,8},{1,5},{5,1},{9,13},{13,9},{2,6},{6,2},{1... | collective-permute-start | bytes 3145736 | tf_op jit(solution)/shard_map/ppermute | solution.py:650
  861.9 54.1 %collective-permute-start.69 = (bf16[1024,512]{0,1:T(8,128)(2,1)S(1)}, bf16[1024,512]{0,1:T(8,128)(2,1)S(1)}, u32[]{:S(2)}, u32[]{:S(2)}) collective-permute-start(bf16[1024,512]{0,1:T(8,128)(2,1)S(1)} %get-tuple-element.212), channel_id=1, source_target_pairs={{0,4},{4,0},{8,12},{12,8},{1,5},{5,1},{9,13},{13,9},{2,6},{6,2},{1... | collective-permute-start | bytes 3145736 | tf_op jit(solution)/shard_map/ppermute | solution.py:650
  894.0 257.1 %collective-permute-start.97 = (f32[16,1024]{1,0:T(8,128)}, f32[16,1024]{1,0:T(8,128)}, u32[]{:S(2)}, u32[]{:S(2)}) collective-permute-start(f32[16,1024]{1,0:T(8,128)} %add.680), channel_id=1, source_target_pairs={{0,8},{4,12},{8,0},{12,4},{1,9},{5,13},{9,1},{13,5},{2,10},{6,14},... | collective-permute-start | bytes 196616 | tf_op jit(solution)/shard_map/ppermute | solution.py:650
  914.5 54.0 %collective-permute-start.58 = (bf16[1024,512]{0,1:T(8,128)(2,1)S(1)}, bf16[1024,512]{0,1:T(8,128)(2,1)}, u32[]{:S(2)}, u32[]{:S(2)}) collective-permute-start(bf16[1024,512]{0,1:T(8,128)(2,1)S(1)} %fusion.27), channel_id=1, source_target_pairs={{0,4},{4,0},{8,12},{12,8},{1,5},{5,1},{9,13},{13,9},{2,6},{6,2},{1... | collective-permute-start | bytes 3145736 | tf_op jit(solution)/shard_map/ppermute | solution.py:650
  915.5 53.0 %collective-permute-start.60 = (bf16[1024,512]{0,1:T(8,128)(2,1)}, bf16[1024,512]{0,1:T(8,128)(2,1)}, u32[]{:S(2)}, u32[]{:S(2)}) collective-permute-start(bf16[1024,512]{0,1:T(8,128)(2,1)} %collective-permute-done.59), channel_id=1, source_target_pairs={{0,4},{4,0},{8,12},{12,8},{1,5},{5,1},{9,13},{13,9},{2,6},{6,2},{1... | collective-permute-start | bytes 3145736 | tf_op jit(solution)/shard_map/ppermute | solution.py:650
  956.4 80.9 %collective-permute-start.73 = (bf16[1024,512]{0,1:T(8,128)(2,1)}, bf16[1024,512]{0,1:T(8,128)(2,1)}, u32[]{:S(2)}, u32[]{:S(2)}) collective-permute-start(bf16[1024,512]{0,1:T(8,128)(2,1)} %add_convert_fusion.10), channel_id=1, source_target_pairs={{0,4},{4,0},{8,12},{12,8},{1,5},{5,1},{9,13},{13,9},{2,6},{6,2},{1... | collective-permute-start | bytes 3145736 | tf_op jit(solution)/shard_map/ppermute | solution.py:650
  959.8 99.0 %collective-permute-start.72 = (bf16[1024,512]{0,1:T(8,128)(2,1)}, bf16[1024,512]{0,1:T(8,128)(2,1)}, u32[]{:S(2)}, u32[]{:S(2)}) collective-permute-start(bf16[1024,512]{0,1:T(8,128)(2,1)} %add_convert_fusion.11), channel_id=1, source_target_pairs={{0,4},{4,0},{8,12},{12,8},{1,5},{5,1},{9,13},{13,9},{2,6},{6,2},{1... | collective-permute-start | bytes 3145736 | tf_op jit(solution)/shard_map/ppermute | solution.py:650
  1058.8 94.7 %collective-permute-start.95 = (f32[16,1024]{1,0:T(8,128)S(1)}, f32[16,1024]{1,0:T(8,128)}, u32[]{:S(2)}, u32[]{:S(2)}) collective-permute-start(f32[16,1024]{1,0:T(8,128)S(1)} %copy-done.100), channel_id=1, source_target_pairs={{0,8},{4,12},{8,0},{12,4},{1,9},{5,13},{9,1},{13,5},{2,10},{6,14},... | collective-permute-start | bytes 196616 | tf_op jit(solution)/shard_map/ppermute | solution.py:650
  1069.2 51.8 %collective-permute-start.98 = (f32[32,1024]{1,0:T(8,128)}, f32[32,1024]{1,0:T(8,128)}, u32[]{:S(2)}, u32[]{:S(2)}) collective-permute-start(f32[32,1024]{1,0:T(8,128)} %maximum_multiply_fusion.2), channel_id=1, source_target_pairs={{0,4},{4,0},{8,12},{12,8},{1,5},{5,1},{9,13},{13,9},{2,6},{6,2},{1... | collective-permute-start | bytes 393224 | tf_op jit(solution)/shard_map/ppermute | solution.py:650
  1123.6 67.1 %collective-permute-start.78 = (bf16[1024,512]{0,1:T(8,128)(2,1)}, bf16[1024,512]{0,1:T(8,128)(2,1)}, u32[]{:S(2)}, u32[]{:S(2)}) collective-permute-start(bf16[1024,512]{0,1:T(8,128)(2,1)} %get-tuple-element.128), channel_id=1, source_target_pairs={{0,8},{4,12},{8,0},{12,4},{1,9},{5,13},{9,1},{13,5},{2,10},{6,14},... | collective-permute-start | bytes 3145736 | tf_op jit(solution)/shard_map/ppermute | solution.py:650
  1357.4 121.8 %collective-permute-start.87 = (bf16[1024,512]{0,1:T(8,128)(2,1)}, bf16[1024,512]{0,1:T(8,128)(2,1)}, u32[]{:S(2)}, u32[]{:S(2)}) collective-permute-start(bf16[1024,512]{0,1:T(8,128)(2,1)} %fusion.88), channel_id=1, source_target_pairs={{0,4},{4,0},{8,12},{12,8},{1,5},{5,1},{9,13},{13,9},{2,6},{6,2},{1... | collective-permute-start | bytes 3145736 | tf_op jit(solution)/shard_map/ppermute | solution.py:650
  1357.5 89.1 %collective-permute-start.88 = (bf16[1024,512]{0,1:T(8,128)(2,1)}, bf16[1024,512]{0,1:T(8,128)(2,1)}, u32[]{:S(2)}, u32[]{:S(2)}) collective-permute-start(bf16[1024,512]{0,1:T(8,128)(2,1)} %fusion.80), channel_id=1, source_target_pairs={{0,4},{4,0},{8,12},{12,8},{1,5},{5,1},{9,13},{13,9},{2,6},{6,2},{1... | collective-permute-start | bytes 3145736 | tf_op jit(solution)/shard_map/ppermute | solution.py:650
  1357.9 123.8 %collective-permute-start.82 = (bf16[1024,512]{0,1:T(8,128)(2,1)}, bf16[1024,512]{0,1:T(8,128)(2,1)}, u32[]{:S(2)}, u32[]{:S(2)}) collective-permute-start(bf16[1024,512]{0,1:T(8,128)(2,1)} %fusion.90), channel_id=1, source_target_pairs={{0,4},{4,0},{8,12},{12,8},{1,5},{5,1},{9,13},{13,9},{2,6},{6,2},{1... | collective-permute-start | bytes 3145736 | tf_op jit(solution)/shard_map/ppermute | solution.py:650
  1365.3 92.4 %all-gather.29.cloned.1.call-start = ((), (), s32[]{:S(2)}) async-start(), calls=%async_computation.8 | async-start | bytes 2555904 | tf_op jit(solution)/shard_map/all_gather | solution.py:990
  1389.1 62.9 %collective-permute-start.83 = (bf16[1024,512]{0,1:T(8,128)(2,1)}, bf16[1024,512]{0,1:T(8,128)(2,1)}, u32[]{:S(2)}, u32[]{:S(2)}) collective-permute-start(bf16[1024,512]{0,1:T(8,128)(2,1)} %fusion.82), channel_id=1, source_target_pairs={{0,4},{4,0},{8,12},{12,8},{1,5},{5,1},{9,13},{13,9},{2,6},{6,2},{1... | collective-permute-start | bytes 3145736 | tf_op jit(solution)/shard_map/ppermute | solution.py:650
  (238 other events, 6272.5 us)
Sparse Core Ops, SparseCore 0:
  17.2 28.9 all-gather.20
  47.8 87.2 all-gather.22
  136.7 79.1 all-gather.26
  217.9 113.8 all-gather.18
  333.2 78.9 all-gather.24
  1404.0 30.9 all-gather.28

commit v2 on v1

--- a/solution.py
+++ b/solution.py
@@ -413,7 +413,7 @@
 
 
 LOG2E = 1.4426950408889634
-CHUNKS = 2
+CHUNKS = 1
 Q_BLOCK = 512
 K_BLOCK = 512
 BF = jnp.bfloat16
@@ -486,8 +486,29 @@
     )(prefix, query, key, value)
 
 
+def row_sums(values):
+    return lax.dot_general(
+        jnp.ones((8, values.shape[1]), F32),
+        values,
+        (((1,), (1,)), ((), ())),
+        precision=lax.Precision.HIGHEST,
+        preferred_element_type=F32,
+    )[0:1]
+
+
 def attend_back_kernel(
-    prefix_ref, q_ref, grad_ref, out_ref, log_ref, k_ref, v_ref, dq_ref, dk_ref, dv_ref
+    prefix_ref,
+    q_ref,
+    grad_ref,
+    out_ref,
+    log_ref,
+    k_ref,
+    v_ref,
+    dq_ref,
+    dk_ref,
+    dv_ref,
+    q_sum_ref,
+    k_sum_ref,
 ):
     rows = q_ref.shape[0]
     start = pl.program_id(1) * rows
@@ -504,13 +525,7 @@
     limit = jnp.maximum(lax.broadcasted_iota(jnp.int32, (1, rows), 1) + start, prefix - 1)
     key_pos = lax.broadcasted_iota(jnp.int32, (K_BLOCK, rows), 0)
     log_total = log_ref[0]
-    delta = lax.dot_general(
-        jnp.ones((8, HEAD), F32),
-        grad.astype(F32) * out_ref[...].astype(F32),
-        (((1,), (1,)), ((), ())),
-        precision=lax.Precision.HIGHEST,
-        preferred_element_type=F32,
-    )[0:1]
+    delta = row_sums(grad.astype(F32) * out_ref[...].astype(F32))
 
     def body(index, d_query):
         at = pl.multiple_of(index * K_BLOCK, K_BLOCK)
@@ -524,11 +539,15 @@
         dk_ref[span, :] += dot_of(d_scores, query, 1, 0)
         return d_query + dot_of(d_scores, key, 0, 0)
 
-    dq_ref[...] = lax.fori_loop(0, blocks, body, jnp.zeros((rows, HEAD), F32)) * HEAD**-0.5
+    d_query = lax.fori_loop(0, blocks, body, jnp.zeros((rows, HEAD), F32)) * HEAD**-0.5
+    dq_ref[...] = d_query
+    q_sum_ref[0] = row_sums(d_query * query.astype(F32))
 
     @pl.when(pl.program_id(1) == pl.num_programs(1) - 1)
     def _():
-        dk_ref[...] = dk_ref[...] * HEAD**-0.5
+        d_key = dk_ref[...] * HEAD**-0.5
+        dk_ref[...] = d_key
+        k_sum_ref[0] = row_sums(d_key * k_ref[...].astype(F32))
 
 
 def attend_back(prefix, query, grad, mixed, log_total, key, value):
@@ -541,6 +560,8 @@
             jax.ShapeDtypeStruct(query.shape, F32),
             jax.ShapeDtypeStruct(key.shape, F32),
             jax.ShapeDtypeStruct(key.shape, F32),
+            jax.ShapeDtypeStruct((heads, 1, rows), F32),
+            jax.ShapeDtypeStruct((heads, 1, length), F32),
         ),
         grid_spec=pltpu.PrefetchScalarGridSpec(
             num_scalar_prefetch=1,
@@ -553,7 +574,13 @@
                 k_spec,
                 k_spec,
             ],
-            out_specs=[q_spec, k_spec, k_spec],
+            out_specs=[
+                q_spec,
+                k_spec,
+                k_spec,
+                pl.BlockSpec((1, 1, Q_BLOCK), lambda h, i, p: (h, 0, i)),
+                pl.BlockSpec((1, 1, length), lambda h, i, p: (h, 0, 0)),
+            ],
         ),
         cost_estimate=pl.CostEstimate(
             flops=7 * rows * length * heads * HEAD,
@@ -619,10 +646,10 @@
     out_ref[:, 2 * width :] = dv_ref[...].astype(BF)
 
 
-def unrotate_rows(raw, d_query, d_key, d_value, scales, backs, gains, cosine, sine):
-    rows, width = d_query.shape
+def unrotate_rows(raw, d_query, d_key, d_value, scales, backs, gains, cosine, sine, first):
+    rows, width = raw.shape[0], d_query.shape[1]
     step = min(512, rows)
-    part = pl.BlockSpec((step, width), lambda i: (i, 0))
+    part = pl.BlockSpec((step, width), lambda i: (i + first // step, 0))
     table = pl.BlockSpec((step, HEAD), lambda i: (i, 0))
     pair = pl.BlockSpec((step, 2), lambda i: (i, 0))
     wide = pl.BlockSpec((step, 3 * width), lambda i: (i, 0))
@@ -646,6 +673,781 @@
     )(raw, d_query, d_key, d_value, scales, backs, gains, cosine, sine)
 
 
+def flip(values):
+    rank = values.shape[1]
+    row = lax.broadcasted_iota(jnp.int32, (rank, rank), 0)
+    unit = (row == lax.broadcasted_iota(jnp.int32, (rank, rank), 1)).astype(BF)
+    return dot_of(unit, values, 1, 1).astype(BF)
+
+
+def row_pack_kernel(set_ref, qkv_ref, attn_ref, expand_ref, reduce_ref, out_ref):
+    for part in range(3):
+        out_ref[16 * part : 16 * part + 16, :] = flip(qkv_ref[part, 0])
+    out_ref[48:64, :] = attn_ref[0]
+    for part in range(2):
+        out_ref[64 + 16 * part : 80 + 16 * part, :] = flip(expand_ref[part, 0])
+    out_ref[96:112, :] = reduce_ref[0]
+
+
+def row_pack_of(which, qkv_low, attn_up, expand_low, reduce_up):
+    width = attn_up.shape[2]
+    up = pl.BlockSpec((1, 16, width), lambda i, c: (c[0], 0, 0))
+
+    def low(parts):
+        return pl.BlockSpec((parts, 1, width, 16), lambda i, c: (0, c[0], 0, 0))
+
+    return pl.pallas_call(
+        row_pack_kernel,
+        out_shape=jax.ShapeDtypeStruct((112, width), BF),
+        grid_spec=pltpu.PrefetchScalarGridSpec(
+            num_scalar_prefetch=1,
+            grid=(1,),
+            in_specs=[low(3), up, low(2), up],
+            out_specs=pl.BlockSpec((112, width), lambda i, c: (0, 0)),
+        ),
+        name="row_pack",
+    )(which, qkv_low, attn_up, expand_low, reduce_up)
+
+
+def col_pack_kernel(set_ref, qkv_ref, attn_ref, expand_ref, reduce_ref, out_ref):
+    sub, ff_sub = qkv_ref.shape[3], expand_ref.shape[3]
+    for part in range(3):
+        out_ref[0, :, part * sub : (part + 1) * sub] = qkv_ref[part, 0]
+    at = 4 * sub
+    out_ref[0, :, 3 * sub : at] = flip(attn_ref[0])
+    for part in range(2):
+        out_ref[0, :, at : at + ff_sub] = expand_ref[part, 0]
+        at += ff_sub
+    out_ref[0, :, at:] = flip(reduce_ref[0])
+
+
+def col_pack_of(which, qkv_up, attn_low, expand_up, reduce_low):
+    cols = which.shape[0] - 1
+    sub, ff_sub = qkv_up.shape[3] // 4, expand_up.shape[3] // 4
+
+    def up(parts, size):
+        return pl.BlockSpec((parts, 1, 16, size), lambda i, c: (0, c[i], 0, c[cols]))
+
+    def low(size):
+        return pl.BlockSpec((1, size, 16), lambda i, c: (c[i], c[cols], 0))
+
+    total = 4 * sub + 3 * ff_sub
+    return pl.pallas_call(
+        col_pack_kernel,
+        out_shape=jax.ShapeDtypeStruct((cols, 16, total), BF),
+        grid_spec=pltpu.PrefetchScalarGridSpec(
+            num_scalar_prefetch=1,
+            grid=(cols,),
+            in_specs=[up(3, sub), low(sub), up(2, ff_sub), low(ff_sub)],
+            out_specs=pl.BlockSpec((1, 16, total), lambda i, c: (i, 0, 0)),
+        ),
+        name="col_pack",
+    )(which, qkv_up, attn_low, expand_up, reduce_low)
+
+
+def cost_of(flops, bytes_accessed):
+    return pl.CostEstimate(flops=int(flops), bytes_accessed=int(bytes_accessed), transcendentals=0)
+
+
+def row_tile(rows):
+    return min(512, rows)
+
+
+def merge_rows_kernel(pair_ref, own_ref, other_ref, low_ref, up_ref, out_ref):
+    def put(piece):
+        for block in range(4):
+            base = piece[(0, block) + (0,) * (len(piece.shape) - 4)].astype(F32)
+            extra = dot_of(low_ref[block, 0], up_ref[...], 0, 0)
+            out_ref[block, 0] = (base + ADAPTER_FACTOR * extra).astype(BF)
+
+    mine = pl.program_id(0) == pair_ref[0]
+    pl.when(mine)(functools.partial(put, own_ref))
+    pl.when(jnp.logical_not(mine))(functools.partial(put, other_ref))
+
+
+def merge_columns_kernel(pair_ref, *refs):
+    *pieces, low_ref, up_ref, out_ref = refs
+    width = out_ref.shape[1] // 4
+
+    def put(piece):
+        for block in range(4):
+            span = slice(block * width, (block + 1) * width)
+            extra = dot_of(low_ref[0], up_ref[:, span], 0, 0)
+            out_ref[:, span] = (piece[0, block].astype(F32) + ADAPTER_FACTOR * extra).astype(BF)
+
+    if len(pieces) == 1:
+        put(pieces[0])
+        return
+    mine = pl.program_id(0) == pair_ref[0]
+    pl.when(mine)(functools.partial(put, pieces[0]))
+    pl.when(jnp.logical_not(mine))(functools.partial(put, pieces[1]))
+
+
+def merge_qkv(pair, own, other, low, up):
+    cols, _, parts, cut, sub = own.shape
+    last = cols * parts - 1
+
+    def piece(half, relative):
+        def place(h, p, c, pair_ref):
+            at = p * cols + c
+            at = jnp.where(h == half(pair_ref[0]), at, jnp.where(h == 0, 0, last))
+            which = lax.rem(at, cols)
+            if relative:
+                which = lax.rem(which - pair_ref[1] + cols, cols)
+            return (which, 0, lax.div(at, cols), 0, 0)
+
+        return pl.BlockSpec((1, 4, 1, cut, sub), place)
+
+    whole = pl.pallas_call(
+        merge_rows_kernel,
+        out_shape=jax.ShapeDtypeStruct((4, 2, cut, parts * cols * sub), BF),
+        grid_spec=pltpu.PrefetchScalarGridSpec(
+            num_scalar_prefetch=1,
+            grid=(2, parts, cols),
+            in_specs=[
+                piece(lambda one: one, False),
+                piece(lambda one: 1 - one, True),
+                pl.BlockSpec((4, 1, 16, cut), lambda h, p, c, one: (0, h, p, 0)),
+                pl.BlockSpec((16, sub), lambda h, p, c, one: (p, c)),
+            ],
+            out_specs=pl.BlockSpec(
+                (4, 1, cut, sub), lambda h, p, c, one: (0, h, 0, p * cols + c)
+            ),
+        ),
+        cost_estimate=cost_of(0, 8 * own.size),
+        name="merge_qkv",
+    )(pair, own, other, low.reshape(16 * parts, 4, 2, cut).transpose(1, 2, 0, 3), up)
+    return whole.reshape(8 * cut, parts * cols * sub)
+
+
+def half_specs(block, cols):
+    def piece(half, relative):
+        def place(h, c, pair_ref):
+            at = jnp.where(h == half(pair_ref[0]), c, jnp.where(h == 0, 0, cols - 1))
+            if relative:
+                at = lax.rem(at - pair_ref[1] + cols, cols)
+            return (at,) + (0,) * (len(block) - 1)
+
+        return pl.BlockSpec(block, place)
+
+    return [piece(lambda one: one, False), piece(lambda one: 1 - one, True)]
+
+
+def merge_expand(pair, own, other, low, up):
+    cols, _, width, cut = own.shape
+    whole = pl.pallas_call(
+        merge_rows_kernel,
+        out_shape=jax.ShapeDtypeStruct((4, 1, width, 2 * cols * cut), BF),
+        grid_spec=pltpu.PrefetchScalarGridSpec(
+            num_scalar_prefetch=1,
+            grid=(2, cols),
+            in_specs=half_specs((1, 4, width, cut), cols)
+            + [
+                pl.BlockSpec((4, 1, 16, width), lambda h, c, one: (0, 0, 0, 0)),
+                pl.BlockSpec((16, cut), lambda h, c, one: (0, 2 * c + h)),
+            ],
+            out_specs=pl.BlockSpec((4, 1, width, cut), lambda h, c, one: (0, 0, 0, 2 * c + h)),
+        ),
+        cost_estimate=cost_of(0, 8 * own.size),
+        name="merge_expand",
+    )(pair, own, other, low.reshape(16, 4, 1, width).transpose(1, 2, 0, 3), up)
+    return whole.reshape(4 * width, 2 * cols * cut)
+
+
+def merge_out(pair, pieces, low, up):
+    cols, _, rows, width = pieces[0].shape
+    takes = len(pieces)
+    block = (1, 4, rows, width)
+    specs = half_specs(block, cols)
+    if takes == 1:
+        specs = [pl.BlockSpec(block, lambda h, c, one: (c, 0, 0, 0))]
+    return pl.pallas_call(
+        merge_columns_kernel,
+        out_shape=jax.ShapeDtypeStruct((takes * cols * rows, 4 * width), BF),
+        grid_spec=pltpu.PrefetchScalarGridSpec(
+            num_scalar_prefetch=1,
+            grid=(takes, cols),
+            in_specs=specs
+            + [
+                pl.BlockSpec((1, 16, rows), lambda h, c, one: (takes * c + h, 0, 0)),
+                pl.BlockSpec((16, 4 * width), lambda h, c, one: (0, 0)),
+            ],
+            out_specs=pl.BlockSpec((rows, 4 * width), lambda h, c, one: (takes * c + h, 0)),
+        ),
+        cost_estimate=cost_of(0, 4 * takes * pieces[0].size),
+        name="merge_out",
+    )(pair, *pieces, low.reshape(16, takes * cols, rows).transpose(1, 0, 2), up)
+
+
+def project_kernel(*refs, right_dim):
+    *lefts, matrix, out = refs
+    left = jnp.concatenate([ref[...] for ref in lefts], axis=1)
+    out[...] = dot_of(left, matrix[...], 1, right_dim).astype(out.dtype)
+
+
+def project(lefts, matrix, right_dim, out_type):
+    rows, depth = lefts[0].shape[0], matrix.shape[right_dim]
+    wide = matrix.shape[1 - right_dim]
+    tile, cut = row_tile(rows), min(512, wide)
+    shape = (depth, cut) if right_dim == 0 else (cut, depth)
+    place = (lambda n, m: (0, n)) if right_dim == 0 else (lambda n, m: (n, 0))
+    return pl.pallas_call(
+        functools.partial(project_kernel, right_dim=right_dim),
+        out_shape=jax.ShapeDtypeStruct((rows, wide), out_type),
+        grid=(wide // cut, rows // tile),
+        in_specs=[pl.BlockSpec((tile, left.shape[1]), lambda n, m: (m, 0)) for left in lefts]
+        + [pl.BlockSpec(shape, place)],
+        out_specs=pl.BlockSpec((tile, cut), lambda n, m: (m, n)),
+        cost_estimate=cost_of(2 * rows * depth * wide, 2 * (rows * depth + depth * wide)),
+        name="project",
+    )(*lefts, matrix)
+
+
+BLOCK = 256
+RING = 5
+
+
+def peer(step):
+    return {"row": lax.axis_index("row") ^ step}
+
+
+def send(source, target, sems, index, step):
+    return pltpu.make_async_remote_copy(
+        src_ref=source,
+        dst_ref=target,
+        send_sem=sems.at[0, index],
+        recv_sem=sems.at[1, index],
+        device_id=peer(step),
+        device_id_type=pl.DeviceIdType.MESH,
+    )
+
+
+def greet():
+    barrier = pltpu.get_barrier_semaphore()
+    for step in (1, 2, 3):
+        pl.semaphore_signal(
+            barrier, inc=1, device_id=peer(step), device_id_type=pl.DeviceIdType.MESH
+        )
+    pl.semaphore_wait(barrier, 3)
+
+
+def exchange_scratch(count, width, gathers):
+    sem = pltpu.SemaphoreType.DMA((2, count))
+    shapes = [
+        pltpu.VMEM((2, 2, BLOCK, width), BF),
+        pltpu.VMEM((count, 2, BLOCK, width), BF),
+        pltpu.VMEM((2, BLOCK, width), F32),
+        pltpu.VMEM((2, BLOCK, width), BF),
+        pltpu.VMEM((count, BLOCK, width), BF),
+        pltpu.VMEM((RING, BLOCK, width), F32),
+        sem,
+        sem,
+    ]
+    if gathers:
+        shapes += [
+            pltpu.VMEM((count, 8, BLOCK), F32),
+            pltpu.VMEM((3, count, 8, BLOCK), F32),
+        ] + [sem] * 6
+    return shapes
+
+
+def run_blocks(count, bufs, compute, stats, finish, own_ref=None, arrived=None):
+    pair_out, pair_in, far, side_out, side_in, near, pair_sem, side_sem, *rest = bufs
+    gathers = own_ref is not None
+    if gathers:
+        stat_own, stat_in, stat_1, stat_2, stat_3, core_sem, far_sem, relay_sem = rest
+        stat_sems = (stat_1, stat_2, stat_3)
+
+    def rows_of(c):
+        return pl.ds(pl.multiple_of(c * BLOCK, BLOCK), BLOCK)
+
+    def to_core(c):
+        return send(pair_out.at[lax.rem(c, 2)], pair_in.at[c], pair_sem, c, 1)
+
+    def to_side(c):
+        return send(side_out.at[lax.rem(c, 2)], side_in.at[c], side_sem, c, 2)
+
+    def to_stat(c, step):
+        return send(stat_own.at[c], stat_in.at[step - 1, c], stat_sems[step - 1], c, step)
+
+    def gather_core(c):
+        return send(own_ref.at[rows_of(c)], arrived[0].at[rows_of(c)], core_sem, c, 1)
+
+    def gather_side(c):
+        return send(own_ref.at[rows_of(c)], arrived[1].at[rows_of(c)], far_sem, c, 2)
+
+    def relay(c):
+        return send(arrived[1].at[rows_of(c)], arrived[2].at[rows_of(c)], relay_sem, c, 1)
+
+    def stage(c, body):
+        pl.when(jnp.logical_and(c >= 0, c < count))(functools.partial(body, c))
+
+    def multiply(c):
+        @pl.when(c >= 2)
+        def _():
+            to_core(c - 2).wait_send()
+
+        slot = lax.rem(c, 2)
+
+        def put(block, value):
+            if block == 0:
+                near[lax.rem(c, RING)] = value
+            elif block == 2:
+                far[slot] = value
+            else:
+                pair_out[slot, block // 2] = value.astype(BF)
+            if block == 3:
+                to_core(c).start()
+
+        compute(c, put)
+
+    def sum_core(c):
+        @pl.when(c >= 2)
+        def _():
+            to_side(c - 2).wait_send()
+
+        to_core(c).wait_recv()
+        slot = lax.rem(c, 2)
+        side_out[slot] = (far[slot] + pair_in[c, 1].astype(F32)).astype(BF)
+        to_side(c).start()
+        at = lax.rem(c, RING)
+        near[at] = near[at] + pair_in[c, 0].astype(F32)
+
+    def sum_side(c):
+        to_side(c).wait_recv()
+        at = lax.rem(c, RING)
+        total = near[at] + side_in[c].astype(F32)
+        if not gathers:
+            finish(c, rows_of(c), total)
+            return
+        near[at] = total
+        stat_own[c] = stats(c, rows_of(c), total)
+        for step in (1, 2, 3):
+            to_stat(c, step).start()
+
+    def normalise(c):
+        total = stat_own[c]
+        for step in (1, 2, 3):
+            to_stat(c, step).wait_recv()
+            total = total + stat_in[step - 1, c]
+        own_ref[rows_of(c), :] = finish(c, rows_of(c), near[lax.rem(c, RING)], total)
+        gather_side(c).start()
+        gather_core(c).start()
+
+    def pass_on(c):
+        gather_side(c).wait_recv()
+        relay(c).start()
+
+    def body(t, carry):
+        stage(t - 1, sum_core)
+        stage(t, multiply)
+        stage(t - 2, sum_side)
+        if gathers:
+            stage(t - 3, normalise)
+            stage(t - 4, pass_on)
+        return carry
+
+    lax.fori_loop(0, count + (4 if gathers else 2), body, 0)
+
+    def close(c, carry):
+        if gathers:
+            for step in (1, 2, 3):
+                to_stat(c, step).wait_send()
+            gather_core(c).wait()
+            gather_side(c).wait_send()
+            relay(c).wait()
+        return carry
+
+    if gathers:
+        lax.fori_loop(0, count, close, 0)
+    for c in range(max(count - 2, 0), count):
+        to_core(c).wait_send()
+        to_side(c).wait_send()
+
+
+def sums_of(*values):
+    out = None
+    for index, value in enumerate(values):
+        pick = lax.broadcasted_iota(jnp.int32, (8, value.shape[1]), 0) == index
+        term = lax.dot_general(
+            pick.astype(F32),
+            value,
+            (((1,), (1,)), ((), ())),
+            precision=lax.Precision.HIGHEST,
+            preferred_element_type=F32,
+        )
+        out = term if out is None else out + term
+    return out
+
+
+def column_of(stats, index):
+    pick = lax.broadcasted_iota(jnp.int32, (8, HEAD), 0) == index
+    wide = lax.dot_general(
+        stats,
+        pick.astype(F32),
+        (((0,), (0,)), ((), ())),
+        precision=lax.Precision.HIGHEST,
+        preferred_element_type=F32,
+    )
+    return wide[:, :1]
+
+
+def branch_kernel(
+    mixed_ref, matrix_ref, tokens_ref, gain_ref, branch_ref, hidden_ref, stat_ref, own_ref, *rest
+):
+    arrived, bufs = rest[:3], rest[3:]
+    width = own_ref.shape[1]
+    count = own_ref.shape[0] // BLOCK
+    greet()
+
+    def compute(c, put):
+        left = mixed_ref[pl.ds(pl.multiple_of(c * BLOCK, BLOCK), BLOCK), :]
+        for block in (1, 3, 2, 0):
+            put(block, dot_of(left, matrix_ref[:, block * width : (block + 1) * width], 1, 0))
+
+    def stats(c, rows, branch):
+        branch_ref[rows, :] = branch
+        return sums_of(branch * branch)
+
+    def finish(c, rows, branch, total):
+        stat_ref[c] = total
+        scale = lax.rsqrt(column_of(total, 0) / D + EPS)
+        hidden = tokens_ref[rows, :].astype(F32) + gain_ref[0:1, :] * branch * scale
+        hidden_ref[rows, :] = hidden
+        return hidden.astype(BF)
+
+    run_blocks(count, bufs, compute, stats, finish, own_ref, arrived)
+
+
+VMEM_SPEC = pl.BlockSpec(memory_space=pltpu.VMEM)
+ANY_SPEC = pl.BlockSpec(memory_space=pl.ANY)
+
+
+def talk_params(number):
+    return pltpu.CompilerParams(
+        collective_id=number, has_side_effects=True, vmem_limit_bytes=63 * 2**20
+    )
+
+
+def branch_call(mixed, matrix, tokens, gain):
+    rows, width = tokens.shape
+    count = rows // BLOCK
+    part = jax.ShapeDtypeStruct((rows, width), BF)
+    whole = jax.ShapeDtypeStruct((rows, width), F32)
+    return pl.pallas_call(
+        branch_kernel,
+        out_shape=[whole, whole, jax.ShapeDtypeStruct((count, 8, BLOCK), F32)] + [part] * 4,
+        in_specs=[VMEM_SPEC] * 4,
+        out_specs=[VMEM_SPEC] * 4 + [ANY_SPEC] * 3,
+        scratch_shapes=exchange_scratch(count, width, True),
+        compiler_params=talk_params(0),
+        cost_estimate=cost_of(8 * rows * width * matrix.shape[0], 2**27),
+        name="branch",
+    )(mixed, matrix, tokens, gain)
+
+
+def load_lefts(lefts, buffer, sems, count):
+    width = buffer.shape[2] // 4
+
+    def copies(c):
+        slot = lax.rem(c, 2)
+        rows = pl.ds(pl.multiple_of(c * BLOCK, BLOCK), BLOCK)
+        return [
+            pltpu.make_async_copy(
+                left.at[rows], buffer.at[slot, :, index * width : (index + 1) * width], sems.at[slot, index]
+            )
+            for index, left in enumerate(lefts)
+        ]
+
+    def start(c):
+        @pl.when(c < count)
+        def _():
+            for copy in copies(c):
+                copy.start()
+
+    def wait(c):
+        for copy in copies(c):
+            copy.wait()
+
+    return start, wait
+
+
+def move_rows(outer, buffer, sems, index, inward):
+    def copy(c):
+        slot = lax.rem(c, 2)
+        rows = pl.ds(pl.multiple_of(c * BLOCK, BLOCK), BLOCK)
+        ends = (outer.at[rows], buffer.at[slot])
+        if not inward:
+            ends = ends[::-1]
+        return pltpu.make_async_copy(*ends, sems.at[index, slot])
+
+    return copy
+
+
+def forward_kernel(x0, x1, x2, x3, gate_hbm, upper_hbm, reduce_hbm, hidden_ref, cot_ref, gain_ref, *rest):
+    act_out, gate_out, upper_out, layer_ref, own_ref, *rest = rest
+    arrived, rest = rest[:3], rest[3:]
+    gate_w, upper_w, reduce_w, lefts, act_buf, gate_buf, upper_buf, w_sem, x_sem, o_sem, *bufs = rest
+    width = own_ref.shape[1]
+    count = own_ref.shape[0] // BLOCK
+    ff = gate_w.shape[1]
+    tile = 512
+    loads = [
+        pltpu.make_async_copy(source, target, w_sem.at[index])
+        for index, (source, target) in enumerate(
+            ((gate_hbm, gate_w), (upper_hbm, upper_w), (reduce_hbm, reduce_w))
+        )
+    ]
+    start_left, wait_left = load_lefts((x0, x1, x2, x3), lefts, x_sem, count)
+    start_left(0)
+    for load in loads:
+        load.start()
+    greet()
+    outs = [
+        move_rows(outer, buffer, o_sem, index, False)
+        for index, (outer, buffer) in enumerate(
+            ((act_out, act_buf), (gate_out, gate_buf), (upper_out, upper_buf))
+        )
+    ]
+
+    def compute(c, put):
+        slot = lax.rem(c, 2)
+        wait_left(c)
+        start_left(c + 1)
+
+        @pl.when(c == 0)
+        def _():
+            for load in loads:
+                load.wait()
+
+        @pl.when(c >= 2)
+        def _():
+            for out in outs:
+                out(c - 2).wait()
+
+        def tiles(n, carry):
+            at = pl.ds(pl.multiple_of(n * tile, tile), tile)
+            left = lefts[slot]
+            gate = dot_of(left, gate_w[:, at], 1, 0)
+            upper = dot_of(left, upper_w[:, at], 1, 0)
+            act_buf[slot, :, at] = (gate * jax.nn.sigmoid(gate) * upper).astype(BF)
+            gate_buf[slot, :, at] = gate.astype(BF)
+            upper_buf[slot, :, at] = upper.astype(BF)
+            return carry
+
+        lax.fori_loop(0, ff // tile, tiles, 0)
+        for out in outs:
+            out(c).start()
+        for block in (1, 3, 2, 0):
+            span = slice(block * width, (block + 1) * width)
+            put(block, dot_of(act_buf[slot], reduce_w[:, span], 1, 0))
+
+    def stats(c, rows, result):
+        weighted = gain_ref[1:2, :] * cot_ref[rows, :].astype(F32)
+        return sums_of(result * result, weighted * result)
+
+    def finish(c, rows, result, total):
+        scale = lax.rsqrt(column_of(total, 0) / D + EPS)
+        gain = gain_ref[1:2, :]
+        layer_ref[rows, :] = (hidden_ref[rows, :] + gain * result * scale).astype(BF)
+        weighted = gain * cot_ref[rows, :].astype(F32)
+        inner = column_of(total, 1)
+        return (scale * weighted - result * (scale * scale * scale * inner / D)).astype(BF)
+
+    run_blocks(count, bufs, compute, stats, finish, own_ref, arrived)
+    for c in range(max(count - 2, 0), count):
+        for out in outs:
+            out(c).wait()
+
+
+def forward_call(lefts, gate_w, upper_w, reduce_w, hidden, cotangent, gain):
+    rows, width = hidden.shape
+    count = rows // BLOCK
+    ff = gate_w.shape[1]
+    part = jax.ShapeDtypeStruct((rows, width), BF)
+    wide = jax.ShapeDtypeStruct((rows, ff), BF)
+    return pl.pallas_call(
+        forward_kernel,
+        out_shape=[wide] * 3 + [part] * 5,
+        in_specs=[ANY_SPEC] * 7 + [VMEM_SPEC] * 3,
+        out_specs=[ANY_SPEC] * 3 + [VMEM_SPEC] * 2 + [ANY_SPEC] * 3,
+        scratch_shapes=[
+            pltpu.VMEM(gate_w.shape, BF),
+            pltpu.VMEM(upper_w.shape, BF),
+            pltpu.VMEM(reduce_w.shape, BF),
+            pltpu.VMEM((2, BLOCK, 4 * width), BF),
+            pltpu.VMEM((2, BLOCK, ff), BF),
+            pltpu.VMEM((2, BLOCK, ff), BF),
+            pltpu.VMEM((2, BLOCK, ff), BF),
+            pltpu.SemaphoreType.DMA((3,)),
+            pltpu.SemaphoreType.DMA((2, 4)),
+            pltpu.SemaphoreType.DMA((3, 2)),
+        ]
+        + exchange_scratch(count, width, True),
+        compiler_params=talk_params(1),
+        cost_estimate=cost_of(24 * rows * width * ff, 2**27),
+        name="forward",
+    )(*lefts, gate_w, upper_w, reduce_w, hidden, cotangent, gain)
+
+
+def backward_kernel(
+    x0, x1, x2, x3, gate_hbm, upper_hbm, reduce_hbm, gate_in, upper_in, cot_ref, branch_ref, stat_ref, gain_ref, *rest
+):
+    d_gate_out, d_upper_out, d_hidden_ref, own_ref, *rest = rest
+    arrived, rest = rest[:3], rest[3:]
+    gate_w, upper_w, reduce_w, lefts, gate_buf, upper_buf, d_gate_buf, d_upper_buf, *rest = rest
+    w_sem, x_sem, i_sem, o_sem, *bufs = rest
+    width = own_ref.shape[1]
+    count = own_ref.shape[0] // BLOCK
+    ff = gate_w.shape[1]
+    tile = 512
+    loads = [
+        pltpu.make_async_copy(source, target, w_sem.at[index])
+        for index, (source, target) in enumerate(
+            ((reduce_hbm, reduce_w), (gate_hbm, gate_w), (upper_hbm, upper_w))
+        )
+    ]
+    start_left, wait_left = load_lefts((x0, x1, x2, x3), lefts, x_sem, count)
+    ins = [
+        move_rows(outer, buffer, i_sem, index, True)
+        for index, (outer, buffer) in enumerate(((gate_in, gate_buf), (upper_in, upper_buf)))
+    ]
+    outs = [
+        move_rows(outer, buffer, o_sem, index, False)
+        for index, (outer, buffer) in enumerate(
+            ((d_gate_out, d_gate_buf), (d_upper_out, d_upper_buf))
+        )
+    ]
+    start_left(0)
+    for one in ins:
+        one(0).start()
+    for load in loads:
+        load.start()
+    greet()
+
+    def compute(c, put):
+        slot = lax.rem(c, 2)
+        wait_left(c)
+        start_left(c + 1)
+        for one in ins:
+            one(c).wait()
+
+        @pl.when(c + 1 < count)
+        def _():
+            for one in ins:
+                one(c + 1).start()
+
+        @pl.when(c == 0)
+        def _():
+            for load in loads:
+                load.wait()
+
+        @pl.when(c >= 2)
+        def _():
+            for out in outs:
+                out(c - 2).wait()
+
+        def tiles(n, carry):
+            at = pl.ds(pl.multiple_of(n * tile, tile), tile)
+            d_act = dot_of(lefts[slot], reduce_w[at, :], 1, 1)
+            gate = gate_buf[slot, :, at].astype(F32)
+            sigma = jax.nn.sigmoid(gate)
+            d_gate = d_act * upper_buf[slot, :, at].astype(F32) * (sigma * (1 + gate * (1 - sigma)))
+            d_gate_buf[slot, :, at] = d_gate.astype(BF)
+            d_upper_buf[slot, :, at] = (d_act * (gate * sigma)).astype(BF)
+            return carry
+
+        lax.fori_loop(0, ff // tile, tiles, 0)
+        for out in outs:
+            out(c).start()
+        for block in (1, 3, 2, 0):
+            span = slice(block * width, (block + 1) * width)
+            put(
+                block,
+                dot_of(d_gate_buf[slot], gate_w[span, :], 1, 1)
+                + dot_of(d_upper_buf[slot], upper_w[span, :], 1, 1),
+            )
+
+    def stats(c, rows, total):
+        d_hidden = cot_ref[rows, :].astype(F32) + total
+        d_hidden_ref[rows, :] = d_hidden
+        return sums_of(gain_ref[0:1, :] * d_hidden * branch_ref[rows, :])
+
+    def finish(c, rows, total, sums):
+        scale = lax.rsqrt(column_of(stat_ref[c], 0) / D + EPS)
+        weighted = gain_ref[0:1, :] * d_hidden_ref[rows, :]
+        inner = column_of(sums, 0)
+        back = scale * scale * scale * inner / D
+        return (scale * weighted - branch_ref[rows, :] * back).astype(BF)
+
+    run_blocks(count, bufs, compute, stats, finish, own_ref, arrived)
+    for c in range(max(count - 2, 0), count):
+        for out in outs:
+            out(c).wait()
+
+
+def backward_call(lefts, gate_w, upper_w, reduce_w, gate, upper, cotangent, branch, stats, gain):
+    rows, width = branch.shape
+    count = rows // BLOCK
+    ff = gate_w.shape[1]
+    part = jax.ShapeDtypeStruct((rows, width), BF)
+    wide = jax.ShapeDtypeStruct((rows, ff), BF)
+    return pl.pallas_call(
+        backward_kernel,
+        out_shape=[wide] * 2 + [jax.ShapeDtypeStruct((rows, width), F32)] + [part] * 4,
+        in_specs=[ANY_SPEC] * 9 + [VMEM_SPEC] * 4,
+        out_specs=[ANY_SPEC] * 2 + [VMEM_SPEC] * 2 + [ANY_SPEC] * 3,
+        scratch_shapes=[
+            pltpu.VMEM(gate_w.shape, BF),
+            pltpu.VMEM(upper_w.shape, BF),
+            pltpu.VMEM(reduce_w.shape, BF),
+            pltpu.VMEM((2, BLOCK, 4 * width), BF),
+            pltpu.VMEM((2, BLOCK, ff), BF),
+            pltpu.VMEM((2, BLOCK, ff), BF),
+            pltpu.VMEM((2, BLOCK, ff), BF),
+            pltpu.VMEM((2, BLOCK, ff), BF),
+            pltpu.SemaphoreType.DMA((3,)),
+            pltpu.SemaphoreType.DMA((2, 4)),
+            pltpu.SemaphoreType.DMA((2, 2)),
+            pltpu.SemaphoreType.DMA((2, 2)),
+        ]
+        + exchange_scratch(count, width, True),
+        compiler_params=talk_params(2),
+        cost_estimate=cost_of(24 * rows * width * ff, 2**27),
+        name="backward",
+    )(*lefts, gate_w, upper_w, reduce_w, gate, upper, cotangent, branch, stats, gain)
+
+
+def input_kernel(d_qkv_ref, matrix_ref, d_hidden_ref, out_ref, *bufs):
+    width = out_ref.shape[1]
+    count = out_ref.shape[0] // BLOCK
+    greet()
+
+    def compute(c, put):
+        left = d_qkv_ref[pl.ds(pl.multiple_of(c * BLOCK, BLOCK), BLOCK), :]
+        for block in (1, 3, 2, 0):
+            put(block, dot_of(left, matrix_ref[block * width : (block + 1) * width, :], 1, 1))
+
+    def finish(c, rows, total):
+        out_ref[rows, :] = d_hidden_ref[rows, :] + total
+
+    run_blocks(count, bufs, compute, None, finish)
+
+
+def input_call(d_qkv, matrix, d_hidden):
+    rows, width = d_hidden.shape
+    return pl.pallas_call(
+        input_kernel,
+        out_shape=jax.ShapeDtypeStruct((rows, width), F32),
+        in_specs=[VMEM_SPEC] * 3,
+        out_specs=VMEM_SPEC,
+        scratch_shapes=exchange_scratch(rows // BLOCK, width, False),
+        compiler_params=talk_params(3),
+        cost_estimate=cost_of(8 * rows * width * d_qkv.shape[1], 2**26),
+        name="input_grad",
+    )(d_qkv, matrix, d_hidden)
+
+
 def across(values, step):
     return lax.ppermute(values, "row", [(i, i ^ step) for i in range(4)])
 
@@ -661,18 +1463,12 @@
     return values + across(values, 2)
 
 
-def scatter_row(parts):
-    near = parts[0].astype(F32) + across(parts[1], 1).astype(F32)
-    far = parts[2].astype(F32) + across(parts[3], 1).astype(F32)
-    return near + across(far.astype(BF), 2).astype(F32)
-
-
-def deal_row(pieces, me):
+def deal_row(piece_for, me):
     out = []
     for step in range(4):
-        piece = lax.dynamic_index_in_dim(pieces, me ^ step, 0, keepdims=False)
+        piece = piece_for(me ^ step)
         out.append(piece if step == 0 else across(piece, step))
-    return out
+    return jnp.stack(out)
 
 
 def gather_col(values):
@@ -681,6 +1477,19 @@
 
 def swap_pair(values):
     return lax.ppermute(values, "dp", [(0, 1), (1, 0)])
+
+
+def round_col(values, cols):
+    shift = lambda k: [(i, (i + k) % cols) for i in range(cols)]
+    return [values] + [lax.ppermute(values, "col", shift(k)) for k in range(1, cols)]
+
+
+def after(values, earlier):
+    return lax.optimization_barrier((values, earlier))[0]
+
+
+def join(parts, axis=0):
+    return parts[0] if len(parts) == 1 else jnp.concatenate(parts, axis=axis)
 
 
 def group_shards(
@@ -714,106 +1523,111 @@
     ff_half = ff_sub // 2
     local = cols * sub
     ff_local = cols * ff_sub
-    out_half = width // 2
     sequence = pair * cols + col
     mine = lax.dynamic_index_in_dim(adapter_set, sequence, 0, keepdims=False)
     prefix = lax.dynamic_slice_in_dim(prefix_length, sequence, 1)
     cols_sets = lax.dynamic_slice_in_dim(adapter_set, pair * cols, cols)
 
-    def own_set(array, axis):
-        return lax.dynamic_index_in_dim(array, mine, axis, keepdims=False)
-
-    row_pack = jnp.concatenate(
-        [
-            own_set(qkv_lowrank, 1).transpose(0, 2, 1).reshape(3 * ADAPTER_RANK, width),
-            own_set(attn_uprank, 0),
-            own_set(expand_lowrank, 1).transpose(0, 2, 1).reshape(2 * ADAPTER_RANK, width),
-            own_set(reduce_uprank, 0),
-        ],
-        axis=0,
-    )
+    row_pack = row_pack_of(mine.reshape(1), qkv_lowrank, attn_uprank, expand_lowrank, reduce_uprank)
     row_all = jnp.concatenate(gather_row(row_pack), axis=1)
     qkv_low = row_all[:48]
     attn_up = row_all[48:64]
     expand_low = row_all[64:96]
     reduce_up = row_all[96:112]
-
-    def col_pack_of(which):
-        one = lambda array, axis: lax.dynamic_index_in_dim(array, which, axis, keepdims=False)
-        cut = lambda array, axis, size: lax.dynamic_slice_in_dim(array, me * size, size, axis)
-        up_qkv = cut(one(qkv_uprank, 1), 2, sub)
-        up_exp = cut(one(expand_uprank, 1), 2, ff_sub)
-        return jnp.concatenate(
+    col_pack = col_pack_of(
+        jnp.concatenate([cols_sets, me.reshape(1)]),
+        qkv_uprank,
+        attn_lowrank,
+        expand_uprank,
+        reduce_lowrank,
+    )
+    col_all = lax.all_to_all(col_pack, "col", split_axis=0, concat_axis=0, tiled=True)
+
+    def own_columns(at, size):
+        return col_all[:, :, at : at + size].transpose(1, 0, 2).reshape(16, cols * size)
+
+    qkv_up = [own_columns(i * sub, sub) for i in range(3)]
+    attn_low = own_columns(3 * sub, sub)
+    expand_up = [own_columns(4 * sub + i * ff_sub, ff_sub) for i in range(2)]
+    reduce_low = own_columns(4 * sub + 2 * ff_sub, ff_sub)
+    gains = lax.dynamic_slice_in_dim(headnorm_gain, me * sub, sub, 1)
+    gains = jnp.stack(round_col(gains, cols))
+    gains = jnp.concatenate(
+        [
+            lax.dynamic_index_in_dim(gains, lax.rem(col - i + cols, cols), 0, keepdims=False)
+            for i in range(cols)
+        ],
+        axis=1,
+    )
+
+    place = jnp.stack([pair, col])
+    in_half = width // 2
+    head_half = sub // 2
+
+    def exchanged(own, other_piece):
+        sent = jnp.stack(
             [
-                up_qkv[0],
-                up_qkv[1],
-                up_qkv[2],
-                cut(one(attn_lowrank, 0), 0, sub).T,
-                up_exp[0],
-                up_exp[1],
-                cut(one(reduce_lowrank, 0), 0, ff_sub).T,
-            ],
-            axis=1,
-        )
-
-    col_pack = jnp.stack([col_pack_of(cols_sets[i]) for i in range(cols)])
-    col_all = lax.all_to_all(col_pack, "col", split_axis=0, concat_axis=0, tiled=True)
-    heads_of = lambda at: col_all[:, :, at : at + sub].transpose(1, 0, 2).reshape(16, local)
-
-    def swap_halves(array):
-        return jnp.where(pair == 0, array, array[:, ::-1])
-
-    def ff_of(at):
-        part = col_all[:, :, at : at + ff_sub].reshape(cols, 16, 2, ff_half)
-        part = part.transpose(1, 2, 0, 3)
-        return swap_halves(part).reshape(16, ff_local)
-
-    qkv_up = [heads_of(i * sub) for i in range(3)]
-    attn_low = heads_of(3 * sub)
-    expand_up = [ff_of(4 * sub), ff_of(4 * sub + ff_sub)]
-    reduce_low = ff_of(4 * sub + 2 * ff_sub)
-    gains = lax.dynamic_slice_in_dim(headnorm_gain, me * sub, sub, 1)
-    gains = gather_col(gains).transpose(1, 0, 2).reshape(2, local)
-
-    def merged(base, low, up):
-        return (base.astype(F32) + ADAPTER_FACTOR * dot_of(low, up, 0, 0)).astype(BF)
-
-    pieces = qkv_weight.reshape(3, width, 4, sub).transpose(2, 0, 1, 3)
-    qkv_all = gather_col(jnp.stack(deal_row(pieces, me)))
-    qkv_all = qkv_all.transpose(2, 1, 3, 0, 4).reshape(3, 4 * width, local)
-    qkv_w = jnp.concatenate(
-        [merged(qkv_all[i], qkv_low[16 * i : 16 * i + 16], qkv_up[i]) for i in range(3)], axis=1
-    )
-
-    pieces = attn_weight.reshape(4, sub, 2, out_half)
-    pieces = lax.dynamic_index_in_dim(pieces, pair, 2, keepdims=False)
-    own = gather_col(jnp.stack(deal_row(pieces, me)))
-    other = swap_pair(own)
-    both = jnp.where(pair == 0, jnp.stack([own, other]), jnp.stack([other, own]))
-    attn_all = both.transpose(1, 3, 2, 0, 4).reshape(local, 4 * width)
-    attn_w = merged(attn_all, attn_low, attn_up)
-
-    expand_w = []
-    for part in range(2):
-        pieces = expand_weight[part].reshape(width, 4, 2, ff_half)
-        pieces = lax.dynamic_index_in_dim(pieces, pair, 2, keepdims=False).transpose(1, 0, 2)
-        own = gather_col(jnp.stack(deal_row(pieces, me)))
-        both = jnp.stack([own, swap_pair(own)])
-        whole = both.transpose(2, 3, 0, 1, 4).reshape(4 * width, ff_local)
-        expand_w.append(merged(whole, expand_low[16 * part : 16 * part + 16], expand_up[part]))
-
-    pieces = reduce_weight.reshape(4, 2, ff_half, width)
-    pieces = lax.dynamic_index_in_dim(pieces, pair, 1, keepdims=False)
-    own = gather_col(jnp.stack(deal_row(pieces, me)))
-    both = jnp.stack([own, swap_pair(own)])
-    whole = both.transpose(0, 1, 3, 2, 4).reshape(ff_local, 4 * width)
-    reduce_w = merged(whole, reduce_low, reduce_up)
-
-    def in_parts(left, matrix):
-        return [
-            dot_of(left, matrix[:, i * width : (i + 1) * width], 1, 0, BF if i in (1, 3) else F32)
-            for i in range(4)
-        ]
+                lax.dynamic_index_in_dim(own, lax.rem(col + k, cols), 0, keepdims=False)
+                for k in range(1, cols)
+            ]
+        )
+        return jnp.concatenate([other_piece[None], swap_pair(sent)])
+
+    def qkv_piece(half):
+        return lambda row: lax.dynamic_slice(
+            qkv_weight, (0, half * in_half, row * sub), (3, in_half, sub)
+        )
+
+    def attn_piece(half, earlier):
+        return lambda row: after(
+            lax.dynamic_slice_in_dim(attn_weight, row * sub + half * head_half, head_half, 0),
+            earlier,
+        )
+
+    def expand_piece(part, half, earlier):
+        return lambda row: after(
+            lax.dynamic_slice(
+                expand_weight[part], (0, row * ff_sub + half * ff_half), (width, ff_half)
+            ),
+            earlier,
+        )
+
+    step = rows // CHUNKS
+    spans = [slice(i * step, (i + 1) * step) for i in range(CHUNKS)]
+    qkv_own = deal_row(qkv_piece(pair), me)
+    attn_own = deal_row(attn_piece(pair, qkv_own), me)
+    gate_own = deal_row(expand_piece(0, pair, attn_own), me)
+    qkv_rest = deal_row(lambda row: after(qkv_piece(1 - pair)(row), gate_own), me)
+    token_parts = []
+    for span in spans:
+        token_parts.append(gather_row(after(tokens[span], qkv_rest)))
+    last = token_parts[-1][3]
+    up_own = deal_row(expand_piece(1, pair, last), me)
+    attn_rest = deal_row(attn_piece(1 - pair, up_own), me)
+    gate_rest = deal_row(expand_piece(0, 1 - pair, attn_rest), me)
+    reduce_own = deal_row(
+        lambda row: after(
+            lax.dynamic_slice_in_dim(reduce_weight, row * ff_sub, ff_sub, 0), gate_rest
+        ),
+        me,
+    )
+    up_rest = deal_row(expand_piece(1, 1 - pair, reduce_own), me)
+    qkv_all = gather_col(qkv_own)
+    attn_all = gather_col(attn_own)
+    gate_all = gather_col(gate_own)
+    up_all = gather_col(up_own)
+    reduce_all = gather_col(reduce_own)
+    qkv_w = merge_qkv(
+        place, qkv_all, exchanged(qkv_all, qkv_rest), qkv_low, jnp.concatenate(qkv_up)
+    )
+    attn_w = merge_out(place, [attn_all, exchanged(attn_all, attn_rest)], attn_low, attn_up)
+    expand_w = [
+        merge_expand(
+            place, whole, exchanged(whole, rest), expand_low[16 * i : 16 * i + 16], expand_up[i]
+        )
+        for i, (whole, rest) in enumerate(((gate_all, gate_rest), (up_all, up_rest)))
+    ]
+    reduce_w = merge_out(place, [reduce_all], reduce_low, reduce_up)
 
     half = HEAD // 2
     freq = THETA ** (-2.0 * jnp.arange(half, dtype=F32) / HEAD)
@@ -821,183 +1635,139 @@
     cosine = jnp.concatenate([jnp.cos(angle)] * 2, axis=1)
     sine = jnp.sin(angle)
     sine = jnp.concatenate([-sine, sine], axis=1)
-    step = rows // CHUNKS
-    spans = [slice(i * step, (i + 1) * step) for i in range(CHUNKS)]
     raws, scales, turned, qkv_inner = [], [], [], []
-    for span in spans:
-        full = jnp.concatenate(gather_row(tokens[span]), axis=1)
-        qkv_inner.append(dot_of(qkv_low, full, 1, 1).astype(BF))
-        raw = dot_of(full, qkv_w, 1, 0)
+
+    def low_of_parts(low, parts):
+        return functools.reduce(
+            jnp.add,
+            [dot_of(low[:, i * width : (i + 1) * width], parts[i], 1, 1) for i in range(4)],
+        )
+
+    for span, parts in zip(spans, token_parts):
+        qkv_inner.append(low_of_parts(qkv_low, parts).astype(BF))
+        raw = project(parts, qkv_w, 0, F32)
         squares = jnp.stack(
             [jnp.sum(raw[:, i * local : (i + 1) * local] ** 2, axis=1) for i in range(2)]
         )
         scale = lax.rsqrt(sum_row(squares) / D + EPS).T
         raws.append(raw)
         scales.append(scale)
-        turned.append(rotate_rows(raw, scale, gains, cosine[span], sine[span]))
-    key = jnp.concatenate([part[1] for part in turned])
-    value = jnp.concatenate([part[2] for part in turned])
-
-    layer_parts, d_hiddens, mixeds, logs, d_mixeds = [], [], [], [], []
-    grads = []
-    for index, span in enumerate(spans):
-        query = turned[index][0]
-        mixed, log_total = attend(prefix, query, key, value, index * step)
-        mixeds.append(mixed)
-        logs.append(log_total)
-        attn_inner = sum_row(dot_of(attn_low, mixed, 0 + 1, 1)).astype(BF)
-        branch = scatter_row(in_parts(mixed, attn_w))
-        branch_scale = lax.rsqrt(sum_row(jnp.sum(branch * branch, axis=1)) / D + EPS)[:, None]
-        hidden = tokens[span].astype(F32) + post_gain[0] * branch * branch_scale
-        hidden_b = hidden.astype(BF)
-        full = jnp.concatenate(gather_row(hidden_b), axis=1)
-        expand_inner = dot_of(expand_low, full, 1, 1).astype(BF)
-        gate = dot_of(full, expand_w[0], 1, 0)
-        upper = dot_of(full, expand_w[1], 1, 0)
-        act = (jax.nn.silu(gate) * upper).astype(BF)
-        gate_b = gate.astype(BF)
-        upper_b = upper.astype(BF)
-        reduce_inner = sum_row(dot_of(reduce_low, act, 1, 1)).astype(BF)
-        result = scatter_row(in_parts(act, reduce_w))
-        incoming = cotangent[span].astype(F32)
-        weighted = post_gain[1] * incoming
-        sums = sum_row(
-            jnp.stack([jnp.sum(result * result, axis=1), jnp.sum(weighted * result, axis=1)])
-        )
-        result_scale = lax.rsqrt(sums[0] / D + EPS)[:, None]
-        layer_parts.append((hidden + post_gain[1] * result * result_scale).astype(BF))
-        d_result = (
-            result_scale * weighted - result * (result_scale**3 * sums[1][:, None] / D)
-        ).astype(BF)
-        full = jnp.concatenate(gather_row(d_result), axis=1)
-        g_reduce_up = ADAPTER_FACTOR * dot_of(reduce_inner, d_result, 1, 0)
-        d_inner = (ADAPTER_FACTOR * dot_of(reduce_up, full, 1, 1)).astype(BF)
-        g_reduce_low = dot_of(d_inner, act, 1, 0)
-        d_act = dot_of(full, reduce_w, 1, 1)
-        gate = gate_b.astype(F32)
-        upper = upper_b.astype(F32)
-        sigma = jax.nn.sigmoid(gate)
-        d_gate = (d_act * upper * sigma * (1 + gate * (1 - sigma))).astype(BF)
-        d_upper = (d_act * gate * sigma).astype(BF)
-        g_expand_up = [
-            ADAPTER_FACTOR * dot_of(expand_inner[:16], d_gate, 1, 0),
-            ADAPTER_FACTOR * dot_of(expand_inner[16:], d_upper, 1, 0),
-        ]
-        d_inner = sum_row(
-            ADAPTER_FACTOR
-            * jnp.concatenate(
-                [dot_of(expand_up[0], d_gate, 1, 1), dot_of(expand_up[1], d_upper, 1, 1)]
-            )
-        ).astype(BF)
-        g_expand_low = dot_of(d_inner, hidden_b, 1, 0)
-        parts = []
-        for i in range(4):
-            cut = slice(i * width, (i + 1) * width)
-            part = dot_of(d_gate, expand_w[0][cut], 1, 1) + dot_of(d_upper, expand_w[1][cut], 1, 1)
-            parts.append(part.astype(BF) if i in (1, 3) else part)
-        d_hidden = incoming + scatter_row(parts)
-        weighted = post_gain[0] * d_hidden
-        inner_sum = sum_row(jnp.sum(weighted * branch, axis=1))[:, None]
-        d_branch = (
-            branch_scale * weighted - branch * (branch_scale**3 * inner_sum / D)
-        ).astype(BF)
-        d_hiddens.append(d_hidden)
-        full = jnp.concatenate(gather_row(d_branch), axis=1)
-        g_attn_up = ADAPTER_FACTOR * dot_of(attn_inner, d_branch, 1, 0)
-        d_inner = (ADAPTER_FACTOR * dot_of(attn_up, full, 1, 1)).astype(BF)
-        g_attn_low = dot_of(d_inner, mixed, 1, 0)
-        d_mixeds.append(dot_of(full, attn_w, 1, 1, BF))
-        grads.append(
-            (g_attn_up, g_expand_low, g_reduce_up, g_attn_low, *g_expand_up, g_reduce_low)
-        )
-
-    d_query, d_key, d_value = attend_back(
-        prefix,
-        jnp.concatenate([part[0] for part in turned]),
-        jnp.concatenate(d_mixeds),
-        jnp.concatenate(mixeds),
-        jnp.concatenate(logs, axis=2),
-        key,
-        value,
-    )
-    grads = [functools.reduce(jnp.add, parts) for parts in zip(*grads)]
-    input_parts, g_low, g_up = [], [], []
+        turned.append(rotate_rows(after(raw, gate_all), scale, gains, cosine[span], sine[span]))
+    key = join([part[1] for part in turned])
+    value = join([part[2] for part in turned])
+
+    query = join([part[0] for part in turned])
+    mixed, log_total = attend(prefix, query, key, value, 0)
+    mixed = after(mixed, up_all)
+    branch, hidden, branch_stats, *hidden_parts = branch_call(mixed, attn_w, tokens, post_gain)
+    act, gate, upper, layer_out, *result_parts = forward_call(
+        hidden_parts, *expand_w, reduce_w, hidden, cotangent, post_gain
+    )
+    d_gate, d_upper, d_hidden, *branch_parts = backward_call(
+        result_parts, *expand_w, reduce_w, gate, upper, cotangent, branch, branch_stats, post_gain
+    )
+    d_mixed = project(branch_parts, attn_w, 1, BF)
+    d_query, d_key, d_value, q_sums, k_sums = attend_back(
+        prefix, query, d_mixed, mixed, log_total, key, value
+    )
+    attn_inner = sum_row(dot_of(attn_low, mixed, 1, 1)).astype(BF)
+    expand_inner = low_of_parts(expand_low, hidden_parts).astype(BF)
+    reduce_inner = sum_row(dot_of(reduce_low, act, 1, 1)).astype(BF)
+    g_reduce_up = ADAPTER_FACTOR * dot_of(reduce_inner, result_parts[0], 1, 0)
+    d_inner = (ADAPTER_FACTOR * low_of_parts(reduce_up, result_parts)).astype(BF)
+    g_reduce_low = dot_of(d_inner, act, 1, 0)
+    g_gate_up = ADAPTER_FACTOR * dot_of(expand_inner[:16], d_gate, 1, 0)
+    g_upper_up = ADAPTER_FACTOR * dot_of(expand_inner[16:], d_upper, 1, 0)
+    d_inner = sum_row(
+        ADAPTER_FACTOR
+        * jnp.concatenate(
+            [dot_of(expand_up[0], d_gate, 1, 1), dot_of(expand_up[1], d_upper, 1, 1)]
+        )
+    ).astype(BF)
+    g_expand_low = dot_of(d_inner, hidden_parts[0], 1, 0)
+    g_attn_up = ADAPTER_FACTOR * dot_of(attn_inner, branch_parts[0], 1, 0)
+    d_inner = (ADAPTER_FACTOR * low_of_parts(attn_up, branch_parts)).astype(BF)
+    g_attn_low = dot_of(d_inner, mixed, 1, 0)
+
+    all_sums = sum_row(jnp.stack([jnp.sum(part[:, 0], axis=0) for part in (q_sums, k_sums)]))
+    d_parts, g_low, g_up = [], [], []
     for index, span in enumerate(spans):
         scale = scales[index]
-        inner = sum_row(
-            jnp.stack(
-                [
-                    jnp.sum(d_query[span] * turned[index][0].astype(F32), axis=1),
-                    jnp.sum(d_key[span] * turned[index][1].astype(F32), axis=1),
-                ]
-            )
-        ).T
         d_qkv = unrotate_rows(
             raws[index],
-            d_query[span],
-            d_key[span],
-            d_value[span],
+            d_query,
+            d_key,
+            d_value,
             scale,
-            scale * scale * inner / D,
+            scale * scale * all_sums[:, span].T / D,
             gains,
             cosine[span],
             sine[span],
-        )
-        part = [d_qkv[:, i * local : (i + 1) * local] for i in range(3)]
-        g_up.append(
-            [
-                ADAPTER_FACTOR * dot_of(qkv_inner[index][16 * i : 16 * i + 16], part[i], 1, 0)
-                for i in range(3)
-            ]
-        )
-        d_inner = sum_row(
-            ADAPTER_FACTOR
-            * jnp.concatenate([dot_of(qkv_up[i], part[i], 1, 1) for i in range(3)])
-        ).astype(BF)
-        g_low.append(dot_of(d_inner, tokens[span], 1, 0))
-        parts = [
-            dot_of(d_qkv, qkv_w[i * width : (i + 1) * width], 1, 1, BF if i in (1, 3) else F32)
-            for i in range(4)
-        ]
-        input_parts.append(d_hiddens[index] + scatter_row(parts))
-    g_qkv_low = functools.reduce(jnp.add, g_low)
-    g_qkv_up = [functools.reduce(jnp.add, parts) for parts in zip(*g_up)]
-    g_attn_up, g_expand_low, g_reduce_up, g_attn_low, g_gate_up, g_upper_up, g_reduce_low = grads
-
-    member = (adapter_set[None, :] == jnp.arange(SETS, dtype=jnp.int32)[:, None]).astype(F32)
-
-    def to_sets(by_sequence):
-        return jnp.einsum(
-            "ks,sab->kab", member, by_sequence.astype(F32), precision=lax.Precision.HIGHEST
+            index * step,
+        )
+        d_parts.append(d_qkv)
+    d_qkv = join(d_parts)
+    input_grad = input_call(d_qkv, qkv_w, d_hidden)
+    part = [d_qkv[:, i * local : (i + 1) * local] for i in range(3)]
+    qkv_inner = join(qkv_inner, 1)
+    g_qkv_up = [
+        ADAPTER_FACTOR * dot_of(qkv_inner[16 * i : 16 * i + 16], part[i], 1, 0) for i in range(3)
+    ]
+    d_inner = sum_row(
+        ADAPTER_FACTOR * jnp.concatenate([dot_of(qkv_up[i], part[i], 1, 1) for i in range(3)])
+    ).astype(BF)
+    g_qkv_low = dot_of(d_inner, tokens, 1, 0)
+
+    def set_of(other, back):
+        sequence = (pair ^ other) * cols + lax.rem(col - back + cols, cols)
+        which = lax.dynamic_index_in_dim(adapter_set, sequence, 0, keepdims=False)
+        return (jnp.arange(SETS, dtype=jnp.int32) == which).astype(F32)
+
+    def to_sets(terms):
+        shape = (SETS,) + (1,) * terms[0][1].ndim
+        return functools.reduce(
+            jnp.add, [hot.reshape(shape) * term.astype(F32)[None] for hot, term in terms]
         )
 
     def sum_groups(pack):
-        return to_sets(lax.all_gather(pack.astype(BF), ("dp", "col"), axis=0, tiled=False))
+        pack = pack.astype(BF)
+        both = jnp.stack([pack, swap_pair(pack)])
+        terms = []
+        for back, arrived in enumerate(round_col(both, cols)):
+            terms += [(set_of(other, back), arrived[other]) for other in range(2)]
+        return to_sets(terms)
 
     early = sum_groups(jnp.concatenate([g_attn_up, g_expand_low, g_reduce_up], axis=0))
     late = sum_groups(g_qkv_low)
 
-    def heads_back(grad):
-        return grad.reshape(16, cols, sub).transpose(1, 0, 2)
-
-    def ff_back(grad):
-        part = swap_halves(grad.reshape(16, 2, cols, ff_half))
-        return part.transpose(2, 0, 1, 3).reshape(cols, 16, ff_sub)
+    def by_col(grad):
+        return grad.reshape(16, cols, -1).transpose(1, 0, 2)
 
     def sum_tokens(pack):
         dealt = lax.all_to_all(pack.astype(BF), "col", split_axis=0, concat_axis=0, tiled=True)
-        every = lax.all_gather(dealt, "row", axis=0, tiled=False)
-        every = lax.all_gather(every, "dp", axis=0, tiled=False)
-        every = every.transpose(0, 2, 3, 1, 4)
-        return to_sets(every.reshape(2 * cols, 16, -1)).reshape(SETS, 16, 4, -1)
+        every = jnp.stack(gather_row(dealt))
+        other = swap_pair(every)
+        terms = []
+        for which in range(2):
+            for index in range(cols):
+                sequence = (pair ^ which) * cols + index
+                chosen = lax.dynamic_index_in_dim(adapter_set, sequence, 0, keepdims=False)
+                hot = (jnp.arange(SETS, dtype=jnp.int32) == chosen).astype(F32)
+                terms.append((hot, (every, other)[which][:, index]))
+        total = to_sets(terms)
+        total = jnp.stack(
+            [lax.dynamic_index_in_dim(total, me ^ row, 1, keepdims=False) for row in range(4)],
+            axis=2,
+        )
+        return total
 
     early_col = sum_tokens(
         jnp.concatenate(
-            [heads_back(g_attn_low), ff_back(g_gate_up), ff_back(g_upper_up), ff_back(g_reduce_low)],
+            [by_col(grad) for grad in (g_attn_low, g_gate_up, g_upper_up, g_reduce_low)],
             axis=2,
         )
     )
-    late_col = sum_tokens(jnp.concatenate([heads_back(grad) for grad in g_qkv_up], axis=2))
+    late_col = sum_tokens(jnp.concatenate([by_col(grad) for grad in g_qkv_up], axis=2))
 
     def low_of(array):
         return array.transpose(0, 2, 1)
@@ -1006,8 +1776,8 @@
         return array[:, :, :, at : at + size].reshape(SETS, 16, 4 * size)
 
     return (
-        jnp.concatenate(layer_parts),
-        jnp.concatenate(input_parts),
+        layer_out,
+        input_grad,
         jnp.stack([low_of(late[:, 16 * i : 16 * i + 16]) for i in range(3)]),
         jnp.stack([piece_of(late_col, i * sub, sub) for i in range(3)]),
         low_of(piece_of(early_col, 0, sub)),

time: 1520 us -> 1140 us (0.75)
  Pallas kernels: 125 us -> 646 us
  matrix products: 393 us -> 66.8 us
  local copies, waits for them, and re-layouts: 282 us -> 61.4 us
  waiting for transfers between devices: 363 us -> 181 us
  blocking collectives: 103 us -> 0 us
  other arithmetic: 144 us -> 88.3 us
    pallas_call x0 -> x13, Pallas kernels: none -> 522 us  [the longest x1 131 us: backward_call(): pl.pallas_call(backward_kernel, out_shape=[wide] * 2 + [jax.ShapeDtypeStr...]
    dot_general x97 -> x32, matrix products: 392 us -> 66.8 us  [dot_of(): lax.dot_general(left, right, (((left_dim,), (right_dim,)), ((), ())), pre...]
    convert_element_type x10 -> x16, local copies, waits for them, and re-layouts: 131 us -> 1.66 us  [to_sets(): term.astype(F32)[None]]
    ppermute x102 -> x51, waiting for transfers between devices: 248 us -> 125 us  [across(): return lax.ppermute(values, 'row', [(i, i ^ step) for i in range(4)])]
    all_gather x6 -> x0, blocking collectives: 103 us -> none  [the longest x2 64.7 us: sum_groups(): lax.all_gather(pack.astype(BF), ('dp', 'col'), axis=0, tiled=False)]
    all_gather x5, waiting for transfers between devices: 99.9 us -> 0.05 us  [gather_col(): return lax.all_gather(values, 'col', axis=0, tiled=False)]
    unnamed x344 -> x148, local copies, waits for them, and re-layouts: 81.6 us -> 18.5 us
    convert_element_type x8 -> x15, other arithmetic: 48.3 us -> 14.8 us  [the longest x4 7.45 us: set_of(): return (jnp.arange(SETS, dtype=jnp.int32) == which).astype(F32)]
  transfers between devices with their start and end apart: 115 -> 76, of which waited for: 28 -> 31; matrix products, arithmetic and copies ran while one was open for 49% -> 17% of each run, Pallas kernels for 4% -> 57%
where the time goes in v2:
time: 1140 us; the launch traced here: 1130 us
  Pallas kernels  646 us (57%)
  waiting for transfers between devices  181 us (16%)
  other arithmetic  88.3 us (8%)
  starting transfers between devices  69.6 us (6%)
  matrix products  66.8 us (6%)
  local copies, waits for them, and re-layouts  61.4 us (5%)
  between operations  15.7 us (1%)
    pallas_call x1, Pallas kernels, backward_call(): pl.pallas_call(backward_kernel, out_shape=[wide] * 2 + [jax.ShapeDtypeStr...  131 us
    pallas_call x1, Pallas kernels, forward_call(): pl.pallas_call(forward_kernel, out_shape=[wide] * 3 + [part] * 5, in_spec...  127 us
    ppermute x51, waiting for transfers between devices, across(): return lax.ppermute(values, 'row', [(i, i ^ step) for i in range(4)])  125 us
    pallas_call x1, Pallas kernels, branch_call(): pl.pallas_call(branch_kernel, out_shape=[whole, whole, jax.ShapeDtypeStru...  108 us
    dot_general x32, matrix products, dot_of(): lax.dot_general(left, right, (((left_dim,), (right_dim,)), ((), ())), pre...  66.8 us
    pallas_call x1, Pallas kernels, attend_back(): pl.pallas_call(attend_back_kernel, out_shape=(jax.ShapeDtypeStruct(query....  65.4 us
    pallas_call x1, Pallas kernels, input_call(): pl.pallas_call(input_kernel, out_shape=jax.ShapeDtypeStruct((rows, width)...  58.9 us
    pallas_call x1, Pallas kernels, attend(): pl.pallas_call(functools.partial(attend_kernel, first=first), out_shape=(...  37.2 us
  transfers between devices with their start and end apart: 76, of which 31 were waited for; matrix products, arithmetic and copies ran while one was open for 17% of the time, Pallas kernels for 57%

profile of v2, /device:TPU:0, one launch (start us, length us, event | category | flops | bytes accessed | tf_op | source)
XLA Modules:
  0.0 1129.1 jit_solution(6882640721928391809)
XLA Ops:
  13.0 4.6 collective-permute-done.2
  38.6 7.4 collective-permute-done.7
  46.0 4.5 collective-permute-done.8
  52.8 47.2 %collective-permute-done.13.refs_2_ = bf16[2048,512]{1,0:T(8,128)(2,1)S(1)} collective-permute-done((bf16[2048,512]{1,0:T(8,128)(2,1)S(1)}, bf16[2048,512]{1,0:T(8,128)(2,1)S(1)}, u32[]{:S(2)}, u32[]{:S(2)}) %collective-permute-start.13) | collective-permute-done | bytes 2097184 | tf_op jit(solution)/shard_map/ppermute | solution.py:1452
  108.7 7.4 collective-permute-done.25
  116.1 4.5 collective-permute-done.26
  137.2 6.0 collective-permute-done.32
  179.2 5.3 all-to-all-start
  239.1 26.6 %collective-permute-done.15 = bf16[3,4,3,256,128]{4,3,2,1,0:T(8,128)(2,1)} collective-permute-done((bf16[3,4,3,256,128]{4,3,2,1,0:T(8,128)(2,1)}, bf16[3,4,3,256,128]{4,3,2,1,0:T(8,128)(2,1)}, u32[]{:S(2)}, u32[]{:S(2)}) %collective-permute-start.15) | collective-permute-done | bytes 2359328 | tf_op jit(solution)/shard_map/ppermute | solution.py:1479
  269.4 18.3 %merge_qkv.1 = bf16[4,2,256,1536]{3,2,1,0:T(8,128)(2,1)} custom-call(s32[2]{0:T(128)} %pad_add_fusion.pair_ref, bf16[4,4,3,256,128]{4,3,2,1,0:T(8,128)(2,1)} %bitcast.462, bf16[4,4,3,256,128]{4,3,2,1,0:T(8,128)(2,1)} %pad_maximum_fusion.2.other_ref, bf16[4,2,48,256]{3,2,1,0:T(8,128)(2,1)} %bitcast.480, bf16[48,512]{1,0:T(8,128)(2,1)} %pad_maximum_fusion.40.up_ref), custom_call_target="tpu_custom_call" | custom-call | bytes 12582912 | tf_op jit(solution)/shard_map/merge_qkv/pallas_call | solution.py:801
  287.7 24.5 %project.2.raw_ref = f32[2048,1536]{1,0:T(8,128)} custom-call(bf16[2048,512]{1,0:T(8,128)(2,1)} %tokens_ref.1, bf16[2048,512]{1,0:T(8,128)(2,1)} %collective-permute-done.12.refs_1_, bf16[2048,512]{1,0:T(8,128)(2,1)} %copy-done.16, bf16[2048,512]{1,0:T(8,128)(2,1)} %copy-done.18, bf16[2048,1536]{1,0:T(8,128)(2,1)} %bitcast.468), custom_call_target="tpu_custom_call" | custom-call | flops 12884901888 | bytes 14680064 | tf_op jit(solution)/shard_map/project/pallas_call | solution.py:894
  318.7 7.5 merge_out.2.matrix_ref.refs_4_
  330.1 5.9 collective-permute-done.39
  352.5 8.7 rotate_rows.1
  361.2 37.2 %attend.1 = (bf16[2048,512]{1,0:T(8,128)(2,1)}, f32[4,1,2048]{2,1,0:T(1,128)}) custom-call(s32[1]{0:T(128)} %dynamic_slice.295.prefix_ref, bf16[2048,512]{1,0:T(8,128)(2,1)} %get-tuple-element.91.q_ref, bf16[2048,512]{1,0:T(8,128)(2,1)} %get-tuple-element.92.k_ref, bf16[2048,512]{1,0:T(8,128)(2,1)} %get-tuple-element.93.v_ref), custom_call_target="tpu_custom_call" | custom-call | flops 6442450944 | bytes 8388608 | tf_op jit(solution)/shard_map/attend/pallas_call | solution.py:468
  401.1 107.6 %branch.1 = (f32[2048,512]{1,0:T(8,128)}, f32[2048,512]{1,0:T(8,128)}, f32[8,8,256]{2,1,0:T(8,128)}, bf16[2048,512]{1,0:T(8,128)(2,1)}, bf16[2048,512]{1,0:T(8,1...) custom-call(bf16[2048,512]{1,0:T(8,128)(2,1)} %get-tuple-element.99.mixed_ref.out_ref, ...), custom_call_target="tpu_custom_call" | custom-call | flops 4294967296 | bytes 134217728 | tf_op jit(solution)/shard_map/branch/pallas_call | solution.py:1137
  521.8 11.3 %merge_expand.3 = bf16[4,1,512,2048]{3,2,1,0:T(8,128)(2,1)} custom-call(s32[2]{0:T(128)} %pad_add_fusion.pair_ref, bf16[4,4,512,256]{3,2,1,0:T(8,128)(2,1)} %bitcast.460, bf16[4,4,512,256]{3,2,1,0:T(8,128)(2,1)} %pad_maximum_fusion.1.other_ref, bf16[4,1,16,512]{3,2,1,0:T(8,128)(2,1)} %bitcast.488, bf16[16,2048]{1,0:T(8,128)(2,1)} %bitcast.481), custom_call_target="tpu_custom_call" | custom-call | bytes 16777216 | tf_op jit(solution)/shard_map/merge_expand/pallas_call | solution.py:838
  537.4 11.2 merge_expand.2
  548.6 8.9 merge_out.3.reduce_hbm
  557.5 127.0 %forward.1 = (bf16[2048,2048]{1,0:T(8,128)(2,1)}, bf16[2048,2048]{1,0:T(8,128)(2,1)}, bf16[2048,2048]{1,0:T(8,128)(2,1)}, bf16[2048,512]{1,0:T(8,128)(2,1)}, bf1...) custom-call(bf16[2048,512]{1,0:T(8,128)(2,1)} %get-tuple-element.104., ...), custom_call_target="tpu_custom_call" | custom-call | flops 51539607552 | bytes 134217728 | tf_op jit(solution)/shard_map/forward/pallas_call | solution.py:1269
  686.8 130.5 %backward.1 = (bf16[2048,2048]{1,0:T(8,128)(2,1)}, bf16[2048,2048]{1,0:T(8,128)(2,1)}, f32[2048,512]{1,0:T(8,128)}, bf16[2048,512]{1,0:T(8,128)(2,1)}, bf16[2048...) custom-call(bf16[2048,512]{1,0:T(8,128)(2,1)} %get-tuple-element.122.x0, ...), custom_call_target="tpu_custom_call" | custom-call | flops 51539607552 | bytes 134217728 | tf_op jit(solution)/shard_map/backward/pallas_call | solution.py:1395
  817.3 5.8 fusion.135
  823.1 4.7 fusion.8
  835.6 8.9 project.3.grad_ref
  844.5 65.4 %attend_back.1 = (f32[2048,512]{1,0:T(8,128)}, f32[2048,512]{1,0:T(8,128)}, f32[2048,512]{1,0:T(8,128)}, f32[4,1,2048]{2,1,0:T(1,128)}, f32[4,1,2048]{2,1,0:T(1,128)}) custom-call(s32[1]{0:T(128)} %dynamic_slice.295.prefix_ref, bf16[2048,512]{1,0:T(8,128)(2,1)} %get-tuple-element.91.q_ref, bf16[2048,512]{1,0:T(8,128)(2,1)} %project.3.grad_ref, ...), custom_call_target="tpu_custom_call" | custom-call | flops 15032385536 | bytes 25165824 | tf_op jit(solution)/shard_map/attend_back/pallas_call | solution.py:557
  918.9 5.9 convolution_convert_fusion
  936.4 13.3 %unrotate_rows.1.d_qkv_ref = bf16[2048,1536]{1,0:T(8,128)(2,1)} custom-call(f32[2048,1536]{1,0:T(8,128)} %project.2.raw_ref, f32[2048,512]{1,0:T(8,128)} %get-tuple-element.135.dq_ref, f32[2048,512]{1,0:T(8,128)} %get-tuple-element.136.dk_ref, f32[2048,512]{1,0:T(8,128)} %get-tuple-element.137.dv_ref, f32[2048,2]{1,0:T(8,128)} %rsqrt_bitcast_fusion.scale_ref, ...), custom_call_target="tpu_custom_call" | custom-call | tf_op jit(solution)/shard_map/unrotate_rows/pallas_call | solution.py:656
  957.9 58.9 %input_grad.1 = f32[2048,512]{1,0:T(8,128)} custom-call(bf16[2048,1536]{1,0:T(8,128)(2,1)} %unrotate_rows.1.d_qkv_ref, bf16[2048,1536]{1,0:T(8,128)(2,1)} %bitcast.469, f32[2048,512]{1,0:T(8,128)} %get-tuple-element.140.d_hidden_ref), custom_call_target="tpu_custom_call" | custom-call | flops 12884901888 | bytes 67108864 | tf_op jit(solution)/shard_map/input_grad/pallas_call | solution.py:1439
  1017.6 5.1 all-to-all-start.1
  1065.5 9.1 collective-permute-done.66
  1087.0 5.5 collective-permute-done.48
  1094.1 6.2 collective-permute-done.57
  (474 shorter events, 312.2 us)
Async XLA Ops:
  7.2 200.7 %all-gather.11.cloned.1.call-start = ((), (), s32[]{:S(2)}) async-start(), calls=%async_computation.3 | async-start | bytes 3932160 | tf_op jit(solution)/shard_map/all_gather | solution.py:1475
  23.0 208.1 %all-gather.17.cloned.1.call-start = ((), (), s32[]{:S(2)}) async-start(), calls=%async_computation.6 | async-start | bytes 1310720 | tf_op jit(solution)/shard_map/all_gather | solution.py:1475
  31.1 310.2 %all-gather.13.cloned.1.call-start = ((), (), s32[]{:S(2)}) async-start(), calls=%async_computation.4 | async-start | bytes 5242880 | tf_op jit(solution)/shard_map/all_gather | solution.py:1475
  51.6 290.4 %all-gather.15.cloned.1.call-start = ((), (), s32[]{:S(2)}) async-start(), calls=%async_computation.5 | async-start | bytes 5242880 | tf_op jit(solution)/shard_map/all_gather | solution.py:1475
  51.7 48.4 %collective-permute-start.13 = (bf16[2048,512]{1,0:T(8,128)(2,1)S(1)}, bf16[2048,512]{1,0:T(8,128)(2,1)S(1)}, u32[]{:S(2)}, u32[]{:S(2)}) collective-permute-start(bf16[2048,512]{1,0:T(8,128)(2,1)S(1)} %copy-done.3), channel_id=1, source_target_pairs={{0,8},{4,12},{8,0},{12,4},{1,9},{5,13},{9,1},{13,5},{2,10},{6,14},... | collective-permute-start | bytes 6291464 | tf_op jit(solution)/shard_map/ppermute | solution.py:1452
  121.8 426.8 %all-gather.19.cloned.1.call-start = ((), (), s32[]{:S(2)}) async-start(), calls=%async_computation.7 | async-start | bytes 10485760 | tf_op jit(solution)/shard_map/all_gather | solution.py:1475
  129.6 13.5 %collective-permute-start.32 = (bf16[512,256]{1,0:T(8,128)(2,1)S(1)}, bf16[512,256]{1,0:T(8,128)(2,1)}, u32[]{:S(2)}, u32[]{:S(2)}) collective-permute-start(bf16[512,256]{1,0:T(8,128)(2,1)S(1)} %get-tuple-element.110), channel_id=1, source_target_pairs={{0,8},{4,12},{8,0},{12,4},{1,9},{5,13},{9,1},{13,5},{2,10},{6,14},... | collective-permute-start | bytes 786440 | tf_op jit(solution)/shard_map/ppermute | solution.py:1452
  145.4 19.5 %collective-permute-start.37 = (bf16[512,512]{1,0:T(8,128)(2,1)}, bf16[512,512]{1,0:T(8,128)(2,1)}, u32[]{:S(2)}, u32[]{:S(2)}) collective-permute-start(bf16[512,512]{1,0:T(8,128)(2,1)} %get-tuple-element.115), channel_id=1, source_target_pairs={{0,12},{4,8},{8,4},{12,0},{1,13},{5,9},{9,5},{13,1},{2,14},{6,10},... | collective-permute-start | bytes 1572872 | tf_op jit(solution)/shard_map/ppermute | solution.py:1452
  145.4 21.4 %collective-permute-start.35 = (bf16[512,512]{1,0:T(8,128)(2,1)}, bf16[512,512]{1,0:T(8,128)(2,1)}, u32[]{:S(2)}, u32[]{:S(2)}) collective-permute-start(bf16[512,512]{1,0:T(8,128)(2,1)} %get-tuple-element.113), channel_id=1, source_target_pairs={{0,4},{4,0},{8,12},{12,8},{1,5},{5,1},{9,13},{13,9},{2,6},{6,2},{1... | collective-permute-start | bytes 1572872 | tf_op jit(solution)/shard_map/ppermute | solution.py:1452
  146.3 24.7 %collective-permute-start.36 = (bf16[512,512]{1,0:T(8,128)(2,1)}, bf16[512,512]{1,0:T(8,128)(2,1)}, u32[]{:S(2)}, u32[]{:S(2)}) collective-permute-start(bf16[512,512]{1,0:T(8,128)(2,1)} %get-tuple-element.114), channel_id=1, source_target_pairs={{0,8},{4,12},{8,0},{12,4},{1,9},{5,13},{9,1},{13,5},{2,10},{6,14},... | collective-permute-start | bytes 1572872 | tf_op jit(solution)/shard_map/ppermute | solution.py:1452
  147.5 59.3 %collective-permute-start.22 = (f32[2,128]{1,0:T(2,128)S(1)}, f32[2,128]{1,0:T(2,128)S(1)}, u32[]{:S(2)}, u32[]{:S(2)}) collective-permute-start(f32[2,128]{1,0:T(2,128)S(1)} %constant_dynamic-slice_fusion.21), channel_id=1, source_target_pairs={{0,2},{1,3},{2,0},{3,1},{4,6},{5,7},{6,4},{7,5},{8,10},{9,11},{10,... | collective-permute-start | bytes 3080 | tf_op jit(solution)/shard_map/ppermute | solution.py:1484
  149.8 57.0 %collective-permute-start.21 = (f32[2,128]{1,0:T(2,128)S(1)}, f32[2,128]{1,0:T(2,128)S(1)}, u32[]{:S(2)}, u32[]{:S(2)}) collective-permute-start(f32[2,128]{1,0:T(2,128)S(1)} %constant_dynamic-slice_fusion.21), channel_id=1, source_target_pairs={{0,1},{1,2},{2,3},{3,0},{4,5},{5,6},{6,7},{7,4},{8,9},{9,10},{10,1... | collective-permute-start | bytes 3080 | tf_op jit(solution)/shard_map/ppermute | solution.py:1484
  164.8 41.9 %collective-permute-start.23 = (f32[2,128]{1,0:T(2,128)S(1)}, f32[2,128]{1,0:T(2,128)S(1)}, u32[]{:S(2)}, u32[]{:S(2)}) collective-permute-start(f32[2,128]{1,0:T(2,128)S(1)} %constant_dynamic-slice_fusion.21), channel_id=1, source_target_pairs={{0,3},{1,0},{2,1},{3,2},{4,7},{5,4},{6,5},{7,6},{8,11},{9,8},{10,9... | collective-permute-start | bytes 3080 | tf_op jit(solution)/shard_map/ppermute | solution.py:1484
  166.8 67.0 %collective-permute-start.12 = (bf16[2048,512]{1,0:T(8,128)(2,1)S(1)}, bf16[2048,512]{1,0:T(8,128)(2,1)}, u32[]{:S(2)}, u32[]{:S(2)}) collective-permute-start(bf16[2048,512]{1,0:T(8,128)(2,1)S(1)} %copy-done.3), channel_id=1, source_target_pairs={{0,4},{4,0},{8,12},{12,8},{1,5},{5,1},{9,13},{13,9},{2,6},{6,2},{1... | collective-permute-start | bytes 6291464 | tf_op jit(solution)/shard_map/ppermute | solution.py:1452
  171.0 36.4 %collective-permute-start.17 = (bf16[112,512]{1,0:T(8,128)(2,1)}, bf16[112,512]{1,0:T(8,128)(2,1)S(1)}, u32[]{:S(2)}, u32[]{:S(2)}) collective-permute-start(bf16[112,512]{1,0:T(8,128)(2,1)} %row_pack.1), channel_id=1, source_target_pairs={{0,8},{4,12},{8,0},{12,4},{1,9},{5,13},{9,1},{13,5},{2,10},{6,14},... | collective-permute-start | bytes 344072 | tf_op jit(solution)/shard_map/ppermute | solution.py:1452
  179.2 38.2 %all-to-all-start = ((bf16[4,16,2048]{2,1,0:T(8,128)(2,1)}), bf16[4,16,2048]{2,1,0:T(8,128)(2,1)S(1)}, u32[]{:S(2)}, u32[]{:S(2)}) async-start(bf16[4,16,2048]{2,1,0:T(8,128)(2,1)} %col_pack.1), calls=%async_computation | async-start | bytes 524288 | tf_op jit(solution)/shard_map/all_to_all | solution.py:1544
  211.4 54.4 %collective-permute-start.15 = (bf16[3,4,3,256,128]{4,3,2,1,0:T(8,128)(2,1)}, bf16[3,4,3,256,128]{4,3,2,1,0:T(8,128)(2,1)}, u32[]{:S(2)}, u32[]{:S(2)}) collective-permute-start(bf16[3,4,3,256,128]{4,3,2,1,0:T(8,128)(2,1)} %pad_maximum_fusion.5), channel_id=1, source_target_pairs={{0,16},{16,0},{1,17},{17,1},{2,18},{18,2},{3,19},{19,3},{4,20},{20... | collective-permute-start | bytes 7077896 | tf_op jit(solution)/shard_map/ppermute | solution.py:1479
  233.2 83.3 %collective-permute-start.30 = (bf16[3,4,64,512]{3,2,1,0:T(8,128)(2,1)}, bf16[3,4,64,512]{3,2,1,0:T(8,128)(2,1)}, u32[]{:S(2)}, u32[]{:S(2)}) collective-permute-start(bf16[3,4,64,512]{3,2,1,0:T(8,128)(2,1)} %pad_maximum_fusion.22), channel_id=1, source_target_pairs={{0,16},{16,0},{1,17},{17,1},{2,18},{18,2},{3,19},{19,3},{4,20},{20... | collective-permute-start | bytes 2359304 | tf_op jit(solution)/shard_map/ppermute | solution.py:1479
  347.3 170.3 %collective-permute-start.41 = (bf16[3,4,512,256]{3,2,1,0:T(8,128)(2,1)}, bf16[3,4,512,256]{3,2,1,0:T(8,128)(2,1)}, u32[]{:S(2)}, u32[]{:S(2)}) collective-permute-start(bf16[3,4,512,256]{3,2,1,0:T(8,128)(2,1)} %pad_maximum_fusion.4), channel_id=1, source_target_pairs={{0,16},{16,0},{1,17},{17,1},{2,18},{18,2},{3,19},{19,3},{4,20},{20... | collective-permute-start | bytes 9437192 | tf_op jit(solution)/shard_map/ppermute | solution.py:1479
  350.9 182.3 %collective-permute-start.34 = (bf16[3,4,512,256]{3,2,1,0:T(8,128)(2,1)}, bf16[3,4,512,256]{3,2,1,0:T(8,128)(2,1)}, u32[]{:S(2)}, u32[]{:S(2)}) collective-permute-start(bf16[3,4,512,256]{3,2,1,0:T(8,128)(2,1)} %pad_maximum_fusion.3), channel_id=1, source_target_pairs={{0,16},{16,0},{1,17},{17,1},{2,18},{18,2},{3,19},{19,3},{4,20},{20... | collective-permute-start | bytes 9437192 | tf_op jit(solution)/shard_map/ppermute | solution.py:1479
  400.7 114.5 %collective-permute-start.58 = (f32[16,2048]{1,0:T(8,128)S(1)}, f32[16,2048]{1,0:T(8,128)S(1)}, u32[]{:S(2)}, u32[]{:S(2)}) collective-permute-start(f32[16,2048]{1,0:T(8,128)S(1)} %fusion.101), channel_id=1, source_target_pairs={{0,4},{4,0},{8,12},{12,8},{1,5},{5,1},{9,13},{13,9},{2,6},{6,2},{1... | collective-permute-start | bytes 393224 | tf_op jit(solution)/shard_map/ppermute | solution.py:1452
  515.8 411.6 %collective-permute-start.59 = (f32[16,2048]{1,0:T(8,128)}, f32[16,2048]{1,0:T(8,128)}, u32[]{:S(2)}, u32[]{:S(2)}) collective-permute-start(f32[16,2048]{1,0:T(8,128)} %add.678), channel_id=1, source_target_pairs={{0,8},{4,12},{8,0},{12,4},{1,9},{5,13},{9,1},{13,5},{2,10},{6,14},... | collective-permute-start | bytes 393224 | tf_op jit(solution)/shard_map/ppermute | solution.py:1452
  834.4 203.0 %collective-permute-start.62 = (f32[16,2048]{1,0:T(8,128)S(1)}, f32[16,2048]{1,0:T(8,128)}, u32[]{:S(2)}, u32[]{:S(2)}) collective-permute-start(f32[16,2048]{1,0:T(8,128)S(1)} %fusion.137), channel_id=1, source_target_pairs={{0,4},{4,0},{8,12},{12,8},{1,5},{5,1},{9,13},{13,9},{2,6},{6,2},{1... | collective-permute-start | bytes 393224 | tf_op jit(solution)/shard_map/ppermute | solution.py:1452
  835.5 204.8 %collective-permute-start.60 = (f32[32,2048]{1,0:T(8,128)}, f32[32,2048]{1,0:T(8,128)}, u32[]{:S(2)}, u32[]{:S(2)}) collective-permute-start(f32[32,2048]{1,0:T(8,128)} %maximum_multiply_fusion.1), channel_id=1, source_target_pairs={{0,4},{4,0},{8,12},{12,8},{1,5},{5,1},{9,13},{13,9},{2,6},{6,2},{1... | collective-permute-start | bytes 786440 | tf_op jit(solution)/shard_map/ppermute | solution.py:1452
  911.7 18.5 %collective-permute-start.42 = (f32[2,2048]{1,0:T(2,128)S(1)}, f32[2,2048]{1,0:T(2,128)S(1)}, u32[]{:S(2)}, u32[]{:S(2)}) collective-permute-start(f32[2,2048]{1,0:T(2,128)S(1)} %pad_maximum_fusion.43), channel_id=1, source_target_pairs={{0,4},{4,0},{8,12},{12,8},{1,5},{5,1},{9,13},{13,9},{2,6},{6,2},{1... | collective-permute-start | bytes 49160 | tf_op jit(solution)/shard_map/ppermute | solution.py:1452
  1028.3 15.8 %all-to-all-start.2 = ((bf16[4,16,1664]{2,1,0:T(8,128)(2,1)}), bf16[4,16,1664]{2,1,0:T(8,128)(2,1)S(1)}, u32[]{:S(2)}, u32[]{:S(2)}) async-start(bf16[4,16,1664]{2,1,0:T(8,128)(2,1)} %pad_maximum_fusion.31), calls=%async_computation.2 | async-start | bytes 425984 | tf_op jit(solution)/shard_map/all_to_all | solution.py:1747
  1036.9 24.5 %collective-permute-start.44 = (f32[48,2048]{1,0:T(8,128)}, f32[48,2048]{1,0:T(8,128)}, u32[]{:S(2)}, u32[]{:S(2)}) collective-permute-start(f32[48,2048]{1,0:T(8,128)} %maximum_multiply_fusion), channel_id=1, source_target_pairs={{0,4},{4,0},{8,12},{12,8},{1,5},{5,1},{9,13},{13,9},{2,6},{6,2},{1... | collective-permute-start | bytes 1179656 | tf_op jit(solution)/shard_map/ppermute | solution.py:1452
  1044.2 20.1 %collective-permute-start.55 = (bf16[4,16,1664]{2,1,0:T(8,128)(2,1)S(1)}, bf16[4,16,1664]{2,1,0:T(8,128)(2,1)}, u32[]{:S(2)}, u32[]{:S(2)}) collective-permute-start(bf16[4,16,1664]{2,1,0:T(8,128)(2,1)S(1)} %all-to-all-done.2), channel_id=1, source_target_pairs={{0,8},{4,12},{8,0},{12,4},{1,9},{5,13},{9,1},{13,5},{2,10},{6,14},... | collective-permute-start | bytes 638984 | tf_op jit(solution)/shard_map/ppermute | solution.py:1452
  1044.9 33.6 %collective-permute-start.54 = (bf16[4,16,1664]{2,1,0:T(8,128)(2,1)S(1)}, bf16[4,16,1664]{2,1,0:T(8,128)(2,1)}, u32[]{:S(2)}, u32[]{:S(2)}) collective-permute-start(bf16[4,16,1664]{2,1,0:T(8,128)(2,1)S(1)} %all-to-all-done.2), channel_id=1, source_target_pairs={{0,4},{4,0},{8,12},{12,8},{1,5},{5,1},{9,13},{13,9},{2,6},{6,2},{1... | collective-permute-start | bytes 638984 | tf_op jit(solution)/shard_map/ppermute | solution.py:1452
  1062.4 14.7 %collective-permute-start.45 = (f32[48,2048]{1,0:T(8,128)S(1)}, f32[48,2048]{1,0:T(8,128)S(1)}, u32[]{:S(2)}, u32[]{:S(2)}) collective-permute-start(f32[48,2048]{1,0:T(8,128)S(1)} %fusion.126), channel_id=1, source_target_pairs={{0,8},{4,12},{8,0},{12,4},{1,9},{5,13},{9,1},{13,5},{2,10},{6,14},... | collective-permute-start | bytes 1179656 | tf_op jit(solution)/shard_map/ppermute | solution.py:1452
  1064.2 14.3 %collective-permute-start.56 = (bf16[4,16,1664]{2,1,0:T(8,128)(2,1)}, bf16[4,16,1664]{2,1,0:T(8,128)(2,1)S(1)}, u32[]{:S(2)}, u32[]{:S(2)}) collective-permute-start(bf16[4,16,1664]{2,1,0:T(8,128)(2,1)} %collective-permute-done.55), channel_id=1, source_target_pairs={{0,4},{4,0},{8,12},{12,8},{1,5},{5,1},{9,13},{13,9},{2,6},{6,2},{1... | collective-permute-start | bytes 638984 | tf_op jit(solution)/shard_map/ppermute | solution.py:1452
  1079.7 20.7 %collective-permute-start.57 = (bf16[4,4,16,1664]{3,2,1,0:T(8,128)(2,1)S(1)}, bf16[4,4,16,1664]{3,2,1,0:T(8,128)(2,1)S(1)}, u32[]{:S(2)}, u32[]{:S(2)}) collective-permute-start(bf16[4,4,16,1664]{3,2,1,0:T(8,128)(2,1)S(1)} %pad_maximum_fusion.19), channel_id=1, source_target_pairs={{0,16},{16,0},{1,17},{17,1},{2,18},{18,2},{3,19},{19,3},{4,20},{20... | collective-permute-start | bytes 2555912 | tf_op jit(solution)/shard_map/ppermute | solution.py:1479
  (114 other events, 1509.2 us)
Sparse Core Ops, SparseCore 0:
  23.1 65.5 all-gather.10
  90.8 26.5 all-gather.16
  119.0 85.8 all-gather.12
  206.3 79.2 all-gather.14
  287.0 148.1 all-gather.18

commit v3 on v2

--- a/solution.py
+++ b/solution.py
@@ -413,7 +413,6 @@
 
 
 LOG2E = 1.4426950408889634
-CHUNKS = 1
 Q_BLOCK = 512
 K_BLOCK = 512
 BF = jnp.bfloat16
@@ -626,75 +625,21 @@
     )(raw, scales, gains, cosine, sine)
 
 
-def unrotate_kernel(
-    raw_ref, dq_ref, dk_ref, dv_ref, scale_ref, back_ref, gain_ref, cos_ref, sin_ref, out_ref
-):
-    width = dq_ref.shape[1]
-    cosine = cos_ref[...]
-    sine = sin_ref[...]
-    for part, grad in ((0, dq_ref), (1, dk_ref)):
-        scale = scale_ref[:, part : part + 1]
-        back = back_ref[:, part : part + 1]
-        for at in range(0, width, HEAD):
-            turned = grad[:, at : at + HEAD]
-            turned = turned * cosine - pltpu.roll(turned, HEAD // 2, 1) * sine
-            turned = turned * gain_ref[part : part + 1, at : at + HEAD] * scale
-            lane = part * width + at
-            out_ref[:, lane : lane + HEAD] = (
-                turned - raw_ref[:, lane : lane + HEAD] * back
-            ).astype(BF)
-    out_ref[:, 2 * width :] = dv_ref[...].astype(BF)
-
-
-def unrotate_rows(raw, d_query, d_key, d_value, scales, backs, gains, cosine, sine, first):
-    rows, width = raw.shape[0], d_query.shape[1]
-    step = min(512, rows)
-    part = pl.BlockSpec((step, width), lambda i: (i + first // step, 0))
-    table = pl.BlockSpec((step, HEAD), lambda i: (i, 0))
-    pair = pl.BlockSpec((step, 2), lambda i: (i, 0))
-    wide = pl.BlockSpec((step, 3 * width), lambda i: (i, 0))
-    return pl.pallas_call(
-        unrotate_kernel,
-        out_shape=jax.ShapeDtypeStruct((rows, 3 * width), BF),
-        grid=(rows // step,),
-        in_specs=[
-            wide,
-            part,
-            part,
-            part,
-            pair,
-            pair,
-            pl.BlockSpec((2, width), lambda i: (0, 0)),
-            table,
-            table,
-        ],
-        out_specs=wide,
-        name="unrotate_rows",
-    )(raw, d_query, d_key, d_value, scales, backs, gains, cosine, sine)
-
-
-def flip(values):
-    rank = values.shape[1]
-    row = lax.broadcasted_iota(jnp.int32, (rank, rank), 0)
-    unit = (row == lax.broadcasted_iota(jnp.int32, (rank, rank), 1)).astype(BF)
-    return dot_of(unit, values, 1, 1).astype(BF)
-
-
 def row_pack_kernel(set_ref, qkv_ref, attn_ref, expand_ref, reduce_ref, out_ref):
     for part in range(3):
-        out_ref[16 * part : 16 * part + 16, :] = flip(qkv_ref[part, 0])
+        out_ref[16 * part : 16 * part + 16, :] = qkv_ref[part, 0]
     out_ref[48:64, :] = attn_ref[0]
     for part in range(2):
-        out_ref[64 + 16 * part : 80 + 16 * part, :] = flip(expand_ref[part, 0])
+        out_ref[64 + 16 * part : 80 + 16 * part, :] = expand_ref[part, 0]
     out_ref[96:112, :] = reduce_ref[0]
 
 
 def row_pack_of(which, qkv_low, attn_up, expand_low, reduce_up):
     width = attn_up.shape[2]
-    up = pl.BlockSpec((1, 16, width), lambda i, c: (c[0], 0, 0))
-
-    def low(parts):
-        return pl.BlockSpec((parts, 1, width, 16), lambda i, c: (0, c[0], 0, 0))
+    one = pl.BlockSpec((1, 16, width), lambda i, c: (c[0], 0, 0))
+
+    def many(parts):
+        return pl.BlockSpec((parts, 1, 16, width), lambda i, c: (0, c[0], 0, 0))
 
     return pl.pallas_call(
         row_pack_kernel,
@@ -702,7 +647,7 @@
         grid_spec=pltpu.PrefetchScalarGridSpec(
             num_scalar_prefetch=1,
             grid=(1,),
-            in_specs=[low(3), up, low(2), up],
+            in_specs=[many(3), one, many(2), one],
             out_specs=pl.BlockSpec((112, width), lambda i, c: (0, 0)),
         ),
         name="row_pack",
@@ -714,22 +659,22 @@
     for part in range(3):
         out_ref[0, :, part * sub : (part + 1) * sub] = qkv_ref[part, 0]
     at = 4 * sub
-    out_ref[0, :, 3 * sub : at] = flip(attn_ref[0])
+    out_ref[0, :, 3 * sub : at] = attn_ref[0]
     for part in range(2):
         out_ref[0, :, at : at + ff_sub] = expand_ref[part, 0]
         at += ff_sub
-    out_ref[0, :, at:] = flip(reduce_ref[0])
+    out_ref[0, :, at:] = reduce_ref[0]
 
 
 def col_pack_of(which, qkv_up, attn_low, expand_up, reduce_low):
     cols = which.shape[0] - 1
     sub, ff_sub = qkv_up.shape[3] // 4, expand_up.shape[3] // 4
 
-    def up(parts, size):
+    def many(parts, size):
         return pl.BlockSpec((parts, 1, 16, size), lambda i, c: (0, c[i], 0, c[cols]))
 
-    def low(size):
-        return pl.BlockSpec((1, size, 16), lambda i, c: (c[i], c[cols], 0))
+    def one(size):
+        return pl.BlockSpec((1, 16, size), lambda i, c: (c[i], 0, c[cols]))
 
     total = 4 * sub + 3 * ff_sub
     return pl.pallas_call(
@@ -738,13 +683,90 @@
         grid_spec=pltpu.PrefetchScalarGridSpec(
             num_scalar_prefetch=1,
             grid=(cols,),
-            in_specs=[up(3, sub), low(sub), up(2, ff_sub), low(ff_sub)],
+            in_specs=[many(3, sub), one(sub), many(2, ff_sub), one(ff_sub)],
             out_specs=pl.BlockSpec((1, 16, total), lambda i, c: (i, 0, 0)),
         ),
         name="col_pack",
     )(which, qkv_up, attn_low, expand_up, reduce_low)
 
 
+def finish_kernel(ids_ref, rows_ref, cols_ref, *outs):
+    qkv_low, qkv_up, attn_low, attn_up, expand_low, expand_up, reduce_low, reduce_up = outs
+    cols = cols_ref.shape[2]
+    groups = 2 * cols
+    here = pl.program_id(0)
+    me = ids_ref[2 * groups]
+
+    def weight(index):
+        return (ids_ref[index] == here).astype(F32)
+
+    total = jnp.zeros(rows_ref.shape[2:], F32)
+    for k in range(cols):
+        for other in range(2):
+            total = total + weight(2 * k + other) * rows_ref[k, other].astype(F32)
+    for part in range(3):
+        qkv_low[part, 0] = total[16 * part : 16 * part + 16]
+    attn_up[0] = total[48:64]
+    for part in range(2):
+        expand_low[part, 0] = total[64 + 16 * part : 80 + 16 * part]
+    reduce_up[0] = total[96:112]
+    sub = qkv_up.shape[3] // 4
+    ff_sub = expand_up.shape[3] // 4
+    for row in range(4):
+        block = me ^ row
+        total = jnp.zeros(cols_ref.shape[3:], F32)
+        for other in range(2):
+            for index in range(cols):
+                one = cols_ref[block, other, index].astype(F32)
+                total = total + weight(groups + other * cols + index) * one
+        near = slice(row * sub, (row + 1) * sub)
+        wide = slice(row * ff_sub, (row + 1) * ff_sub)
+        for part in range(3):
+            qkv_up[part, 0, :, near] = total[:, part * sub : (part + 1) * sub]
+        attn_low[0, :, near] = total[:, 3 * sub : 4 * sub]
+        for part in range(2):
+            at = 4 * sub + part * ff_sub
+            expand_up[part, 0, :, wide] = total[:, at : at + ff_sub]
+        reduce_low[0, :, wide] = total[:, 4 * sub + 2 * ff_sub :]
+
+
+def finish_call(ids, rows, cols, sub, ff_sub):
+    width = rows.shape[3]
+    shapes = [
+        (3, width),
+        (3, 4 * sub),
+        (0, 4 * sub),
+        (0, width),
+        (2, width),
+        (2, 4 * ff_sub),
+        (0, 4 * ff_sub),
+        (0, width),
+    ]
+    out_shape, out_specs = [], []
+    for parts, size in shapes:
+        if parts:
+            out_shape.append(jax.ShapeDtypeStruct((parts, SETS, 16, size), F32))
+            out_specs.append(pl.BlockSpec((parts, 1, 16, size), lambda k, c: (0, k, 0, 0)))
+        else:
+            out_shape.append(jax.ShapeDtypeStruct((SETS, 16, size), F32))
+            out_specs.append(pl.BlockSpec((1, 16, size), lambda k, c: (k, 0, 0)))
+
+    def whole(array):
+        return pl.BlockSpec(array.shape, lambda k, c: (0,) * array.ndim)
+
+    return pl.pallas_call(
+        finish_kernel,
+        out_shape=out_shape,
+        grid_spec=pltpu.PrefetchScalarGridSpec(
+            num_scalar_prefetch=1,
+            grid=(SETS,),
+            in_specs=[whole(rows), whole(cols)],
+            out_specs=out_specs,
+        ),
+        name="finish",
+    )(ids, rows, cols)
+
+
 def cost_of(flops, bytes_accessed):
     return pl.CostEstimate(flops=int(flops), bytes_accessed=int(bytes_accessed), transcendentals=0)
 
@@ -756,13 +778,30 @@
 def merge_rows_kernel(pair_ref, own_ref, other_ref, low_ref, up_ref, out_ref):
     def put(piece):
         for block in range(4):
-            base = piece[(0, block) + (0,) * (len(piece.shape) - 4)].astype(F32)
+            base = piece[0, block].astype(F32)
             extra = dot_of(low_ref[block, 0], up_ref[...], 0, 0)
             out_ref[block, 0] = (base + ADAPTER_FACTOR * extra).astype(BF)
 
     mine = pl.program_id(0) == pair_ref[0]
     pl.when(mine)(functools.partial(put, own_ref))
     pl.when(jnp.logical_not(mine))(functools.partial(put, other_ref))
+
+
+def merge_qkv_kernel(pair_ref, own_ref, other_ref, low_ref, up_ref, out_ref):
+    cols, sub = own_ref.shape[0], own_ref.shape[4]
+
+    def put(piece, back):
+        for block in range(4):
+            extra = dot_of(low_ref[block, 0], up_ref[...], 0, 0)
+            for index in range(cols):
+                at = lax.rem(index - back + cols, cols)
+                lanes = slice(index * sub, (index + 1) * sub)
+                base = piece[at, block, 0].astype(F32)
+                out_ref[block, 0, :, lanes] = (base + ADAPTER_FACTOR * extra[:, lanes]).astype(BF)
+
+    mine = pl.program_id(0) == pair_ref[0]
+    pl.when(mine)(functools.partial(put, own_ref, 0))
+    pl.when(jnp.logical_not(mine))(functools.partial(put, other_ref, pair_ref[1]))
 
 
 def merge_columns_kernel(pair_ref, *refs):
@@ -785,34 +824,27 @@
 
 def merge_qkv(pair, own, other, low, up):
     cols, _, parts, cut, sub = own.shape
-    last = cols * parts - 1
-
-    def piece(half, relative):
-        def place(h, p, c, pair_ref):
-            at = p * cols + c
-            at = jnp.where(h == half(pair_ref[0]), at, jnp.where(h == 0, 0, last))
-            which = lax.rem(at, cols)
-            if relative:
-                which = lax.rem(which - pair_ref[1] + cols, cols)
-            return (which, 0, lax.div(at, cols), 0, 0)
-
-        return pl.BlockSpec((1, 4, 1, cut, sub), place)
+
+    def piece(half):
+        def place(h, p, pair_ref):
+            mine = h == half(pair_ref[0])
+            return (0, 0, jnp.where(mine, p, jnp.where(h == 0, 0, parts - 1)), 0, 0)
+
+        return pl.BlockSpec((cols, 4, 1, cut, sub), place)
 
     whole = pl.pallas_call(
-        merge_rows_kernel,
+        merge_qkv_kernel,
         out_shape=jax.ShapeDtypeStruct((4, 2, cut, parts * cols * sub), BF),
         grid_spec=pltpu.PrefetchScalarGridSpec(
             num_scalar_prefetch=1,
-            grid=(2, parts, cols),
+            grid=(2, parts),
             in_specs=[
-                piece(lambda one: one, False),
-                piece(lambda one: 1 - one, True),
-                pl.BlockSpec((4, 1, 16, cut), lambda h, p, c, one: (0, h, p, 0)),
-                pl.BlockSpec((16, sub), lambda h, p, c, one: (p, c)),
+                piece(lambda one: one),
+                piece(lambda one: 1 - one),
+                pl.BlockSpec((4, 1, 16, cut), lambda h, p, one: (0, h, p, 0)),
+                pl.BlockSpec((16, cols * sub), lambda h, p, one: (p, 0)),
             ],
-            out_specs=pl.BlockSpec(
-                (4, 1, cut, sub), lambda h, p, c, one: (0, h, 0, p * cols + c)
-            ),
+            out_specs=pl.BlockSpec((4, 1, cut, cols * sub), lambda h, p, one: (0, h, 0, p)),
         ),
         cost_estimate=cost_of(0, 8 * own.size),
         name="merge_qkv",
@@ -951,7 +983,7 @@
     return shapes
 
 
-def run_blocks(count, bufs, compute, stats, finish, own_ref=None, arrived=None):
+def run_blocks(count, bufs, compute, stats, finish, own_ref=None, arrived=None, extra=None):
     pair_out, pair_in, far, side_out, side_in, near, pair_sem, side_sem, *rest = bufs
     gathers = own_ref is not None
     if gathers:
@@ -1012,8 +1044,12 @@
         to_side(c).start()
         at = lax.rem(c, RING)
         near[at] = near[at] + pair_in[c, 0].astype(F32)
+        if extra is not None:
+            extra[0](c)
 
     def sum_side(c):
+        if extra is not None:
+            extra[1](c)
         to_side(c).wait_recv()
         at = lax.rem(c, RING)
         total = near[at] + side_in[c].astype(F32)
@@ -1093,12 +1129,32 @@
 
 
 def branch_kernel(
-    mixed_ref, matrix_ref, tokens_ref, gain_ref, branch_ref, hidden_ref, stat_ref, own_ref, *rest
+    mixed_ref,
+    matrix_ref,
+    tokens_ref,
+    gain_ref,
+    gate_all,
+    gate_rest,
+    upper_all,
+    upper_rest,
+    branch_ref,
+    hidden_ref,
+    stat_ref,
+    own_ref,
+    *rest,
 ):
-    arrived, bufs = rest[:3], rest[3:]
+    arrived, halves, rest = rest[:3], rest[3:5], rest[5:]
+    swap_sems, local_sem, *bufs = rest
     width = own_ref.shape[1]
     count = own_ref.shape[0] // BLOCK
-    greet()
+    greet_all([peer(step) for step in (1, 2, 3)] + [other_of_pair()])
+    swaps = []
+    for index, (whole, rest_half) in enumerate(((gate_all, gate_rest), (upper_all, upper_rest))):
+        swaps += exchange_halves(
+            whole, rest_half, halves[index], swap_sems.at[index], local_sem.at[index]
+        )
+    for copy in swaps:
+        copy.start()
 
     def compute(c, put):
         left = mixed_ref[pl.ds(pl.multiple_of(c * BLOCK, BLOCK), BLOCK), :]
@@ -1117,6 +1173,7 @@
         return hidden.astype(BF)
 
     run_blocks(count, bufs, compute, stats, finish, own_ref, arrived)
+    wait_all(swaps)
 
 
 VMEM_SPEC = pl.BlockSpec(memory_space=pltpu.VMEM)
@@ -1129,21 +1186,29 @@
     )
 
 
-def branch_call(mixed, matrix, tokens, gain):
+def branch_call(mixed, matrix, tokens, gain, halves):
     rows, width = tokens.shape
     count = rows // BLOCK
+    cols = halves[0].shape[0]
     part = jax.ShapeDtypeStruct((rows, width), BF)
     whole = jax.ShapeDtypeStruct((rows, width), F32)
+    half = jax.ShapeDtypeStruct(halves[0].shape, BF)
     return pl.pallas_call(
         branch_kernel,
-        out_shape=[whole, whole, jax.ShapeDtypeStruct((count, 8, BLOCK), F32)] + [part] * 4,
-        in_specs=[VMEM_SPEC] * 4,
-        out_specs=[VMEM_SPEC] * 4 + [ANY_SPEC] * 3,
-        scratch_shapes=exchange_scratch(count, width, True),
+        out_shape=[whole, whole, jax.ShapeDtypeStruct((count, 8, BLOCK), F32)]
+        + [part] * 4
+        + [half] * 2,
+        in_specs=[VMEM_SPEC] * 4 + [ANY_SPEC] * 4,
+        out_specs=[VMEM_SPEC] * 4 + [ANY_SPEC] * 5,
+        scratch_shapes=[
+            pltpu.SemaphoreType.DMA((2, 2, cols - 1)),
+            pltpu.SemaphoreType.DMA((2,)),
+        ]
+        + exchange_scratch(count, width, True),
         compiler_params=talk_params(0),
         cost_estimate=cost_of(8 * rows * width * matrix.shape[0], 2**27),
         name="branch",
-    )(mixed, matrix, tokens, gain)
+    )(mixed, matrix, tokens, gain, *halves)
 
 
 def load_lefts(lefts, buffer, sems, count):
@@ -1418,44 +1483,513 @@
     )(*lefts, gate_w, upper_w, reduce_w, gate, upper, cotangent, branch, stats, gain)
 
 
-def input_kernel(d_qkv_ref, matrix_ref, d_hidden_ref, out_ref, *bufs):
+def input_kernel(
+    raw_hbm,
+    dq_hbm,
+    dk_hbm,
+    dv_hbm,
+    matrix_ref,
+    d_hidden_ref,
+    scale_ref,
+    back_ref,
+    gain_ref,
+    cos_ref,
+    sin_ref,
+    tokens_ref,
+    inner_ref,
+    up_ref,
+    out_ref,
+    low_grad_ref,
+    up_grad_ref,
+    raw_buf,
+    dq_buf,
+    dk_buf,
+    dv_buf,
+    left_ref,
+    inner_out,
+    inner_in,
+    inner_mid,
+    inner_far,
+    in_sem,
+    core_sem,
+    far_sem,
+    *bufs,
+):
     width = out_ref.shape[1]
+    local = dq_buf.shape[2]
     count = out_ref.shape[0] // BLOCK
+    ins = [
+        move_rows(outer, buffer, in_sem, index, True)
+        for index, (outer, buffer) in enumerate(
+            ((raw_hbm, raw_buf), (dq_hbm, dq_buf), (dk_hbm, dk_buf), (dv_hbm, dv_buf))
+        )
+    ]
+    for one in ins:
+        one(0).start()
+    low_grad_ref[...] = jnp.zeros_like(low_grad_ref)
+    up_grad_ref[...] = jnp.zeros_like(up_grad_ref)
     greet()
 
+    def inner_core(c):
+        return send(inner_out.at[lax.rem(c, 2)], inner_in.at[c], core_sem, c, 1)
+
+    def inner_side(c):
+        return send(inner_mid.at[lax.rem(c, 2)], inner_far.at[c], far_sem, c, 2)
+
+    def after_core(c):
+        @pl.when(c >= 2)
+        def _():
+            inner_side(c - 2).wait_send()
+
+        inner_core(c).wait_recv()
+        slot = lax.rem(c, 2)
+        inner_mid[slot] = inner_out[slot] + inner_in[c]
+        inner_side(c).start()
+
+    def after_side(c):
+        inner_side(c).wait_recv()
+        total = (inner_mid[lax.rem(c, 2)] + inner_far[c]).astype(BF)
+        low_grad_ref[...] += dot_of(total, tokens_ref[span_of(c, BLOCK), :], 1, 0)
+
     def compute(c, put):
-        left = d_qkv_ref[pl.ds(pl.multiple_of(c * BLOCK, BLOCK), BLOCK), :]
+        slot = lax.rem(c, 2)
+        for one in ins:
+            one(c).wait()
+
+        @pl.when(c + 1 < count)
+        def _():
+            for one in ins:
+                one(c + 1).start()
+
+        @pl.when(c >= 2)
+        def _():
+            inner_core(c - 2).wait_send()
+
+        rows = span_of(c, BLOCK)
+        cosine = cos_ref[rows, :]
+        sine = sin_ref[rows, :]
+        for part, grad in ((0, dq_buf), (1, dk_buf)):
+            scale = scale_ref[rows, part : part + 1]
+            back = back_ref[rows, part : part + 1]
+            for at in range(0, local, HEAD):
+                turned = grad[slot, :, at : at + HEAD]
+                turned = turned * cosine - pltpu.roll(turned, HEAD // 2, 1) * sine
+                turned = turned * gain_ref[part : part + 1, at : at + HEAD] * scale
+                lane = part * local + at
+                left_ref[:, lane : lane + HEAD] = (
+                    turned - raw_buf[slot, :, lane : lane + HEAD] * back
+                ).astype(BF)
+        left_ref[:, 2 * local :] = dv_buf[slot].astype(BF)
+        for part in range(3):
+            own = slice(16 * part, 16 * part + 16)
+            grad = left_ref[:, part * local : (part + 1) * local]
+            inner_out[slot, own, :] = ADAPTER_FACTOR * dot_of(up_ref[own, :], grad, 1, 1)
+            up_grad_ref[own, :] += ADAPTER_FACTOR * dot_of(inner_ref[own, rows], grad, 1, 0)
+        inner_core(c).start()
+        left = left_ref[...]
         for block in (1, 3, 2, 0):
             put(block, dot_of(left, matrix_ref[block * width : (block + 1) * width, :], 1, 1))
 
     def finish(c, rows, total):
         out_ref[rows, :] = d_hidden_ref[rows, :] + total
 
-    run_blocks(count, bufs, compute, None, finish)
-
-
-def input_call(d_qkv, matrix, d_hidden):
+    run_blocks(count, bufs, compute, None, finish, extra=(after_core, after_side))
+    for c in range(max(count - 2, 0), count):
+        inner_core(c).wait_send()
+        inner_side(c).wait_send()
+
+
+def input_call(
+    raw, d_query, d_key, d_value, matrix, d_hidden, scales, backs, gains, cosine, sine, *adapters
+):
     rows, width = d_hidden.shape
+    local = d_query.shape[1]
+    count = rows // BLOCK
+    part = pltpu.VMEM((2, BLOCK, local), F32)
+    sem = pltpu.SemaphoreType.DMA((2, count))
     return pl.pallas_call(
         input_kernel,
-        out_shape=jax.ShapeDtypeStruct((rows, width), F32),
-        in_specs=[VMEM_SPEC] * 3,
-        out_specs=VMEM_SPEC,
-        scratch_shapes=exchange_scratch(rows // BLOCK, width, False),
+        out_shape=[
+            jax.ShapeDtypeStruct((rows, width), F32),
+            jax.ShapeDtypeStruct((48, width), F32),
+            jax.ShapeDtypeStruct((48, local), F32),
+        ],
+        in_specs=[ANY_SPEC] * 4 + [VMEM_SPEC] * 10,
+        out_specs=[VMEM_SPEC] * 3,
+        scratch_shapes=[
+            pltpu.VMEM((2, BLOCK, 3 * local), F32),
+            part,
+            part,
+            part,
+            pltpu.VMEM((BLOCK, 3 * local), BF),
+            pltpu.VMEM((2, 48, BLOCK), F32),
+            pltpu.VMEM((count, 48, BLOCK), F32),
+            pltpu.VMEM((2, 48, BLOCK), F32),
+            pltpu.VMEM((count, 48, BLOCK), F32),
+            pltpu.SemaphoreType.DMA((4, 2)),
+            sem,
+            sem,
+        ]
+        + exchange_scratch(count, width, False),
         compiler_params=talk_params(3),
-        cost_estimate=cost_of(8 * rows * width * d_qkv.shape[1], 2**26),
+        cost_estimate=cost_of(24 * rows * width * local, 2**26),
         name="input_grad",
-    )(d_qkv, matrix, d_hidden)
+    )(raw, d_query, d_key, d_value, matrix, d_hidden, scales, backs, gains, cosine, sine, *adapters)
+
+
+def deal(items, outs, sems):
+    me = lax.axis_index("row")
+    copies = []
+    for index, (view, out) in enumerate(zip(items, outs)):
+        mine = [pltpu.make_async_copy(view(me), out.at[0], sems.at[0, index, 0])]
+        for step in (1, 2, 3):
+            mine.append(
+                pltpu.make_async_remote_copy(
+                    src_ref=view(me ^ step),
+                    dst_ref=out.at[step],
+                    send_sem=sems.at[0, index, step],
+                    recv_sem=sems.at[1, index, step],
+                    device_id=peer(step),
+                    device_id_type=pl.DeviceIdType.MESH,
+                )
+            )
+        copies.append(mine)
+    return copies
+
+
+def start_all(copies):
+    for step in (2, 3, 1, 0):
+        copies[step].start()
+
+
+def wait_all(copies):
+    for copy in copies:
+        copy.wait()
+
+
+def span_of(at, size):
+    return pl.ds(pl.multiple_of(at * size, size), size)
+
+
+def qkv_view(ref, half):
+    _, rows, columns = ref.shape
+    return lambda row: ref.at[:, span_of(half, rows // 2), span_of(row, columns // 4)]
+
+
+def attn_view(ref, half):
+    cut = ref.shape[0] // 8
+    return lambda row: ref.at[span_of(2 * row + half, cut)]
+
+
+def expand_view(ref, part, half):
+    cut = ref.shape[2] // 8
+    return lambda row: ref.at[part, :, span_of(2 * row + half, cut)]
+
+
+def reduce_view(ref):
+    cut = ref.shape[0] // 4
+    return lambda row: ref.at[span_of(row, cut)]
+
+
+def like_views(shapes):
+    return [jax.ShapeDtypeStruct((4, *shape), BF) for shape in shapes]
+
+
+def first_deal_kernel(qkv_ref, attn_ref, qkv_out, attn_out, sems):
+    half = lax.axis_index("dp")
+    greet()
+    copies = deal([qkv_view(qkv_ref, half), attn_view(attn_ref, half)], [qkv_out, attn_out], sems)
+    for one in copies:
+        start_all(one)
+    for one in copies:
+        wait_all(one)
+
+
+def first_deal(qkv_weight, attn_weight):
+    parts, rows, columns = qkv_weight.shape
+    return pl.pallas_call(
+        first_deal_kernel,
+        out_shape=like_views(
+            [(parts, rows // 2, columns // 4), (attn_weight.shape[0] // 8, attn_weight.shape[1])]
+        ),
+        in_specs=[ANY_SPEC] * 2,
+        out_specs=[ANY_SPEC] * 2,
+        scratch_shapes=[pltpu.SemaphoreType.DMA((2, 2, 4))],
+        compiler_params=talk_params(4),
+        cost_estimate=cost_of(0, 2**26),
+        name="first_deal",
+    )(qkv_weight, attn_weight)
+
+
+def second_deal_kernel(qkv_ref, attn_ref, expand_ref, tokens_ref, pack_ref, *rest):
+    *outs, t1, t2, t3, p1, p2, p3, sems, token_sem, pack_sem = rest
+    half = lax.axis_index("dp")
+    greet()
+    gate, rest_qkv, rest_attn, upper = deal(
+        [
+            expand_view(expand_ref, 0, half),
+            qkv_view(qkv_ref, 1 - half),
+            attn_view(attn_ref, 1 - half),
+            expand_view(expand_ref, 1, half),
+        ],
+        outs,
+        sems,
+    )
+    gathers = []
+    for source, targets, one_sem in ((pack_ref, (p1, p2, p3), pack_sem), (tokens_ref, (t1, t2, t3), token_sem)):
+        gathers.append(
+            (
+                send(source, targets[1], one_sem, 1, 2),
+                send(source, targets[0], one_sem, 0, 1),
+                send(targets[1], targets[2], one_sem, 2, 1),
+            )
+        )
+    start_all(gate)
+    start_all(rest_qkv)
+    start_all(rest_attn)
+    for side, core, _ in gathers:
+        side.start()
+        core.start()
+    start_all(upper)
+    for side, core, relay in gathers:
+        side.wait_recv()
+        relay.start()
+    for one in (gate, rest_qkv, rest_attn, upper):
+        wait_all(one)
+    for side, core, relay in gathers:
+        side.wait_send()
+        core.wait()
+        relay.wait()
+
+
+def second_deal(qkv_weight, attn_weight, expand_weight, tokens, pack):
+    parts, rows, columns = qkv_weight.shape
+    cut = expand_weight.shape[2] // 8
+    wide = (expand_weight.shape[1], cut)
+    sem = pltpu.SemaphoreType.DMA((2, 3))
+    return pl.pallas_call(
+        second_deal_kernel,
+        out_shape=like_views(
+            [
+                wide,
+                (parts, rows // 2, columns // 4),
+                (attn_weight.shape[0] // 8, attn_weight.shape[1]),
+                wide,
+            ]
+        )
+        + [jax.ShapeDtypeStruct(tokens.shape, BF)] * 3
+        + [jax.ShapeDtypeStruct(pack.shape, BF)] * 3,
+        in_specs=[ANY_SPEC] * 5,
+        out_specs=[ANY_SPEC] * 10,
+        scratch_shapes=[pltpu.SemaphoreType.DMA((2, 4, 4)), sem, sem],
+        compiler_params=talk_params(5),
+        cost_estimate=cost_of(0, 2**27),
+        name="second_deal",
+    )(qkv_weight, attn_weight, expand_weight, tokens, pack)
+
+
+def greet_all(peers):
+    barrier = pltpu.get_barrier_semaphore()
+    for device in peers:
+        pl.semaphore_signal(barrier, inc=1, device_id=device, device_id_type=pl.DeviceIdType.MESH)
+    pl.semaphore_wait(barrier, len(peers))
+
+
+def copy_to(source, target, sems, index, device):
+    return pltpu.make_async_remote_copy(
+        src_ref=source,
+        dst_ref=target,
+        send_sem=sems.at[0, index],
+        recv_sem=sems.at[1, index],
+        device_id=device,
+        device_id_type=pl.DeviceIdType.MESH,
+    )
+
+
+def other_of_pair():
+    return {"dp": 1 - lax.axis_index("dp")}
+
+
+def exchange_halves(whole, rest, out, sems, local_sem):
+    cols = whole.shape[0]
+    col = lax.axis_index("col")
+    copies = [pltpu.make_async_copy(rest, out.at[0], local_sem)]
+    for k in range(1, cols):
+        place = lax.rem(col + k, cols)
+        copies.append(copy_to(whole.at[place], out.at[k], sems, k - 1, other_of_pair()))
+    return copies
+
+
+def send_round(view, out, sems, local_sem):
+    cols = out.shape[0]
+    col = lax.axis_index("col")
+    local = pltpu.make_async_copy(view(col), out.at[col], local_sem)
+    sends = []
+    arrivals = []
+    for k in range(1, cols):
+        place = lax.rem(col + k, cols)
+        came = lax.rem(col - k + cols, cols)
+        sends.append(copy_to(view(place), out.at[col], sems, k - 1, {"col": place}))
+        arrivals.append(copy_to(view(place), out.at[came], sems, k - 1, {"col": place}))
+
+    def wait():
+        local.wait()
+        for one in arrivals:
+            one.wait_recv()
+        for one in sends:
+            one.wait_send()
+
+    return [local, *sends], wait
+
+
+def row_and_col_peers():
+    cols = lax.axis_size("col")
+    col = lax.axis_index("col")
+    return [peer(step) for step in (1, 2, 3)] + [
+        {"col": lax.rem(col + k, cols)} for k in range(1, cols)
+    ]
+
+
+def third_deal_kernel(
+    expand_ref, reduce_ref, qkv_all, qkv_rest, attn_all, attn_rest, pack_ref, gain_ref, *rest
+):
+    *outs, qkv_out, attn_out, pack_out, gain_out = rest[:7]
+    deal_sem, qkv_sem, attn_sem, pack_sem, gain_sem, local_sem = rest[7:]
+    other = 1 - lax.axis_index("dp")
+    me = lax.axis_index("row")
+    greet_all(row_and_col_peers() + [other_of_pair()])
+    sub = gain_out.shape[2]
+    swaps = exchange_halves(qkv_all, qkv_rest, qkv_out, qkv_sem, local_sem.at[0])
+    swaps += exchange_halves(attn_all, attn_rest, attn_out, attn_sem, local_sem.at[1])
+    packs, wait_packs = send_round(lambda place: pack_ref.at[place], pack_out, pack_sem, local_sem.at[2])
+    gains, wait_gains = send_round(
+        lambda place: gain_ref.at[:, span_of(me, sub)], gain_out, gain_sem, local_sem.at[3]
+    )
+    for copy in packs + gains + swaps:
+        copy.start()
+    copies = deal(
+        [
+            reduce_view(reduce_ref),
+            expand_view(expand_ref, 0, other),
+            expand_view(expand_ref, 1, other),
+        ],
+        outs,
+        deal_sem,
+    )
+    for one in copies:
+        start_all(one)
+    wait_packs()
+    wait_gains()
+    for one in copies:
+        wait_all(one)
+    wait_all(swaps)
+
+
+def third_deal(expand_weight, reduce_weight, qkv_all, qkv_rest, attn_all, attn_rest, pack, gain):
+    wide = (expand_weight.shape[1], expand_weight.shape[2] // 8)
+    cols = qkv_all.shape[0]
+    round_sem = pltpu.SemaphoreType.DMA((2, cols - 1))
+    return pl.pallas_call(
+        third_deal_kernel,
+        out_shape=like_views([(reduce_weight.shape[0] // 4, reduce_weight.shape[1]), wide, wide])
+        + [
+            jax.ShapeDtypeStruct(qkv_all.shape, BF),
+            jax.ShapeDtypeStruct(attn_all.shape, BF),
+            jax.ShapeDtypeStruct(pack.shape, BF),
+            jax.ShapeDtypeStruct((cols, gain.shape[0], gain.shape[1] // 4), F32),
+        ],
+        in_specs=[ANY_SPEC] * 8,
+        out_specs=[ANY_SPEC] * 7,
+        scratch_shapes=[
+            pltpu.SemaphoreType.DMA((2, 3, 4)),
+            round_sem,
+            round_sem,
+            round_sem,
+            round_sem,
+            pltpu.SemaphoreType.DMA((4,)),
+        ],
+        compiler_params=talk_params(6),
+        cost_estimate=cost_of(0, 2**27),
+        name="third_deal",
+    )(expand_weight, reduce_weight, qkv_all, qkv_rest, attn_all, attn_rest, pack, gain)
+
+
+def groups_kernel(row_ref, col_ref, rows_out, cols_out, local_sem, pair_sem, round_sem, deal_sem, row_sem):
+    cols = col_ref.shape[0]
+    col = lax.axis_index("col")
+    places = [lax.rem(col + k, cols) for k in range(cols)]
+    to = copy_to
+    greet_all(row_and_col_peers() + [other_of_pair()])
+    swap_rows = to(row_ref, rows_out.at[0, 1], pair_sem, 0, other_of_pair())
+    swap_rows.start()
+    dealt = [
+        to(col_ref.at[places[k]], cols_out.at[0, 0, col], deal_sem, k - 1, {"col": places[k]})
+        for k in range(1, cols)
+    ]
+    for copy in dealt:
+        copy.start()
+    keep_rows = pltpu.make_async_copy(row_ref, rows_out.at[0, 0], local_sem.at[0])
+    keep_cols = pltpu.make_async_copy(col_ref.at[col], cols_out.at[0, 0, col], local_sem.at[1])
+    keep_rows.start()
+    keep_cols.start()
+    for k in range(1, cols):
+        came = lax.rem(col - k + cols, cols)
+        to(col_ref.at[came], cols_out.at[0, 0, came], deal_sem, k - 1, {"col": places[k]}).wait_recv()
+    keep_cols.wait()
+    swap_cols = to(cols_out.at[0, 0], cols_out.at[0, 1], pair_sem, 1, other_of_pair())
+    swap_cols.start()
+    keep_rows.wait()
+    swap_rows.wait_recv()
+    rounds = [
+        to(rows_out.at[0], rows_out.at[k], round_sem, k - 1, {"col": places[k]})
+        for k in range(1, cols)
+    ]
+    for copy in rounds:
+        copy.start()
+    swap_cols.wait_recv()
+    side = to(cols_out.at[0], cols_out.at[2], row_sem, 1, peer(2))
+    core = to(cols_out.at[0], cols_out.at[1], row_sem, 0, peer(1))
+    relay = to(cols_out.at[2], cols_out.at[3], row_sem, 2, peer(1))
+    side.start()
+    core.start()
+    side.wait_recv()
+    relay.start()
+    core.wait()
+    relay.wait()
+    side.wait_send()
+    for copy in rounds:
+        copy.wait()
+    for copy in dealt:
+        copy.wait_send()
+    swap_rows.wait_send()
+    swap_cols.wait_send()
+
+
+def groups_call(row_pack, col_pack):
+    cols = col_pack.shape[0]
+    return pl.pallas_call(
+        groups_kernel,
+        out_shape=[
+            jax.ShapeDtypeStruct((cols, 2, *row_pack.shape), BF),
+            jax.ShapeDtypeStruct((4, 2, *col_pack.shape), BF),
+        ],
+        in_specs=[ANY_SPEC] * 2,
+        out_specs=[ANY_SPEC] * 2,
+        scratch_shapes=[
+            pltpu.SemaphoreType.DMA((2,)),
+            pltpu.SemaphoreType.DMA((2, 2)),
+            pltpu.SemaphoreType.DMA((2, cols - 1)),
+            pltpu.SemaphoreType.DMA((2, cols - 1)),
+            pltpu.SemaphoreType.DMA((2, 3)),
+        ],
+        compiler_params=talk_params(7),
+        cost_estimate=cost_of(0, 2**26),
+        name="groups",
+    )(row_pack, col_pack)
 
 
 def across(values, step):
     return lax.ppermute(values, "row", [(i, i ^ step) for i in range(4)])
-
-
-def gather_row(own):
-    core = across(own, 1)
-    side = across(own, 2)
-    return [own, core, side, across(side, 1)]
 
 
 def sum_row(values):
@@ -1463,14 +1997,6 @@
     return values + across(values, 2)
 
 
-def deal_row(piece_for, me):
-    out = []
-    for step in range(4):
-        piece = piece_for(me ^ step)
-        out.append(piece if step == 0 else across(piece, step))
-    return jnp.stack(out)
-
-
 def gather_col(values):
     return lax.all_gather(values, "col", axis=0, tiled=False)
 
@@ -1486,10 +2012,6 @@
 
 def after(values, earlier):
     return lax.optimization_barrier((values, earlier))[0]
-
-
-def join(parts, axis=0):
-    return parts[0] if len(parts) == 1 else jnp.concatenate(parts, axis=axis)
 
 
 def group_shards(
@@ -1528,20 +2050,50 @@
     prefix = lax.dynamic_slice_in_dim(prefix_length, sequence, 1)
     cols_sets = lax.dynamic_slice_in_dim(adapter_set, pair * cols, cols)
 
-    row_pack = row_pack_of(mine.reshape(1), qkv_lowrank, attn_uprank, expand_lowrank, reduce_uprank)
-    row_all = jnp.concatenate(gather_row(row_pack), axis=1)
+    row_pack = row_pack_of(
+        mine.reshape(1),
+        qkv_lowrank.transpose(0, 1, 3, 2),
+        attn_uprank,
+        expand_lowrank.transpose(0, 1, 3, 2),
+        reduce_uprank,
+    )
+    col_pack = col_pack_of(
+        jnp.concatenate([cols_sets, me.reshape(1)]),
+        qkv_uprank,
+        attn_lowrank.transpose(0, 2, 1),
+        expand_uprank,
+        reduce_lowrank.transpose(0, 2, 1),
+    )
+
+    place = jnp.stack([pair, col])
+
+    qkv_own, attn_own = first_deal(qkv_weight, attn_weight)
+    col_pack = after(col_pack, qkv_own)
+    gate_own, qkv_rest, attn_rest, up_own, *others = second_deal(
+        qkv_weight, attn_weight, expand_weight, tokens, after(row_pack, qkv_own)
+    )
+    token_parts = [tokens, *others[:3]]
+    row_all = jnp.concatenate([row_pack, *others[3:]], axis=1)
     qkv_low = row_all[:48]
     attn_up = row_all[48:64]
     expand_low = row_all[64:96]
     reduce_up = row_all[96:112]
-    col_pack = col_pack_of(
-        jnp.concatenate([cols_sets, me.reshape(1)]),
-        qkv_uprank,
-        attn_lowrank,
-        expand_uprank,
-        reduce_lowrank,
-    )
-    col_all = lax.all_to_all(col_pack, "col", split_axis=0, concat_axis=0, tiled=True)
+    qkv_all = gather_col(qkv_own)
+    attn_all = gather_col(attn_own)
+    gate_all = gather_col(gate_own)
+    up_all = gather_col(up_own)
+    reduce_own, gate_rest, up_rest, qkv_other, attn_other, col_all, gains = third_deal(
+        expand_weight,
+        after(reduce_weight, others[0]),
+        qkv_all,
+        qkv_rest,
+        attn_all,
+        attn_rest,
+        col_pack,
+        headnorm_gain,
+    )
+    reduce_all = gather_col(reduce_own)
+    gains = gains.transpose(1, 0, 2).reshape(2, local)
 
     def own_columns(at, size):
         return col_all[:, :, at : at + size].transpose(1, 0, 2).reshape(16, cols * size)
@@ -1550,84 +2102,10 @@
     attn_low = own_columns(3 * sub, sub)
     expand_up = [own_columns(4 * sub + i * ff_sub, ff_sub) for i in range(2)]
     reduce_low = own_columns(4 * sub + 2 * ff_sub, ff_sub)
-    gains = lax.dynamic_slice_in_dim(headnorm_gain, me * sub, sub, 1)
-    gains = jnp.stack(round_col(gains, cols))
-    gains = jnp.concatenate(
-        [
-            lax.dynamic_index_in_dim(gains, lax.rem(col - i + cols, cols), 0, keepdims=False)
-            for i in range(cols)
-        ],
-        axis=1,
-    )
-
-    place = jnp.stack([pair, col])
-    in_half = width // 2
-    head_half = sub // 2
-
-    def exchanged(own, other_piece):
-        sent = jnp.stack(
-            [
-                lax.dynamic_index_in_dim(own, lax.rem(col + k, cols), 0, keepdims=False)
-                for k in range(1, cols)
-            ]
-        )
-        return jnp.concatenate([other_piece[None], swap_pair(sent)])
-
-    def qkv_piece(half):
-        return lambda row: lax.dynamic_slice(
-            qkv_weight, (0, half * in_half, row * sub), (3, in_half, sub)
-        )
-
-    def attn_piece(half, earlier):
-        return lambda row: after(
-            lax.dynamic_slice_in_dim(attn_weight, row * sub + half * head_half, head_half, 0),
-            earlier,
-        )
-
-    def expand_piece(part, half, earlier):
-        return lambda row: after(
-            lax.dynamic_slice(
-                expand_weight[part], (0, row * ff_sub + half * ff_half), (width, ff_half)
-            ),
-            earlier,
-        )
-
-    step = rows // CHUNKS
-    spans = [slice(i * step, (i + 1) * step) for i in range(CHUNKS)]
-    qkv_own = deal_row(qkv_piece(pair), me)
-    attn_own = deal_row(attn_piece(pair, qkv_own), me)
-    gate_own = deal_row(expand_piece(0, pair, attn_own), me)
-    qkv_rest = deal_row(lambda row: after(qkv_piece(1 - pair)(row), gate_own), me)
-    token_parts = []
-    for span in spans:
-        token_parts.append(gather_row(after(tokens[span], qkv_rest)))
-    last = token_parts[-1][3]
-    up_own = deal_row(expand_piece(1, pair, last), me)
-    attn_rest = deal_row(attn_piece(1 - pair, up_own), me)
-    gate_rest = deal_row(expand_piece(0, 1 - pair, attn_rest), me)
-    reduce_own = deal_row(
-        lambda row: after(
-            lax.dynamic_slice_in_dim(reduce_weight, row * ff_sub, ff_sub, 0), gate_rest
-        ),
-        me,
-    )
-    up_rest = deal_row(expand_piece(1, 1 - pair, reduce_own), me)
-    qkv_all = gather_col(qkv_own)
-    attn_all = gather_col(attn_own)
-    gate_all = gather_col(gate_own)
-    up_all = gather_col(up_own)
-    reduce_all = gather_col(reduce_own)
-    qkv_w = merge_qkv(
-        place, qkv_all, exchanged(qkv_all, qkv_rest), qkv_low, jnp.concatenate(qkv_up)
-    )
-    attn_w = merge_out(place, [attn_all, exchanged(attn_all, attn_rest)], attn_low, attn_up)
-    expand_w = [
-        merge_expand(
-            place, whole, exchanged(whole, rest), expand_low[16 * i : 16 * i + 16], expand_up[i]
-        )
-        for i, (whole, rest) in enumerate(((gate_all, gate_rest), (up_all, up_rest)))
-    ]
-    reduce_w = merge_out(place, [reduce_all], reduce_low, reduce_up)
+
+    qkv_up = jnp.concatenate(qkv_up)
+    qkv_w = merge_qkv(place, qkv_all, qkv_other, qkv_low, qkv_up)
+    attn_w = merge_out(place, [attn_all, attn_other], attn_low, attn_up)
 
     half = HEAD // 2
     freq = THETA ** (-2.0 * jnp.arange(half, dtype=F32) / HEAD)
@@ -1635,7 +2113,6 @@
     cosine = jnp.concatenate([jnp.cos(angle)] * 2, axis=1)
     sine = jnp.sin(angle)
     sine = jnp.concatenate([-sine, sine], axis=1)
-    raws, scales, turned, qkv_inner = [], [], [], []
 
     def low_of_parts(low, parts):
         return functools.reduce(
@@ -1643,23 +2120,23 @@
             [dot_of(low[:, i * width : (i + 1) * width], parts[i], 1, 1) for i in range(4)],
         )
 
-    for span, parts in zip(spans, token_parts):
-        qkv_inner.append(low_of_parts(qkv_low, parts).astype(BF))
-        raw = project(parts, qkv_w, 0, F32)
-        squares = jnp.stack(
-            [jnp.sum(raw[:, i * local : (i + 1) * local] ** 2, axis=1) for i in range(2)]
+    raw = project(token_parts, qkv_w, 0, F32)
+    squares = jnp.stack(
+        [jnp.sum(raw[:, i * local : (i + 1) * local] ** 2, axis=1) for i in range(2)]
+    )
+    scale = lax.rsqrt(sum_row(squares) / D + EPS)
+    query, key, value = rotate_rows(raw, scale.T, gains, cosine, sine)
+    mixed, log_total = attend(prefix, query, key, value, 0)
+    branch, hidden, branch_stats, *hidden_parts, gate_other, up_other = branch_call(
+        mixed, attn_w, tokens, post_gain, (gate_all, gate_rest, up_all, up_rest)
+    )
+    expand_w = [
+        merge_expand(
+            place, whole, other, expand_low[16 * i : 16 * i + 16], expand_up[i]
         )
-        scale = lax.rsqrt(sum_row(squares) / D + EPS).T
-        raws.append(raw)
-        scales.append(scale)
-        turned.append(rotate_rows(after(raw, gate_all), scale, gains, cosine[span], sine[span]))
-    key = join([part[1] for part in turned])
-    value = join([part[2] for part in turned])
-
-    query = join([part[0] for part in turned])
-    mixed, log_total = attend(prefix, query, key, value, 0)
-    mixed = after(mixed, up_all)
-    branch, hidden, branch_stats, *hidden_parts = branch_call(mixed, attn_w, tokens, post_gain)
+        for i, (whole, other) in enumerate(((gate_all, gate_other), (up_all, up_other)))
+    ]
+    reduce_w = merge_out(place, [reduce_all], reduce_low, reduce_up)
     act, gate, upper, layer_out, *result_parts = forward_call(
         hidden_parts, *expand_w, reduce_w, hidden, cotangent, post_gain
     )
@@ -1690,102 +2167,57 @@
     g_attn_low = dot_of(d_inner, mixed, 1, 0)
 
     all_sums = sum_row(jnp.stack([jnp.sum(part[:, 0], axis=0) for part in (q_sums, k_sums)]))
-    d_parts, g_low, g_up = [], [], []
-    for index, span in enumerate(spans):
-        scale = scales[index]
-        d_qkv = unrotate_rows(
-            raws[index],
-            d_query,
-            d_key,
-            d_value,
-            scale,
-            scale * scale * all_sums[:, span].T / D,
-            gains,
-            cosine[span],
-            sine[span],
-            index * step,
-        )
-        d_parts.append(d_qkv)
-    d_qkv = join(d_parts)
-    input_grad = input_call(d_qkv, qkv_w, d_hidden)
-    part = [d_qkv[:, i * local : (i + 1) * local] for i in range(3)]
-    qkv_inner = join(qkv_inner, 1)
-    g_qkv_up = [
-        ADAPTER_FACTOR * dot_of(qkv_inner[16 * i : 16 * i + 16], part[i], 1, 0) for i in range(3)
-    ]
-    d_inner = sum_row(
-        ADAPTER_FACTOR * jnp.concatenate([dot_of(qkv_up[i], part[i], 1, 1) for i in range(3)])
-    ).astype(BF)
-    g_qkv_low = dot_of(d_inner, tokens, 1, 0)
-
-    def set_of(other, back):
-        sequence = (pair ^ other) * cols + lax.rem(col - back + cols, cols)
-        which = lax.dynamic_index_in_dim(adapter_set, sequence, 0, keepdims=False)
-        return (jnp.arange(SETS, dtype=jnp.int32) == which).astype(F32)
-
-    def to_sets(terms):
-        shape = (SETS,) + (1,) * terms[0][1].ndim
-        return functools.reduce(
-            jnp.add, [hot.reshape(shape) * term.astype(F32)[None] for hot, term in terms]
-        )
-
-    def sum_groups(pack):
-        pack = pack.astype(BF)
-        both = jnp.stack([pack, swap_pair(pack)])
-        terms = []
-        for back, arrived in enumerate(round_col(both, cols)):
-            terms += [(set_of(other, back), arrived[other]) for other in range(2)]
-        return to_sets(terms)
-
-    early = sum_groups(jnp.concatenate([g_attn_up, g_expand_low, g_reduce_up], axis=0))
-    late = sum_groups(g_qkv_low)
+    qkv_inner = low_of_parts(qkv_low, token_parts).astype(BF)
+    input_grad, g_qkv_low, g_qkv_up = input_call(
+        raw,
+        d_query,
+        d_key,
+        d_value,
+        qkv_w,
+        d_hidden,
+        scale.T,
+        (scale * scale * all_sums / D).T,
+        gains,
+        cosine,
+        sine,
+        tokens,
+        qkv_inner,
+        qkv_up,
+    )
 
     def by_col(grad):
         return grad.reshape(16, cols, -1).transpose(1, 0, 2)
 
-    def sum_tokens(pack):
-        dealt = lax.all_to_all(pack.astype(BF), "col", split_axis=0, concat_axis=0, tiled=True)
-        every = jnp.stack(gather_row(dealt))
-        other = swap_pair(every)
-        terms = []
-        for which in range(2):
-            for index in range(cols):
-                sequence = (pair ^ which) * cols + index
-                chosen = lax.dynamic_index_in_dim(adapter_set, sequence, 0, keepdims=False)
-                hot = (jnp.arange(SETS, dtype=jnp.int32) == chosen).astype(F32)
-                terms.append((hot, (every, other)[which][:, index]))
-        total = to_sets(terms)
-        total = jnp.stack(
-            [lax.dynamic_index_in_dim(total, me ^ row, 1, keepdims=False) for row in range(4)],
-            axis=2,
-        )
-        return total
-
-    early_col = sum_tokens(
-        jnp.concatenate(
-            [by_col(grad) for grad in (g_attn_low, g_gate_up, g_upper_up, g_reduce_low)],
-            axis=2,
-        )
-    )
-    late_col = sum_tokens(jnp.concatenate([by_col(grad) for grad in g_qkv_up], axis=2))
-
-    def low_of(array):
-        return array.transpose(0, 2, 1)
-
-    def piece_of(array, at, size):
-        return array[:, :, :, at : at + size].reshape(SETS, 16, 4 * size)
-
+    row_pack = jnp.concatenate([g_qkv_low, g_attn_up, g_expand_low, g_reduce_up], axis=0)
+    col_pack = jnp.concatenate(
+        [
+            by_col(grad)
+            for grad in (g_qkv_up[:16], g_qkv_up[16:32], g_qkv_up[32:], g_attn_low, g_gate_up, g_upper_up, g_reduce_low)
+        ],
+        axis=2,
+    )
+    every_row, every_col = groups_call(row_pack.astype(BF), col_pack.astype(BF))
+    row_ids = [
+        adapter_set[(pair ^ other) * cols + lax.rem(col - k + cols, cols)]
+        for k in range(cols)
+        for other in range(2)
+    ]
+    col_ids = [adapter_set[(pair ^ other) * cols + index] for other in range(2) for index in range(cols)]
+    ids = jnp.stack(row_ids + col_ids + [me])
+    qkv_low, qkv_up, attn_low, attn_up, expand_low, expand_up, reduce_low, reduce_up = finish_call(
+        ids, every_row, every_col, sub, ff_sub
+    )
     return (
         layer_out,
         input_grad,
-        jnp.stack([low_of(late[:, 16 * i : 16 * i + 16]) for i in range(3)]),
-        jnp.stack([piece_of(late_col, i * sub, sub) for i in range(3)]),
-        low_of(piece_of(early_col, 0, sub)),
-        early[:, :16],
-        jnp.stack([low_of(early[:, 16 + 16 * i : 32 + 16 * i]) for i in range(2)]),
-        jnp.stack([piece_of(early_col, sub + i * ff_sub, ff_sub) for i in range(2)]),
-        low_of(piece_of(early_col, sub + 2 * ff_sub, ff_sub)),
-        early[:, 48:64],
+        qkv_low.transpose(0, 1, 3, 2),
+        qkv_up,
+        attn_low.transpose(0, 2, 1),
+        attn_up,
+        expand_low.transpose(0, 1, 3, 2),
+        expand_up,
+        reduce_low.transpose(0, 2, 1),
+        reduce_up,
     )
 
 

time: 1140 us -> 1040 us (0.912)
  Pallas kernels: 646 us -> 882 us
  waiting for transfers between devices: 181 us -> 9.85 us
  other arithmetic: 88.3 us -> 23.4 us
  starting transfers between devices: 69.6 us -> 7.23 us
  local copies, waits for them, and re-layouts: 61.4 us -> 30.9 us
    pallas_call x3 -> x7, Pallas kernels: 90.5 us -> 291 us  [the longest x1 84.4 us: second_deal(): pl.pallas_call(second_deal_kernel, out_shape=like_views([wide, (parts, ro...]
    ppermute x51 -> x10, waiting for transfers between devices: 125 us -> 7.76 us  [across(): return lax.ppermute(values, 'row', [(i, i ^ step) for i in range(4)])]
    ppermute x17 -> x0, waiting for transfers between devices: 52.2 us -> none  [the longest x8 37.1 us: swap_pair(): return lax.ppermute(values, 'dp', [(0, 1), (1, 0)])]
    pallas_call x1, Pallas kernels: 108 us -> 146 us  [branch_call(): pl.pallas_call(branch_kernel, out_shape=[whole, whole, jax.ShapeDtypeStru...]
    ppermute x51 -> x10, starting transfers between devices: 32.1 us -> 7.03 us  [across(): return lax.ppermute(values, 'row', [(i, i ^ step) for i in range(4)])]
    another operation x22 -> x2, other arithmetic: 25.7 us -> 2.08 us  [the longest x7 9.89 us: deal_row(): return jnp.stack(out)]
    ppermute x17 -> x0, starting transfers between devices: 23.3 us -> none  [the longest x9 15 us: round_col(): lax.ppermute(values, 'col', shift(k))]
    concatenate x9 -> x2, other arithmetic: 16.9 us -> 0.71 us  [the longest x1 0.67 us: group_shards(): jnp.concatenate([g_qkv_low, g_attn_up, g_expand_low, g_reduce_up], axis=0)]
  transfers between devices with their start and end apart: 76 -> 15, of which waited for: 31 -> 4; matrix products, arithmetic and copies ran while one was open for 17% -> 10% of each run, Pallas kernels for 57% -> 81%
where the time goes in v3:
time: 1040 us; the launch traced here: 1020 us
  Pallas kernels  882 us (85%)
  matrix products  56.6 us (5%)
  local copies, waits for them, and re-layouts  30.9 us (3%)
  other arithmetic  23.4 us (2%)
  between operations  14.7 us (1%)
    pallas_call x1, Pallas kernels, branch_call(): pl.pallas_call(branch_kernel, out_shape=[whole, whole, jax.ShapeDtypeStru...  146 us
    pallas_call x1, Pallas kernels, backward_call(): pl.pallas_call(backward_kernel, out_shape=[wide] * 2 + [jax.ShapeDtypeStr...  129 us
    pallas_call x1, Pallas kernels, forward_call(): pl.pallas_call(forward_kernel, out_shape=[wide] * 3 + [part] * 5, in_spec...  128 us
    pallas_call x1, Pallas kernels, second_deal(): pl.pallas_call(second_deal_kernel, out_shape=like_views([wide, (parts, ro...  84.4 us
    pallas_call x1, Pallas kernels, third_deal(): pl.pallas_call(third_deal_kernel, out_shape=like_views([(reduce_weight.sh...  73.6 us
    pallas_call x1, Pallas kernels, input_call(): pl.pallas_call(input_kernel, out_shape=[jax.ShapeDtypeStruct((rows, width...  69.8 us
    pallas_call x1, Pallas kernels, attend_back(): pl.pallas_call(attend_back_kernel, out_shape=(jax.ShapeDtypeStruct(query....  65.2 us
    dot_general x25, matrix products, dot_of(): lax.dot_general(left, right, (((left_dim,), (right_dim,)), ((), ())), pre...  56.6 us
  transfers between devices with their start and end apart: 15, of which 4 were waited for; matrix products, arithmetic and copies ran while one was open for 10% of the time, Pallas kernels for 81%

profile of v3, /device:TPU:0, one launch (start us, length us, event | category | flops | bytes accessed | tf_op | source)
XLA Modules:
  0.0 1024.8 jit_solution(13064229297732242941)
XLA Ops:
  7.2 15.8 %first_deal.1 = (bf16[4,3,256,128]{3,2,1,0:T(8,128)(2,1)}, bf16[4,64,512]{2,1,0:T(8,128)(2,1)}) custom-call(bf16[3,512,512]{2,1,0:T(8,128)(2,1)} %qkv_ref.4, bf16[512,512]{1,0:T(8,128)(2,1)} %attn_ref.5), custom_call_target="tpu_custom_call" | custom-call | bytes 67108864 | tf_op jit(solution)/shard_map/first_deal/pallas_call | solution.py:1710
  26.9 84.4 %second_deal.1 = (bf16[4,512,256]{2,1,0:T(8,128)(2,1)}, bf16[4,3,256,128]{3,2,1,0:T(8,128)(2,1)}, bf16[4,64,512]{2,1,0:T(8,128)(2,1)}, bf16[4,512,256]{2,1,0:T(8...) custom-call(bf16[3,512,512]{2,1,0:T(8,128)(2,1)} %qkv_ref.4, ...), custom_call_target="tpu_custom_call" | custom-call | bytes 134217728 | tf_op jit(solution)/shard_map/second_deal/pallas_call | solution.py:1770
  112.6 3.6 col_pack.1.pack_ref
  116.9 73.6 %third_deal.1 = (bf16[4,512,512]{2,1,0:T(8,128)(2,1)}, bf16[4,512,256]{2,1,0:T(8,128)(2,1)}, bf16[4,512,256]{2,1,0:T(8,128)(2,1)}, bf16[4,4,3,256,128]{4,3,2,1,0...) custom-call(bf16[2,512,2048]{2,1,0:T(8,128)(2,1)} %expand_ref.5, ...), custom_call_target="tpu_custom_call" | custom-call | bytes 134217728 | tf_op jit(solution)/shard_map/third_deal/pallas_call | solution.py:1892
  197.9 3.7 fusion.15
  203.6 9.4 merge_qkv.1
  213.0 24.0 %project.2.raw_ref.raw_hbm = f32[2048,1536]{1,0:T(8,128)} custom-call(bf16[2048,512]{1,0:T(8,128)(2,1)} %tokens_ref.5, bf16[2048,512]{1,0:T(8,128)(2,1)} %get-tuple-element.81.refs_1_, bf16[2048,512]{1,0:T(8,128)(2,1)} %get-tuple-element.82.refs_2_, bf16[2048,512]{1,0:T(8,128)(2,1)} %get-tuple-element.83.refs_3_, bf16[2048,1536]{1,0:T(8,128)(2,1)} %bitcast.186), custom_call_target="tpu_custom_call" | custom-call | flops 12884901888 | bytes 14680064 | tf_op jit(solution)/shard_map/project/pallas_call | solution.py:926
  237.1 4.1 fusion.1
  247.5 10.7 %stack.40.ids_ref = s32[17]{0:T(128)} concatenate(s32[1]{0:T(128)} %get-tuple-element.183, s32[1]{0:T(128)} %get-tuple-element.182, s32[1]{0:T(128)} %get-tuple-element.181, s32[1]{0:T(128)} %get-tuple-element.180, s32[1]{0:T(128)} %get-tuple-element.179, s32[1]{0:T(128)} %get-tuple-element.178, s32[1]{0:T(128)} %get-tuple-element.177, s32[1]{0:T(128)} %get-tuple-element.176, ...), dimensions={0} | concatenate | bytes 136 | tf_op jit(solution)/shard_map/stack | solution.py:2206
  260.3 8.7 rotate_rows.1
  269.0 36.8 %attend.1 = (bf16[2048,512]{1,0:T(8,128)(2,1)}, f32[4,1,2048]{2,1,0:T(1,128)}) custom-call(s32[1]{0:T(128)} %dynamic_slice.58.prefix_ref, bf16[2048,512]{1,0:T(8,128)(2,1)} %get-tuple-element.95.q_ref, bf16[2048,512]{1,0:T(8,128)(2,1)} %get-tuple-element.96.k_ref, bf16[2048,512]{1,0:T(8,128)(2,1)} %get-tuple-element.97.v_ref), custom_call_target="tpu_custom_call" | custom-call | flops 6442450944 | bytes 8388608 | tf_op jit(solution)/shard_map/attend/pallas_call | solution.py:467
  311.6 7.5 merge_out.2.matrix_ref.refs_4_
  320.2 146.0 %branch.1 = (f32[2048,512]{1,0:T(8,128)}, f32[2048,512]{1,0:T(8,128)}, f32[8,8,256]{2,1,0:T(8,128)}, bf16[2048,512]{1,0:T(8,128)(2,1)}, bf16[2048,512]{1,0:T(8,1...) custom-call(bf16[2048,512]{1,0:T(8,128)(2,1)} %get-tuple-element.98., ...), custom_call_target="tpu_custom_call" | custom-call | flops 4294967296 | bytes 134217728 | tf_op jit(solution)/shard_map/branch/pallas_call | solution.py:1196
  466.2 11.1 %merge_expand.2 = bf16[4,1,512,2048]{3,2,1,0:T(8,128)(2,1)} custom-call(s32[2]{0:T(128)} %pad_add_fusion.pair_ref, bf16[4,4,512,256]{3,2,1,0:T(8,128)(2,1)} %bitcast.176, bf16[4,4,512,256]{3,2,1,0:T(8,128)(2,1)} %get-tuple-element.108.other_ref, bf16[4,1,16,512]{3,2,1,0:T(8,128)(2,1)} %bitcast.201, bf16[16,2048]{1,0:T(8,128)(2,1)} %bitcast.193), custom_call_target="tpu_custom_call" | custom-call | bytes 16777216 | tf_op jit(solution)/shard_map/merge_expand/pallas_call | solution.py:870
  477.3 11.3 %merge_expand.3 = bf16[4,1,512,2048]{3,2,1,0:T(8,128)(2,1)} custom-call(s32[2]{0:T(128)} %pad_add_fusion.pair_ref, bf16[4,4,512,256]{3,2,1,0:T(8,128)(2,1)} %bitcast.178, bf16[4,4,512,256]{3,2,1,0:T(8,128)(2,1)} %get-tuple-element.109.other_ref, bf16[4,1,16,512]{3,2,1,0:T(8,128)(2,1)} %bitcast.200, bf16[16,2048]{1,0:T(8,128)(2,1)} %bitcast.191), custom_call_target="tpu_custom_call" | custom-call | bytes 16777216 | tf_op jit(solution)/shard_map/merge_expand/pallas_call | solution.py:870
  493.3 9.0 merge_out.3.reduce_hbm
  502.3 127.8 %forward.1 = (bf16[2048,2048]{1,0:T(8,128)(2,1)}, bf16[2048,2048]{1,0:T(8,128)(2,1)}, bf16[2048,2048]{1,0:T(8,128)(2,1)}, bf16[2048,512]{1,0:T(8,128)(2,1)}, bf1...) custom-call(bf16[2048,512]{1,0:T(8,128)(2,1)} %get-tuple-element.104., ...), custom_call_target="tpu_custom_call" | custom-call | flops 51539607552 | bytes 134217728 | tf_op jit(solution)/shard_map/forward/pallas_call | solution.py:1334
  630.1 2.9 fusion.37
  633.0 128.8 %backward.1 = (bf16[2048,2048]{1,0:T(8,128)(2,1)}, bf16[2048,2048]{1,0:T(8,128)(2,1)}, f32[2048,512]{1,0:T(8,128)}, bf16[2048,512]{1,0:T(8,128)(2,1)}, bf16[2048...) custom-call(bf16[2048,512]{1,0:T(8,128)(2,1)} %get-tuple-element.113.x0, ...), custom_call_target="tpu_custom_call" | custom-call | flops 51539607552 | bytes 134217728 | tf_op jit(solution)/shard_map/backward/pallas_call | solution.py:1460
  761.9 5.8 fusion.54
  767.7 5.4 fusion.8
  778.5 9.1 project.3.grad_ref
  787.6 65.2 %attend_back.1 = (f32[2048,512]{1,0:T(8,128)}, f32[2048,512]{1,0:T(8,128)}, f32[2048,512]{1,0:T(8,128)}, f32[4,1,2048]{2,1,0:T(1,128)}, f32[4,1,2048]{2,1,0:T(1,128)}) custom-call(s32[1]{0:T(128)} %dynamic_slice.58.prefix_ref, bf16[2048,512]{1,0:T(8,128)(2,1)} %get-tuple-element.95.q_ref, bf16[2048,512]{1,0:T(8,128)(2,1)} %project.3.grad_ref, ...), custom_call_target="tpu_custom_call" | custom-call | flops 15032385536 | bytes 25165824 | tf_op jit(solution)/shard_map/attend_back/pallas_call | solution.py:556
  857.7 2.9 convolution_add_fusion.10
  860.6 2.5 fusion.14
  867.6 5.9 convolution_convert_fusion
  873.5 6.3 fusion.56
  889.5 69.8 %input_grad.1 = (f32[2048,512]{1,0:T(8,128)}, f32[48,512]{1,0:T(8,128)}, f32[48,512]{1,0:T(8,128)}) custom-call(f32[2048,1536]{1,0:T(8,128)} %project.2.raw_ref.raw_hbm, f32[2048,512]{1,0:T(8,128)} %get-tuple-element.126.dq_hbm, f32[2048,512]{1,0:T(8,128)} %get-tuple-element.127.dk_hbm, f32[2048,512]{1,0:T(8,128)} %get-tuple-element.128.dv_hbm, ...), custom_call_target="tpu_custom_call" | custom-call | flops 12884901888 | bytes 67108864 | tf_op jit(solution)/shard_map/input_grad/pallas_call | solution.py:1610
  965.7 3.3 collective-permute-done.9
  969.4 4.4 collective-permute-done.7
  974.9 29.2 %groups.1 = (bf16[4,2,112,512]{3,2,1,0:T(8,128)(2,1)}, bf16[4,2,4,16,2048]{4,3,2,1,0:T(8,128)(2,1)}) custom-call(bf16[112,512]{1,0:T(8,128)(2,1)} %pad_maximum_fusion.3.row_ref, bf16[4,16,2048]{2,1,0:T(8,128)(2,1)} %copy-done.27), custom_call_target="tpu_custom_call" | custom-call | bytes 67108864 | tf_op jit(solution)/shard_map/groups/pallas_call | solution.py:1970
  1004.1 9.0 finish.1
  (190 shorter events, 72.1 us)
Async XLA Ops:
  7.2 16.8 %copy-start.33 = (s32[8]{0:T(128)S(1)}, s32[8]{0:T(128)}, u32[]{:S(2)}) copy-start(s32[8]{0:T(128)} %param.35) | copy-start | bytes 100
  7.2 109.0 %all-gather.13.cloned.1.call-start = ((), (), s32[]{:S(2)}) async-start(), calls=%async_computation.1 | async-start | bytes 1310720 | tf_op jit(solution)/shard_map/all_gather | solution.py:2001
  23.1 93.8 %all-gather.11.cloned.1.call-start = ((), (), s32[]{:S(2)}) async-start(), calls=%async_computation | async-start | bytes 3932160 | tf_op jit(solution)/shard_map/all_gather | solution.py:2001
  23.9 296.3 %all-gather.15.cloned.1.call-start = ((), (), s32[]{:S(2)}) async-start(), calls=%async_computation.2 | async-start | bytes 5242880 | tf_op jit(solution)/shard_map/all_gather | solution.py:2001
  111.3 208.9 %all-gather.17.cloned.1.call-start = ((), (), s32[]{:S(2)}) async-start(), calls=%async_computation.3 | async-start | bytes 5242880 | tf_op jit(solution)/shard_map/all_gather | solution.py:2001
  111.9 381.4 %all-gather.19.cloned.1.call-start = ((), (), s32[]{:S(2)}) async-start(), calls=%async_computation.4 | async-start | bytes 10485760 | tf_op jit(solution)/shard_map/all_gather | solution.py:2001
  241.2 2.0 collective-permute-start
  243.3 15.3 %collective-permute-start.1 = (f32[2,2048]{1,0:T(2,128)S(1)}, f32[2,2048]{1,0:T(2,128)S(1)}, u32[]{:S(2)}, u32[]{:S(2)}) collective-permute-start(f32[2,2048]{1,0:T(2,128)S(1)} %fusion.51), channel_id=1, source_target_pairs={{0,8},{4,12},{8,0},{12,4},{1,9},{5,13},{9,1},{13,5},{2,10},{6,14},... | collective-permute-start | bytes 49160 | tf_op jit(solution)/shard_map/ppermute | solution.py:1992
  259.0 10.0 copy-start.4
  308.1 10.9 %collective-permute-start.4 = (f32[16,2048]{1,0:T(8,128)S(1)}, f32[16,2048]{1,0:T(8,128)S(1)}, u32[]{:S(2)}, u32[]{:S(2)}) collective-permute-start(f32[16,2048]{1,0:T(8,128)S(1)} %fusion.34), channel_id=1, source_target_pairs={{0,4},{4,0},{8,12},{12,8},{1,5},{5,1},{9,13},{13,9},{2,6},{6,2},{1... | collective-permute-start | bytes 393224 | tf_op jit(solution)/shard_map/ppermute | solution.py:1992
  319.7 563.7 %collective-permute-start.5 = (f32[16,2048]{1,0:T(8,128)}, f32[16,2048]{1,0:T(8,128)}, u32[]{:S(2)}, u32[]{:S(2)}) collective-permute-start(f32[16,2048]{1,0:T(8,128)} %add.253), channel_id=1, source_target_pairs={{0,8},{4,12},{8,0},{12,4},{1,9},{5,13},{9,1},{13,5},{2,10},{6,14},... | collective-permute-start | bytes 393224 | tf_op jit(solution)/shard_map/ppermute | solution.py:1992
  477.3 11.3 %copy-start.6 = (bf16[2048,512]{1,0:T(8,128)(2,1)S(1)}, bf16[2048,512]{1,0:T(8,128)(2,1)}, u32[]{:S(2)}) copy-start(bf16[2048,512]{1,0:T(8,128)(2,1)} %get-tuple-element.104.x0) | copy-start | bytes 6291460
  633.0 128.8 %copy-start.26 = (bf16[4,2,8,512]{3,2,0,1:T(8,128)(2,1)S(1)}, bf16[4,2,8,512]{3,2,0,1:T(8,128)(2,1)}, u32[]{:S(2)}) copy-start(bf16[4,2,8,512]{3,2,0,1:T(8,128)(2,1)} %copy.121) | copy-start | bytes 196612
  761.9 11.2 %slice-start = ((s8[8388608]{0:T(1024)(128)(4,1)}), s8[4194304]{0:T(1024)(128)(4,1)S(1)}, s32[]{:S(2)}) async-start(s8[8388608]{0:T(1024)(128)(4,1)} %bitcast.173), calls=%async_computation.5 | async-start | bytes 8388608
  767.7 5.4 slice-start.1
  854.4 26.6 %collective-permute-start.2 = (f32[2,2048]{1,0:T(2,128)S(1)}, f32[2,2048]{1,0:T(2,128)S(1)}, u32[]{:S(2)}, u32[]{:S(2)}) collective-permute-start(f32[2,2048]{1,0:T(2,128)S(1)} %pad_maximum_fusion.9), channel_id=1, source_target_pairs={{0,4},{4,0},{8,12},{12,8},{1,5},{5,1},{9,13},{13,9},{2,6},{6,2},{1... | collective-permute-start | bytes 49160 | tf_op jit(solution)/shard_map/ppermute | solution.py:1992
  855.3 5.3 copy-start
  867.6 5.9 copy-start.28
  879.8 81.7 %collective-permute-start.8 = (f32[16,2048]{1,0:T(8,128)}, f32[16,2048]{1,0:T(8,128)}, u32[]{:S(2)}, u32[]{:S(2)}) collective-permute-start(f32[16,2048]{1,0:T(8,128)} %fusion.56), channel_id=1, source_target_pairs={{0,4},{4,0},{8,12},{12,8},{1,5},{5,1},{9,13},{13,9},{2,6},{6,2},{1... | collective-permute-start | bytes 393224 | tf_op jit(solution)/shard_map/ppermute | solution.py:1992
  880.6 82.9 %collective-permute-start.6 = (f32[32,2048]{1,0:T(8,128)}, f32[32,2048]{1,0:T(8,128)}, u32[]{:S(2)}, u32[]{:S(2)}) collective-permute-start(f32[32,2048]{1,0:T(8,128)} %maximum_multiply_fusion), channel_id=1, source_target_pairs={{0,4},{4,0},{8,12},{12,8},{1,5},{5,1},{9,13},{13,9},{2,6},{6,2},{1... | collective-permute-start | bytes 786440 | tf_op jit(solution)/shard_map/ppermute | solution.py:1992
  881.5 5.5 copy-start.3
  881.5 5.5 copy-start.5
  881.9 3.8 collective-permute-start.3
  889.5 70.9 %copy-start.30 = (bf16[16,2048]{1,0:T(8,128)(2,1)S(1)}, bf16[16,2048]{1,0:T(8,128)(2,1)}, u32[]{:S(2)}) copy-start(bf16[16,2048]{1,0:T(8,128)(2,1)} %fusion.8) | copy-start | bytes 196612
  889.5 70.9 %copy-start.29 = (bf16[16,2048]{1,0:T(8,128)(2,1)S(1)}, bf16[16,2048]{1,0:T(8,128)(2,1)}, u32[]{:S(2)}) copy-start(bf16[16,2048]{1,0:T(8,128)(2,1)} %fusion.9) | copy-start | bytes 196612
  889.5 72.0 %copy-start.31 = (bf16[16,2048]{1,0:T(8,128)(2,1)S(1)}, bf16[16,2048]{1,0:T(8,128)(2,1)}, u32[]{:S(2)}) copy-start(bf16[16,2048]{1,0:T(8,128)(2,1)} %convolution_convert_fusion) | copy-start | bytes 196612
  959.2 9.8 copy-start.8
  960.3 13.5 %copy-start.7 = (bf16[2048,512]{1,0:T(8,128)(2,1)S(1)}, bf16[2048,512]{1,0:T(8,128)(2,1)}, u32[]{:S(2)}) copy-start(bf16[2048,512]{1,0:T(8,128)(2,1)} %get-tuple-element.104.x0) | copy-start | bytes 6291460
  961.5 12.8 %copy-start.27 = (bf16[4,16,2048]{2,1,0:T(8,128)(2,1)}, bf16[4,16,2048]{2,1,0:T(8,128)(2,1)S(1)}, u32[]{:S(2)}) copy-start(bf16[4,16,2048]{2,1,0:T(8,128)(2,1)S(1)} %fusion.17.col_ref) | copy-start | bytes 786436
  962.6 6.4 collective-permute-start.9
  964.5 9.3 collective-permute-start.7
  1004.1 9.0 copy-start.14
  (22 other events, 49.4 us)
Sparse Core Ops, SparseCore 0:
  23.2 29.0 all-gather.12
  53.9 62.9 all-gather.10
  118.5 79.3 all-gather.14
  199.4 79.2 all-gather.16
  280.1 148.1 all-gather.18

commit v4 on v3

--- a/solution.py
+++ b/solution.py
@@ -415,6 +415,7 @@
 LOG2E = 1.4426950408889634
 Q_BLOCK = 512
 K_BLOCK = 512
+HEADS_AT_ONCE = 2
 BF = jnp.bfloat16
 F32 = jnp.float32
 
@@ -425,25 +426,20 @@
     )
 
 
-def attend_kernel(prefix_ref, q_ref, k_ref, v_ref, out_ref, log_ref, *, first):
-    rows = q_ref.shape[0]
-    start = first + pl.program_id(1) * rows
-    prefix = prefix_ref[0]
-    blocks = lax.div(jnp.maximum(start + rows, prefix) + K_BLOCK - 1, K_BLOCK)
-    query = q_ref[...]
-    limit = jnp.maximum(lax.broadcasted_iota(jnp.int32, (1, rows), 1) + start, prefix - 1)
+def attend_rows(query, limit, key_of, value_of, blocks):
+    rows = query.shape[0]
     key_pos = lax.broadcasted_iota(jnp.int32, (K_BLOCK, rows), 0)
 
     def body(index, carry):
         top, total, mixed = carry
         at = pl.multiple_of(index * K_BLOCK, K_BLOCK)
-        scores = dot_of(k_ref[pl.ds(at, K_BLOCK), :], query, 1, 1) * (HEAD**-0.5 * LOG2E)
+        scores = dot_of(key_of(at), query, 1, 1) * (HEAD**-0.5 * LOG2E)
         scores = jnp.where(key_pos <= limit - at, scores, NEG)
         top_now = jnp.maximum(top, jnp.max(scores, axis=0, keepdims=True))
         fade = jnp.exp2(top - top_now)
         powers = jnp.exp2(scores - top_now)
         total = fade * total + jnp.sum(powers, axis=0, keepdims=True)
-        mixed = mixed * fade + dot_of(v_ref[pl.ds(at, K_BLOCK), :], powers.astype(BF), 0, 0)
+        mixed = mixed * fade + dot_of(value_of(at), powers.astype(BF), 0, 0)
         return top_now, total, mixed
 
     top, total, mixed = lax.fori_loop(
@@ -456,33 +452,7 @@
             jnp.zeros((HEAD, rows), F32),
         ),
     )
-    out_ref[...] = (mixed / total).T.astype(BF)
-    log_ref[0] = top + jnp.log2(total)
-
-
-def attend(prefix, query, key, value, first):
-    rows, length, heads = query.shape[0], key.shape[0], query.shape[1] // HEAD
-    q_spec = pl.BlockSpec((Q_BLOCK, HEAD), lambda h, i, p: (i, h))
-    k_spec = pl.BlockSpec((length, HEAD), lambda h, i, p: (0, h))
-    return pl.pallas_call(
-        functools.partial(attend_kernel, first=first),
-        out_shape=(
-            jax.ShapeDtypeStruct(query.shape, BF),
-            jax.ShapeDtypeStruct((heads, 1, rows), F32),
-        ),
-        grid_spec=pltpu.PrefetchScalarGridSpec(
-            num_scalar_prefetch=1,
-            grid=(heads, rows // Q_BLOCK),
-            in_specs=[q_spec, k_spec, k_spec],
-            out_specs=[q_spec, pl.BlockSpec((1, 1, Q_BLOCK), lambda h, i, p: (h, 0, i))],
-        ),
-        cost_estimate=pl.CostEstimate(
-            flops=3 * rows * length * heads * HEAD,
-            bytes_accessed=8 * rows * heads * HEAD,
-            transcendentals=rows * length * heads,
-        ),
-        name="attend",
-    )(prefix, query, key, value)
+    return mixed / total, top + jnp.log2(total)
 
 
 def row_sums(values):
@@ -519,40 +489,49 @@
         dk_ref[...] = jnp.zeros_like(dk_ref)
         dv_ref[...] = jnp.zeros_like(dv_ref)
 
-    query = q_ref[...]
-    grad = grad_ref[...]
     limit = jnp.maximum(lax.broadcasted_iota(jnp.int32, (1, rows), 1) + start, prefix - 1)
     key_pos = lax.broadcasted_iota(jnp.int32, (K_BLOCK, rows), 0)
-    log_total = log_ref[0]
-    delta = row_sums(grad.astype(F32) * out_ref[...].astype(F32))
-
-    def body(index, d_query):
+    heads = [slice(h * HEAD, (h + 1) * HEAD) for h in range(HEADS_AT_ONCE)]
+    deltas = [
+        row_sums(grad_ref[:, lanes].astype(F32) * out_ref[:, lanes].astype(F32)) for lanes in heads
+    ]
+
+    def body(index, carry):
         at = pl.multiple_of(index * K_BLOCK, K_BLOCK)
         span = pl.ds(at, K_BLOCK)
-        key = k_ref[span, :]
-        scores = dot_of(key, query, 1, 1) * (HEAD**-0.5 * LOG2E)
-        probs = jnp.where(key_pos <= limit - at, jnp.exp2(scores - log_total), 0.0)
-        d_probs = dot_of(v_ref[span, :], grad, 1, 1)
-        d_scores = (probs * (d_probs - delta)).astype(BF)
-        dv_ref[span, :] += dot_of(probs.astype(BF), grad, 1, 0)
-        dk_ref[span, :] += dot_of(d_scores, query, 1, 0)
-        return d_query + dot_of(d_scores, key, 0, 0)
-
-    d_query = lax.fori_loop(0, blocks, body, jnp.zeros((rows, HEAD), F32)) * HEAD**-0.5
-    dq_ref[...] = d_query
-    q_sum_ref[0] = row_sums(d_query * query.astype(F32))
+        seen = key_pos <= limit - at
+        sums = []
+        for h, lanes in enumerate(heads):
+            query, grad, key = q_ref[:, lanes], grad_ref[:, lanes], k_ref[span, lanes]
+            scores = dot_of(key, query, 1, 1) * (HEAD**-0.5 * LOG2E)
+            probs = jnp.where(seen, jnp.exp2(scores - log_ref[h]), 0.0)
+            d_probs = dot_of(v_ref[span, lanes], grad, 1, 1)
+            d_scores = (probs * (d_probs - deltas[h])).astype(BF)
+            dv_ref[span, lanes] += dot_of(probs.astype(BF), grad, 1, 0)
+            dk_ref[span, lanes] += dot_of(d_scores, query, 1, 0)
+            sums.append(carry[h] + dot_of(d_scores, key, 0, 0))
+        return tuple(sums)
+
+    d_queries = lax.fori_loop(0, blocks, body, (jnp.zeros((rows, HEAD), F32),) * len(heads))
+    for h, lanes in enumerate(heads):
+        d_query = d_queries[h] * HEAD**-0.5
+        dq_ref[:, lanes] = d_query
+        q_sum_ref[h] = row_sums(d_query * q_ref[:, lanes].astype(F32))
 
     @pl.when(pl.program_id(1) == pl.num_programs(1) - 1)
     def _():
-        d_key = dk_ref[...] * HEAD**-0.5
-        dk_ref[...] = d_key
-        k_sum_ref[0] = row_sums(d_key * k_ref[...].astype(F32))
+        for h, lanes in enumerate(heads):
+            d_key = dk_ref[:, lanes] * HEAD**-0.5
+            dk_ref[:, lanes] = d_key
+            k_sum_ref[h] = row_sums(d_key * k_ref[:, lanes].astype(F32))
 
 
 def attend_back(prefix, query, grad, mixed, log_total, key, value):
     rows, length, heads = query.shape[0], key.shape[0], query.shape[1] // HEAD
-    q_spec = pl.BlockSpec((Q_BLOCK, HEAD), lambda h, i, p: (i, h))
-    k_spec = pl.BlockSpec((length, HEAD), lambda h, i, p: (0, h))
+    wide = HEADS_AT_ONCE * HEAD
+    q_spec = pl.BlockSpec((Q_BLOCK, wide), lambda h, i, p: (i, h))
+    k_spec = pl.BlockSpec((length, wide), lambda h, i, p: (0, h))
+    row_spec = pl.BlockSpec((HEADS_AT_ONCE, 1, Q_BLOCK), lambda h, i, p: (h, 0, i))
     return pl.pallas_call(
         attend_back_kernel,
         out_shape=(
@@ -564,21 +543,14 @@
         ),
         grid_spec=pltpu.PrefetchScalarGridSpec(
             num_scalar_prefetch=1,
-            grid=(heads, rows // Q_BLOCK),
-            in_specs=[
-                q_spec,
-                q_spec,
-                q_spec,
-                pl.BlockSpec((1, 1, Q_BLOCK), lambda h, i, p: (h, 0, i)),
-                k_spec,
-                k_spec,
-            ],
+            grid=(heads // HEADS_AT_ONCE, rows // Q_BLOCK),
+            in_specs=[q_spec, q_spec, q_spec, row_spec, k_spec, k_spec],
             out_specs=[
                 q_spec,
                 k_spec,
                 k_spec,
-                pl.BlockSpec((1, 1, Q_BLOCK), lambda h, i, p: (h, 0, i)),
-                pl.BlockSpec((1, 1, length), lambda h, i, p: (h, 0, 0)),
+                row_spec,
+                pl.BlockSpec((HEADS_AT_ONCE, 1, length), lambda h, i, p: (h, 0, 0)),
             ],
         ),
         cost_estimate=pl.CostEstimate(
@@ -594,8 +566,9 @@
     width = q_ref.shape[1]
     cosine = cos_ref[...]
     sine = sin_ref[...]
+    scales = scale_ref[...]
     for part, out in ((0, q_ref), (1, k_ref)):
-        scale = scale_ref[:, part : part + 1]
+        scale = column_of(scales, part)
         for at in range(0, width, HEAD):
             normed = raw_ref[:, part * width + at : part * width + at + HEAD] * scale
             normed = normed * gain_ref[part : part + 1, at : at + HEAD]
@@ -615,7 +588,7 @@
         grid=(rows // step,),
         in_specs=[
             pl.BlockSpec((step, 3 * width), lambda i: (i, 0)),
-            pl.BlockSpec((step, 2), lambda i: (i, 0)),
+            pl.BlockSpec((8, step), lambda i: (0, i)),
             pl.BlockSpec((2, width), lambda i: (0, 0)),
             table,
             table,
@@ -911,28 +884,35 @@
     )(pair, *pieces, low.reshape(16, takes * cols, rows).transpose(1, 0, 2), up)
 
 
-def project_kernel(*refs, right_dim):
-    *lefts, matrix, out = refs
-    left = jnp.concatenate([ref[...] for ref in lefts], axis=1)
-    out[...] = dot_of(left, matrix[...], 1, right_dim).astype(out.dtype)
-
-
-def project(lefts, matrix, right_dim, out_type):
-    rows, depth = lefts[0].shape[0], matrix.shape[right_dim]
-    wide = matrix.shape[1 - right_dim]
-    tile, cut = row_tile(rows), min(512, wide)
-    shape = (depth, cut) if right_dim == 0 else (cut, depth)
-    place = (lambda n, m: (0, n)) if right_dim == 0 else (lambda n, m: (n, 0))
+def mixed_back_kernel(x0, x1, x2, x3, matrix_ref, up_ref, out_ref, inner_ref):
+    left = jnp.concatenate([x0[...], x1[...], x2[...], x3[...]], axis=1)
+    out_ref[...] = dot_of(left, matrix_ref[...], 1, 1).astype(BF)
+    inner_ref[...] = (ADAPTER_FACTOR * dot_of(up_ref[...], left, 1, 1)).astype(BF)
+
+
+def mixed_back(lefts, matrix, up):
+    rows, width = lefts[0].shape
+    local = matrix.shape[0]
+    tile = row_tile(rows)
+
+    def whole(array):
+        return pl.BlockSpec(array.shape, lambda m: (0, 0))
+
     return pl.pallas_call(
-        functools.partial(project_kernel, right_dim=right_dim),
-        out_shape=jax.ShapeDtypeStruct((rows, wide), out_type),
-        grid=(wide // cut, rows // tile),
-        in_specs=[pl.BlockSpec((tile, left.shape[1]), lambda n, m: (m, 0)) for left in lefts]
-        + [pl.BlockSpec(shape, place)],
-        out_specs=pl.BlockSpec((tile, cut), lambda n, m: (m, n)),
-        cost_estimate=cost_of(2 * rows * depth * wide, 2 * (rows * depth + depth * wide)),
-        name="project",
-    )(*lefts, matrix)
+        mixed_back_kernel,
+        out_shape=[
+            jax.ShapeDtypeStruct((rows, local), BF),
+            jax.ShapeDtypeStruct((16, rows), BF),
+        ],
+        grid=(rows // tile,),
+        in_specs=[pl.BlockSpec((tile, width), lambda m: (m, 0))] * 4 + [whole(matrix), whole(up)],
+        out_specs=[
+            pl.BlockSpec((tile, local), lambda m: (m, 0)),
+            pl.BlockSpec((16, tile), lambda m: (0, m)),
+        ],
+        cost_estimate=cost_of(8 * rows * width * local, 8 * width * (rows + local)),
+        name="mixed_back",
+    )(*lefts, matrix, up)
 
 
 BLOCK = 256
@@ -1129,14 +1109,19 @@
 
 
 def branch_kernel(
-    mixed_ref,
+    q_ref,
+    k_ref,
+    v_ref,
+    limit_ref,
     matrix_ref,
     tokens_ref,
     gain_ref,
     gate_all,
-    gate_rest,
+    gate_part,
     upper_all,
     upper_rest,
+    mixed_ref,
+    log_ref,
     branch_ref,
     hidden_ref,
     stat_ref,
@@ -1148,15 +1133,38 @@
     width = own_ref.shape[1]
     count = own_ref.shape[0] // BLOCK
     greet_all([peer(step) for step in (1, 2, 3)] + [other_of_pair()])
-    swaps = []
-    for index, (whole, rest_half) in enumerate(((gate_all, gate_rest), (upper_all, upper_rest))):
-        swaps += exchange_halves(
-            whole, rest_half, halves[index], swap_sems.at[index], local_sem.at[index]
-        )
+    later = range(2, gate_all.shape[0])
+    swaps = exchange_halves(
+        gate_all, None, halves[0], swap_sems.at[0], local_sem.at[0], later
+    )
+    swaps += exchange_halves(upper_all, upper_rest, halves[1], swap_sems.at[1], local_sem.at[1])
     for copy in swaps:
         copy.start()
 
+    heads = log_ref.shape[0]
+
+    def attend(group):
+        rows = span_of(group, Q_BLOCK)
+        reach = jnp.maximum((group + 1) * Q_BLOCK, SEQUENCE_LENGTH // 2)
+
+        def head(h, carry):
+            lanes = span_of(h, HEAD)
+            mixed, logs = attend_rows(
+                q_ref[rows, lanes],
+                limit_ref[:, rows],
+                lambda at: k_ref[pl.ds(at, K_BLOCK), lanes],
+                lambda at: v_ref[pl.ds(at, K_BLOCK), lanes],
+                reach // K_BLOCK,
+            )
+            mixed_ref[rows, lanes] = mixed.T.astype(BF)
+            log_ref[h, :, rows] = logs
+            return carry
+
+        lax.fori_loop(0, heads, head, 0)
+
     def compute(c, put):
+        ratio = Q_BLOCK // BLOCK
+        pl.when(lax.rem(c, ratio) == 0)(lambda: attend(c // ratio))
         left = mixed_ref[pl.ds(pl.multiple_of(c * BLOCK, BLOCK), BLOCK), :]
         for block in (1, 3, 2, 0):
             put(block, dot_of(left, matrix_ref[:, block * width : (block + 1) * width], 1, 0))
@@ -1186,8 +1194,9 @@
     )
 
 
-def branch_call(mixed, matrix, tokens, gain, halves):
+def branch_call(query, key, value, limit, matrix, tokens, gain, halves):
     rows, width = tokens.shape
+    local = query.shape[1]
     count = rows // BLOCK
     cols = halves[0].shape[0]
     part = jax.ShapeDtypeStruct((rows, width), BF)
@@ -1195,20 +1204,27 @@
     half = jax.ShapeDtypeStruct(halves[0].shape, BF)
     return pl.pallas_call(
         branch_kernel,
-        out_shape=[whole, whole, jax.ShapeDtypeStruct((count, 8, BLOCK), F32)]
+        out_shape=[
+            jax.ShapeDtypeStruct((rows, local), BF),
+            jax.ShapeDtypeStruct((local // HEAD, 1, rows), F32),
+            whole,
+            whole,
+            jax.ShapeDtypeStruct((count, 8, BLOCK), F32),
+        ]
         + [part] * 4
         + [half] * 2,
-        in_specs=[VMEM_SPEC] * 4 + [ANY_SPEC] * 4,
-        out_specs=[VMEM_SPEC] * 4 + [ANY_SPEC] * 5,
+        in_specs=[VMEM_SPEC] * 7 + [ANY_SPEC] * 4,
+        out_specs=[VMEM_SPEC] * 6 + [ANY_SPEC] * 5,
         scratch_shapes=[
             pltpu.SemaphoreType.DMA((2, 2, cols - 1)),
             pltpu.SemaphoreType.DMA((2,)),
         ]
         + exchange_scratch(count, width, True),
+        input_output_aliases={8: 9},
         compiler_params=talk_params(0),
         cost_estimate=cost_of(8 * rows * width * matrix.shape[0], 2**27),
         name="branch",
-    )(mixed, matrix, tokens, gain, *halves)
+    )(query, key, value, limit, matrix, tokens, gain, *halves)
 
 
 def load_lefts(lefts, buffer, sems, count):
@@ -1249,14 +1265,34 @@
     return copy
 
 
-def forward_kernel(x0, x1, x2, x3, gate_hbm, upper_hbm, reduce_hbm, hidden_ref, cot_ref, gain_ref, *rest):
-    act_out, gate_out, upper_out, layer_ref, own_ref, *rest = rest
+def forward_kernel(
+    x0,
+    x1,
+    x2,
+    x3,
+    gate_hbm,
+    upper_hbm,
+    reduce_hbm,
+    hidden_ref,
+    cot_ref,
+    gain_ref,
+    expand_low_ref,
+    reduce_low_ref,
+    act_out,
+    gate_out,
+    upper_out,
+    layer_ref,
+    expand_inner_ref,
+    reduce_inner_ref,
+    own_ref,
+    *rest,
+):
     arrived, rest = rest[:3], rest[3:]
     gate_w, upper_w, reduce_w, lefts, act_buf, gate_buf, upper_buf, w_sem, x_sem, o_sem, *bufs = rest
     width = own_ref.shape[1]
     count = own_ref.shape[0] // BLOCK
     ff = gate_w.shape[1]
-    tile = 512
+    tile = min(1024, ff)
     loads = [
         pltpu.make_async_copy(source, target, w_sem.at[index])
         for index, (source, target) in enumerate(
@@ -1282,8 +1318,8 @@
 
         @pl.when(c == 0)
         def _():
-            for load in loads:
-                load.wait()
+            loads[0].wait()
+            loads[1].wait()
 
         @pl.when(c >= 2)
         def _():
@@ -1303,9 +1339,17 @@
         lax.fori_loop(0, ff // tile, tiles, 0)
         for out in outs:
             out(c).start()
+
+        @pl.when(c == 0)
+        def _():
+            loads[2].wait()
+
         for block in (1, 3, 2, 0):
             span = slice(block * width, (block + 1) * width)
             put(block, dot_of(act_buf[slot], reduce_w[:, span], 1, 0))
+        rows = span_of(c, BLOCK)
+        expand_inner_ref[:, rows] = dot_of(expand_low_ref[...], lefts[slot], 1, 1).astype(BF)
+        reduce_inner_ref[:, rows] = dot_of(reduce_low_ref[...], act_buf[slot], 1, 1)
 
     def stats(c, rows, result):
         weighted = gain_ref[1:2, :] * cot_ref[rows, :].astype(F32)
@@ -1325,7 +1369,7 @@
             out(c).wait()
 
 
-def forward_call(lefts, gate_w, upper_w, reduce_w, hidden, cotangent, gain):
+def forward_call(lefts, gate_w, upper_w, reduce_w, hidden, cotangent, gain, low, reduce_low):
     rows, width = hidden.shape
     count = rows // BLOCK
     ff = gate_w.shape[1]
@@ -1333,9 +1377,15 @@
     wide = jax.ShapeDtypeStruct((rows, ff), BF)
     return pl.pallas_call(
         forward_kernel,
-        out_shape=[wide] * 3 + [part] * 5,
-        in_specs=[ANY_SPEC] * 7 + [VMEM_SPEC] * 3,
-        out_specs=[ANY_SPEC] * 3 + [VMEM_SPEC] * 2 + [ANY_SPEC] * 3,
+        out_shape=[wide] * 3
+        + [
+            part,
+            jax.ShapeDtypeStruct((32, rows), BF),
+            jax.ShapeDtypeStruct((16, rows), F32),
+        ]
+        + [part] * 4,
+        in_specs=[ANY_SPEC] * 7 + [VMEM_SPEC] * 5,
+        out_specs=[ANY_SPEC] * 3 + [VMEM_SPEC] * 4 + [ANY_SPEC] * 3,
         scratch_shapes=[
             pltpu.VMEM(gate_w.shape, BF),
             pltpu.VMEM(upper_w.shape, BF),
@@ -1352,20 +1402,41 @@
         compiler_params=talk_params(1),
         cost_estimate=cost_of(24 * rows * width * ff, 2**27),
         name="forward",
-    )(*lefts, gate_w, upper_w, reduce_w, hidden, cotangent, gain)
+    )(*lefts, gate_w, upper_w, reduce_w, hidden, cotangent, gain, low, reduce_low)
 
 
 def backward_kernel(
-    x0, x1, x2, x3, gate_hbm, upper_hbm, reduce_hbm, gate_in, upper_in, cot_ref, branch_ref, stat_ref, gain_ref, *rest
+    x0,
+    x1,
+    x2,
+    x3,
+    gate_hbm,
+    upper_hbm,
+    reduce_hbm,
+    gate_in,
+    upper_in,
+    cot_ref,
+    branch_ref,
+    stat_ref,
+    gain_ref,
+    reduce_up_ref,
+    expand_up_ref,
+    expand_inner_ref,
+    d_hidden_ref,
+    reduce_inner_ref,
+    d_inner_ref,
+    up_grad_ref,
+    own_ref,
+    *rest,
 ):
-    d_gate_out, d_upper_out, d_hidden_ref, own_ref, *rest = rest
     arrived, rest = rest[:3], rest[3:]
     gate_w, upper_w, reduce_w, lefts, gate_buf, upper_buf, d_gate_buf, d_upper_buf, *rest = rest
-    w_sem, x_sem, i_sem, o_sem, *bufs = rest
+    w_sem, x_sem, i_sem, *bufs = rest
     width = own_ref.shape[1]
     count = own_ref.shape[0] // BLOCK
     ff = gate_w.shape[1]
-    tile = 512
+    up_grad_ref[...] = jnp.zeros_like(up_grad_ref)
+    tile = min(1024, ff)
     loads = [
         pltpu.make_async_copy(source, target, w_sem.at[index])
         for index, (source, target) in enumerate(
@@ -1377,12 +1448,6 @@
         move_rows(outer, buffer, i_sem, index, True)
         for index, (outer, buffer) in enumerate(((gate_in, gate_buf), (upper_in, upper_buf)))
     ]
-    outs = [
-        move_rows(outer, buffer, o_sem, index, False)
-        for index, (outer, buffer) in enumerate(
-            ((d_gate_out, d_gate_buf), (d_upper_out, d_upper_buf))
-        )
-    ]
     start_left(0)
     for one in ins:
         one(0).start()
@@ -1404,13 +1469,7 @@
 
         @pl.when(c == 0)
         def _():
-            for load in loads:
-                load.wait()
-
-        @pl.when(c >= 2)
-        def _():
-            for out in outs:
-                out(c - 2).wait()
+            loads[0].wait()
 
         def tiles(n, carry):
             at = pl.ds(pl.multiple_of(n * tile, tile), tile)
@@ -1418,19 +1477,31 @@
             gate = gate_buf[slot, :, at].astype(F32)
             sigma = jax.nn.sigmoid(gate)
             d_gate = d_act * upper_buf[slot, :, at].astype(F32) * (sigma * (1 + gate * (1 - sigma)))
-            d_gate_buf[slot, :, at] = d_gate.astype(BF)
-            d_upper_buf[slot, :, at] = (d_act * (gate * sigma)).astype(BF)
+            d_gate_buf[:, at] = d_gate.astype(BF)
+            d_upper_buf[:, at] = (d_act * (gate * sigma)).astype(BF)
             return carry
 
         lax.fori_loop(0, ff // tile, tiles, 0)
-        for out in outs:
-            out(c).start()
+        @pl.when(c == 0)
+        def _():
+            loads[1].wait()
+            loads[2].wait()
+
         for block in (1, 3, 2, 0):
             span = slice(block * width, (block + 1) * width)
             put(
                 block,
-                dot_of(d_gate_buf[slot], gate_w[span, :], 1, 1)
-                + dot_of(d_upper_buf[slot], upper_w[span, :], 1, 1),
+                dot_of(d_gate_buf[...], gate_w[span, :], 1, 1)
+                + dot_of(d_upper_buf[...], upper_w[span, :], 1, 1),
+            )
+        rows = span_of(c, BLOCK)
+        inner = dot_of(reduce_up_ref[...], lefts[slot], 1, 1)
+        reduce_inner_ref[:, rows] = (ADAPTER_FACTOR * inner).astype(BF)
+        for part, grad in enumerate((d_gate_buf, d_upper_buf)):
+            own = slice(16 * part, 16 * part + 16)
+            d_inner_ref[own, rows] = ADAPTER_FACTOR * dot_of(expand_up_ref[own, :], grad[...], 1, 1)
+            up_grad_ref[own, :] += ADAPTER_FACTOR * dot_of(
+                expand_inner_ref[own, rows], grad[...], 1, 0
             )
 
     def stats(c, rows, total):
@@ -1446,22 +1517,26 @@
         return (scale * weighted - branch_ref[rows, :] * back).astype(BF)
 
     run_blocks(count, bufs, compute, stats, finish, own_ref, arrived)
-    for c in range(max(count - 2, 0), count):
-        for out in outs:
-            out(c).wait()
-
-
-def backward_call(lefts, gate_w, upper_w, reduce_w, gate, upper, cotangent, branch, stats, gain):
+
+
+def backward_call(
+    lefts, gate_w, upper_w, reduce_w, gate, upper, cotangent, branch, stats, gain, *adapters
+):
     rows, width = branch.shape
     count = rows // BLOCK
     ff = gate_w.shape[1]
     part = jax.ShapeDtypeStruct((rows, width), BF)
-    wide = jax.ShapeDtypeStruct((rows, ff), BF)
     return pl.pallas_call(
         backward_kernel,
-        out_shape=[wide] * 2 + [jax.ShapeDtypeStruct((rows, width), F32)] + [part] * 4,
-        in_specs=[ANY_SPEC] * 9 + [VMEM_SPEC] * 4,
-        out_specs=[ANY_SPEC] * 2 + [VMEM_SPEC] * 2 + [ANY_SPEC] * 3,
+        out_shape=[
+            jax.ShapeDtypeStruct((rows, width), F32),
+            jax.ShapeDtypeStruct((16, rows), BF),
+            jax.ShapeDtypeStruct((32, rows), F32),
+            jax.ShapeDtypeStruct((32, ff), F32),
+        ]
+        + [part] * 4,
+        in_specs=[ANY_SPEC] * 9 + [VMEM_SPEC] * 7,
+        out_specs=[VMEM_SPEC] * 5 + [ANY_SPEC] * 3,
         scratch_shapes=[
             pltpu.VMEM(gate_w.shape, BF),
             pltpu.VMEM(upper_w.shape, BF),
@@ -1469,18 +1544,19 @@
             pltpu.VMEM((2, BLOCK, 4 * width), BF),
             pltpu.VMEM((2, BLOCK, ff), BF),
             pltpu.VMEM((2, BLOCK, ff), BF),
-            pltpu.VMEM((2, BLOCK, ff), BF),
-            pltpu.VMEM((2, BLOCK, ff), BF),
+            pltpu.VMEM((BLOCK, ff), BF),
+            pltpu.VMEM((BLOCK, ff), BF),
             pltpu.SemaphoreType.DMA((3,)),
             pltpu.SemaphoreType.DMA((2, 4)),
-            pltpu.SemaphoreType.DMA((2, 2)),
             pltpu.SemaphoreType.DMA((2, 2)),
         ]
         + exchange_scratch(count, width, True),
         compiler_params=talk_params(2),
         cost_estimate=cost_of(24 * rows * width * ff, 2**27),
         name="backward",
-    )(*lefts, gate_w, upper_w, reduce_w, gate, upper, cotangent, branch, stats, gain)
+    )(
+        *lefts, gate_w, upper_w, reduce_w, gate, upper, cotangent, branch, stats, gain, *adapters
+    )
 
 
 def input_kernel(
@@ -1491,7 +1567,8 @@
     matrix_ref,
     d_hidden_ref,
     scale_ref,
-    back_ref,
+    q_sum_ref,
+    k_sum_ref,
     gain_ref,
     cos_ref,
     sin_ref,
@@ -1510,9 +1587,13 @@
     inner_in,
     inner_mid,
     inner_far,
+    sum_own,
+    sum_in,
+    back_ref,
     in_sem,
     core_sem,
     far_sem,
+    sum_sem,
     *bufs,
 ):
     width = out_ref.shape[1]
@@ -1528,7 +1609,20 @@
         one(0).start()
     low_grad_ref[...] = jnp.zeros_like(low_grad_ref)
     up_grad_ref[...] = jnp.zeros_like(up_grad_ref)
+    sum_own[...] = jnp.zeros_like(sum_own)
+    for row, part in enumerate((q_sum_ref, k_sum_ref)):
+        total = part[0]
+        for h in range(1, part.shape[0]):
+            total = total + part[h]
+        sum_own[row : row + 1, :] = total
     greet()
+    exchanges = [send(sum_own, sum_in.at[step - 1], sum_sem, step - 1, step) for step in (1, 2, 3)]
+    for copy in exchanges:
+        copy.start()
+    for copy in exchanges:
+        copy.wait()
+    total = sum_own[...] + sum_in[0] + sum_in[1] + sum_in[2]
+    back_ref[...] = scale_ref[...] * scale_ref[...] * total / D
 
     def inner_core(c):
         return send(inner_out.at[lax.rem(c, 2)], inner_in.at[c], core_sem, c, 1)
@@ -1569,8 +1663,8 @@
         cosine = cos_ref[rows, :]
         sine = sin_ref[rows, :]
         for part, grad in ((0, dq_buf), (1, dk_buf)):
-            scale = scale_ref[rows, part : part + 1]
-            back = back_ref[rows, part : part + 1]
+            scale = column_of(scale_ref[:, rows], part)
+            back = column_of(back_ref[:, rows], part)
             for at in range(0, local, HEAD):
                 turned = grad[slot, :, at : at + HEAD]
                 turned = turned * cosine - pltpu.roll(turned, HEAD // 2, 1) * sine
@@ -1600,7 +1694,7 @@
 
 
 def input_call(
-    raw, d_query, d_key, d_value, matrix, d_hidden, scales, backs, gains, cosine, sine, *adapters
+    raw, d_query, d_key, d_value, matrix, d_hidden, scales, q_sums, k_sums, *others
 ):
     rows, width = d_hidden.shape
     local = d_query.shape[1]
@@ -1614,7 +1708,7 @@
             jax.ShapeDtypeStruct((48, width), F32),
             jax.ShapeDtypeStruct((48, local), F32),
         ],
-        in_specs=[ANY_SPEC] * 4 + [VMEM_SPEC] * 10,
+        in_specs=[ANY_SPEC] * 4 + [VMEM_SPEC] * 11,
         out_specs=[VMEM_SPEC] * 3,
         scratch_shapes=[
             pltpu.VMEM((2, BLOCK, 3 * local), F32),
@@ -1626,15 +1720,19 @@
             pltpu.VMEM((count, 48, BLOCK), F32),
             pltpu.VMEM((2, 48, BLOCK), F32),
             pltpu.VMEM((count, 48, BLOCK), F32),
+            pltpu.VMEM((8, rows), F32),
+            pltpu.VMEM((3, 8, rows), F32),
+            pltpu.VMEM((8, rows), F32),
             pltpu.SemaphoreType.DMA((4, 2)),
             sem,
             sem,
+            pltpu.SemaphoreType.DMA((2, 3)),
         ]
         + exchange_scratch(count, width, False),
         compiler_params=talk_params(3),
         cost_estimate=cost_of(24 * rows * width * local, 2**26),
         name="input_grad",
-    )(raw, d_query, d_key, d_value, matrix, d_hidden, scales, backs, gains, cosine, sine, *adapters)
+    )(raw, d_query, d_key, d_value, matrix, d_hidden, scales, q_sums, k_sums, *others)
 
 
 def deal(items, outs, sems):
@@ -1810,11 +1908,14 @@
     return {"dp": 1 - lax.axis_index("dp")}
 
 
-def exchange_halves(whole, rest, out, sems, local_sem):
+def exchange_halves(whole, rest, out, sems, local_sem, steps=None):
     cols = whole.shape[0]
     col = lax.axis_index("col")
-    copies = [pltpu.make_async_copy(rest, out.at[0], local_sem)]
-    for k in range(1, cols):
+    copies = []
+    for k in range(cols) if steps is None else steps:
+        if k == 0:
+            copies.append(pltpu.make_async_copy(rest, out.at[0], local_sem))
+            continue
         place = lax.rem(col + k, cols)
         copies.append(copy_to(whole.at[place], out.at[k], sems, k - 1, other_of_pair()))
     return copies
@@ -1912,6 +2013,82 @@
         cost_estimate=cost_of(0, 2**27),
         name="third_deal",
     )(expand_weight, reduce_weight, qkv_all, qkv_rest, attn_all, attn_rest, pack, gain)
+
+
+def front_kernel(
+    x0,
+    x1,
+    x2,
+    x3,
+    matrix_ref,
+    low_ref,
+    gate_all,
+    gate_rest,
+    raw_ref,
+    square_ref,
+    inner_ref,
+    gate_out,
+    swap_sem,
+    local_sem,
+):
+    local = raw_ref.shape[1] // 3
+    first = exchange_halves(gate_all, gate_rest, gate_out, swap_sem, local_sem.at[0], range(2))
+
+    @pl.when(pl.program_id(0) == 0)
+    def _():
+        greet_all([other_of_pair()])
+        for copy in first:
+            copy.start()
+
+    left = jnp.concatenate([x0[...], x1[...], x2[...], x3[...]], axis=1)
+    squares = []
+    for part in range(3):
+        lanes = slice(part * local, (part + 1) * local)
+        product = dot_of(left, matrix_ref[:, lanes], 1, 0)
+        raw_ref[:, lanes] = product
+        squares.append(product * product)
+    square_ref[...] = sums_of(*squares[:2])
+    inner_ref[...] = dot_of(low_ref[...], left, 1, 1).astype(BF)
+
+    @pl.when(pl.program_id(0) == pl.num_programs(0) - 1)
+    def _():
+        wait_all(first)
+
+
+def front_call(lefts, matrix, low, gate_all, gate_rest):
+    rows, width = lefts[0].shape
+    wide = matrix.shape[1]
+    tile = row_tile(rows)
+    cols = gate_all.shape[0]
+
+    def whole(array):
+        return pl.BlockSpec(array.shape, lambda m: (0, 0))
+
+    return pl.pallas_call(
+        front_kernel,
+        out_shape=[
+            jax.ShapeDtypeStruct((rows, wide), F32),
+            jax.ShapeDtypeStruct((8, rows), F32),
+            jax.ShapeDtypeStruct((48, rows), BF),
+            jax.ShapeDtypeStruct(gate_all.shape, BF),
+        ],
+        grid=(rows // tile,),
+        in_specs=[pl.BlockSpec((tile, width), lambda m: (m, 0))] * 4
+        + [whole(matrix), whole(low), ANY_SPEC, ANY_SPEC],
+        out_specs=[
+            pl.BlockSpec((tile, wide), lambda m: (m, 0)),
+            pl.BlockSpec((8, tile), lambda m: (0, m)),
+            pl.BlockSpec((48, tile), lambda m: (0, m)),
+            ANY_SPEC,
+        ],
+        scratch_shapes=[
+            pltpu.SemaphoreType.DMA((2, cols - 1)),
+            pltpu.SemaphoreType.DMA((1,)),
+        ],
+        compiler_params=talk_params(8),
+        cost_estimate=cost_of(8 * rows * width * wide, 2**26),
+        name="front",
+    )(*lefts, matrix, low, gate_all, gate_rest)
 
 
 def groups_kernel(row_ref, col_ref, rows_out, cols_out, local_sem, pair_sem, round_sem, deal_sem, row_sem):
@@ -2114,21 +2291,21 @@
     sine = jnp.sin(angle)
     sine = jnp.concatenate([-sine, sine], axis=1)
 
-    def low_of_parts(low, parts):
-        return functools.reduce(
-            jnp.add,
-            [dot_of(low[:, i * width : (i + 1) * width], parts[i], 1, 1) for i in range(4)],
-        )
-
-    raw = project(token_parts, qkv_w, 0, F32)
-    squares = jnp.stack(
-        [jnp.sum(raw[:, i * local : (i + 1) * local] ** 2, axis=1) for i in range(2)]
+    raw, squares, qkv_inner, gate_part = front_call(
+        token_parts, qkv_w, qkv_low, gate_all, gate_rest
     )
     scale = lax.rsqrt(sum_row(squares) / D + EPS)
-    query, key, value = rotate_rows(raw, scale.T, gains, cosine, sine)
-    mixed, log_total = attend(prefix, query, key, value, 0)
-    branch, hidden, branch_stats, *hidden_parts, gate_other, up_other = branch_call(
-        mixed, attn_w, tokens, post_gain, (gate_all, gate_rest, up_all, up_rest)
+    query, key, value = rotate_rows(raw, scale, gains, cosine, sine)
+    limit = jnp.maximum(jnp.arange(rows, dtype=jnp.int32), prefix - 1)[None]
+    mixed, log_total, branch, hidden, branch_stats, *hidden_parts, gate_other, up_other = branch_call(
+        query,
+        key,
+        value,
+        limit,
+        attn_w,
+        tokens,
+        post_gain,
+        (gate_all, gate_part, up_all, up_rest),
     )
     expand_w = [
         merge_expand(
@@ -2137,37 +2314,35 @@
         for i, (whole, other) in enumerate(((gate_all, gate_other), (up_all, up_other)))
     ]
     reduce_w = merge_out(place, [reduce_all], reduce_low, reduce_up)
-    act, gate, upper, layer_out, *result_parts = forward_call(
-        hidden_parts, *expand_w, reduce_w, hidden, cotangent, post_gain
-    )
-    d_gate, d_upper, d_hidden, *branch_parts = backward_call(
-        result_parts, *expand_w, reduce_w, gate, upper, cotangent, branch, branch_stats, post_gain
-    )
-    d_mixed = project(branch_parts, attn_w, 1, BF)
+    act, gate, upper, layer_out, expand_inner, reduce_inner, *result_parts = forward_call(
+        hidden_parts, *expand_w, reduce_w, hidden, cotangent, post_gain, expand_low, reduce_low
+    )
+    d_hidden, d_reduce_inner, d_expand_inner, g_expand_up, *branch_parts = backward_call(
+        result_parts,
+        *expand_w,
+        reduce_w,
+        gate,
+        upper,
+        cotangent,
+        branch,
+        branch_stats,
+        post_gain,
+        reduce_up,
+        jnp.concatenate(expand_up),
+        expand_inner,
+    )
+    d_mixed, d_attn_inner = mixed_back(branch_parts, attn_w, attn_up)
     d_query, d_key, d_value, q_sums, k_sums = attend_back(
         prefix, query, d_mixed, mixed, log_total, key, value
     )
     attn_inner = sum_row(dot_of(attn_low, mixed, 1, 1)).astype(BF)
-    expand_inner = low_of_parts(expand_low, hidden_parts).astype(BF)
-    reduce_inner = sum_row(dot_of(reduce_low, act, 1, 1)).astype(BF)
+    reduce_inner = sum_row(reduce_inner).astype(BF)
+    d_expand_inner = sum_row(d_expand_inner).astype(BF)
     g_reduce_up = ADAPTER_FACTOR * dot_of(reduce_inner, result_parts[0], 1, 0)
-    d_inner = (ADAPTER_FACTOR * low_of_parts(reduce_up, result_parts)).astype(BF)
-    g_reduce_low = dot_of(d_inner, act, 1, 0)
-    g_gate_up = ADAPTER_FACTOR * dot_of(expand_inner[:16], d_gate, 1, 0)
-    g_upper_up = ADAPTER_FACTOR * dot_of(expand_inner[16:], d_upper, 1, 0)
-    d_inner = sum_row(
-        ADAPTER_FACTOR
-        * jnp.concatenate(
-            [dot_of(expand_up[0], d_gate, 1, 1), dot_of(expand_up[1], d_upper, 1, 1)]
-        )
-    ).astype(BF)
-    g_expand_low = dot_of(d_inner, hidden_parts[0], 1, 0)
+    g_reduce_low = dot_of(d_reduce_inner, act, 1, 0)
+    g_expand_low = dot_of(d_expand_inner, hidden_parts[0], 1, 0)
     g_attn_up = ADAPTER_FACTOR * dot_of(attn_inner, branch_parts[0], 1, 0)
-    d_inner = (ADAPTER_FACTOR * low_of_parts(attn_up, branch_parts)).astype(BF)
-    g_attn_low = dot_of(d_inner, mixed, 1, 0)
-
-    all_sums = sum_row(jnp.stack([jnp.sum(part[:, 0], axis=0) for part in (q_sums, k_sums)]))
-    qkv_inner = low_of_parts(qkv_low, token_parts).astype(BF)
+    g_attn_low = dot_of(d_attn_inner, mixed, 1, 0)
     input_grad, g_qkv_low, g_qkv_up = input_call(
         raw,
         d_query,
@@ -2175,8 +2350,9 @@
         d_value,
         qkv_w,
         d_hidden,
-        scale.T,
-        (scale * scale * all_sums / D).T,
+        scale,
+        q_sums,
+        k_sums,
         gains,
         cosine,
         sine,
@@ -2192,18 +2368,26 @@
     col_pack = jnp.concatenate(
         [
             by_col(grad)
-            for grad in (g_qkv_up[:16], g_qkv_up[16:32], g_qkv_up[32:], g_attn_low, g_gate_up, g_upper_up, g_reduce_low)
+            for grad in (
+                g_qkv_up[:16],
+                g_qkv_up[16:32],
+                g_qkv_up[32:],
+                g_attn_low,
+                g_expand_up[:16],
+                g_expand_up[16:],
+                g_reduce_low,
+            )
         ],
         axis=2,
     )
     every_row, every_col = groups_call(row_pack.astype(BF), col_pack.astype(BF))
-    row_ids = [
-        adapter_set[(pair ^ other) * cols + lax.rem(col - k + cols, cols)]
-        for k in range(cols)
-        for other in range(2)
-    ]
-    col_ids = [adapter_set[(pair ^ other) * cols + index] for other in range(2) for index in range(cols)]
-    ids = jnp.stack(row_ids + col_ids + [me])
+    place_of = jnp.arange(2 * cols, dtype=jnp.int32)
+    row_place = (pair ^ (place_of % 2)) * cols + (col - place_of // 2 + cols) % cols
+    col_place = (pair ^ (place_of // cols)) * cols + place_of % cols
+    places = jnp.concatenate([row_place, col_place])
+    chosen = places[:, None] == jnp.arange(2 * cols, dtype=jnp.int32)[None, :]
+    ids = jnp.sum(jnp.where(chosen, adapter_set[None, :], 0), axis=1)
+    ids = jnp.concatenate([ids, me.reshape(1)])
     qkv_low, qkv_up, attn_low, attn_up, expand_low, expand_up, reduce_low, reduce_up = finish_call(
         ids, every_row, every_col, sub, ff_sub
     )

time: 1040 us -> 923 us (0.89)
  matrix products: 56.6 us -> 11.1 us
  Pallas kernels: 882 us -> 841 us
  local copies, waits for them, and re-layouts: 30.9 us -> 12.3 us
    dot_general x25 -> x6, matrix products: 56.6 us -> 11.1 us  [dot_of(): lax.dot_general(left, right, (((left_dim,), (right_dim,)), ((), ())), pre...]
    pallas_call x6 -> x5, Pallas kernels: 473 us -> 431 us  [the longest x1 130 us: backward_call(): pl.pallas_call(backward_kernel, out_shape=[jax.ShapeDtypeStruct((rows, wi...]
    another operation x2 -> x0, local copies, waits for them, and re-layouts: 11.1 us -> none  [the longest x1 10.7 us: group_shards(): ids = jnp.stack(row_ids + col_ids + [me])]
  transfers between devices with their start and end apart: 15 -> 13, of which waited for: 4 -> 5; matrix products, arithmetic and copies ran while one was open for 10% -> 3% of each run, Pallas kernels for 81% -> 86%
where the time goes in v4:
time: 923 us; the launch traced here: 912 us
  Pallas kernels  841 us (91%)
  between operations  15.4 us (2%)
  other arithmetic  14.1 us (2%)
  waiting for transfers between devices  13.3 us (1%)
  local copies, waits for them, and re-layouts  12.3 us (1%)
  matrix products  11.1 us (1%)
    pallas_call x1, Pallas kernels, backward_call(): pl.pallas_call(backward_kernel, out_shape=[jax.ShapeDtypeStruct((rows, wi...  130 us
    pallas_call x1, Pallas kernels, branch_call(): pl.pallas_call(branch_kernel, out_shape=[jax.ShapeDtypeStruct((rows, loca...  127 us
    pallas_call x1, Pallas kernels, forward_call(): pl.pallas_call(forward_kernel, out_shape=[wide] * 3 + [part, jax.ShapeDty...  125 us
    pallas_call x1, Pallas kernels, second_deal(): pl.pallas_call(second_deal_kernel, out_shape=like_views([wide, (parts, ro...  84.4 us
    pallas_call x1, Pallas kernels, input_call(): pl.pallas_call(input_kernel, out_shape=[jax.ShapeDtypeStruct((rows, width...  73.7 us
    pallas_call x1, Pallas kernels, third_deal(): pl.pallas_call(third_deal_kernel, out_shape=like_views([(reduce_weight.sh...  73.4 us
    pallas_call x1, Pallas kernels, attend_back(): pl.pallas_call(attend_back_kernel, out_shape=(jax.ShapeDtypeStruct(query....  59.6 us
    pallas_call x1, Pallas kernels, front_call(): pl.pallas_call(front_kernel, out_shape=[jax.ShapeDtypeStruct((rows, wide)...  38.9 us
  transfers between devices with their start and end apart: 13, of which 5 were waited for; matrix products, arithmetic and copies ran while one was open for 3% of the time, Pallas kernels for 86%

profile of v4, /device:TPU:0, one launch (start us, length us, event | category | flops | bytes accessed | tf_op | source)
XLA Modules:
  0.0 911.9 jit_solution(11601037804443890575)
XLA Ops:
  7.2 15.8 %first_deal.1 = (bf16[4,3,256,128]{3,2,1,0:T(8,128)(2,1)}, bf16[4,64,512]{2,1,0:T(8,128)(2,1)}) custom-call(bf16[3,512,512]{2,1,0:T(8,128)(2,1)} %qkv_ref.4, bf16[512,512]{1,0:T(8,128)(2,1)} %attn_ref.5), custom_call_target="tpu_custom_call" | custom-call | bytes 67108864 | tf_op jit(solution)/shard_map/first_deal/pallas_call | solution.py:1808
  24.5 2.1 row_pack.1.pack_ref
  26.6 84.4 %second_deal.1 = (bf16[4,512,256]{2,1,0:T(8,128)(2,1)}, bf16[4,3,256,128]{3,2,1,0:T(8,128)(2,1)}, bf16[4,64,512]{2,1,0:T(8,128)(2,1)}, bf16[4,512,256]{2,1,0:T(8...) custom-call(bf16[3,512,512]{2,1,0:T(8,128)(2,1)} %qkv_ref.4, ...), custom_call_target="tpu_custom_call" | custom-call | bytes 134217728 | tf_op jit(solution)/shard_map/second_deal/pallas_call | solution.py:1868
  112.3 3.6 col_pack.1.pack_ref
  116.9 73.4 %third_deal.1 = (bf16[4,512,512]{2,1,0:T(8,128)(2,1)}, bf16[4,512,256]{2,1,0:T(8,128)(2,1)}, bf16[4,512,256]{2,1,0:T(8,128)(2,1)}, bf16[4,4,3,256,128]{4,3,2,1,0...) custom-call(bf16[2,512,2048]{2,1,0:T(8,128)(2,1)} %expand_ref.5, ...), custom_call_target="tpu_custom_call" | custom-call | bytes 134217728 | tf_op jit(solution)/shard_map/third_deal/pallas_call | solution.py:1993
  197.7 3.7 fusion.3
  201.5 1.9 pad_maximum_fusion
  204.1 9.5 %merge_qkv.1 = bf16[4,2,256,1536]{3,2,1,0:T(8,128)(2,1)} custom-call(s32[2]{0:T(128)} %pad_add_fusion.pair_ref, bf16[4,4,3,256,128]{4,3,2,1,0:T(8,128)(2,1)} %bitcast.150, bf16[4,4,3,256,128]{4,3,2,1,0:T(8,128)(2,1)} %get-tuple-element.98.other_ref, bf16[4,2,48,256]{3,2,1,0:T(8,128)(2,1)} %bitcast.160, bf16[48,512]{1,0:T(8,128)(2,1)} %copy-done.20), custom_call_target="tpu_custom_call" | custom-call | bytes 12582912 | tf_op jit(solution)/shard_map/merge_qkv/pallas_call | solution.py:808
  213.5 38.9 %front.1 = (f32[2048,1536]{1,0:T(8,128)}, f32[8,2048]{1,0:T(8,128)}, bf16[48,2048]{1,0:T(8,128)(2,1)}, bf16[4,4,512,256]{3,2,1,0:T(8,128)(2,1)}) custom-call(bf16[2048,512]{1,0:T(8,128)(2,1)} %tokens_ref.5, bf16[2048,512]{1,0:T(8,128)(2,1)} %get-tuple-element.90.x1, bf16[2048,512]{1,0:T(8,128)(2,1)} %get-tuple-element.91.x2, ...), custom_call_target="tpu_custom_call" | custom-call | flops 12884901888 | bytes 67108864 | tf_op jit(solution)/shard_map/front/pallas_call | solution.py:2067
  254.8 1.6 collective-permute-start.1
  258.4 7.3 merge_out.2.matrix_ref
  266.3 10.8 %rotate_rows.1 = (bf16[2048,512]{1,0:T(8,128)(2,1)}, bf16[2048,512]{1,0:T(8,128)(2,1)}, bf16[2048,512]{1,0:T(8,128)(2,1)}) custom-call(f32[2048,1536]{1,0:T(8,128)} %get-tuple-element.105.raw_ref.raw_hbm, f32[8,2048]{1,0:T(8,128)} %add_rsqrt_fusion.scale_ref, f32[2,512]{1,0:T(2,128)} %bitcast.176, f32[2048,128]{1,0:T(8,128)} %get-tuple-element.189.cos_ref, ...), custom_call_target="tpu_custom_call" | custom-call | tf_op jit(solution)/shard_map/rotate_rows/pallas_call | solution.py:585
  277.1 1.6 all-gather.17.cloned.1.call-done
  278.7 126.7 %branch.1 = (bf16[2048,512]{1,0:T(8,128)(2,1)}, f32[4,1,2048]{2,1,0:T(1,128)}, f32[2048,512]{1,0:T(8,128)}, f32[2048,512]{1,0:T(8,128)}, f32[8,8,256]{2,1,0:T(8,...) custom-call(bf16[2048,512]{1,0:T(8,128)(2,1)} %get-tuple-element.108, ...), custom_call_target="tpu_custom_call", output_to_operand_aliasing={{9}: (8, {})} | custom-call | flops 4294967296 | bytes 134217728 | tf_op jit(solution)/shard_map/branch/pallas_call | solution.py:1205
  405.4 2.2 fusion.7
  408.3 11.1 %merge_expand.3 = bf16[4,1,512,2048]{3,2,1,0:T(8,128)(2,1)} custom-call(s32[2]{0:T(128)} %pad_add_fusion.pair_ref, bf16[4,4,512,256]{3,2,1,0:T(8,128)(2,1)} %bitcast.148, bf16[4,4,512,256]{3,2,1,0:T(8,128)(2,1)} %get-tuple-element.120.other_ref, bf16[4,1,16,512]{3,2,1,0:T(8,128)(2,1)} %bitcast.168, bf16[16,2048]{1,0:T(8,128)(2,1)} %bitcast.164), custom_call_target="tpu_custom_call" | custom-call | bytes 16777216 | tf_op jit(solution)/shard_map/merge_expand/pallas_call | solution.py:843
  419.4 11.2 %merge_expand.2 = bf16[4,1,512,2048]{3,2,1,0:T(8,128)(2,1)} custom-call(s32[2]{0:T(128)} %pad_add_fusion.pair_ref, bf16[4,4,512,256]{3,2,1,0:T(8,128)(2,1)} %bitcast.146, bf16[4,4,512,256]{3,2,1,0:T(8,128)(2,1)} %get-tuple-element.119.other_ref, bf16[4,1,16,512]{3,2,1,0:T(8,128)(2,1)} %bitcast.167, bf16[16,2048]{1,0:T(8,128)(2,1)} %bitcast.162), custom_call_target="tpu_custom_call" | custom-call | bytes 16777216 | tf_op jit(solution)/shard_map/merge_expand/pallas_call | solution.py:843
  431.8 8.9 merge_out.3.reduce_hbm
  440.8 125.2 %forward.1 = (bf16[2048,2048]{1,0:T(8,128)(2,1)}, bf16[2048,2048]{1,0:T(8,128)(2,1)}, bf16[2048,2048]{1,0:T(8,128)(2,1)}, bf16[2048,512]{1,0:T(8,128)(2,1)}, bf1...) custom-call(bf16[2048,512]{1,0:T(8,128)(2,1)} %get-tuple-element.115, ...), custom_call_target="tpu_custom_call" | custom-call | flops 51539607552 | bytes 134217728 | tf_op jit(solution)/shard_map/forward/pallas_call | solution.py:1378
  566.0 130.5 %backward.1 = (f32[2048,512]{1,0:T(8,128)}, bf16[16,2048]{1,0:T(8,128)(2,1)}, f32[32,2048]{1,0:T(8,128)}, f32[32,2048]{1,0:T(8,128)}, bf16[2048,512]{1,0:T(8,128...) custom-call(bf16[2048,512]{1,0:T(8,128)(2,1)} %get-tuple-element.124.x0, ...), custom_call_target="tpu_custom_call" | custom-call | flops 51539607552 | bytes 134217728 | tf_op jit(solution)/shard_map/backward/pallas_call | solution.py:1529
  696.5 10.2 %mixed_back.1 = (bf16[2048,512]{1,0:T(8,128)(2,1)}, bf16[16,2048]{1,0:T(8,128)(2,1)}) custom-call(bf16[2048,512]{1,0:T(8,128)(2,1)} %get-tuple-element.133.x0, bf16[2048,512]{1,0:T(8,128)(2,1)} %get-tuple-element.134.x1, bf16[2048,512]{1,0:T(8,128)(2,1)} %get-tuple-element.135.x2, bf16[2048,512]{1,0:T(8,128)(2,1)} %get-tuple-element.136.x3, ...), custom_call_target="tpu_custom_call" | custom-call | flops 4294967296 | bytes 10485760 | tf_op jit(solution)/shard_map/mixed_back/pallas_call | solution.py:901
  706.7 1.8 fusion.2
  708.5 59.6 %attend_back.1 = (f32[2048,512]{1,0:T(8,128)}, f32[2048,512]{1,0:T(8,128)}, f32[2048,512]{1,0:T(8,128)}, f32[4,1,2048]{2,1,0:T(1,128)}, f32[4,1,2048]{2,1,0:T(1,128)}) custom-call(s32[1]{0:T(128)} %dynamic_slice.12.prefix_ref, bf16[2048,512]{1,0:T(8,128)(2,1)} %get-tuple-element.108.q_ref, bf16[2048,512]{1,0:T(8,128)(2,1)} %get-tuple-element.137.grad_ref, ...), custom_call_target="tpu_custom_call" | custom-call | flops 15032385536 | bytes 25165824 | tf_op jit(solution)/shard_map/attend_back/pallas_call | solution.py:535
  768.2 73.7 %input_grad.1 = (f32[2048,512]{1,0:T(8,128)}, f32[48,512]{1,0:T(8,128)}, f32[48,512]{1,0:T(8,128)}) custom-call(f32[2048,1536]{1,0:T(8,128)} %get-tuple-element.105.raw_ref.raw_hbm, f32[2048,512]{1,0:T(8,128)} %get-tuple-element.140.dq_hbm, f32[2048,512]{1,0:T(8,128)} %get-tuple-element.141.dk_hbm, f32[2048,512]{1,0:T(8,128)} %get-tuple-element.142.dv_hbm, ...), custom_call_target="tpu_custom_call" | custom-call | flops 12884901888 | bytes 67108864 | tf_op jit(solution)/shard_map/input_grad/pallas_call | solution.py:1704
  843.5 4.7 convolution_convert_fusion
  850.5 1.5 collective-permute-start.5
  852.1 4.2 collective-permute-done.7
  856.7 4.4 collective-permute-done.5
  862.2 28.8 %groups.1 = (bf16[4,2,112,512]{3,2,1,0:T(8,128)(2,1)}, bf16[4,2,4,16,2048]{4,3,2,1,0:T(8,128)(2,1)}) custom-call(bf16[112,512]{1,0:T(8,128)(2,1)} %pad_maximum_fusion.5.row_ref, bf16[4,16,2048]{2,1,0:T(8,128)(2,1)} %copy-done.13), custom_call_target="tpu_custom_call" | custom-call | bytes 67108864 | tf_op jit(solution)/shard_map/groups/pallas_call | solution.py:2147
  891.0 9.0 finish.1
  901.3 1.6 copy-done.1
  903.0 2.0 copy.143
  (129 shorter events, 24.6 us)
Async XLA Ops:
  7.2 16.7 %copy-start.23 = (s32[8]{0:T(128)S(1)}, s32[8]{0:T(128)}, u32[]{:S(2)}) copy-start(s32[8]{0:T(128)} %param.35) | copy-start | bytes 100
  7.2 108.7 %all-gather.13.cloned.1.call-start = ((), (), s32[]{:S(2)}) async-start(), calls=%async_computation.1 | async-start | bytes 1310720 | tf_op jit(solution)/shard_map/all_gather | solution.py:2178
  23.1 93.8 %all-gather.11.cloned.1.call-start = ((), (), s32[]{:S(2)}) async-start(), calls=%async_computation | async-start | bytes 3932160 | tf_op jit(solution)/shard_map/all_gather | solution.py:2178
  23.9 189.7 %all-gather.15.cloned.1.call-start = ((), (), s32[]{:S(2)}) async-start(), calls=%async_computation.2 | async-start | bytes 5242880 | tf_op jit(solution)/shard_map/all_gather | solution.py:2178
  111.0 167.7 %all-gather.17.cloned.1.call-start = ((), (), s32[]{:S(2)}) async-start(), calls=%async_computation.3 | async-start | bytes 5242880 | tf_op jit(solution)/shard_map/all_gather | solution.py:2178
  111.6 320.2 %all-gather.19.cloned.1.call-start = ((), (), s32[]{:S(2)}) async-start(), calls=%async_computation.4 | async-start | bytes 10485760 | tf_op jit(solution)/shard_map/all_gather | solution.py:2178
  190.4 2.0 copy-start.22
  191.5 10.0 %copy-start.10 = (bf16[48,2048]{1,0:T(8,128)(2,1)}, bf16[48,2048]{1,0:T(8,128)(2,1)S(1)}, u32[]{:S(2)}) copy-start(bf16[48,2048]{1,0:T(8,128)(2,1)S(1)} %slice.79.low_ref) | copy-start | bytes 589828
  201.5 2.0 copy-start.15
  252.4 1.5 collective-permute-start
  254.8 10.9 %collective-permute-start.1 = (f32[8,2048]{1,0:T(8,128)S(1)}, f32[8,2048]{1,0:T(8,128)S(1)}, u32[]{:S(2)}, u32[]{:S(2)}) collective-permute-start(f32[8,2048]{1,0:T(8,128)S(1)} %add.70), channel_id=1, source_target_pairs={{0,8},{4,12},{8,0},{12,4},{1,9},{5,13},{9,1},{13,5},{2,10},{6,14},... | collective-permute-start | bytes 196616 | tf_op jit(solution)/shard_map/ppermute | solution.py:2169
  257.7 149.9 %copy-start.12 = (bf16[4,2,8,512]{3,2,0,1:T(8,128)(2,1)}, bf16[4,2,8,512]{3,2,0,1:T(8,128)(2,1)S(1)}, u32[]{:S(2)}) copy-start(bf16[4,2,8,512]{3,2,0,1:T(8,128)(2,1)S(1)} %copy.106) | copy-start | bytes 196612
  257.8 149.9 %copy-start.11 = (bf16[4,2,8,512]{3,2,0,1:T(8,128)(2,1)}, bf16[4,2,8,512]{3,2,0,1:T(8,128)(2,1)S(1)}, u32[]{:S(2)}) copy-start(bf16[4,2,8,512]{3,2,0,1:T(8,128)(2,1)S(1)} %copy.105) | copy-start | bytes 196612
  407.6 23.0 %collective-permute-start.2 = (f32[16,2048]{1,0:T(8,128)S(1)}, f32[16,2048]{1,0:T(8,128)S(1)}, u32[]{:S(2)}, u32[]{:S(2)}) collective-permute-start(f32[16,2048]{1,0:T(8,128)S(1)} %fusion.7), channel_id=1, source_target_pairs={{0,4},{4,0},{8,12},{12,8},{1,5},{5,1},{9,13},{13,9},{2,6},{6,2},{1... | collective-permute-start | bytes 393224 | tf_op jit(solution)/shard_map/ppermute | solution.py:2169
  431.2 417.0 %collective-permute-start.3 = (f32[16,2048]{1,0:T(8,128)}, f32[16,2048]{1,0:T(8,128)}, u32[]{:S(2)}, u32[]{:S(2)}) collective-permute-start(f32[16,2048]{1,0:T(8,128)} %add.80), channel_id=1, source_target_pairs={{0,8},{4,12},{8,0},{12,4},{1,9},{5,13},{9,1},{13,5},{2,10},{6,14},... | collective-permute-start | bytes 393224 | tf_op jit(solution)/shard_map/ppermute | solution.py:2169
  696.4 10.2 %copy-start = (bf16[2048,512]{1,0:T(8,128)(2,1)S(1)}, bf16[2048,512]{1,0:T(8,128)(2,1)}, u32[]{:S(2)}) copy-start(bf16[2048,512]{1,0:T(8,128)(2,1)} %get-tuple-element.138.out_ref) | copy-start | bytes 6291460
  768.2 74.7 %copy-start.16 = (f32[32,2048]{1,0:T(8,128)S(1)}, f32[32,2048]{1,0:T(8,128)}, u32[]{:S(2)}) copy-start(f32[32,2048]{1,0:T(8,128)} %get-tuple-element.153) | copy-start | bytes 786436
  768.2 74.7 %copy-start.14 = (f32[32,2048]{1,0:T(8,128)S(1)}, f32[32,2048]{1,0:T(8,128)}, u32[]{:S(2)}) copy-start(f32[32,2048]{1,0:T(8,128)} %get-tuple-element.149) | copy-start | bytes 786436
  768.2 74.8 %copy-start.18 = (f32[16,2048]{1,0:T(8,128)S(1)}, f32[16,2048]{1,0:T(8,128)}, u32[]{:S(2)}) copy-start(f32[16,2048]{1,0:T(8,128)} %get-tuple-element.150) | copy-start | bytes 393220
  768.2 75.3 %copy-start.17 = (bf16[16,2048]{1,0:T(8,128)(2,1)S(1)}, bf16[16,2048]{1,0:T(8,128)(2,1)}, u32[]{:S(2)}) copy-start(bf16[16,2048]{1,0:T(8,128)(2,1)} %get-tuple-element.154) | copy-start | bytes 196612
  842.9 7.6 collective-permute-start.4
  843.0 6.9 collective-permute-start.6
  843.5 4.8 copy-start.21
  843.5 4.8 copy-start.4
  848.2 1.6 copy-start.19
  848.2 8.1 copy-start.3
  849.8 11.3 %copy-start.5 = (bf16[2048,512]{1,0:T(8,128)(2,1)S(1)}, bf16[2048,512]{1,0:T(8,128)(2,1)}, u32[]{:S(2)}) copy-start(bf16[2048,512]{1,0:T(8,128)(2,1)} %get-tuple-element.115.x0) | copy-start | bytes 6291460
  849.9 6.4 collective-permute-start.7
  850.5 11.0 %copy-start.13 = (bf16[4,16,2048]{2,1,0:T(8,128)(2,1)}, bf16[4,16,2048]{2,1,0:T(8,128)(2,1)S(1)}, u32[]{:S(2)}) copy-start(bf16[4,16,2048]{2,1,0:T(8,128)(2,1)S(1)} %fusion.4.col_ref) | copy-start | bytes 786436
  850.5 10.5 %collective-permute-start.5 = (f32[32,2048]{1,0:T(8,128)S(1)}, f32[32,2048]{1,0:T(8,128)S(1)}, u32[]{:S(2)}, u32[]{:S(2)}) collective-permute-start(f32[32,2048]{1,0:T(8,128)S(1)} %add.82), channel_id=1, source_target_pairs={{0,8},{4,12},{8,0},{12,4},{1,9},{5,13},{9,1},{13,5},{2,10},{6,14},... | collective-permute-start | bytes 786440 | tf_op jit(solution)/shard_map/ppermute | solution.py:2169
  891.0 9.0 copy-start.6
  900.0 2.9 copy-start.1
  (5 other events, 4.5 us)
Sparse Core Ops, SparseCore 0:
  23.2 29.0 all-gather.12
  53.9 62.9 all-gather.10
  118.5 79.3 all-gather.14
  199.4 79.2 all-gather.16
  280.1 148.1 all-gather.18

commit v5 on v4

--- a/solution.py
+++ b/solution.py
@@ -455,14 +455,17 @@
     return mixed / total, top + jnp.log2(total)
 
 
+def in_parts(values, count):
+    parts = []
+    for _ in range(count):
+        part = values.astype(BF)
+        parts.append(part)
+        values = values - part.astype(F32)
+    return parts
+
+
 def row_sums(values):
-    return lax.dot_general(
-        jnp.ones((8, values.shape[1]), F32),
-        values,
-        (((1,), (1,)), ((), ())),
-        precision=lax.Precision.HIGHEST,
-        preferred_element_type=F32,
-    )[0:1]
+    return sums_of(values)[0:1]
 
 
 def attend_back_kernel(
@@ -667,40 +670,36 @@
     qkv_low, qkv_up, attn_low, attn_up, expand_low, expand_up, reduce_low, reduce_up = outs
     cols = cols_ref.shape[2]
     groups = 2 * cols
-    here = pl.program_id(0)
+    step = pl.program_id(0)
     me = ids_ref[2 * groups]
-
-    def weight(index):
-        return (ids_ref[index] == here).astype(F32)
-
-    total = jnp.zeros(rows_ref.shape[2:], F32)
-    for k in range(cols):
-        for other in range(2):
-            total = total + weight(2 * k + other) * rows_ref[k, other].astype(F32)
-    for part in range(3):
-        qkv_low[part, 0] = total[16 * part : 16 * part + 16]
-    attn_up[0] = total[48:64]
-    for part in range(2):
-        expand_low[part, 0] = total[64 + 16 * part : 80 + 16 * part]
-    reduce_up[0] = total[96:112]
     sub = qkv_up.shape[3] // 4
     ff_sub = expand_up.shape[3] // 4
+
+    @pl.when(step == 0)
+    def _():
+        for out in outs:
+            out[...] = jnp.zeros_like(out)
+
+    here = ids_ref[step]
+    term = rows_ref[step // 2, lax.rem(step, 2)].astype(F32)
+    for part in range(3):
+        qkv_low[part, here] += term[16 * part : 16 * part + 16]
+    attn_up[here] += term[48:64]
+    for part in range(2):
+        expand_low[part, here] += term[64 + 16 * part : 80 + 16 * part]
+    reduce_up[here] += term[96:112]
+    here = ids_ref[groups + step]
     for row in range(4):
-        block = me ^ row
-        total = jnp.zeros(cols_ref.shape[3:], F32)
-        for other in range(2):
-            for index in range(cols):
-                one = cols_ref[block, other, index].astype(F32)
-                total = total + weight(groups + other * cols + index) * one
+        term = cols_ref[me ^ row, step // cols, lax.rem(step, cols)].astype(F32)
         near = slice(row * sub, (row + 1) * sub)
         wide = slice(row * ff_sub, (row + 1) * ff_sub)
         for part in range(3):
-            qkv_up[part, 0, :, near] = total[:, part * sub : (part + 1) * sub]
-        attn_low[0, :, near] = total[:, 3 * sub : 4 * sub]
+            qkv_up[part, here, :, near] += term[:, part * sub : (part + 1) * sub]
+        attn_low[here, :, near] += term[:, 3 * sub : 4 * sub]
         for part in range(2):
             at = 4 * sub + part * ff_sub
-            expand_up[part, 0, :, wide] = total[:, at : at + ff_sub]
-        reduce_low[0, :, wide] = total[:, 4 * sub + 2 * ff_sub :]
+            expand_up[part, here, :, wide] += term[:, at : at + ff_sub]
+        reduce_low[here, :, wide] += term[:, 4 * sub + 2 * ff_sub :]
 
 
 def finish_call(ids, rows, cols, sub, ff_sub):
@@ -719,10 +718,10 @@
     for parts, size in shapes:
         if parts:
             out_shape.append(jax.ShapeDtypeStruct((parts, SETS, 16, size), F32))
-            out_specs.append(pl.BlockSpec((parts, 1, 16, size), lambda k, c: (0, k, 0, 0)))
+            out_specs.append(pl.BlockSpec((parts, SETS, 16, size), lambda k, c: (0, 0, 0, 0)))
         else:
             out_shape.append(jax.ShapeDtypeStruct((SETS, 16, size), F32))
-            out_specs.append(pl.BlockSpec((1, 16, size), lambda k, c: (k, 0, 0)))
+            out_specs.append(pl.BlockSpec((SETS, 16, size), lambda k, c: (0, 0, 0)))
 
     def whole(array):
         return pl.BlockSpec(array.shape, lambda k, c: (0,) * array.ndim)
@@ -732,7 +731,7 @@
         out_shape=out_shape,
         grid_spec=pltpu.PrefetchScalarGridSpec(
             num_scalar_prefetch=1,
-            grid=(SETS,),
+            grid=(2 * cols.shape[2],),
             in_specs=[whole(rows), whole(cols)],
             out_specs=out_specs,
         ),
@@ -963,7 +962,9 @@
     return shapes
 
 
-def run_blocks(count, bufs, compute, stats, finish, own_ref=None, arrived=None, extra=None):
+def run_blocks(
+    count, bufs, compute, stats, finish, own_ref=None, arrived=None, extra=None, own_rows=None
+):
     pair_out, pair_in, far, side_out, side_in, near, pair_sem, side_sem, *rest = bufs
     gathers = own_ref is not None
     if gathers:
@@ -1049,6 +1050,8 @@
         own_ref[rows_of(c), :] = finish(c, rows_of(c), near[lax.rem(c, RING)], total)
         gather_side(c).start()
         gather_core(c).start()
+        if own_rows is not None:
+            own_rows(c).start()
 
     def pass_on(c):
         gather_side(c).wait_recv()
@@ -1085,27 +1088,17 @@
     out = None
     for index, value in enumerate(values):
         pick = lax.broadcasted_iota(jnp.int32, (8, value.shape[1]), 0) == index
-        term = lax.dot_general(
-            pick.astype(F32),
-            value,
-            (((1,), (1,)), ((), ())),
-            precision=lax.Precision.HIGHEST,
-            preferred_element_type=F32,
-        )
-        out = term if out is None else out + term
+        pick = pick.astype(F32).astype(BF)
+        for part in in_parts(value, 2):
+            term = dot_of(pick, part, 1, 1)
+            out = term if out is None else out + term
     return out
 
 
 def column_of(stats, index):
-    pick = lax.broadcasted_iota(jnp.int32, (8, HEAD), 0) == index
-    wide = lax.dot_general(
-        stats,
-        pick.astype(F32),
-        (((0,), (0,)), ((), ())),
-        precision=lax.Precision.HIGHEST,
-        preferred_element_type=F32,
-    )
-    return wide[:, :1]
+    parts = jnp.concatenate(in_parts(stats, 3), axis=0)
+    pick = lax.rem(lax.broadcasted_iota(jnp.int32, (parts.shape[0], HEAD), 0), 8) == index
+    return dot_of(parts, pick.astype(F32).astype(BF), 0, 0)[:, :1]
 
 
 def branch_kernel(
@@ -1227,6 +1220,23 @@
     )(query, key, value, limit, matrix, tokens, gain, *halves)
 
 
+def rows_out(buffer, outer, sems, index):
+    def copy(c):
+        rows = span_of(c, BLOCK)
+        return pltpu.make_async_copy(buffer.at[rows], outer.at[rows], sems.at[index, c])
+
+    return copy
+
+
+def wait_rows(count, *copies):
+    def body(c, carry):
+        for copy in copies:
+            copy(c).wait()
+        return carry
+
+    lax.fori_loop(0, count, body, 0)
+
+
 def load_lefts(lefts, buffer, sems, count):
     width = buffer.shape[2] // 4
 
@@ -1273,22 +1283,23 @@
     gate_hbm,
     upper_hbm,
     reduce_hbm,
-    hidden_ref,
-    cot_ref,
+    hidden_hbm,
+    cot_hbm,
     gain_ref,
     expand_low_ref,
     reduce_low_ref,
     act_out,
     gate_out,
     upper_out,
-    layer_ref,
+    layer_out,
     expand_inner_ref,
     reduce_inner_ref,
-    own_ref,
+    own_out,
     *rest,
 ):
     arrived, rest = rest[:3], rest[3:]
-    gate_w, upper_w, reduce_w, lefts, act_buf, gate_buf, upper_buf, w_sem, x_sem, o_sem, *bufs = rest
+    gate_w, upper_w, reduce_w, lefts, act_buf, gate_buf, upper_buf, *rest = rest
+    hidden_ref, cot_ref, layer_ref, own_ref, w_sem, x_sem, o_sem, r_sem, *bufs = rest
     width = own_ref.shape[1]
     count = own_ref.shape[0] // BLOCK
     ff = gate_w.shape[1]
@@ -1296,13 +1307,21 @@
     loads = [
         pltpu.make_async_copy(source, target, w_sem.at[index])
         for index, (source, target) in enumerate(
-            ((gate_hbm, gate_w), (upper_hbm, upper_w), (reduce_hbm, reduce_w))
+            (
+                (gate_hbm, gate_w),
+                (upper_hbm, upper_w),
+                (reduce_hbm, reduce_w),
+                (cot_hbm, cot_ref),
+                (hidden_hbm, hidden_ref),
+            )
         )
     ]
     start_left, wait_left = load_lefts((x0, x1, x2, x3), lefts, x_sem, count)
     start_left(0)
     for load in loads:
         load.start()
+    layer_rows = rows_out(layer_ref, layer_out, r_sem, 0)
+    own_rows = rows_out(own_ref, own_out, r_sem, 1)
     greet()
     outs = [
         move_rows(outer, buffer, o_sem, index, False)
@@ -1352,6 +1371,11 @@
         reduce_inner_ref[:, rows] = dot_of(reduce_low_ref[...], act_buf[slot], 1, 1)
 
     def stats(c, rows, result):
+        @pl.when(c == 0)
+        def _():
+            loads[3].wait()
+            loads[4].wait()
+
         weighted = gain_ref[1:2, :] * cot_ref[rows, :].astype(F32)
         return sums_of(result * result, weighted * result)
 
@@ -1359,11 +1383,13 @@
         scale = lax.rsqrt(column_of(total, 0) / D + EPS)
         gain = gain_ref[1:2, :]
         layer_ref[rows, :] = (hidden_ref[rows, :] + gain * result * scale).astype(BF)
+        layer_rows(c).start()
         weighted = gain * cot_ref[rows, :].astype(F32)
         inner = column_of(total, 1)
         return (scale * weighted - result * (scale * scale * scale * inner / D)).astype(BF)
 
-    run_blocks(count, bufs, compute, stats, finish, own_ref, arrived)
+    run_blocks(count, bufs, compute, stats, finish, own_ref, arrived, own_rows=own_rows)
+    wait_rows(count, layer_rows, own_rows)
     for c in range(max(count - 2, 0), count):
         for out in outs:
             out(c).wait()
@@ -1384,8 +1410,8 @@
             jax.ShapeDtypeStruct((16, rows), F32),
         ]
         + [part] * 4,
-        in_specs=[ANY_SPEC] * 7 + [VMEM_SPEC] * 5,
-        out_specs=[ANY_SPEC] * 3 + [VMEM_SPEC] * 4 + [ANY_SPEC] * 3,
+        in_specs=[ANY_SPEC] * 9 + [VMEM_SPEC] * 3,
+        out_specs=[ANY_SPEC] * 4 + [VMEM_SPEC] * 2 + [ANY_SPEC] * 4,
         scratch_shapes=[
             pltpu.VMEM(gate_w.shape, BF),
             pltpu.VMEM(upper_w.shape, BF),
@@ -1394,9 +1420,14 @@
             pltpu.VMEM((2, BLOCK, ff), BF),
             pltpu.VMEM((2, BLOCK, ff), BF),
             pltpu.VMEM((2, BLOCK, ff), BF),
-            pltpu.SemaphoreType.DMA((3,)),
+            pltpu.VMEM((rows, width), F32),
+            pltpu.VMEM((rows, width), BF),
+            pltpu.VMEM((rows, width), BF),
+            pltpu.VMEM((rows, width), BF),
+            pltpu.SemaphoreType.DMA((5,)),
             pltpu.SemaphoreType.DMA((2, 4)),
             pltpu.SemaphoreType.DMA((3, 2)),
+            pltpu.SemaphoreType.DMA((2, count)),
         ]
         + exchange_scratch(count, width, True),
         compiler_params=talk_params(1),
@@ -1415,23 +1446,23 @@
     reduce_hbm,
     gate_in,
     upper_in,
-    cot_ref,
-    branch_ref,
+    cot_hbm,
+    branch_hbm,
     stat_ref,
     gain_ref,
     reduce_up_ref,
     expand_up_ref,
     expand_inner_ref,
-    d_hidden_ref,
+    d_hidden_out,
     reduce_inner_ref,
     d_inner_ref,
     up_grad_ref,
-    own_ref,
+    own_out,
     *rest,
 ):
     arrived, rest = rest[:3], rest[3:]
     gate_w, upper_w, reduce_w, lefts, gate_buf, upper_buf, d_gate_buf, d_upper_buf, *rest = rest
-    w_sem, x_sem, i_sem, *bufs = rest
+    branch_ref, cot_ref, d_hidden_ref, own_ref, w_sem, x_sem, i_sem, r_sem, *bufs = rest
     width = own_ref.shape[1]
     count = own_ref.shape[0] // BLOCK
     ff = gate_w.shape[1]
@@ -1440,7 +1471,13 @@
     loads = [
         pltpu.make_async_copy(source, target, w_sem.at[index])
         for index, (source, target) in enumerate(
-            ((reduce_hbm, reduce_w), (gate_hbm, gate_w), (upper_hbm, upper_w))
+            (
+                (reduce_hbm, reduce_w),
+                (gate_hbm, gate_w),
+                (upper_hbm, upper_w),
+                (cot_hbm, cot_ref),
+                (branch_hbm, branch_ref),
+            )
         )
     ]
     start_left, wait_left = load_lefts((x0, x1, x2, x3), lefts, x_sem, count)
@@ -1453,6 +1490,8 @@
         one(0).start()
     for load in loads:
         load.start()
+    hidden_rows = rows_out(d_hidden_ref, d_hidden_out, r_sem, 0)
+    own_rows = rows_out(own_ref, own_out, r_sem, 1)
     greet()
 
     def compute(c, put):
@@ -1505,8 +1544,14 @@
             )
 
     def stats(c, rows, total):
+        @pl.when(c == 0)
+        def _():
+            loads[3].wait()
+            loads[4].wait()
+
         d_hidden = cot_ref[rows, :].astype(F32) + total
         d_hidden_ref[rows, :] = d_hidden
+        hidden_rows(c).start()
         return sums_of(gain_ref[0:1, :] * d_hidden * branch_ref[rows, :])
 
     def finish(c, rows, total, sums):
@@ -1516,7 +1561,8 @@
         back = scale * scale * scale * inner / D
         return (scale * weighted - branch_ref[rows, :] * back).astype(BF)
 
-    run_blocks(count, bufs, compute, stats, finish, own_ref, arrived)
+    run_blocks(count, bufs, compute, stats, finish, own_ref, arrived, own_rows=own_rows)
+    wait_rows(count, hidden_rows, own_rows)
 
 
 def backward_call(
@@ -1535,8 +1581,8 @@
             jax.ShapeDtypeStruct((32, ff), F32),
         ]
         + [part] * 4,
-        in_specs=[ANY_SPEC] * 9 + [VMEM_SPEC] * 7,
-        out_specs=[VMEM_SPEC] * 5 + [ANY_SPEC] * 3,
+        in_specs=[ANY_SPEC] * 11 + [VMEM_SPEC] * 5,
+        out_specs=[ANY_SPEC] + [VMEM_SPEC] * 3 + [ANY_SPEC] * 4,
         scratch_shapes=[
             pltpu.VMEM(gate_w.shape, BF),
             pltpu.VMEM(upper_w.shape, BF),
@@ -1546,9 +1592,14 @@
             pltpu.VMEM((2, BLOCK, ff), BF),
             pltpu.VMEM((BLOCK, ff), BF),
             pltpu.VMEM((BLOCK, ff), BF),
-            pltpu.SemaphoreType.DMA((3,)),
+            pltpu.VMEM((rows, width), F32),
+            pltpu.VMEM((rows, width), BF),
+            pltpu.VMEM((rows, width), F32),
+            pltpu.VMEM((rows, width), BF),
+            pltpu.SemaphoreType.DMA((5,)),
             pltpu.SemaphoreType.DMA((2, 4)),
             pltpu.SemaphoreType.DMA((2, 2)),
+            pltpu.SemaphoreType.DMA((2, count)),
         ]
         + exchange_scratch(count, width, True),
         compiler_params=talk_params(2),
@@ -1564,24 +1615,41 @@
     dq_hbm,
     dk_hbm,
     dv_hbm,
-    matrix_ref,
-    d_hidden_ref,
+    act_hbm,
+    mixed_hbm,
+    branch_hbm,
+    hidden_hbm,
+    result_hbm,
+    matrix_hbm,
+    d_hidden_hbm,
+    tokens_hbm,
     scale_ref,
     q_sum_ref,
     k_sum_ref,
     gain_ref,
     cos_ref,
     sin_ref,
-    tokens_ref,
     inner_ref,
     up_ref,
-    out_ref,
-    low_grad_ref,
-    up_grad_ref,
+    part_ref,
+    d_inner_ref,
+    expand_grad_ref,
+    out_hbm,
+    rows_out_hbm,
+    cols_out_hbm,
     raw_buf,
     dq_buf,
     dk_buf,
     dv_buf,
+    act_buf,
+    mixed_buf,
+    branch_buf,
+    hidden_buf,
+    result_buf,
+    matrix_ref,
+    d_hidden_ref,
+    tokens_ref,
+    out_ref,
     left_ref,
     inner_out,
     inner_in,
@@ -1589,40 +1657,83 @@
     inner_far,
     sum_own,
     sum_in,
-    back_ref,
+    columns,
+    up_all,
+    part_in,
+    part_mid,
+    part_far,
     in_sem,
     core_sem,
     far_sem,
     sum_sem,
+    part_sem,
+    load_sem,
+    r_sem,
+    row_grad_ref,
+    attn_grad_ref,
+    reduce_grad_ref,
+    row_pack,
+    col_pack,
     *bufs,
 ):
+    group_sems, bufs = bufs[:5], bufs[5:]
     width = out_ref.shape[1]
     local = dq_buf.shape[2]
     count = out_ref.shape[0] // BLOCK
     ins = [
         move_rows(outer, buffer, in_sem, index, True)
         for index, (outer, buffer) in enumerate(
-            ((raw_hbm, raw_buf), (dq_hbm, dq_buf), (dk_hbm, dk_buf), (dv_hbm, dv_buf))
+            (
+                (raw_hbm, raw_buf),
+                (dq_hbm, dq_buf),
+                (dk_hbm, dk_buf),
+                (dv_hbm, dv_buf),
+                (act_hbm, act_buf),
+                (mixed_hbm, mixed_buf),
+                (branch_hbm, branch_buf),
+                (hidden_hbm, hidden_buf),
+                (result_hbm, result_buf),
+            )
         )
     ]
     for one in ins:
         one(0).start()
-    low_grad_ref[...] = jnp.zeros_like(low_grad_ref)
-    up_grad_ref[...] = jnp.zeros_like(up_grad_ref)
+    loads = [
+        pltpu.make_async_copy(source, target, load_sem.at[index])
+        for index, (source, target) in enumerate(
+            ((matrix_hbm, matrix_ref), (d_hidden_hbm, d_hidden_ref), (tokens_hbm, tokens_ref))
+        )
+    ]
+    for load in loads:
+        load.start()
+    out_rows = rows_out(out_ref, out_hbm, r_sem, 0)
+    for grad in (row_grad_ref, attn_grad_ref, reduce_grad_ref):
+        grad[...] = jnp.zeros_like(grad)
+    up_all[...] = jnp.zeros_like(up_all)
     sum_own[...] = jnp.zeros_like(sum_own)
     for row, part in enumerate((q_sum_ref, k_sum_ref)):
         total = part[0]
         for h in range(1, part.shape[0]):
             total = total + part[h]
         sum_own[row : row + 1, :] = total
-    greet()
+    greet_all(row_and_col_peers() + [other_of_pair()])
     exchanges = [send(sum_own, sum_in.at[step - 1], sum_sem, step - 1, step) for step in (1, 2, 3)]
     for copy in exchanges:
         copy.start()
+    part_core = send(part_ref, part_in, part_sem, 0, 1)
+    part_side = send(part_mid, part_far, part_sem, 1, 2)
+    part_core.start()
+    part_core.wait()
+    part_mid[...] = (part_ref[...].astype(F32) + part_in[...].astype(F32)).astype(BF)
+    part_side.start()
     for copy in exchanges:
         copy.wait()
     total = sum_own[...] + sum_in[0] + sum_in[1] + sum_in[2]
-    back_ref[...] = scale_ref[...] * scale_ref[...] * total / D
+    scales = scale_ref[...]
+    backs = scales * scales * total / D
+    for part in range(2):
+        columns[part] = jnp.broadcast_to(column_of(scales, part), columns.shape[1:])
+        columns[2 + part] = jnp.broadcast_to(column_of(backs, part), columns.shape[1:])
 
     def inner_core(c):
         return send(inner_out.at[lax.rem(c, 2)], inner_in.at[c], core_sem, c, 1)
@@ -1637,13 +1748,14 @@
 
         inner_core(c).wait_recv()
         slot = lax.rem(c, 2)
-        inner_mid[slot] = inner_out[slot] + inner_in[c]
+        total = inner_out[slot].astype(F32) + inner_in[c].astype(F32)
+        inner_mid[slot] = total.astype(BF)
         inner_side(c).start()
 
     def after_side(c):
         inner_side(c).wait_recv()
-        total = (inner_mid[lax.rem(c, 2)] + inner_far[c]).astype(BF)
-        low_grad_ref[...] += dot_of(total, tokens_ref[span_of(c, BLOCK), :], 1, 0)
+        total = inner_mid[lax.rem(c, 2)].astype(F32) + inner_far[c].astype(F32)
+        row_grad_ref[:48, :] += dot_of(total.astype(BF), tokens_ref[span_of(c, BLOCK), :], 1, 0)
 
     def compute(c, put):
         slot = lax.rem(c, 2)
@@ -1663,8 +1775,8 @@
         cosine = cos_ref[rows, :]
         sine = sin_ref[rows, :]
         for part, grad in ((0, dq_buf), (1, dk_buf)):
-            scale = column_of(scale_ref[:, rows], part)
-            back = column_of(back_ref[:, rows], part)
+            scale = columns[part, rows, :]
+            back = columns[2 + part, rows, :]
             for at in range(0, local, HEAD):
                 turned = grad[slot, :, at : at + HEAD]
                 turned = turned * cosine - pltpu.roll(turned, HEAD // 2, 1) * sine
@@ -1674,65 +1786,135 @@
                     turned - raw_buf[slot, :, lane : lane + HEAD] * back
                 ).astype(BF)
         left_ref[:, 2 * local :] = dv_buf[slot].astype(BF)
-        for part in range(3):
-            own = slice(16 * part, 16 * part + 16)
-            grad = left_ref[:, part * local : (part + 1) * local]
-            inner_out[slot, own, :] = ADAPTER_FACTOR * dot_of(up_ref[own, :], grad, 1, 1)
-            up_grad_ref[own, :] += ADAPTER_FACTOR * dot_of(inner_ref[own, rows], grad, 1, 0)
+        left = left_ref[...]
+        inner_out[slot] = (ADAPTER_FACTOR * dot_of(up_ref[...], left, 1, 1)).astype(BF)
         inner_core(c).start()
-        left = left_ref[...]
+        up_all[...] += dot_of(inner_ref[:, rows], left, 1, 0)
+
+        @pl.when(c == 0)
+        def _():
+            for load in loads:
+                load.wait()
+            part_side.wait()
+
         for block in (1, 3, 2, 0):
             put(block, dot_of(left, matrix_ref[block * width : (block + 1) * width, :], 1, 1))
+        whole = part_mid[:, rows].astype(F32) + part_far[:, rows].astype(F32)
+        whole = whole.astype(BF)
+        for at, size, first, other, factor in (
+            (48, 16, 0, branch_buf, ADAPTER_FACTOR),
+            (64, 32, 32, hidden_buf, 1.0),
+            (96, 16, 16, result_buf, ADAPTER_FACTOR),
+        ):
+            term = dot_of(whole[first : first + size], other[slot], 1, 0)
+            row_grad_ref[at : at + size, :] += factor * term
+        attn_grad_ref[...] += dot_of(d_inner_ref[:16, rows], mixed_buf[slot], 1, 0)
+        reduce_grad_ref[...] += dot_of(d_inner_ref[16:, rows], act_buf[slot], 1, 0)
 
     def finish(c, rows, total):
         out_ref[rows, :] = d_hidden_ref[rows, :] + total
+        out_rows(c).start()
 
     run_blocks(count, bufs, compute, None, finish, extra=(after_core, after_side))
+    row_pack[...] = row_grad_ref[...].astype(BF)
+    cols = col_pack.shape[0]
+    pieces = [
+        (up_all, 16 * part, part * local, local, ADAPTER_FACTOR) for part in range(3)
+    ]
+    ff = reduce_grad_ref.shape[1]
+    pieces += [
+        (attn_grad_ref, 0, 0, local, 1.0),
+        (expand_grad_ref, 0, 0, ff, 1.0),
+        (expand_grad_ref, 16, 0, ff, 1.0),
+        (reduce_grad_ref, 0, 0, ff, 1.0),
+    ]
+    lane = 0
+    for ref, row, at, size, factor in pieces:
+        size = size // cols
+        for index in range(cols):
+            piece = ref[row : row + 16, at + index * size : at + (index + 1) * size]
+            col_pack[index, :, lane : lane + size] = (factor * piece).astype(BF)
+        lane += size
+    exchange_groups(row_pack, col_pack, rows_out_hbm, cols_out_hbm, group_sems)
+    wait_rows(count, out_rows)
     for c in range(max(count - 2, 0), count):
         inner_core(c).wait_send()
         inner_side(c).wait_send()
 
 
 def input_call(
-    raw, d_query, d_key, d_value, matrix, d_hidden, scales, q_sums, k_sums, *others
+    raw, d_query, d_key, d_value, act, mixed, branch, hidden, result, matrix, d_hidden, *others
 ):
     rows, width = d_hidden.shape
     local = d_query.shape[1]
+    ff = act.shape[1]
+    cols = lax.axis_size("col")
+    lanes = (4 * local + 3 * ff) // cols
     count = rows // BLOCK
-    part = pltpu.VMEM((2, BLOCK, local), F32)
+    grad = pltpu.VMEM((2, BLOCK, local), F32)
+    part = pltpu.VMEM((2, BLOCK, width), BF)
+    inner = pltpu.VMEM((2, 48, BLOCK), BF)
+    arrived = pltpu.VMEM((count, 48, BLOCK), BF)
+    total = pltpu.VMEM((64, rows), BF)
     sem = pltpu.SemaphoreType.DMA((2, count))
     return pl.pallas_call(
         input_kernel,
         out_shape=[
             jax.ShapeDtypeStruct((rows, width), F32),
-            jax.ShapeDtypeStruct((48, width), F32),
-            jax.ShapeDtypeStruct((48, local), F32),
+            jax.ShapeDtypeStruct((cols, 2, 112, width), BF),
+            jax.ShapeDtypeStruct((4, 2, cols, 16, lanes), BF),
         ],
-        in_specs=[ANY_SPEC] * 4 + [VMEM_SPEC] * 11,
-        out_specs=[VMEM_SPEC] * 3,
+        in_specs=[ANY_SPEC] * 12 + [VMEM_SPEC] * 11,
+        out_specs=[ANY_SPEC] * 3,
         scratch_shapes=[
             pltpu.VMEM((2, BLOCK, 3 * local), F32),
+            grad,
+            grad,
+            grad,
+            pltpu.VMEM((2, BLOCK, ff), BF),
+            pltpu.VMEM((2, BLOCK, local), BF),
             part,
             part,
             part,
+            pltpu.VMEM(matrix.shape, BF),
+            pltpu.VMEM((rows, width), F32),
+            pltpu.VMEM((rows, width), BF),
+            pltpu.VMEM((rows, width), F32),
             pltpu.VMEM((BLOCK, 3 * local), BF),
-            pltpu.VMEM((2, 48, BLOCK), F32),
-            pltpu.VMEM((count, 48, BLOCK), F32),
-            pltpu.VMEM((2, 48, BLOCK), F32),
-            pltpu.VMEM((count, 48, BLOCK), F32),
+            inner,
+            arrived,
+            inner,
+            arrived,
             pltpu.VMEM((8, rows), F32),
             pltpu.VMEM((3, 8, rows), F32),
-            pltpu.VMEM((8, rows), F32),
-            pltpu.SemaphoreType.DMA((4, 2)),
+            pltpu.VMEM((4, rows, HEAD), F32),
+            pltpu.VMEM((48, 3 * local), F32),
+            total,
+            total,
+            total,
+            pltpu.SemaphoreType.DMA((9, 2)),
             sem,
             sem,
             pltpu.SemaphoreType.DMA((2, 3)),
+            pltpu.SemaphoreType.DMA((2, 2)),
+            pltpu.SemaphoreType.DMA((3,)),
+            pltpu.SemaphoreType.DMA((1, count)),
+            pltpu.VMEM((112, width), F32),
+            pltpu.VMEM((16, local), F32),
+            pltpu.VMEM((16, ff), F32),
+            pltpu.VMEM((112, width), BF),
+            pltpu.VMEM((cols, 16, lanes), BF),
+            pltpu.SemaphoreType.DMA((2,)),
+            pltpu.SemaphoreType.DMA((2, 2)),
+            pltpu.SemaphoreType.DMA((2, cols - 1)),
+            pltpu.SemaphoreType.DMA((2, cols - 1)),
+            pltpu.SemaphoreType.DMA((2, 2, 3)),
         ]
         + exchange_scratch(count, width, False),
         compiler_params=talk_params(3),
         cost_estimate=cost_of(24 * rows * width * local, 2**26),
         name="input_grad",
-    )(raw, d_query, d_key, d_value, matrix, d_hidden, scales, q_sums, k_sums, *others)
+    )(raw, d_query, d_key, d_value, act, mixed, branch, hidden, result, matrix, d_hidden, *others)
 
 
 def deal(items, outs, sems):
@@ -2091,12 +2273,12 @@
     )(*lefts, matrix, low, gate_all, gate_rest)
 
 
-def groups_kernel(row_ref, col_ref, rows_out, cols_out, local_sem, pair_sem, round_sem, deal_sem, row_sem):
+def exchange_groups(row_ref, col_ref, rows_out, cols_out, sems):
+    local_sem, pair_sem, round_sem, deal_sem, row_sem = sems
     cols = col_ref.shape[0]
     col = lax.axis_index("col")
     places = [lax.rem(col + k, cols) for k in range(cols)]
     to = copy_to
-    greet_all(row_and_col_peers() + [other_of_pair()])
     swap_rows = to(row_ref, rows_out.at[0, 1], pair_sem, 0, other_of_pair())
     swap_rows.start()
     dealt = [
@@ -2115,6 +2297,16 @@
     keep_cols.wait()
     swap_cols = to(cols_out.at[0, 0], cols_out.at[0, 1], pair_sem, 1, other_of_pair())
     swap_cols.start()
+
+    def spread(which):
+        side = to(cols_out.at[0, which], cols_out.at[2, which], row_sem.at[which], 1, peer(2))
+        core = to(cols_out.at[0, which], cols_out.at[1, which], row_sem.at[which], 0, peer(1))
+        relay = to(cols_out.at[2, which], cols_out.at[3, which], row_sem.at[which], 2, peer(1))
+        side.start()
+        core.start()
+        return side, core, relay
+
+    spreads = [spread(0)]
     keep_rows.wait()
     swap_rows.wait_recv()
     rounds = [
@@ -2124,45 +2316,20 @@
     for copy in rounds:
         copy.start()
     swap_cols.wait_recv()
-    side = to(cols_out.at[0], cols_out.at[2], row_sem, 1, peer(2))
-    core = to(cols_out.at[0], cols_out.at[1], row_sem, 0, peer(1))
-    relay = to(cols_out.at[2], cols_out.at[3], row_sem, 2, peer(1))
-    side.start()
-    core.start()
-    side.wait_recv()
-    relay.start()
-    core.wait()
-    relay.wait()
-    side.wait_send()
+    spreads.append(spread(1))
+    for side, core, relay in spreads:
+        side.wait_recv()
+        relay.start()
+    for side, core, relay in spreads:
+        core.wait()
+        relay.wait()
+        side.wait_send()
     for copy in rounds:
         copy.wait()
     for copy in dealt:
         copy.wait_send()
     swap_rows.wait_send()
     swap_cols.wait_send()
-
-
-def groups_call(row_pack, col_pack):
-    cols = col_pack.shape[0]
-    return pl.pallas_call(
-        groups_kernel,
-        out_shape=[
-            jax.ShapeDtypeStruct((cols, 2, *row_pack.shape), BF),
-            jax.ShapeDtypeStruct((4, 2, *col_pack.shape), BF),
-        ],
-        in_specs=[ANY_SPEC] * 2,
-        out_specs=[ANY_SPEC] * 2,
-        scratch_shapes=[
-            pltpu.SemaphoreType.DMA((2,)),
-            pltpu.SemaphoreType.DMA((2, 2)),
-            pltpu.SemaphoreType.DMA((2, cols - 1)),
-            pltpu.SemaphoreType.DMA((2, cols - 1)),
-            pltpu.SemaphoreType.DMA((2, 3)),
-        ],
-        compiler_params=talk_params(7),
-        cost_estimate=cost_of(0, 2**26),
-        name="groups",
-    )(row_pack, col_pack)
 
 
 def across(values, step):
@@ -2280,6 +2447,11 @@
     expand_up = [own_columns(4 * sub + i * ff_sub, ff_sub) for i in range(2)]
     reduce_low = own_columns(4 * sub + 2 * ff_sub, ff_sub)
 
+    diagonal_up = jnp.concatenate(
+        [
+            jnp.pad(up, ((0, 0), (i * local, (2 - i) * local))) for i, up in enumerate(qkv_up)
+        ]
+    )
     qkv_up = jnp.concatenate(qkv_up)
     qkv_w = merge_qkv(place, qkv_all, qkv_other, qkv_low, qkv_up)
     attn_w = merge_out(place, [attn_all, attn_other], attn_low, attn_up)
@@ -2335,52 +2507,35 @@
     d_query, d_key, d_value, q_sums, k_sums = attend_back(
         prefix, query, d_mixed, mixed, log_total, key, value
     )
-    attn_inner = sum_row(dot_of(attn_low, mixed, 1, 1)).astype(BF)
-    reduce_inner = sum_row(reduce_inner).astype(BF)
-    d_expand_inner = sum_row(d_expand_inner).astype(BF)
-    g_reduce_up = ADAPTER_FACTOR * dot_of(reduce_inner, result_parts[0], 1, 0)
-    g_reduce_low = dot_of(d_reduce_inner, act, 1, 0)
-    g_expand_low = dot_of(d_expand_inner, hidden_parts[0], 1, 0)
-    g_attn_up = ADAPTER_FACTOR * dot_of(attn_inner, branch_parts[0], 1, 0)
-    g_attn_low = dot_of(d_attn_inner, mixed, 1, 0)
-    input_grad, g_qkv_low, g_qkv_up = input_call(
+    partials = jnp.concatenate(
+        [dot_of(attn_low, mixed, 1, 1), reduce_inner, d_expand_inner]
+    ).astype(BF)
+    input_grad, every_row, every_col = input_call(
         raw,
         d_query,
         d_key,
         d_value,
+        act,
+        mixed,
+        branch_parts[0],
+        hidden_parts[0],
+        result_parts[0],
         qkv_w,
         d_hidden,
+        tokens,
         scale,
         q_sums,
         k_sums,
         gains,
         cosine,
         sine,
-        tokens,
         qkv_inner,
-        qkv_up,
-    )
-
-    def by_col(grad):
-        return grad.reshape(16, cols, -1).transpose(1, 0, 2)
-
-    row_pack = jnp.concatenate([g_qkv_low, g_attn_up, g_expand_low, g_reduce_up], axis=0)
-    col_pack = jnp.concatenate(
-        [
-            by_col(grad)
-            for grad in (
-                g_qkv_up[:16],
-                g_qkv_up[16:32],
-                g_qkv_up[32:],
-                g_attn_low,
-                g_expand_up[:16],
-                g_expand_up[16:],
-                g_reduce_low,
-            )
-        ],
-        axis=2,
-    )
-    every_row, every_col = groups_call(row_pack.astype(BF), col_pack.astype(BF))
+        diagonal_up,
+        partials,
+        jnp.concatenate([d_attn_inner, d_reduce_inner]),
+        g_expand_up,
+    )
+
     place_of = jnp.arange(2 * cols, dtype=jnp.int32)
     row_place = (pair ^ (place_of % 2)) * cols + (col - place_of // 2 + cols) % cols
     col_place = (pair ^ (place_of // cols)) * cols + place_of % cols

time: 923 us -> 883 us (0.957)
  Pallas kernels: 841 us -> 822 us
  matrix products: 11.1 us -> 0.64 us
    pallas_call x1 -> x0, Pallas kernels: 28.8 us -> none  [groups_call(): pl.pallas_call(groups_kernel, out_shape=[jax.ShapeDtypeStruct((cols, 2, *...]
    pallas_call x1, Pallas kernels: 73.7 us -> 93.8 us  [input_call(): pl.pallas_call(input_kernel, out_shape=[jax.ShapeDtypeStruct((rows, width...]
    dot_general x6 -> x1, matrix products: 11.1 us -> 0.64 us  [dot_of(): lax.dot_general(left, right, (((left_dim,), (right_dim,)), ((), ())), pre...]
  transfers between devices with their start and end apart: 13 -> 7, of which waited for: 5 -> 3; matrix products, arithmetic and copies ran while one was open for 3% -> 2% of each run, Pallas kernels for 86% -> 43%
where the time goes in v5:
time: 883 us; the launch traced here: 872 us
  Pallas kernels  822 us (93%)
  other arithmetic  16.2 us (2%)
  between operations  15.2 us (2%)
  local copies, waits for them, and re-layouts  11.5 us (1%)
    pallas_call x1, Pallas kernels, backward_call(): pl.pallas_call(backward_kernel, out_shape=[jax.ShapeDtypeStruct((rows, wi...  131 us
    pallas_call x1, Pallas kernels, branch_call(): pl.pallas_call(branch_kernel, out_shape=[jax.ShapeDtypeStruct((rows, loca...  127 us
    pallas_call x1, Pallas kernels, forward_call(): pl.pallas_call(forward_kernel, out_shape=[wide] * 3 + [part, jax.ShapeDty...  125 us
    pallas_call x1, Pallas kernels, input_call(): pl.pallas_call(input_kernel, out_shape=[jax.ShapeDtypeStruct((rows, width...  93.8 us
    pallas_call x1, Pallas kernels, second_deal(): pl.pallas_call(second_deal_kernel, out_shape=like_views([wide, (parts, ro...  84.4 us
    pallas_call x1, Pallas kernels, third_deal(): pl.pallas_call(third_deal_kernel, out_shape=like_views([(reduce_weight.sh...  73.4 us
    pallas_call x1, Pallas kernels, attend_back(): pl.pallas_call(attend_back_kernel, out_shape=(jax.ShapeDtypeStruct(query....  53.4 us
    pallas_call x1, Pallas kernels, front_call(): pl.pallas_call(front_kernel, out_shape=[jax.ShapeDtypeStruct((rows, wide)...  38.9 us
  transfers between devices with their start and end apart: 7, of which 3 were waited for; matrix products, arithmetic and copies ran while one was open for 2% of the time, Pallas kernels for 43%

profile of v5, /device:TPU:0, one launch (start us, length us, event | category | flops | bytes accessed | tf_op | source)
XLA Modules:
  0.0 872.0 jit_solution(9993498938986396703)
XLA Ops:
  7.2 15.8 %first_deal.1 = (bf16[4,3,256,128]{3,2,1,0:T(8,128)(2,1)}, bf16[4,64,512]{2,1,0:T(8,128)(2,1)}) custom-call(bf16[3,512,512]{2,1,0:T(8,128)(2,1)} %qkv_ref.4, bf16[512,512]{1,0:T(8,128)(2,1)} %attn_ref.5), custom_call_target="tpu_custom_call" | custom-call | bytes 67108864 | tf_op jit(solution)/shard_map/first_deal/pallas_call | solution.py:1990
  24.5 2.1 row_pack.1.pack_ref
  26.6 84.4 %second_deal.1 = (bf16[4,512,256]{2,1,0:T(8,128)(2,1)}, bf16[4,3,256,128]{3,2,1,0:T(8,128)(2,1)}, bf16[4,64,512]{2,1,0:T(8,128)(2,1)}, bf16[4,512,256]{2,1,0:T(8...) custom-call(bf16[3,512,512]{2,1,0:T(8,128)(2,1)} %qkv_ref.4, ...), custom_call_target="tpu_custom_call" | custom-call | bytes 134217728 | tf_op jit(solution)/shard_map/second_deal/pallas_call | solution.py:2050
  112.3 3.6 col_pack.1.pack_ref
  115.9 1.0 all-gather.11.cloned.1.call-done
  116.9 73.4 %third_deal.1 = (bf16[4,512,512]{2,1,0:T(8,128)(2,1)}, bf16[4,512,256]{2,1,0:T(8,128)(2,1)}, bf16[4,512,256]{2,1,0:T(8,128)(2,1)}, bf16[4,4,3,256,128]{4,3,2,1,0...) custom-call(bf16[2,512,2048]{2,1,0:T(8,128)(2,1)} %expand_ref.5, ...), custom_call_target="tpu_custom_call" | custom-call | bytes 134217728 | tf_op jit(solution)/shard_map/third_deal/pallas_call | solution.py:2175
  190.4 0.8 copy-done.2
  198.2 3.7 fusion
  201.9 1.9 pad_maximum_fusion
  204.5 9.5 %merge_qkv.1 = bf16[4,2,256,1536]{3,2,1,0:T(8,128)(2,1)} custom-call(s32[2]{0:T(128)} %pad_add_fusion.pair_ref, bf16[4,4,3,256,128]{4,3,2,1,0:T(8,128)(2,1)} %bitcast.79, bf16[4,4,3,256,128]{4,3,2,1,0:T(8,128)(2,1)} %get-tuple-element.96.other_ref, bf16[4,2,48,256]{3,2,1,0:T(8,128)(2,1)} %bitcast.87, bf16[48,512]{1,0:T(8,128)(2,1)} %pad_maximum_fusion.11.up_ref), custom_call_target="tpu_custom_call" | custom-call | bytes 12582912 | tf_op jit(solution)/shard_map/merge_qkv/pallas_call | solution.py:807
  214.6 38.9 %front.1 = (f32[2048,1536]{1,0:T(8,128)}, f32[8,2048]{1,0:T(8,128)}, bf16[48,2048]{1,0:T(8,128)(2,1)}, bf16[4,4,512,256]{3,2,1,0:T(8,128)(2,1)}) custom-call(bf16[2048,512]{1,0:T(8,128)(2,1)} %tokens_hbm.1, bf16[2048,512]{1,0:T(8,128)(2,1)} %get-tuple-element.88.x1, bf16[2048,512]{1,0:T(8,128)(2,1)} %get-tuple-element.89.x2, ...), custom_call_target="tpu_custom_call" | custom-call | flops 12884901888 | bytes 67108864 | tf_op jit(solution)/shard_map/front/pallas_call | solution.py:2249
  254.3 0.8 collective-permute-done
  255.0 0.8 add.58
  255.9 1.6 collective-permute-start.1
  259.5 7.3 merge_out.2.matrix_ref
  267.4 9.7 %rotate_rows.1 = (bf16[2048,512]{1,0:T(8,128)(2,1)}, bf16[2048,512]{1,0:T(8,128)(2,1)}, bf16[2048,512]{1,0:T(8,128)(2,1)}) custom-call(f32[2048,1536]{1,0:T(8,128)} %get-tuple-element.103.raw_ref.raw_hbm, f32[8,2048]{1,0:T(8,128)} %add_rsqrt_fusion.scale_ref, f32[2,512]{1,0:T(2,128)} %bitcast.102, f32[2048,128]{1,0:T(8,128)} %get-tuple-element.182.cos_ref, ...), custom_call_target="tpu_custom_call" | custom-call | tf_op jit(solution)/shard_map/rotate_rows/pallas_call | solution.py:588
  277.1 1.6 all-gather.17.cloned.1.call-done
  278.7 126.6 %branch.1 = (bf16[2048,512]{1,0:T(8,128)(2,1)}, f32[4,1,2048]{2,1,0:T(1,128)}, f32[2048,512]{1,0:T(8,128)}, f32[2048,512]{1,0:T(8,128)}, f32[8,8,256]{2,1,0:T(8,...) custom-call(bf16[2048,512]{1,0:T(8,128)(2,1)} %get-tuple-element.106, ...), custom_call_target="tpu_custom_call", output_to_operand_aliasing={{9}: (8, {})} | custom-call | flops 4294967296 | bytes 134217728 | tf_op jit(solution)/shard_map/branch/pallas_call | solution.py:1198
  405.3 11.1 %merge_expand.3 = bf16[4,1,512,2048]{3,2,1,0:T(8,128)(2,1)} custom-call(s32[2]{0:T(128)} %pad_add_fusion.pair_ref, bf16[4,4,512,256]{3,2,1,0:T(8,128)(2,1)} %bitcast.77, bf16[4,4,512,256]{3,2,1,0:T(8,128)(2,1)} %get-tuple-element.118.other_ref, bf16[4,1,16,512]{3,2,1,0:T(8,128)(2,1)} %bitcast.95, bf16[16,2048]{1,0:T(8,128)(2,1)} %bitcast.91), custom_call_target="tpu_custom_call" | custom-call | bytes 16777216 | tf_op jit(solution)/shard_map/merge_expand/pallas_call | solution.py:842
  416.5 11.3 %merge_expand.2 = bf16[4,1,512,2048]{3,2,1,0:T(8,128)(2,1)} custom-call(s32[2]{0:T(128)} %pad_add_fusion.pair_ref, bf16[4,4,512,256]{3,2,1,0:T(8,128)(2,1)} %bitcast.75, bf16[4,4,512,256]{3,2,1,0:T(8,128)(2,1)} %get-tuple-element.117.other_ref, bf16[4,1,16,512]{3,2,1,0:T(8,128)(2,1)} %bitcast.94, bf16[16,2048]{1,0:T(8,128)(2,1)} %bitcast.89), custom_call_target="tpu_custom_call" | custom-call | bytes 16777216 | tf_op jit(solution)/shard_map/merge_expand/pallas_call | solution.py:842
  428.4 9.0 %merge_out.3.reduce_hbm = bf16[2048,2048]{1,0:T(8,128)(2,1)} custom-call(s32[2]{0:T(128)} %pad_add_fusion.pair_ref, bf16[4,4,512,512]{3,2,1,0:T(8,128)(2,1)} %bitcast.80, bf16[4,16,512]{2,1,0:T(8,128)(2,1)} %get-tuple-element.172.refs_1_, bf16[16,2048]{1,0:T(8,128)(2,1)} %get-tuple-element.162.refs_2_.reduce_up_ref), custom_call_target="tpu_custom_call" | custom-call | bytes 16777216 | tf_op jit(solution)/shard_map/merge_out/pallas_call | solution.py:868
  437.4 125.0 %forward.1 = (bf16[2048,2048]{1,0:T(8,128)(2,1)}, bf16[2048,2048]{1,0:T(8,128)(2,1)}, bf16[2048,2048]{1,0:T(8,128)(2,1)}, bf16[2048,512]{1,0:T(8,128)(2,1)}, bf1...) custom-call(bf16[2048,512]{1,0:T(8,128)(2,1)} %get-tuple-element.113, ...), custom_call_target="tpu_custom_call" | custom-call | flops 51539607552 | bytes 134217728 | tf_op jit(solution)/shard_map/forward/pallas_call | solution.py:1404
  562.5 130.5 %backward.1 = (f32[2048,512]{1,0:T(8,128)}, bf16[16,2048]{1,0:T(8,128)(2,1)}, f32[32,2048]{1,0:T(8,128)}, f32[32,2048]{1,0:T(8,128)}, bf16[2048,512]{1,0:T(8,128...) custom-call(bf16[2048,512]{1,0:T(8,128)(2,1)} %get-tuple-element.122.x0.result_hbm, ...), custom_call_target="tpu_custom_call" | custom-call | flops 51539607552 | bytes 134217728 | tf_op jit(solution)/shard_map/backward/pallas_call | solution.py:1575
  693.0 1.0 convert.11
  694.0 10.1 %mixed_back.1 = (bf16[2048,512]{1,0:T(8,128)(2,1)}, bf16[16,2048]{1,0:T(8,128)(2,1)}) custom-call(bf16[2048,512]{1,0:T(8,128)(2,1)} %get-tuple-element.131.x0.branch_hbm, bf16[2048,512]{1,0:T(8,128)(2,1)} %get-tuple-element.132.x1, bf16[2048,512]{1,0:T(8,128)(2,1)} %get-tuple-element.133.x2, bf16[2048,512]{1,0:T(8,128)(2,1)} %get-tuple-element.134.x3, ...), custom_call_target="tpu_custom_call" | custom-call | flops 4294967296 | bytes 10485760 | tf_op jit(solution)/shard_map/mixed_back/pallas_call | solution.py:900
  704.1 1.5 pad_maximum_fusion.6.d_inner_ref
  705.7 53.4 %attend_back.1 = (f32[2048,512]{1,0:T(8,128)}, f32[2048,512]{1,0:T(8,128)}, f32[2048,512]{1,0:T(8,128)}, f32[4,1,2048]{2,1,0:T(1,128)}, f32[4,1,2048]{2,1,0:T(1,128)}) custom-call(s32[1]{0:T(128)} %dynamic_slice.12.prefix_ref, bf16[2048,512]{1,0:T(8,128)(2,1)} %get-tuple-element.106.q_ref, bf16[2048,512]{1,0:T(8,128)(2,1)} %get-tuple-element.135.grad_ref, ...), custom_call_target="tpu_custom_call" | custom-call | flops 15032385536 | bytes 25165824 | tf_op jit(solution)/shard_map/attend_back/pallas_call | solution.py:538
  759.8 93.8 %input_grad.1 = (f32[2048,512]{1,0:T(8,128)}, bf16[4,2,112,512]{3,2,1,0:T(8,128)(2,1)}, bf16[4,2,4,16,2048]{4,3,2,1,0:T(8,128)(2,1)}) custom-call(f32[2048,1536]{1,0:T(8,128)} %get-tuple-element.103.raw_ref.raw_hbm, f32[2048,512]{1,0:T(8,128)} %get-tuple-element.138.dq_hbm, f32[2048,512]{1,0:T(8,128)} %get-tuple-element.139.dk_hbm, ...), custom_call_target="tpu_custom_call" | custom-call | flops 12884901888 | bytes 67108864 | tf_op jit(solution)/shard_map/input_grad/pallas_call | solution.py:1860
  853.6 6.5 finish.1
  860.1 1.3 copy.100
  861.4 1.6 copy-done.1
  863.0 2.0 copy.101
  (82 shorter events, 15.1 us)
Async XLA Ops:
  7.2 16.7 %copy-start.14 = (s32[8]{0:T(128)S(1)}, s32[8]{0:T(128)}, u32[]{:S(2)}) copy-start(s32[8]{0:T(128)} %param.35) | copy-start | bytes 100
  7.2 108.7 %all-gather.13.cloned.1.call-start = ((), (), s32[]{:S(2)}) async-start(), calls=%async_computation.1 | async-start | bytes 1310720 | tf_op jit(solution)/shard_map/all_gather | solution.py:2345
  23.1 93.8 %all-gather.11.cloned.1.call-start = ((), (), s32[]{:S(2)}) async-start(), calls=%async_computation | async-start | bytes 3932160 | tf_op jit(solution)/shard_map/all_gather | solution.py:2345
  23.9 190.8 %all-gather.15.cloned.1.call-start = ((), (), s32[]{:S(2)}) async-start(), calls=%async_computation.2 | async-start | bytes 5242880 | tf_op jit(solution)/shard_map/all_gather | solution.py:2345
  111.0 167.7 %all-gather.17.cloned.1.call-start = ((), (), s32[]{:S(2)}) async-start(), calls=%async_computation.3 | async-start | bytes 5242880 | tf_op jit(solution)/shard_map/all_gather | solution.py:2345
  111.6 316.8 %all-gather.19.cloned.1.call-start = ((), (), s32[]{:S(2)}) async-start(), calls=%async_computation.4 | async-start | bytes 10485760 | tf_op jit(solution)/shard_map/all_gather | solution.py:2345
  190.3 0.9 copy-start.2
  190.3 0.9 copy-start.4
  190.3 1.0 copy-start.5
  190.4 1.0 copy-start.6
  190.4 2.0 copy-start.13
  191.5 10.5 %copy-start.7 = (bf16[48,2048]{1,0:T(8,128)(2,1)}, bf16[48,2048]{1,0:T(8,128)(2,1)S(1)}, u32[]{:S(2)}) copy-start(bf16[48,2048]{1,0:T(8,128)(2,1)S(1)} %slice.54.low_ref) | copy-start | bytes 589828
  201.9 1.9 copy-start.10
  253.5 1.5 collective-permute-start
  254.3 12.5 %copy-start.9 = (bf16[4,2,8,512]{3,2,0,1:T(8,128)(2,1)}, bf16[4,2,8,512]{3,2,0,1:T(8,128)(2,1)S(1)}, u32[]{:S(2)}) copy-start(bf16[4,2,8,512]{3,2,0,1:T(8,128)(2,1)S(1)} %copy.78) | copy-start | bytes 196612
  254.3 12.5 %copy-start.8 = (bf16[4,2,8,512]{3,2,0,1:T(8,128)(2,1)}, bf16[4,2,8,512]{3,2,0,1:T(8,128)(2,1)S(1)}, u32[]{:S(2)}) copy-start(bf16[4,2,8,512]{3,2,0,1:T(8,128)(2,1)S(1)} %copy.77) | copy-start | bytes 196612
  255.9 10.9 %collective-permute-start.1 = (f32[8,2048]{1,0:T(8,128)S(1)}, f32[8,2048]{1,0:T(8,128)S(1)}, u32[]{:S(2)}, u32[]{:S(2)}) collective-permute-start(f32[8,2048]{1,0:T(8,128)S(1)} %add.58), channel_id=1, source_target_pairs={{0,8},{4,12},{8,0},{12,4},{1,9},{5,13},{9,1},{13,5},{2,10},{6,14},... | collective-permute-start | bytes 196616 | tf_op jit(solution)/shard_map/ppermute | solution.py:2336
  416.5 11.3 %copy-start = (bf16[2048,512]{1,0:T(8,128)(2,1)S(1)}, bf16[2048,512]{1,0:T(8,128)(2,1)}, u32[]{:S(2)}) copy-start(bf16[2048,512]{1,0:T(8,128)(2,1)} %get-tuple-element.136.out_ref.mixed_hbm) | copy-start | bytes 6291460
  562.4 131.5 %copy-start.11 = (f32[16,2048]{1,0:T(8,128)S(1)}, f32[16,2048]{1,0:T(8,128)}, u32[]{:S(2)}) copy-start(f32[16,2048]{1,0:T(8,128)} %get-tuple-element.146) | copy-start | bytes 393220
  694.0 10.1 %copy-start.12 = (bf16[16,2048]{1,0:T(8,128)(2,1)S(1)}, bf16[16,2048]{1,0:T(8,128)(2,1)}, u32[]{:S(2)}) copy-start(bf16[16,2048]{1,0:T(8,128)(2,1)} %get-tuple-element.149) | copy-start | bytes 196612
  853.6 6.5 copy-start.3
  860.1 2.9 copy-start.1
Sparse Core Ops, SparseCore 0:
  23.2 29.0 all-gather.12
  53.9 62.9 all-gather.10
  118.5 79.3 all-gather.14
  199.4 79.2 all-gather.16
  280.1 148.1 all-gather.18

commit v6 on v5

--- a/solution.py
+++ b/solution.py
@@ -415,9 +415,10 @@
 LOG2E = 1.4426950408889634
 Q_BLOCK = 512
 K_BLOCK = 512
-HEADS_AT_ONCE = 2
 BF = jnp.bfloat16
 F32 = jnp.float32
+VMEM_SPEC = pl.BlockSpec(memory_space=pltpu.VMEM)
+ANY_SPEC = pl.BlockSpec(memory_space=pl.ANY)
 
 
 def dot_of(left, right, left_dim, right_dim, out=F32):
@@ -469,11 +470,15 @@
 
 
 def attend_back_kernel(
-    prefix_ref,
     q_ref,
-    grad_ref,
+    x0,
+    x1,
+    x2,
+    x3,
+    matrix_ref,
+    up_ref,
     out_ref,
-    log_ref,
+    probs_hbm,
     k_ref,
     v_ref,
     dq_ref,
@@ -481,20 +486,36 @@
     dv_ref,
     q_sum_ref,
     k_sum_ref,
+    inner_ref,
+    grad_ref,
+    probs_ref,
+    sems,
 ):
-    rows = q_ref.shape[0]
-    start = pl.program_id(1) * rows
-    prefix = prefix_ref[0]
-    blocks = lax.div(jnp.maximum(start + rows, prefix) + K_BLOCK - 1, K_BLOCK)
-
-    @pl.when(pl.program_id(1) == 0)
+    rows, local = q_ref.shape
+    group = pl.program_id(0)
+    heads = [slice(at, at + HEAD) for at in range(0, local, HEAD)]
+    blocks = jnp.maximum((group + 1) * rows, SEQUENCE_LENGTH // 2) // K_BLOCK
+
+    def fetch(index):
+        slot = lax.rem(index, 2)
+        return [
+            pltpu.make_async_copy(
+                probs_hbm.at[h, group, index], probs_ref.at[slot, h], sems.at[slot, h]
+            )
+            for h in range(len(heads))
+        ]
+
+    for copy in fetch(0):
+        copy.start()
+    left = jnp.concatenate([x0[...], x1[...], x2[...], x3[...]], axis=1)
+    grad_ref[...] = dot_of(left, matrix_ref[...], 1, 1).astype(BF)
+    inner_ref[...] = (ADAPTER_FACTOR * dot_of(up_ref[...], left, 1, 1)).astype(BF)
+
+    @pl.when(group == 0)
     def _():
         dk_ref[...] = jnp.zeros_like(dk_ref)
         dv_ref[...] = jnp.zeros_like(dv_ref)
 
-    limit = jnp.maximum(lax.broadcasted_iota(jnp.int32, (1, rows), 1) + start, prefix - 1)
-    key_pos = lax.broadcasted_iota(jnp.int32, (K_BLOCK, rows), 0)
-    heads = [slice(h * HEAD, (h + 1) * HEAD) for h in range(HEADS_AT_ONCE)]
     deltas = [
         row_sums(grad_ref[:, lanes].astype(F32) * out_ref[:, lanes].astype(F32)) for lanes in heads
     ]
@@ -502,15 +523,22 @@
     def body(index, carry):
         at = pl.multiple_of(index * K_BLOCK, K_BLOCK)
         span = pl.ds(at, K_BLOCK)
-        seen = key_pos <= limit - at
+        slot = lax.rem(index, 2)
+        for copy in fetch(index):
+            copy.wait()
+
+        @pl.when(index + 1 < blocks)
+        def _():
+            for copy in fetch(index + 1):
+                copy.start()
+
         sums = []
         for h, lanes in enumerate(heads):
             query, grad, key = q_ref[:, lanes], grad_ref[:, lanes], k_ref[span, lanes]
-            scores = dot_of(key, query, 1, 1) * (HEAD**-0.5 * LOG2E)
-            probs = jnp.where(seen, jnp.exp2(scores - log_ref[h]), 0.0)
+            probs = probs_ref[slot, h]
             d_probs = dot_of(v_ref[span, lanes], grad, 1, 1)
-            d_scores = (probs * (d_probs - deltas[h])).astype(BF)
-            dv_ref[span, lanes] += dot_of(probs.astype(BF), grad, 1, 0)
+            d_scores = (probs.astype(F32) * (d_probs - deltas[h])).astype(BF)
+            dv_ref[span, lanes] += dot_of(probs, grad, 1, 0)
             dk_ref[span, lanes] += dot_of(d_scores, query, 1, 0)
             sums.append(carry[h] + dot_of(d_scores, key, 0, 0))
         return tuple(sums)
@@ -521,7 +549,7 @@
         dq_ref[:, lanes] = d_query
         q_sum_ref[h] = row_sums(d_query * q_ref[:, lanes].astype(F32))
 
-    @pl.when(pl.program_id(1) == pl.num_programs(1) - 1)
+    @pl.when(group == pl.num_programs(0) - 1)
     def _():
         for h, lanes in enumerate(heads):
             d_key = dk_ref[:, lanes] * HEAD**-0.5
@@ -529,12 +557,15 @@
             k_sum_ref[h] = row_sums(d_key * k_ref[:, lanes].astype(F32))
 
 
-def attend_back(prefix, query, grad, mixed, log_total, key, value):
-    rows, length, heads = query.shape[0], key.shape[0], query.shape[1] // HEAD
-    wide = HEADS_AT_ONCE * HEAD
-    q_spec = pl.BlockSpec((Q_BLOCK, wide), lambda h, i, p: (i, h))
-    k_spec = pl.BlockSpec((length, wide), lambda h, i, p: (0, h))
-    row_spec = pl.BlockSpec((HEADS_AT_ONCE, 1, Q_BLOCK), lambda h, i, p: (h, 0, i))
+def attend_back(query, lefts, matrix, up, mixed, probs, key, value):
+    rows, length, local = query.shape[0], key.shape[0], query.shape[1]
+    heads = local // HEAD
+    q_spec = pl.BlockSpec((Q_BLOCK, local), lambda i: (i, 0))
+    x_spec = pl.BlockSpec((Q_BLOCK, lefts[0].shape[1]), lambda i: (i, 0))
+
+    def whole(array):
+        return pl.BlockSpec(array.shape, lambda i: (0,) * array.ndim)
+
     return pl.pallas_call(
         attend_back_kernel,
         out_shape=(
@@ -543,26 +574,32 @@
             jax.ShapeDtypeStruct(key.shape, F32),
             jax.ShapeDtypeStruct((heads, 1, rows), F32),
             jax.ShapeDtypeStruct((heads, 1, length), F32),
+            jax.ShapeDtypeStruct((16, rows), BF),
         ),
-        grid_spec=pltpu.PrefetchScalarGridSpec(
-            num_scalar_prefetch=1,
-            grid=(heads // HEADS_AT_ONCE, rows // Q_BLOCK),
-            in_specs=[q_spec, q_spec, q_spec, row_spec, k_spec, k_spec],
-            out_specs=[
-                q_spec,
-                k_spec,
-                k_spec,
-                row_spec,
-                pl.BlockSpec((HEADS_AT_ONCE, 1, length), lambda h, i, p: (h, 0, 0)),
-            ],
-        ),
+        grid=(rows // Q_BLOCK,),
+        in_specs=[q_spec]
+        + [x_spec] * 4
+        + [whole(matrix), whole(up), q_spec, ANY_SPEC, whole(key), whole(value)],
+        out_specs=[
+            q_spec,
+            whole(key),
+            whole(value),
+            pl.BlockSpec((heads, 1, Q_BLOCK), lambda i: (0, 0, i)),
+            pl.BlockSpec((heads, 1, length), lambda i: (0, 0, 0)),
+            pl.BlockSpec((16, Q_BLOCK), lambda i: (0, i)),
+        ],
+        scratch_shapes=[
+            pltpu.VMEM((Q_BLOCK, local), BF),
+            pltpu.VMEM((2, heads, K_BLOCK, Q_BLOCK), BF),
+            pltpu.SemaphoreType.DMA((2, heads)),
+        ],
         cost_estimate=pl.CostEstimate(
             flops=7 * rows * length * heads * HEAD,
             bytes_accessed=24 * rows * heads * HEAD,
-            transcendentals=rows * length * heads,
+            transcendentals=0,
         ),
         name="attend_back",
-    )(prefix, query, grad, mixed, log_total, key, value)
+    )(query, *lefts, matrix, up, mixed, probs, key, value)
 
 
 def rotate_kernel(raw_ref, scale_ref, gain_ref, cos_ref, sin_ref, q_ref, k_ref, v_ref):
@@ -883,37 +920,6 @@
     )(pair, *pieces, low.reshape(16, takes * cols, rows).transpose(1, 0, 2), up)
 
 
-def mixed_back_kernel(x0, x1, x2, x3, matrix_ref, up_ref, out_ref, inner_ref):
-    left = jnp.concatenate([x0[...], x1[...], x2[...], x3[...]], axis=1)
-    out_ref[...] = dot_of(left, matrix_ref[...], 1, 1).astype(BF)
-    inner_ref[...] = (ADAPTER_FACTOR * dot_of(up_ref[...], left, 1, 1)).astype(BF)
-
-
-def mixed_back(lefts, matrix, up):
-    rows, width = lefts[0].shape
-    local = matrix.shape[0]
-    tile = row_tile(rows)
-
-    def whole(array):
-        return pl.BlockSpec(array.shape, lambda m: (0, 0))
-
-    return pl.pallas_call(
-        mixed_back_kernel,
-        out_shape=[
-            jax.ShapeDtypeStruct((rows, local), BF),
-            jax.ShapeDtypeStruct((16, rows), BF),
-        ],
-        grid=(rows // tile,),
-        in_specs=[pl.BlockSpec((tile, width), lambda m: (m, 0))] * 4 + [whole(matrix), whole(up)],
-        out_specs=[
-            pl.BlockSpec((tile, local), lambda m: (m, 0)),
-            pl.BlockSpec((16, tile), lambda m: (0, m)),
-        ],
-        cost_estimate=cost_of(8 * rows * width * local, 8 * width * (rows + local)),
-        name="mixed_back",
-    )(*lefts, matrix, up)
-
-
 BLOCK = 256
 RING = 5
 
@@ -963,7 +969,16 @@
 
 
 def run_blocks(
-    count, bufs, compute, stats, finish, own_ref=None, arrived=None, extra=None, own_rows=None
+    count,
+    bufs,
+    compute,
+    stats,
+    finish,
+    own_ref=None,
+    arrived=None,
+    extra=None,
+    own_rows=None,
+    idle=None,
 ):
     pair_out, pair_in, far, side_out, side_in, near, pair_sem, side_sem, *rest = bufs
     gathers = own_ref is not None
@@ -1064,6 +1079,8 @@
         if gathers:
             stage(t - 3, normalise)
             stage(t - 4, pass_on)
+        if idle is not None:
+            pl.when(t >= 1)(lambda: idle(t - 1))
         return carry
 
     lax.fori_loop(0, count + (4 if gathers else 2), body, 0)
@@ -1110,35 +1127,35 @@
     tokens_ref,
     gain_ref,
     gate_all,
-    gate_part,
+    gate_other,
     upper_all,
-    upper_rest,
+    upper_other,
     mixed_ref,
-    log_ref,
     branch_ref,
     hidden_ref,
     stat_ref,
     own_ref,
     *rest,
 ):
-    arrived, halves, rest = rest[:3], rest[3:5], rest[5:]
-    swap_sems, local_sem, *bufs = rest
+    arrived, halves, probs_hbm, rest = rest[:3], rest[3:5], rest[5], rest[6:]
+    swap_sems, stage, stage_sem, log_ref, *bufs = rest
     width = own_ref.shape[1]
     count = own_ref.shape[0] // BLOCK
     greet_all([peer(step) for step in (1, 2, 3)] + [other_of_pair()])
-    later = range(2, gate_all.shape[0])
-    swaps = exchange_halves(
-        gate_all, None, halves[0], swap_sems.at[0], local_sem.at[0], later
-    )
-    swaps += exchange_halves(upper_all, upper_rest, halves[1], swap_sems.at[1], local_sem.at[1])
+    cols = gate_all.shape[0]
+    swaps = exchange_halves(gate_all, halves[0], swap_sems.at[0], range(2, cols))
+    swaps += exchange_halves(upper_all, halves[1], swap_sems.at[1], range(1, cols))
     for copy in swaps:
         copy.start()
 
-    heads = log_ref.shape[0]
+    heads = mixed_ref.shape[1] // HEAD
+    key_pos = lax.broadcasted_iota(jnp.int32, (K_BLOCK, Q_BLOCK), 0)
+
+    def blocks_of(group):
+        return jnp.maximum((group + 1) * Q_BLOCK, SEQUENCE_LENGTH // 2) // K_BLOCK
 
     def attend(group):
         rows = span_of(group, Q_BLOCK)
-        reach = jnp.maximum((group + 1) * Q_BLOCK, SEQUENCE_LENGTH // 2)
 
         def head(h, carry):
             lanes = span_of(h, HEAD)
@@ -1147,7 +1164,7 @@
                 limit_ref[:, rows],
                 lambda at: k_ref[pl.ds(at, K_BLOCK), lanes],
                 lambda at: v_ref[pl.ds(at, K_BLOCK), lanes],
-                reach // K_BLOCK,
+                blocks_of(group),
             )
             mixed_ref[rows, lanes] = mixed.T.astype(BF)
             log_ref[h, :, rows] = logs
@@ -1155,8 +1172,48 @@
 
         lax.fori_loop(0, heads, head, 0)
 
+    ratio = Q_BLOCK // BLOCK
+    share = heads // ratio
+
+    def keep_some(turn):
+        group = turn // ratio
+        rows = span_of(group, Q_BLOCK)
+        blocks = blocks_of(group)
+        first = lax.rem(turn, ratio) * share
+
+        def head(h, carry):
+            lanes = span_of(h, HEAD)
+
+            def out(index):
+                slot = lax.rem(index, 2)
+                return pltpu.make_async_copy(
+                    stage.at[slot], probs_hbm.at[h, group, index], stage_sem.at[slot]
+                )
+
+            def keep(index, carry):
+                @pl.when(index >= 2)
+                def _():
+                    out(index - 2).wait()
+
+                at = pl.multiple_of(index * K_BLOCK, K_BLOCK)
+                scores = dot_of(k_ref[pl.ds(at, K_BLOCK), lanes], q_ref[rows, lanes], 1, 1)
+                powers = jnp.exp2(scores * (HEAD**-0.5 * LOG2E) - log_ref[h, :, rows])
+                seen = key_pos <= limit_ref[:, rows] - at
+                stage[lax.rem(index, 2)] = jnp.where(seen, powers, 0.0).astype(BF)
+                out(index).start()
+                return carry
+
+            lax.fori_loop(0, blocks, keep, 0)
+            out(blocks - 2).wait()
+            out(blocks - 1).wait()
+            return carry
+
+        lax.fori_loop(first, first + share, head, 0)
+
+    def idle(turn):
+        pl.when(turn < count)(lambda: keep_some(turn))
+
     def compute(c, put):
-        ratio = Q_BLOCK // BLOCK
         pl.when(lax.rem(c, ratio) == 0)(lambda: attend(c // ratio))
         left = mixed_ref[pl.ds(pl.multiple_of(c * BLOCK, BLOCK), BLOCK), :]
         for block in (1, 3, 2, 0):
@@ -1173,12 +1230,8 @@
         hidden_ref[rows, :] = hidden
         return hidden.astype(BF)
 
-    run_blocks(count, bufs, compute, stats, finish, own_ref, arrived)
+    run_blocks(count, bufs, compute, stats, finish, own_ref, arrived, idle=idle)
     wait_all(swaps)
-
-
-VMEM_SPEC = pl.BlockSpec(memory_space=pltpu.VMEM)
-ANY_SPEC = pl.BlockSpec(memory_space=pl.ANY)
 
 
 def talk_params(number):
@@ -1199,21 +1252,27 @@
         branch_kernel,
         out_shape=[
             jax.ShapeDtypeStruct((rows, local), BF),
-            jax.ShapeDtypeStruct((local // HEAD, 1, rows), F32),
             whole,
             whole,
             jax.ShapeDtypeStruct((count, 8, BLOCK), F32),
         ]
         + [part] * 4
-        + [half] * 2,
+        + [half] * 2
+        + [
+            jax.ShapeDtypeStruct(
+                (local // HEAD, rows // Q_BLOCK, rows // K_BLOCK, K_BLOCK, Q_BLOCK), BF
+            )
+        ],
         in_specs=[VMEM_SPEC] * 7 + [ANY_SPEC] * 4,
-        out_specs=[VMEM_SPEC] * 6 + [ANY_SPEC] * 5,
+        out_specs=[VMEM_SPEC] * 5 + [ANY_SPEC] * 6,
         scratch_shapes=[
             pltpu.SemaphoreType.DMA((2, 2, cols - 1)),
+            pltpu.VMEM((2, K_BLOCK, Q_BLOCK), BF),
             pltpu.SemaphoreType.DMA((2,)),
+            pltpu.VMEM((local // HEAD, 1, rows), F32),
         ]
         + exchange_scratch(count, width, True),
-        input_output_aliases={8: 9},
+        input_output_aliases={8: 8, 10: 9},
         compiler_params=talk_params(0),
         cost_estimate=cost_of(8 * rows * width * matrix.shape[0], 2**27),
         name="branch",
@@ -1303,23 +1362,25 @@
     width = own_ref.shape[1]
     count = own_ref.shape[0] // BLOCK
     ff = gate_w.shape[1]
-    tile = min(1024, ff)
+    tile = ff // 2
     loads = [
         pltpu.make_async_copy(source, target, w_sem.at[index])
         for index, (source, target) in enumerate(
             (
-                (gate_hbm, gate_w),
-                (upper_hbm, upper_w),
+                (gate_hbm.at[:, :tile], gate_w.at[:, :tile]),
+                (upper_hbm.at[:, :tile], upper_w.at[:, :tile]),
                 (reduce_hbm, reduce_w),
                 (cot_hbm, cot_ref),
                 (hidden_hbm, hidden_ref),
+                (gate_hbm.at[:, tile:], gate_w.at[:, tile:]),
+                (upper_hbm.at[:, tile:], upper_w.at[:, tile:]),
             )
         )
     ]
     start_left, wait_left = load_lefts((x0, x1, x2, x3), lefts, x_sem, count)
     start_left(0)
-    for load in loads:
-        load.start()
+    for index in (0, 1, 5, 6, 2, 3, 4):
+        loads[index].start()
     layer_rows = rows_out(layer_ref, layer_out, r_sem, 0)
     own_rows = rows_out(own_ref, own_out, r_sem, 1)
     greet()
@@ -1346,6 +1407,11 @@
                 out(c - 2).wait()
 
         def tiles(n, carry):
+            @pl.when(jnp.logical_and(c == 0, n == 1))
+            def _():
+                loads[5].wait()
+                loads[6].wait()
+
             at = pl.ds(pl.multiple_of(n * tile, tile), tile)
             left = lefts[slot]
             gate = dot_of(left, gate_w[:, at], 1, 0)
@@ -1424,7 +1490,7 @@
             pltpu.VMEM((rows, width), BF),
             pltpu.VMEM((rows, width), BF),
             pltpu.VMEM((rows, width), BF),
-            pltpu.SemaphoreType.DMA((5,)),
+            pltpu.SemaphoreType.DMA((7,)),
             pltpu.SemaphoreType.DMA((2, 4)),
             pltpu.SemaphoreType.DMA((3, 2)),
             pltpu.SemaphoreType.DMA((2, count)),
@@ -1467,16 +1533,17 @@
     count = own_ref.shape[0] // BLOCK
     ff = gate_w.shape[1]
     up_grad_ref[...] = jnp.zeros_like(up_grad_ref)
-    tile = min(1024, ff)
+    tile = ff // 2
     loads = [
         pltpu.make_async_copy(source, target, w_sem.at[index])
         for index, (source, target) in enumerate(
             (
-                (reduce_hbm, reduce_w),
+                (reduce_hbm.at[:tile], reduce_w.at[:tile]),
                 (gate_hbm, gate_w),
                 (upper_hbm, upper_w),
                 (cot_hbm, cot_ref),
                 (branch_hbm, branch_ref),
+                (reduce_hbm.at[tile:], reduce_w.at[tile:]),
             )
         )
     ]
@@ -1488,8 +1555,8 @@
     start_left(0)
     for one in ins:
         one(0).start()
-    for load in loads:
-        load.start()
+    for index in (0, 5, 1, 2, 3, 4):
+        loads[index].start()
     hidden_rows = rows_out(d_hidden_ref, d_hidden_out, r_sem, 0)
     own_rows = rows_out(own_ref, own_out, r_sem, 1)
     greet()
@@ -1511,6 +1578,10 @@
             loads[0].wait()
 
         def tiles(n, carry):
+            @pl.when(jnp.logical_and(c == 0, n == 1))
+            def _():
+                loads[5].wait()
+
             at = pl.ds(pl.multiple_of(n * tile, tile), tile)
             d_act = dot_of(lefts[slot], reduce_w[at, :], 1, 1)
             gate = gate_buf[slot, :, at].astype(F32)
@@ -1596,7 +1667,7 @@
             pltpu.VMEM((rows, width), BF),
             pltpu.VMEM((rows, width), F32),
             pltpu.VMEM((rows, width), BF),
-            pltpu.SemaphoreType.DMA((5,)),
+            pltpu.SemaphoreType.DMA((6,)),
             pltpu.SemaphoreType.DMA((2, 4)),
             pltpu.SemaphoreType.DMA((2, 2)),
             pltpu.SemaphoreType.DMA((2, count)),
@@ -1975,44 +2046,66 @@
     return [jax.ShapeDtypeStruct((4, *shape), BF) for shape in shapes]
 
 
-def first_deal_kernel(qkv_ref, attn_ref, qkv_out, attn_out, sems):
+def attn_deal_kernel(attn_ref, attn_out, sems):
+    greet()
+    (copies,) = deal([attn_view(attn_ref, lax.axis_index("dp"))], [attn_out], sems)
+    start_all(copies)
+    wait_all(copies)
+
+
+def attn_deal(attn_weight):
+    return pl.pallas_call(
+        attn_deal_kernel,
+        out_shape=like_views([(attn_weight.shape[0] // 8, attn_weight.shape[1])])[0],
+        in_specs=[ANY_SPEC],
+        out_specs=ANY_SPEC,
+        scratch_shapes=[pltpu.SemaphoreType.DMA((2, 1, 4))],
+        compiler_params=talk_params(4),
+        cost_estimate=cost_of(0, 2**25),
+        name="attn_deal",
+    )(attn_weight)
+
+
+def first_deal_kernel(qkv_ref, expand_ref, qkv_out, gate_out, sems):
     half = lax.axis_index("dp")
     greet()
-    copies = deal([qkv_view(qkv_ref, half), attn_view(attn_ref, half)], [qkv_out, attn_out], sems)
+    copies = deal([qkv_view(qkv_ref, half), expand_view(expand_ref, 0, half)], [qkv_out, gate_out], sems)
     for one in copies:
         start_all(one)
     for one in copies:
         wait_all(one)
 
 
-def first_deal(qkv_weight, attn_weight):
+def first_deal(qkv_weight, expand_weight):
     parts, rows, columns = qkv_weight.shape
     return pl.pallas_call(
         first_deal_kernel,
         out_shape=like_views(
-            [(parts, rows // 2, columns // 4), (attn_weight.shape[0] // 8, attn_weight.shape[1])]
+            [
+                (parts, rows // 2, columns // 4),
+                (expand_weight.shape[1], expand_weight.shape[2] // 8),
+            ]
         ),
         in_specs=[ANY_SPEC] * 2,
         out_specs=[ANY_SPEC] * 2,
         scratch_shapes=[pltpu.SemaphoreType.DMA((2, 2, 4))],
-        compiler_params=talk_params(4),
+        compiler_params=talk_params(9),
         cost_estimate=cost_of(0, 2**26),
         name="first_deal",
-    )(qkv_weight, attn_weight)
+    )(qkv_weight, expand_weight)
 
 
 def second_deal_kernel(qkv_ref, attn_ref, expand_ref, tokens_ref, pack_ref, *rest):
-    *outs, t1, t2, t3, p1, p2, p3, sems, token_sem, pack_sem = rest
+    qkv_other, attn_other, upper_out, t1, t2, t3, p1, p2, p3, sems, token_sem, pack_sem = rest
     half = lax.axis_index("dp")
     greet()
-    gate, rest_qkv, rest_attn, upper = deal(
+    rest_qkv, rest_attn, upper = deal(
         [
-            expand_view(expand_ref, 0, half),
             qkv_view(qkv_ref, 1 - half),
             attn_view(attn_ref, 1 - half),
             expand_view(expand_ref, 1, half),
         ],
-        outs,
+        [qkv_other.at[0], attn_other.at[0], upper_out],
         sems,
     )
     gathers = []
@@ -2024,7 +2117,6 @@
                 send(targets[1], targets[2], one_sem, 2, 1),
             )
         )
-    start_all(gate)
     start_all(rest_qkv)
     start_all(rest_attn)
     for side, core, _ in gathers:
@@ -2034,7 +2126,7 @@
     for side, core, relay in gathers:
         side.wait_recv()
         relay.start()
-    for one in (gate, rest_qkv, rest_attn, upper):
+    for one in (rest_qkv, rest_attn, upper):
         wait_all(one)
     for side, core, relay in gathers:
         side.wait_send()
@@ -2042,26 +2134,23 @@
         relay.wait()
 
 
-def second_deal(qkv_weight, attn_weight, expand_weight, tokens, pack):
+def second_deal(qkv_weight, attn_weight, expand_weight, tokens, pack, cols):
     parts, rows, columns = qkv_weight.shape
     cut = expand_weight.shape[2] // 8
     wide = (expand_weight.shape[1], cut)
     sem = pltpu.SemaphoreType.DMA((2, 3))
     return pl.pallas_call(
         second_deal_kernel,
-        out_shape=like_views(
-            [
-                wide,
-                (parts, rows // 2, columns // 4),
-                (attn_weight.shape[0] // 8, attn_weight.shape[1]),
-                wide,
-            ]
-        )
+        out_shape=[
+            jax.ShapeDtypeStruct((cols, 4, parts, rows // 2, columns // 4), BF),
+            jax.ShapeDtypeStruct((cols, 4, attn_weight.shape[0] // 8, attn_weight.shape[1]), BF),
+            jax.ShapeDtypeStruct((4, *wide), BF),
+        ]
         + [jax.ShapeDtypeStruct(tokens.shape, BF)] * 3
         + [jax.ShapeDtypeStruct(pack.shape, BF)] * 3,
         in_specs=[ANY_SPEC] * 5,
-        out_specs=[ANY_SPEC] * 10,
-        scratch_shapes=[pltpu.SemaphoreType.DMA((2, 4, 4)), sem, sem],
+        out_specs=[ANY_SPEC] * 9,
+        scratch_shapes=[pltpu.SemaphoreType.DMA((2, 3, 4)), sem, sem],
         compiler_params=talk_params(5),
         cost_estimate=cost_of(0, 2**27),
         name="second_deal",
@@ -2090,14 +2179,11 @@
     return {"dp": 1 - lax.axis_index("dp")}
 
 
-def exchange_halves(whole, rest, out, sems, local_sem, steps=None):
+def exchange_halves(whole, out, sems, steps):
     cols = whole.shape[0]
     col = lax.axis_index("col")
     copies = []
-    for k in range(cols) if steps is None else steps:
-        if k == 0:
-            copies.append(pltpu.make_async_copy(rest, out.at[0], local_sem))
-            continue
+    for k in steps:
         place = lax.rem(col + k, cols)
         copies.append(copy_to(whole.at[place], out.at[k], sems, k - 1, other_of_pair()))
     return copies
@@ -2134,16 +2220,17 @@
 
 
 def third_deal_kernel(
-    expand_ref, reduce_ref, qkv_all, qkv_rest, attn_all, attn_rest, pack_ref, gain_ref, *rest
+    expand_ref, reduce_ref, qkv_all, qkv_other, attn_all, attn_other, pack_ref, gain_ref, *rest
 ):
-    *outs, qkv_out, attn_out, pack_out, gain_out = rest[:7]
+    reduce_out, gate_out, upper_out, qkv_out, attn_out, pack_out, gain_out = rest[:7]
     deal_sem, qkv_sem, attn_sem, pack_sem, gain_sem, local_sem = rest[7:]
     other = 1 - lax.axis_index("dp")
     me = lax.axis_index("row")
     greet_all(row_and_col_peers() + [other_of_pair()])
     sub = gain_out.shape[2]
-    swaps = exchange_halves(qkv_all, qkv_rest, qkv_out, qkv_sem, local_sem.at[0])
-    swaps += exchange_halves(attn_all, attn_rest, attn_out, attn_sem, local_sem.at[1])
+    steps = range(1, qkv_all.shape[0])
+    swaps = exchange_halves(qkv_all, qkv_out, qkv_sem, steps)
+    swaps += exchange_halves(attn_all, attn_out, attn_sem, steps)
     packs, wait_packs = send_round(lambda place: pack_ref.at[place], pack_out, pack_sem, local_sem.at[2])
     gains, wait_gains = send_round(
         lambda place: gain_ref.at[:, span_of(me, sub)], gain_out, gain_sem, local_sem.at[3]
@@ -2156,7 +2243,7 @@
             expand_view(expand_ref, 0, other),
             expand_view(expand_ref, 1, other),
         ],
-        outs,
+        [reduce_out, gate_out.at[0], upper_out.at[0]],
         deal_sem,
     )
     for one in copies:
@@ -2168,13 +2255,14 @@
     wait_all(swaps)
 
 
-def third_deal(expand_weight, reduce_weight, qkv_all, qkv_rest, attn_all, attn_rest, pack, gain):
+def third_deal(expand_weight, reduce_weight, qkv_all, qkv_other, attn_all, attn_other, pack, gain):
     wide = (expand_weight.shape[1], expand_weight.shape[2] // 8)
     cols = qkv_all.shape[0]
     round_sem = pltpu.SemaphoreType.DMA((2, cols - 1))
     return pl.pallas_call(
         third_deal_kernel,
-        out_shape=like_views([(reduce_weight.shape[0] // 4, reduce_weight.shape[1]), wide, wide])
+        out_shape=like_views([(reduce_weight.shape[0] // 4, reduce_weight.shape[1])])
+        + [jax.ShapeDtypeStruct((cols, 4, *wide), BF)] * 2
         + [
             jax.ShapeDtypeStruct(qkv_all.shape, BF),
             jax.ShapeDtypeStruct(attn_all.shape, BF),
@@ -2191,10 +2279,11 @@
             round_sem,
             pltpu.SemaphoreType.DMA((4,)),
         ],
+        input_output_aliases={3: 3, 5: 4},
         compiler_params=talk_params(6),
         cost_estimate=cost_of(0, 2**27),
         name="third_deal",
-    )(expand_weight, reduce_weight, qkv_all, qkv_rest, attn_all, attn_rest, pack, gain)
+    )(expand_weight, reduce_weight, qkv_all, qkv_other, attn_all, attn_other, pack, gain)
 
 
 def front_kernel(
@@ -2205,16 +2294,15 @@
     matrix_ref,
     low_ref,
     gate_all,
-    gate_rest,
+    gate_other,
     raw_ref,
     square_ref,
     inner_ref,
     gate_out,
     swap_sem,
-    local_sem,
 ):
     local = raw_ref.shape[1] // 3
-    first = exchange_halves(gate_all, gate_rest, gate_out, swap_sem, local_sem.at[0], range(2))
+    first = exchange_halves(gate_all, gate_out, swap_sem, range(1, 2))
 
     @pl.when(pl.program_id(0) == 0)
     def _():
@@ -2237,7 +2325,7 @@
         wait_all(first)
 
 
-def front_call(lefts, matrix, low, gate_all, gate_rest):
+def front_call(lefts, matrix, low, gate_all, gate_other):
     rows, width = lefts[0].shape
     wide = matrix.shape[1]
     tile = row_tile(rows)
@@ -2265,12 +2353,12 @@
         ],
         scratch_shapes=[
             pltpu.SemaphoreType.DMA((2, cols - 1)),
-            pltpu.SemaphoreType.DMA((1,)),
         ],
+        input_output_aliases={7: 3},
         compiler_params=talk_params(8),
         cost_estimate=cost_of(8 * rows * width * wide, 2**26),
         name="front",
-    )(*lefts, matrix, low, gate_all, gate_rest)
+    )(*lefts, matrix, low, gate_all, gate_other)
 
 
 def exchange_groups(row_ref, col_ref, rows_out, cols_out, sems):
@@ -2394,8 +2482,10 @@
     prefix = lax.dynamic_slice_in_dim(prefix_length, sequence, 1)
     cols_sets = lax.dynamic_slice_in_dim(adapter_set, pair * cols, cols)
 
+    attn_own = attn_deal(attn_weight)
+    qkv_own, gate_own = first_deal(after(qkv_weight, attn_own), expand_weight)
     row_pack = row_pack_of(
-        mine.reshape(1),
+        after(mine.reshape(1), qkv_own),
         qkv_lowrank.transpose(0, 1, 3, 2),
         attn_uprank,
         expand_lowrank.transpose(0, 1, 3, 2),
@@ -2411,10 +2501,9 @@
 
     place = jnp.stack([pair, col])
 
-    qkv_own, attn_own = first_deal(qkv_weight, attn_weight)
     col_pack = after(col_pack, qkv_own)
-    gate_own, qkv_rest, attn_rest, up_own, *others = second_deal(
-        qkv_weight, attn_weight, expand_weight, tokens, after(row_pack, qkv_own)
+    qkv_other, attn_other, up_own, *others = second_deal(
+        qkv_weight, attn_weight, expand_weight, tokens, row_pack, cols
     )
     token_parts = [tokens, *others[:3]]
     row_all = jnp.concatenate([row_pack, *others[3:]], axis=1)
@@ -2424,15 +2513,15 @@
     reduce_up = row_all[96:112]
     qkv_all = gather_col(qkv_own)
     attn_all = gather_col(attn_own)
-    gate_all = gather_col(gate_own)
+    gate_all = gather_col(after(gate_own, row_pack))
     up_all = gather_col(up_own)
-    reduce_own, gate_rest, up_rest, qkv_other, attn_other, col_all, gains = third_deal(
+    reduce_own, gate_other, up_other, qkv_other, attn_other, col_all, gains = third_deal(
         expand_weight,
         after(reduce_weight, others[0]),
         qkv_all,
-        qkv_rest,
+        qkv_other,
         attn_all,
-        attn_rest,
+        attn_other,
         col_pack,
         headnorm_gain,
     )
@@ -2463,13 +2552,13 @@
     sine = jnp.sin(angle)
     sine = jnp.concatenate([-sine, sine], axis=1)
 
-    raw, squares, qkv_inner, gate_part = front_call(
-        token_parts, qkv_w, qkv_low, gate_all, gate_rest
+    raw, squares, qkv_inner, gate_other = front_call(
+        token_parts, qkv_w, qkv_low, gate_all, gate_other
     )
     scale = lax.rsqrt(sum_row(squares) / D + EPS)
     query, key, value = rotate_rows(raw, scale, gains, cosine, sine)
     limit = jnp.maximum(jnp.arange(rows, dtype=jnp.int32), prefix - 1)[None]
-    mixed, log_total, branch, hidden, branch_stats, *hidden_parts, gate_other, up_other = branch_call(
+    mixed, branch, hidden, branch_stats, *hidden_parts, gate_other, up_other, probs = branch_call(
         query,
         key,
         value,
@@ -2477,7 +2566,7 @@
         attn_w,
         tokens,
         post_gain,
-        (gate_all, gate_part, up_all, up_rest),
+        (gate_all, gate_other, up_all, up_other),
     )
     expand_w = [
         merge_expand(
@@ -2503,9 +2592,8 @@
         jnp.concatenate(expand_up),
         expand_inner,
     )
-    d_mixed, d_attn_inner = mixed_back(branch_parts, attn_w, attn_up)
-    d_query, d_key, d_value, q_sums, k_sums = attend_back(
-        prefix, query, d_mixed, mixed, log_total, key, value
+    d_query, d_key, d_value, q_sums, k_sums, d_attn_inner = attend_back(
+        query, branch_parts, attn_w, attn_up, mixed, probs, key, value
     )
     partials = jnp.concatenate(
         [dot_of(attn_low, mixed, 1, 1), reduce_inner, d_expand_inner]

time: 883 us -> 870 us (0.985)
  Pallas kernels: 822 us -> 803 us
    pallas_call x2, Pallas kernels: 94.5 us -> 80.6 us  [the longest x1 73.2 us: second_deal(): pl.pallas_call(second_deal_kernel, out_shape=[jax.ShapeDtypeStruct((cols,...]
  transfers between devices with their start and end apart: 7 -> 7, of which waited for: 3 -> 3; matrix products, arithmetic and copies ran while one was open for 2% -> 2% of each run, Pallas kernels for 43% -> 45%
where the time goes in v6:
time: 870 us; the launch traced here: 855 us
  Pallas kernels  803 us (92%)
  other arithmetic  16.3 us (2%)
  between operations  15 us (2%)
  local copies, waits for them, and re-layouts  11.5 us (1%)
    pallas_call x1, Pallas kernels, backward_call(): pl.pallas_call(backward_kernel, out_shape=[jax.ShapeDtypeStruct((rows, wi...  131 us
    pallas_call x1, Pallas kernels, branch_call(): pl.pallas_call(branch_kernel, out_shape=[jax.ShapeDtypeStruct((rows, loca...  127 us
    pallas_call x1, Pallas kernels, forward_call(): pl.pallas_call(forward_kernel, out_shape=[wide] * 3 + [part, jax.ShapeDty...  125 us
    pallas_call x1, Pallas kernels, input_call(): pl.pallas_call(input_kernel, out_shape=[jax.ShapeDtypeStruct((rows, width...  93.9 us
    pallas_call x1, Pallas kernels, third_deal(): pl.pallas_call(third_deal_kernel, out_shape=like_views([(reduce_weight.sh...  74.2 us
    pallas_call x1, Pallas kernels, second_deal(): pl.pallas_call(second_deal_kernel, out_shape=[jax.ShapeDtypeStruct((cols,...  73.2 us
    pallas_call x1, Pallas kernels, attend_back(): pl.pallas_call(attend_back_kernel, out_shape=(jax.ShapeDtypeStruct(query....  49.7 us
    pallas_call x1, Pallas kernels, front_call(): pl.pallas_call(front_kernel, out_shape=[jax.ShapeDtypeStruct((rows, wide)...  30.3 us
  transfers between devices with their start and end apart: 7, of which 3 were waited for; matrix products, arithmetic and copies ran while one was open for 2% of the time, Pallas kernels for 45%

profile of v6, /device:TPU:0, one launch (start us, length us, event | category | flops | bytes accessed | tf_op | source)
XLA Modules:
  0.0 855.2 jit_solution(2762072723139862402)
XLA Ops:
  7.2 7.3 attn_deal.1
  14.7 22.7 %first_deal.1 = (bf16[4,3,256,128]{3,2,1,0:T(8,128)(2,1)}, bf16[4,512,256]{2,1,0:T(8,128)(2,1)}) custom-call(bf16[3,512,512]{2,1,0:T(8,128)(2,1)} %qkv_ref.3, bf16[2,512,2048]{2,1,0:T(8,128)(2,1)} %expand_ref.7), custom_call_target="tpu_custom_call" | custom-call | bytes 67108864 | tf_op jit(solution)/shard_map/first_deal/pallas_call | solution.py:2081
  38.1 2.1 row_pack.1.pack_ref
  40.3 73.2 %second_deal.1 = (bf16[4,4,3,256,128]{4,3,2,1,0:T(8,128)(2,1)}, bf16[4,4,64,512]{3,2,1,0:T(8,128)(2,1)}, bf16[4,512,256]{2,1,0:T(8,128)(2,1)}, bf16[2048,512]{1,...) custom-call(bf16[3,512,512]{2,1,0:T(8,128)(2,1)} %qkv_ref.3, ...), custom_call_target="tpu_custom_call" | custom-call | bytes 134217728 | tf_op jit(solution)/shard_map/second_deal/pallas_call | solution.py:2142
  114.2 3.6 col_pack.1.pack_ref
  117.8 74.2 %third_deal.1 = (bf16[4,512,512]{2,1,0:T(8,128)(2,1)}, bf16[4,4,512,256]{3,2,1,0:T(8,128)(2,1)}, bf16[4,4,512,256]{3,2,1,0:T(8,128)(2,1)}, bf16[4,4,3,256,128]{4...) custom-call(bf16[2,512,2048]{2,1,0:T(8,128)(2,1)} %expand_ref.7, ...), custom_call_target="tpu_custom_call", output_to_operand_aliasing={{3}: (3, {}), {4}: (5, {})} | custom-call | bytes 134217728 | tf_op jit(solution)/shard_map/third_deal/pallas_call | solution.py:2262
  192.1 0.8 copy-done.2
  200.0 3.7 fusion
  203.7 2.0 pad_maximum_fusion
  206.4 9.1 %merge_qkv.1 = bf16[4,2,256,1536]{3,2,1,0:T(8,128)(2,1)} custom-call(s32[2]{0:T(128)} %pad_add_fusion.pair_ref, bf16[4,4,3,256,128]{4,3,2,1,0:T(8,128)(2,1)} %bitcast.79, bf16[4,4,3,256,128]{4,3,2,1,0:T(8,128)(2,1)} %get-tuple-element.96.other_ref, bf16[4,2,48,256]{3,2,1,0:T(8,128)(2,1)} %bitcast.87, bf16[48,512]{1,0:T(8,128)(2,1)} %pad_maximum_fusion.11.up_ref), custom_call_target="tpu_custom_call" | custom-call | bytes 12582912 | tf_op jit(solution)/shard_map/merge_qkv/pallas_call | solution.py:844
  216.1 30.3 %front.1 = (f32[2048,1536]{1,0:T(8,128)}, f32[8,2048]{1,0:T(8,128)}, bf16[48,2048]{1,0:T(8,128)(2,1)}, bf16[4,4,512,256]{3,2,1,0:T(8,128)(2,1)}) custom-call(bf16[2048,512]{1,0:T(8,128)(2,1)} %tokens_hbm.1, bf16[2048,512]{1,0:T(8,128)(2,1)} %get-tuple-element.89.x1, bf16[2048,512]{1,0:T(8,128)(2,1)} %get-tuple-element.90.x2, ...), custom_call_target="tpu_custom_call", output_to_operand_aliasing={{3}: (7, {})} | custom-call | flops 12884901888 | bytes 67108864 | tf_op jit(solution)/shard_map/front/pallas_call | solution.py:2337
  247.2 0.8 collective-permute-done
  248.0 0.8 add.58
  248.8 1.6 collective-permute-start.1
  252.4 7.3 merge_out.2.matrix_ref
  260.4 9.7 %rotate_rows.1 = (bf16[2048,512]{1,0:T(8,128)(2,1)}, bf16[2048,512]{1,0:T(8,128)(2,1)}, bf16[2048,512]{1,0:T(8,128)(2,1)}) custom-call(f32[2048,1536]{1,0:T(8,128)} %get-tuple-element.104.raw_ref.raw_hbm, f32[8,2048]{1,0:T(8,128)} %add_rsqrt_fusion.scale_ref, f32[2,512]{1,0:T(2,128)} %bitcast.102, f32[2048,128]{1,0:T(8,128)} %get-tuple-element.182.cos_ref, ...), custom_call_target="tpu_custom_call" | custom-call | tf_op jit(solution)/shard_map/rotate_rows/pallas_call | solution.py:625
  270.1 5.6 all-gather.17.cloned.1.call-done
  275.7 126.5 %branch.1 = (bf16[2048,512]{1,0:T(8,128)(2,1)}, f32[2048,512]{1,0:T(8,128)}, f32[2048,512]{1,0:T(8,128)}, f32[8,8,256]{2,1,0:T(8,128)}, bf16[2048,512]{1,0:T(8,1...) custom-call(bf16[2048,512]{1,0:T(8,128)(2,1)} %get-tuple-element.107, ...), custom_call_target="tpu_custom_call", output_to_operand_aliasing={{8}: (8, {}), {9}: (10, {})} | custom-call | flops 4294967296 | bytes 134217728 | tf_op jit(solution)/shard_map/branch/pallas_call | solution.py:1251
  402.2 11.1 %merge_expand.3 = bf16[4,1,512,2048]{3,2,1,0:T(8,128)(2,1)} custom-call(s32[2]{0:T(128)} %pad_add_fusion.pair_ref, bf16[4,4,512,256]{3,2,1,0:T(8,128)(2,1)} %bitcast.77, bf16[4,4,512,256]{3,2,1,0:T(8,128)(2,1)} %get-tuple-element.119.other_ref, bf16[4,1,16,512]{3,2,1,0:T(8,128)(2,1)} %bitcast.95, bf16[16,2048]{1,0:T(8,128)(2,1)} %bitcast.91), custom_call_target="tpu_custom_call" | custom-call | bytes 16777216 | tf_op jit(solution)/shard_map/merge_expand/pallas_call | solution.py:879
  413.3 11.3 %merge_expand.2 = bf16[4,1,512,2048]{3,2,1,0:T(8,128)(2,1)} custom-call(s32[2]{0:T(128)} %pad_add_fusion.pair_ref, bf16[4,4,512,256]{3,2,1,0:T(8,128)(2,1)} %bitcast.75, bf16[4,4,512,256]{3,2,1,0:T(8,128)(2,1)} %get-tuple-element.118.other_ref, bf16[4,1,16,512]{3,2,1,0:T(8,128)(2,1)} %bitcast.94, bf16[16,2048]{1,0:T(8,128)(2,1)} %bitcast.89), custom_call_target="tpu_custom_call" | custom-call | bytes 16777216 | tf_op jit(solution)/shard_map/merge_expand/pallas_call | solution.py:879
  425.3 9.0 %merge_out.3.reduce_hbm = bf16[2048,2048]{1,0:T(8,128)(2,1)} custom-call(s32[2]{0:T(128)} %pad_add_fusion.pair_ref, bf16[4,4,512,512]{3,2,1,0:T(8,128)(2,1)} %bitcast.80, bf16[4,16,512]{2,1,0:T(8,128)(2,1)} %get-tuple-element.172.refs_1_, bf16[16,2048]{1,0:T(8,128)(2,1)} %get-tuple-element.162.refs_2_.reduce_up_ref), custom_call_target="tpu_custom_call" | custom-call | bytes 16777216 | tf_op jit(solution)/shard_map/merge_out/pallas_call | solution.py:905
  434.4 125.2 %forward.1 = (bf16[2048,2048]{1,0:T(8,128)(2,1)}, bf16[2048,2048]{1,0:T(8,128)(2,1)}, bf16[2048,2048]{1,0:T(8,128)(2,1)}, bf16[2048,512]{1,0:T(8,128)(2,1)}, bf1...) custom-call(bf16[2048,512]{1,0:T(8,128)(2,1)} %get-tuple-element.114, ...), custom_call_target="tpu_custom_call" | custom-call | flops 51539607552 | bytes 134217728 | tf_op jit(solution)/shard_map/forward/pallas_call | solution.py:1470
  559.5 130.6 %backward.1 = (f32[2048,512]{1,0:T(8,128)}, bf16[16,2048]{1,0:T(8,128)(2,1)}, f32[32,2048]{1,0:T(8,128)}, f32[32,2048]{1,0:T(8,128)}, bf16[2048,512]{1,0:T(8,128...) custom-call(bf16[2048,512]{1,0:T(8,128)(2,1)} %get-tuple-element.123.x0.result_hbm, ...), custom_call_target="tpu_custom_call" | custom-call | flops 51539607552 | bytes 134217728 | tf_op jit(solution)/shard_map/backward/pallas_call | solution.py:1646
  690.2 1.0 convert.11
  691.2 49.7 %attend_back.1 = (f32[2048,512]{1,0:T(8,128)}, f32[2048,512]{1,0:T(8,128)}, f32[2048,512]{1,0:T(8,128)}, f32[4,1,2048]{2,1,0:T(1,128)}, f32[4,1,2048]{2,1,0:T(1,128)}, /*index=5*/bf16[16,2048]{1,0:T(8,128)(2,1)}) custom-call(bf16[2048,512]{1,0:T(8,128)(2,1)} %get-tuple-element.107.q_ref, bf16[2048,512]{1,0:T(8,128)(2,1)} %get-tuple-element.132.x0.branch_hbm, ...), custom_call_target="tpu_custom_call" | custom-call | flops 15032385536 | bytes 25165824 | tf_op jit(solution)/shard_map/attend_back/pallas_call | solution.py:569
  740.9 1.5 pad_maximum_fusion.6.d_inner_ref
  742.4 0.7 pad_maximum_fusion.3.part_ref
  743.2 93.9 %input_grad.1 = (f32[2048,512]{1,0:T(8,128)}, bf16[4,2,112,512]{3,2,1,0:T(8,128)(2,1)}, bf16[4,2,4,16,2048]{4,3,2,1,0:T(8,128)(2,1)}) custom-call(f32[2048,1536]{1,0:T(8,128)} %get-tuple-element.104.raw_ref.raw_hbm, f32[2048,512]{1,0:T(8,128)} %get-tuple-element.138.dq_hbm, f32[2048,512]{1,0:T(8,128)} %get-tuple-element.139.dk_hbm, ...), custom_call_target="tpu_custom_call" | custom-call | flops 12884901888 | bytes 67108864 | tf_op jit(solution)/shard_map/input_grad/pallas_call | solution.py:1931
  837.1 6.5 finish.1
  843.5 1.3 copy.108
  844.8 1.6 copy-done.1
  846.5 2.0 copy.109
  (82 shorter events, 13.4 us)
Async XLA Ops:
  7.2 110.6 %all-gather.13.cloned.1.call-start = ((), (), s32[]{:S(2)}) async-start(), calls=%async_computation.1 | async-start | bytes 1310720 | tf_op jit(solution)/shard_map/all_gather | solution.py:2433
  14.6 22.9 %copy-start.14 = (s32[8]{0:T(128)S(1)}, s32[8]{0:T(128)}, u32[]{:S(2)}) copy-start(s32[8]{0:T(128)} %param.35) | copy-start | bytes 100
  14.6 103.2 %all-gather.11.cloned.1.call-start = ((), (), s32[]{:S(2)}) async-start(), calls=%async_computation | async-start | bytes 3932160 | tf_op jit(solution)/shard_map/all_gather | solution.py:2433
  37.4 178.7 %all-gather.15.cloned.1.call-start = ((), (), s32[]{:S(2)}) async-start(), calls=%async_computation.2 | async-start | bytes 5242880 | tf_op jit(solution)/shard_map/all_gather | solution.py:2433
  40.2 235.5 %all-gather.17.cloned.1.call-start = ((), (), s32[]{:S(2)}) async-start(), calls=%async_computation.3 | async-start | bytes 5242880 | tf_op jit(solution)/shard_map/all_gather | solution.py:2433
  113.5 311.8 %all-gather.19.cloned.1.call-start = ((), (), s32[]{:S(2)}) async-start(), calls=%async_computation.4 | async-start | bytes 10485760 | tf_op jit(solution)/shard_map/all_gather | solution.py:2433
  192.0 0.9 copy-start.2
  192.0 0.9 copy-start.4
  192.0 1.0 copy-start.5
  192.0 1.0 copy-start.6
  192.1 2.0 copy-start.13
  193.2 10.6 %copy-start.7 = (bf16[48,2048]{1,0:T(8,128)(2,1)}, bf16[48,2048]{1,0:T(8,128)(2,1)S(1)}, u32[]{:S(2)}) copy-start(bf16[48,2048]{1,0:T(8,128)(2,1)S(1)} %slice.54.low_ref) | copy-start | bytes 589828
  203.7 2.0 copy-start.10
  246.4 1.5 collective-permute-start
  247.2 12.5 %copy-start.9 = (bf16[4,2,8,512]{3,2,0,1:T(8,128)(2,1)}, bf16[4,2,8,512]{3,2,0,1:T(8,128)(2,1)S(1)}, u32[]{:S(2)}) copy-start(bf16[4,2,8,512]{3,2,0,1:T(8,128)(2,1)S(1)} %copy.82) | copy-start | bytes 196612
  247.2 12.5 %copy-start.8 = (bf16[4,2,8,512]{3,2,0,1:T(8,128)(2,1)}, bf16[4,2,8,512]{3,2,0,1:T(8,128)(2,1)S(1)}, u32[]{:S(2)}) copy-start(bf16[4,2,8,512]{3,2,0,1:T(8,128)(2,1)S(1)} %copy.81) | copy-start | bytes 196612
  248.8 10.9 %collective-permute-start.1 = (f32[8,2048]{1,0:T(8,128)S(1)}, f32[8,2048]{1,0:T(8,128)S(1)}, u32[]{:S(2)}, u32[]{:S(2)}) collective-permute-start(f32[8,2048]{1,0:T(8,128)S(1)} %add.58), channel_id=1, source_target_pairs={{0,8},{4,12},{8,0},{12,4},{1,9},{5,13},{9,1},{13,5},{2,10},{6,14},... | collective-permute-start | bytes 196616 | tf_op jit(solution)/shard_map/ppermute | solution.py:2424
  413.3 11.3 %copy-start = (bf16[2048,512]{1,0:T(8,128)(2,1)S(1)}, bf16[2048,512]{1,0:T(8,128)(2,1)}, u32[]{:S(2)}) copy-start(bf16[2048,512]{1,0:T(8,128)(2,1)} %get-tuple-element.136.out_ref.mixed_hbm) | copy-start | bytes 6291460
  559.5 131.6 %copy-start.11 = (f32[16,2048]{1,0:T(8,128)S(1)}, f32[16,2048]{1,0:T(8,128)}, u32[]{:S(2)}) copy-start(f32[16,2048]{1,0:T(8,128)} %get-tuple-element.146) | copy-start | bytes 393220
  691.2 49.7 %copy-start.12 = (bf16[16,2048]{1,0:T(8,128)(2,1)S(1)}, bf16[16,2048]{1,0:T(8,128)(2,1)}, u32[]{:S(2)}) copy-start(bf16[16,2048]{1,0:T(8,128)(2,1)} %get-tuple-element.149) | copy-start | bytes 196612
  837.0 6.5 copy-start.3
  843.5 2.9 copy-start.1
Sparse Core Ops, SparseCore 0:
  14.7 29.0 all-gather.12
  45.4 62.9 all-gather.10
  110.0 84.9 all-gather.14
  196.4 79.2 all-gather.16
  277.1 148.1 all-gather.18

commit v7 on v6

--- a/solution.py
+++ b/solution.py
@@ -1080,7 +1080,7 @@
             stage(t - 3, normalise)
             stage(t - 4, pass_on)
         if idle is not None:
-            pl.when(t >= 1)(lambda: idle(t - 1))
+            pl.when(t >= 2)(lambda: idle(t - 2))
         return carry
 
     lax.fori_loop(0, count + (4 if gathers else 2), body, 0)

time: 870 us -> 869 us (level)
  no operation moved by 1% of the time
where the time goes in v7:
time: 869 us; the launch traced here: 855 us
  Pallas kernels  803 us (92%)
  other arithmetic  16.3 us (2%)
  between operations  15 us (2%)
  local copies, waits for them, and re-layouts  11.5 us (1%)
    pallas_call x1, Pallas kernels, backward_call(): pl.pallas_call(backward_kernel, out_shape=[jax.ShapeDtypeStruct((rows, wi...  131 us
    pallas_call x1, Pallas kernels, branch_call(): pl.pallas_call(branch_kernel, out_shape=[jax.ShapeDtypeStruct((rows, loca...  127 us
    pallas_call x1, Pallas kernels, forward_call(): pl.pallas_call(forward_kernel, out_shape=[wide] * 3 + [part, jax.ShapeDty...  125 us
    pallas_call x1, Pallas kernels, input_call(): pl.pallas_call(input_kernel, out_shape=[jax.ShapeDtypeStruct((rows, width...  93.9 us
    pallas_call x1, Pallas kernels, third_deal(): pl.pallas_call(third_deal_kernel, out_shape=like_views([(reduce_weight.sh...  74.2 us
    pallas_call x1, Pallas kernels, second_deal(): pl.pallas_call(second_deal_kernel, out_shape=[jax.ShapeDtypeStruct((cols,...  73.2 us
    pallas_call x1, Pallas kernels, attend_back(): pl.pallas_call(attend_back_kernel, out_shape=(jax.ShapeDtypeStruct(query....  49.7 us
    pallas_call x1, Pallas kernels, front_call(): pl.pallas_call(front_kernel, out_shape=[jax.ShapeDtypeStruct((rows, wide)...  30.3 us
  transfers between devices with their start and end apart: 7, of which 3 were waited for; matrix products, arithmetic and copies ran while one was open for 2% of the time, Pallas kernels for 45%

profile of v7, /device:TPU:0, one launch (start us, length us, event | category | flops | bytes accessed | tf_op | source)
XLA Modules:
  0.0 855.2 jit_solution(10598606575895602691)
XLA Ops:
  7.2 7.3 attn_deal.1
  14.7 22.7 %first_deal.1 = (bf16[4,3,256,128]{3,2,1,0:T(8,128)(2,1)}, bf16[4,512,256]{2,1,0:T(8,128)(2,1)}) custom-call(bf16[3,512,512]{2,1,0:T(8,128)(2,1)} %qkv_ref.3, bf16[2,512,2048]{2,1,0:T(8,128)(2,1)} %expand_ref.7), custom_call_target="tpu_custom_call" | custom-call | bytes 67108864 | tf_op jit(solution)/shard_map/first_deal/pallas_call | solution.py:2081
  38.1 2.1 row_pack.1.pack_ref
  40.3 73.2 %second_deal.1 = (bf16[4,4,3,256,128]{4,3,2,1,0:T(8,128)(2,1)}, bf16[4,4,64,512]{3,2,1,0:T(8,128)(2,1)}, bf16[4,512,256]{2,1,0:T(8,128)(2,1)}, bf16[2048,512]{1,...) custom-call(bf16[3,512,512]{2,1,0:T(8,128)(2,1)} %qkv_ref.3, ...), custom_call_target="tpu_custom_call" | custom-call | bytes 134217728 | tf_op jit(solution)/shard_map/second_deal/pallas_call | solution.py:2142
  114.2 3.6 col_pack.1.pack_ref
  117.8 74.2 %third_deal.1 = (bf16[4,512,512]{2,1,0:T(8,128)(2,1)}, bf16[4,4,512,256]{3,2,1,0:T(8,128)(2,1)}, bf16[4,4,512,256]{3,2,1,0:T(8,128)(2,1)}, bf16[4,4,3,256,128]{4...) custom-call(bf16[2,512,2048]{2,1,0:T(8,128)(2,1)} %expand_ref.7, ...), custom_call_target="tpu_custom_call", output_to_operand_aliasing={{3}: (3, {}), {4}: (5, {})} | custom-call | bytes 134217728 | tf_op jit(solution)/shard_map/third_deal/pallas_call | solution.py:2262
  192.1 0.8 copy-done.2
  200.0 3.7 fusion
  203.7 2.0 pad_maximum_fusion
  206.4 9.1 %merge_qkv.1 = bf16[4,2,256,1536]{3,2,1,0:T(8,128)(2,1)} custom-call(s32[2]{0:T(128)} %pad_add_fusion.pair_ref, bf16[4,4,3,256,128]{4,3,2,1,0:T(8,128)(2,1)} %bitcast.79, bf16[4,4,3,256,128]{4,3,2,1,0:T(8,128)(2,1)} %get-tuple-element.96.other_ref, bf16[4,2,48,256]{3,2,1,0:T(8,128)(2,1)} %bitcast.87, bf16[48,512]{1,0:T(8,128)(2,1)} %pad_maximum_fusion.11.up_ref), custom_call_target="tpu_custom_call" | custom-call | bytes 12582912 | tf_op jit(solution)/shard_map/merge_qkv/pallas_call | solution.py:844
  216.1 30.3 %front.1 = (f32[2048,1536]{1,0:T(8,128)}, f32[8,2048]{1,0:T(8,128)}, bf16[48,2048]{1,0:T(8,128)(2,1)}, bf16[4,4,512,256]{3,2,1,0:T(8,128)(2,1)}) custom-call(bf16[2048,512]{1,0:T(8,128)(2,1)} %tokens_hbm.1, bf16[2048,512]{1,0:T(8,128)(2,1)} %get-tuple-element.89.x1, bf16[2048,512]{1,0:T(8,128)(2,1)} %get-tuple-element.90.x2, ...), custom_call_target="tpu_custom_call", output_to_operand_aliasing={{3}: (7, {})} | custom-call | flops 12884901888 | bytes 67108864 | tf_op jit(solution)/shard_map/front/pallas_call | solution.py:2337
  247.2 0.8 collective-permute-done
  248.0 0.8 add.58
  248.8 1.6 collective-permute-start.1
  252.4 7.3 merge_out.2.matrix_ref
  260.4 9.7 %rotate_rows.1 = (bf16[2048,512]{1,0:T(8,128)(2,1)}, bf16[2048,512]{1,0:T(8,128)(2,1)}, bf16[2048,512]{1,0:T(8,128)(2,1)}) custom-call(f32[2048,1536]{1,0:T(8,128)} %get-tuple-element.104.raw_ref.raw_hbm, f32[8,2048]{1,0:T(8,128)} %add_rsqrt_fusion.scale_ref, f32[2,512]{1,0:T(2,128)} %bitcast.102, f32[2048,128]{1,0:T(8,128)} %get-tuple-element.182.cos_ref, ...), custom_call_target="tpu_custom_call" | custom-call | tf_op jit(solution)/shard_map/rotate_rows/pallas_call | solution.py:625
  270.1 5.6 all-gather.17.cloned.1.call-done
  275.7 126.5 %branch.1 = (bf16[2048,512]{1,0:T(8,128)(2,1)}, f32[2048,512]{1,0:T(8,128)}, f32[2048,512]{1,0:T(8,128)}, f32[8,8,256]{2,1,0:T(8,128)}, bf16[2048,512]{1,0:T(8,1...) custom-call(bf16[2048,512]{1,0:T(8,128)(2,1)} %get-tuple-element.107, ...), custom_call_target="tpu_custom_call", output_to_operand_aliasing={{8}: (8, {}), {9}: (10, {})} | custom-call | flops 4294967296 | bytes 134217728 | tf_op jit(solution)/shard_map/branch/pallas_call | solution.py:1251
  402.2 11.1 %merge_expand.3 = bf16[4,1,512,2048]{3,2,1,0:T(8,128)(2,1)} custom-call(s32[2]{0:T(128)} %pad_add_fusion.pair_ref, bf16[4,4,512,256]{3,2,1,0:T(8,128)(2,1)} %bitcast.77, bf16[4,4,512,256]{3,2,1,0:T(8,128)(2,1)} %get-tuple-element.119.other_ref, bf16[4,1,16,512]{3,2,1,0:T(8,128)(2,1)} %bitcast.95, bf16[16,2048]{1,0:T(8,128)(2,1)} %bitcast.91), custom_call_target="tpu_custom_call" | custom-call | bytes 16777216 | tf_op jit(solution)/shard_map/merge_expand/pallas_call | solution.py:879
  413.3 11.3 %merge_expand.2 = bf16[4,1,512,2048]{3,2,1,0:T(8,128)(2,1)} custom-call(s32[2]{0:T(128)} %pad_add_fusion.pair_ref, bf16[4,4,512,256]{3,2,1,0:T(8,128)(2,1)} %bitcast.75, bf16[4,4,512,256]{3,2,1,0:T(8,128)(2,1)} %get-tuple-element.118.other_ref, bf16[4,1,16,512]{3,2,1,0:T(8,128)(2,1)} %bitcast.94, bf16[16,2048]{1,0:T(8,128)(2,1)} %bitcast.89), custom_call_target="tpu_custom_call" | custom-call | bytes 16777216 | tf_op jit(solution)/shard_map/merge_expand/pallas_call | solution.py:879
  425.3 9.0 %merge_out.3.reduce_hbm = bf16[2048,2048]{1,0:T(8,128)(2,1)} custom-call(s32[2]{0:T(128)} %pad_add_fusion.pair_ref, bf16[4,4,512,512]{3,2,1,0:T(8,128)(2,1)} %bitcast.80, bf16[4,16,512]{2,1,0:T(8,128)(2,1)} %get-tuple-element.172.refs_1_, bf16[16,2048]{1,0:T(8,128)(2,1)} %get-tuple-element.162.refs_2_.reduce_up_ref), custom_call_target="tpu_custom_call" | custom-call | bytes 16777216 | tf_op jit(solution)/shard_map/merge_out/pallas_call | solution.py:905
  434.4 125.2 %forward.1 = (bf16[2048,2048]{1,0:T(8,128)(2,1)}, bf16[2048,2048]{1,0:T(8,128)(2,1)}, bf16[2048,2048]{1,0:T(8,128)(2,1)}, bf16[2048,512]{1,0:T(8,128)(2,1)}, bf1...) custom-call(bf16[2048,512]{1,0:T(8,128)(2,1)} %get-tuple-element.114, ...), custom_call_target="tpu_custom_call" | custom-call | flops 51539607552 | bytes 134217728 | tf_op jit(solution)/shard_map/forward/pallas_call | solution.py:1470
  559.5 130.6 %backward.1 = (f32[2048,512]{1,0:T(8,128)}, bf16[16,2048]{1,0:T(8,128)(2,1)}, f32[32,2048]{1,0:T(8,128)}, f32[32,2048]{1,0:T(8,128)}, bf16[2048,512]{1,0:T(8,128...) custom-call(bf16[2048,512]{1,0:T(8,128)(2,1)} %get-tuple-element.123.x0.result_hbm, ...), custom_call_target="tpu_custom_call" | custom-call | flops 51539607552 | bytes 134217728 | tf_op jit(solution)/shard_map/backward/pallas_call | solution.py:1646
  690.2 1.0 convert.11
  691.2 49.7 %attend_back.1 = (f32[2048,512]{1,0:T(8,128)}, f32[2048,512]{1,0:T(8,128)}, f32[2048,512]{1,0:T(8,128)}, f32[4,1,2048]{2,1,0:T(1,128)}, f32[4,1,2048]{2,1,0:T(1,128)}, /*index=5*/bf16[16,2048]{1,0:T(8,128)(2,1)}) custom-call(bf16[2048,512]{1,0:T(8,128)(2,1)} %get-tuple-element.107.q_ref, bf16[2048,512]{1,0:T(8,128)(2,1)} %get-tuple-element.132.x0.branch_hbm, ...), custom_call_target="tpu_custom_call" | custom-call | flops 15032385536 | bytes 25165824 | tf_op jit(solution)/shard_map/attend_back/pallas_call | solution.py:569
  740.9 1.5 pad_maximum_fusion.6.d_inner_ref
  742.4 0.7 pad_maximum_fusion.3.part_ref
  743.2 93.9 %input_grad.1 = (f32[2048,512]{1,0:T(8,128)}, bf16[4,2,112,512]{3,2,1,0:T(8,128)(2,1)}, bf16[4,2,4,16,2048]{4,3,2,1,0:T(8,128)(2,1)}) custom-call(f32[2048,1536]{1,0:T(8,128)} %get-tuple-element.104.raw_ref.raw_hbm, f32[2048,512]{1,0:T(8,128)} %get-tuple-element.138.dq_hbm, f32[2048,512]{1,0:T(8,128)} %get-tuple-element.139.dk_hbm, ...), custom_call_target="tpu_custom_call" | custom-call | flops 12884901888 | bytes 67108864 | tf_op jit(solution)/shard_map/input_grad/pallas_call | solution.py:1931
  837.1 6.5 finish.1
  843.5 1.3 copy.108
  844.8 1.6 copy-done.1
  846.5 2.0 copy.109
  (82 shorter events, 13.4 us)
Async XLA Ops:
  7.2 110.6 %all-gather.13.cloned.1.call-start = ((), (), s32[]{:S(2)}) async-start(), calls=%async_computation.1 | async-start | bytes 1310720 | tf_op jit(solution)/shard_map/all_gather | solution.py:2433
  14.6 22.9 %copy-start.14 = (s32[8]{0:T(128)S(1)}, s32[8]{0:T(128)}, u32[]{:S(2)}) copy-start(s32[8]{0:T(128)} %param.35) | copy-start | bytes 100
  14.6 103.2 %all-gather.11.cloned.1.call-start = ((), (), s32[]{:S(2)}) async-start(), calls=%async_computation | async-start | bytes 3932160 | tf_op jit(solution)/shard_map/all_gather | solution.py:2433
  37.4 178.7 %all-gather.15.cloned.1.call-start = ((), (), s32[]{:S(2)}) async-start(), calls=%async_computation.2 | async-start | bytes 5242880 | tf_op jit(solution)/shard_map/all_gather | solution.py:2433
  40.2 235.5 %all-gather.17.cloned.1.call-start = ((), (), s32[]{:S(2)}) async-start(), calls=%async_computation.3 | async-start | bytes 5242880 | tf_op jit(solution)/shard_map/all_gather | solution.py:2433
  113.5 311.8 %all-gather.19.cloned.1.call-start = ((), (), s32[]{:S(2)}) async-start(), calls=%async_computation.4 | async-start | bytes 10485760 | tf_op jit(solution)/shard_map/all_gather | solution.py:2433
  192.0 0.9 copy-start.2
  192.0 0.9 copy-start.4
  192.0 1.0 copy-start.5
  192.0 1.0 copy-start.6
  192.1 2.0 copy-start.13
  193.2 10.6 %copy-start.7 = (bf16[48,2048]{1,0:T(8,128)(2,1)}, bf16[48,2048]{1,0:T(8,128)(2,1)S(1)}, u32[]{:S(2)}) copy-start(bf16[48,2048]{1,0:T(8,128)(2,1)S(1)} %slice.54.low_ref) | copy-start | bytes 589828
  203.7 2.0 copy-start.10
  246.4 1.5 collective-permute-start
  247.2 12.5 %copy-start.9 = (bf16[4,2,8,512]{3,2,0,1:T(8,128)(2,1)}, bf16[4,2,8,512]{3,2,0,1:T(8,128)(2,1)S(1)}, u32[]{:S(2)}) copy-start(bf16[4,2,8,512]{3,2,0,1:T(8,128)(2,1)S(1)} %copy.82) | copy-start | bytes 196612
  247.2 12.5 %copy-start.8 = (bf16[4,2,8,512]{3,2,0,1:T(8,128)(2,1)}, bf16[4,2,8,512]{3,2,0,1:T(8,128)(2,1)S(1)}, u32[]{:S(2)}) copy-start(bf16[4,2,8,512]{3,2,0,1:T(8,128)(2,1)S(1)} %copy.81) | copy-start | bytes 196612
  248.8 10.9 %collective-permute-start.1 = (f32[8,2048]{1,0:T(8,128)S(1)}, f32[8,2048]{1,0:T(8,128)S(1)}, u32[]{:S(2)}, u32[]{:S(2)}) collective-permute-start(f32[8,2048]{1,0:T(8,128)S(1)} %add.58), channel_id=1, source_target_pairs={{0,8},{4,12},{8,0},{12,4},{1,9},{5,13},{9,1},{13,5},{2,10},{6,14},... | collective-permute-start | bytes 196616 | tf_op jit(solution)/shard_map/ppermute | solution.py:2424
  413.3 11.3 %copy-start = (bf16[2048,512]{1,0:T(8,128)(2,1)S(1)}, bf16[2048,512]{1,0:T(8,128)(2,1)}, u32[]{:S(2)}) copy-start(bf16[2048,512]{1,0:T(8,128)(2,1)} %get-tuple-element.136.out_ref.mixed_hbm) | copy-start | bytes 6291460
  559.5 131.6 %copy-start.11 = (f32[16,2048]{1,0:T(8,128)S(1)}, f32[16,2048]{1,0:T(8,128)}, u32[]{:S(2)}) copy-start(f32[16,2048]{1,0:T(8,128)} %get-tuple-element.146) | copy-start | bytes 393220
  691.2 49.7 %copy-start.12 = (bf16[16,2048]{1,0:T(8,128)(2,1)S(1)}, bf16[16,2048]{1,0:T(8,128)(2,1)}, u32[]{:S(2)}) copy-start(bf16[16,2048]{1,0:T(8,128)(2,1)} %get-tuple-element.149) | copy-start | bytes 196612
  837.0 6.5 copy-start.3
  843.5 2.9 copy-start.1
Sparse Core Ops, SparseCore 0:
  14.7 29.0 all-gather.12
  45.4 62.9 all-gather.10
  110.0 84.9 all-gather.14
  196.4 79.2 all-gather.16
  277.1 148.1 all-gather.18
